TPU v7x, 32 devices: a whole 2x2x4 slice. The times are simulated.
32 devices in a mesh: row: 4 (over z), col: 4 (over x, core), filt: 2 (over y).
Axes of the slice: x: 2, y: 2, z: 4, core: 2. Of those that a mesh axis runs over, the one named last changes fastest.
Arguments:
- features: bfloat16 [512, 64, 512], P('filt', 'row', 'col'), may hold values from -6 to 6
- kernel: bfloat16 [3, 3, 512, 512], replicated, may hold values from -0.09375 to 0.09375
- bias: float32 [512], replicated, may hold values from -3 to 3
Outputs:
- convolved: bfloat16 [512, 64, 512], P('filt', 'row', 'col')
All inputs are finite; a program needn't handle non-finite values.
Results may differ from a plain program's by a relative error of at most 0.001.
Values may be sent and summed in bfloat16 or wider, within the bound.
No kernel may reach another device: no remote copies, remote signals or barrier semaphores. Data moves between devices by JAX's collectives and lax.ppermute only.
A program may use at most 64 MiB of HBM per device.

v0:
```python
import jax
import jax.numpy as jnp
from jax import lax
from jax.sharding import PartitionSpec as P


def padded_2(block, sides, width):
    for axis, dim in sides:
        count = lax.axis_size(axis)
        forward = [(i, i + 1) for i in range(count - 1)]
        backward = [(target, source) for source, target in forward]
        low = lax.ppermute(
            lax.slice_in_dim(block, block.shape[dim] - width, None, axis=dim), axis, forward
        )
        high = lax.ppermute(lax.slice_in_dim(block, 0, width, axis=dim), axis, backward)
        block = jnp.concatenate([low, block, high], axis=dim)
    return block


def spread(value, axis, source):
    kept = jnp.where(lax.axis_index(axis) == source, value, 0).astype(value.dtype)
    return lax.psum(kept, axis)


def convolve(padded, weights):
    return lax.conv_general_dilated(
        padded[None],
        weights,
        (1, 1),
        "VALID",
        dimension_numbers=("NCHW", "HWIO", "NCHW"),
        preferred_element_type=jnp.float32,
    )[0]


def body(features, kernel, bias):
    groups = lax.axis_size("filt")
    slab = features.shape[0]
    width_out = kernel.shape[3] // groups
    owner = lax.axis_index("filt")
    own_kernel = lax.dynamic_slice_in_dim(kernel, owner * width_out, width_out, 3)
    own_bias = lax.dynamic_slice_in_dim(bias, owner * width_out, width_out, 0)[:, None, None]
    empty = jnp.zeros((width_out, features.shape[1], features.shape[2]), jnp.float32)
    padded = padded_2(features, (("row", 1), ("col", 2)), 1)

    def one_turn(index, total):
        incoming = spread(padded, "filt", index)
        weights = lax.dynamic_slice_in_dim(own_kernel, index * slab, slab, 2)
        return total + convolve(incoming, weights)

    total = lax.fori_loop(0, groups, one_turn, empty)
    return (total + own_bias).astype(jnp.bfloat16)


def solution(mesh):
    return jax.shard_map(
        body,
        mesh=mesh,
        in_specs=(P("filt", "row", "col"), P(), P()),
        out_specs=P("filt", "row", "col"),
        check_vma=False,
    )
```

profile of v0, /device:TPU:0, one launch (start us, length us, event | category | flops | bytes accessed | tf_op | source)
XLA Modules:
  0.0 156.9 jit_solution(2922200560185519218)
XLA Ops:
  6.5 1.6 %copy.7 = bf16[256,16,128]{0,2,1:T(8,128)(2,1)S(1)} copy(bf16[256,16,128]{2,1,0:T(8,128)(2,1)} %param.5) | data formatting | bytes 2097152 | tf_op args[0]
  8.2 4.9 %collective-permute-start = (bf16[256,1,128]{0,2,1:T(8,128)(2,1)S(1)}, bf16[256,1,128]{0,2,1:T(8,128)(2,1)S(1)}, u32[]{:S(2)}, u32[]{:S(2)}) collective-permute-start(bf16[256,1,128]{0,2,1:T(8,128)(2,1)S(1)} %get-tuple-element.141), channel_id=1, source_target_pairs={{0,8},{8,16},{16,24},{1,9},{9,17},{17,25},{2,10},{10,18},{18,26},{... | collective-permute-start | bytes 196616 | tf_op jit(solution)/shard_map/ppermute | solution.py:12
  13.1 1.3 collective-permute-start.1
  14.4 0.6 collective-permute-done
  15.0 4.3 %collective-permute-done.1 = bf16[256,1,128]{0,2,1:T(8,128)(2,1)S(1)} collective-permute-done((bf16[256,1,128]{0,2,1:T(8,128)(2,1)S(1)}, bf16[256,1,128]{0,2,1:T(8,128)(2,1)S(1)}, u32[]{:S(2)}, u32[]{:S(2)}) %collective-permute-start.1) | collective-permute-done | bytes 65568 | tf_op jit(solution)/shard_map/ppermute | solution.py:15
  19.3 1.3 collective-permute-start.2
  20.6 0.0 copy-start.3
  20.6 1.3 collective-permute-start.3
  21.9 3.2 %constant_dynamic-slice_fusion = bf16[3,3,512,256]{3,2,1,0:T(8,128)(2,1)} fusion(bf16[3,3,512,512]{3,2,1,0:T(8,128)(2,1)} %param.6, s32[]{:T(128)S(6)} %select_n.36), kind=kLoop, calls=%fused_computation.22 | loop fusion | bytes 4718596 | tf_op jit(solution)/shard_map/dynamic_slice | solution.py:41
  25.2 0.0 copy-done.3
  25.2 0.1 dynamic_slice.17
  25.3 0.0 collective-permute-done.2
  25.3 0.2 collective-permute-done.3
  25.4 1.8 %pad_maximum_fusion = bf16[256,18,130]{0,2,1:T(8,128)(2,1)} fusion(bf16[256,18,1]{0,2,1:T(2,128)(2,1)S(1)} %collective-permute-done.3, bf16[256,1,128]{0,2,1:T(8,128)(2,1)S(1)} %collective-permute-done.1, bf16[256,16,128]{0,2,1:T(8,128)(2,1)S(1)} %copy.7, bf16[256,1,128]{0,2,1:T(8,128)(2,1)S(1)} %collective-permute-done, ...), kind=kLoop, calls=%fused_computation.18 | loop fusion | flops 5990400 | bytes 2396160 | tf_op jit(solution)/shard_map/concatenate | solution.py:16
  27.2 0.0 copy-done.4
  27.2 119.0 %while.16 = (s32[]{:T(128)}, f32[256,16,128]{0,1,2:T(8,128)}, bf16[256,18,130]{0,2,1:T(8,128)(2,1)}, bf16[3,3,512,256]{3,2,1,0:T(8,128)(2,1)}, s32[]{:T(128)}, /...) while((s32[]{:T(128)}, f32[256,16,128]{0,1,2:T(8,128)}, ...), condition=%wide.region_2.3_spmd.clone, body=%wide.region_0.2_spmd.clone.sunk | while | flops 2573920256 | bytes 59192640 | solution.py:51
  27.2 0.0 all-reduce.2.cloned.1.call-start
  27.2 2.4 %select_bitcast_fusion.2 = bf16[1,256,18,130]{1,3,2,0:T(8,128)(2,1)} fusion(bf16[256,18,130]{0,2,1:T(8,128)(2,1)} %get-tuple-element.192, pred[]{:T(512)S(6)} %eq.12), kind=kLoop, calls=%fused_computation.10.clone.1 | loop fusion | flops 599040 | bytes 2396161 | tf_op jit(solution)/shard_map/while/body/eval_jaxpr/broadcast_in_dim | solution.py:27
  29.6 0.0 all-reduce.2.cloned.1.call-update
  29.7 48.3 %all-reduce.2.cloned.1.call-done = bf16[1,256,18,130]{1,3,2,0:T(8,128)(2,1)} async-done(((bf16[1,256,18,130]{1,3,2,0:T(8,128)(2,1)}), bf16[1,256,18,130]{1,3,2,0:T(8,128)(2,1)}) %all-reduce.2.cloned.1.call-update) | async-done | bytes 1198096 | tf_op jit(solution)/shard_map/while/body/eval_jaxpr/psum | solution.py:22
  77.9 1.4 pad.47
  79.3 0.5 reshape.17
  79.8 0.0 copy-start.2
  79.8 0.3 copy.13
  80.2 1.3 copy-done.2
  81.5 3.0 %convolution_select_fusion.2 = f32[16,8,17,256]{3,1,2,0:T(8,128)S(1)} fusion(bf16[256,18,1,7,2]{0,3,4,1,2:T(8,128)(2,1)S(1)} %slice.32, bf16[256,18,1,8,17]{0,3,4,1,2:T(8,128)(2,1)S(1)} %copy.13, bf16[3,3,512,256]{3,2,1,0:T(8,128)(2,1)S(1)} %copy-done.2, s32[]{:T(128)S(6)} %select_n.47, pred[8,17]{0,1:T(8,128)(4,1)S(1)} %get-tuple-element.200), kind=kOutput, calls=%fused_computation.4.clone.1 | convolution fusion | flops 2571673600 | bytes 4811780 | tf_op jit(solution)/shard_map/while/body/eval_jaxpr/conv_general_dilated | solution.py:26
  84.5 0.0 copy-start
  84.5 0.7 copy.14
  85.3 0.9 copy-done
  86.1 0.7 fusion.20
  86.8 0.0 copy-start.1
  86.8 1.3 copy-done.1
  88.1 0.0 all-reduce.2.cloned.1.call-start
  88.1 1.1 select_bitcast_fusion.2
  89.3 0.0 all-reduce.2.cloned.1.call-update
  89.3 46.7 %all-reduce.2.cloned.1.call-done = bf16[1,256,18,130]{1,3,2,0:T(8,128)(2,1)} async-done(((bf16[1,256,18,130]{1,3,2,0:T(8,128)(2,1)}), bf16[1,256,18,130]{1,3,2,0:T(8,128)(2,1)}) %all-reduce.2.cloned.1.call-update) | async-done | bytes 1198096 | tf_op jit(solution)/shard_map/while/body/eval_jaxpr/psum | solution.py:22
  136.0 1.4 pad.47
  137.4 0.5 reshape.17
  137.9 0.0 copy-start.2
  137.9 0.3 copy.13
  138.2 1.3 copy-done.2
  139.5 3.0 %convolution_select_fusion.2 = f32[16,8,17,256]{3,1,2,0:T(8,128)S(1)} fusion(bf16[256,18,1,7,2]{0,3,4,1,2:T(8,128)(2,1)S(1)} %slice.32, bf16[256,18,1,8,17]{0,3,4,1,2:T(8,128)(2,1)S(1)} %copy.13, bf16[3,3,512,256]{3,2,1,0:T(8,128)(2,1)S(1)} %copy-done.2, s32[]{:T(128)S(6)} %select_n.47, pred[8,17]{0,1:T(8,128)(4,1)S(1)} %get-tuple-element.200), kind=kOutput, calls=%fused_computation.4.clone.1 | convolution fusion | flops 2571673600 | bytes 4811780 | tf_op jit(solution)/shard_map/while/body/eval_jaxpr/conv_general_dilated | solution.py:26
  142.6 0.7 copy.14
  143.3 0.9 copy-done
  144.2 0.7 fusion.20
  144.9 1.3 copy-done.1
  146.2 2.5 %copy.10 = f32[256,16,128]{2,1,0:T(8,128)S(1)} copy(f32[256,16,128]{0,1,2:T(8,128)} %get-tuple-element.115) | data formatting | bytes 4194304 | tf_op jit(solution)/shard_map/while | solution.py:51
  148.7 1.3 add_convert_fusion
  (8 shorter events, 0.1 us)
Async XLA Ops:
  8.2 6.8 %collective-permute-start = (bf16[256,1,128]{0,2,1:T(8,128)(2,1)S(1)}, bf16[256,1,128]{0,2,1:T(8,128)(2,1)S(1)}, u32[]{:S(2)}, u32[]{:S(2)}) collective-permute-start(bf16[256,1,128]{0,2,1:T(8,128)(2,1)S(1)} %get-tuple-element.141), channel_id=1, source_target_pairs={{0,8},{8,16},{16,24},{1,9},{9,17},{17,25},{2,10},{10,18},{18,26},{... | collective-permute-start | bytes 196616 | tf_op jit(solution)/shard_map/ppermute | solution.py:12
  13.1 6.2 %collective-permute-start.1 = (bf16[256,1,128]{0,2,1:T(8,128)(2,1)S(1)}, bf16[256,1,128]{0,2,1:T(8,128)(2,1)S(1)}, u32[]{:S(2)}, u32[]{:S(2)}) collective-permute-start(bf16[256,1,128]{0,2,1:T(8,128)(2,1)S(1)} %get-tuple-element.142), channel_id=1, source_target_pairs={{8,0},{16,8},{24,16},{9,1},{17,9},{25,17},{10,2},{18,10},{26,18},{... | collective-permute-start | bytes 196616 | tf_op jit(solution)/shard_map/ppermute | solution.py:15
  19.3 5.9 %collective-permute-start.2 = (bf16[256,18,1]{0,2,1:T(2,128)(2,1)S(1)}, bf16[256,18,1]{0,2,1:T(2,128)(2,1)S(1)}, u32[]{:S(2)}, u32[]{:S(2)}) collective-permute-start(bf16[256,18,1]{0,2,1:T(2,128)(2,1)S(1)} %get-tuple-element.139), channel_id=1, source_target_pairs={{0,2},{2,4},{4,6},{1,3},{3,5},{5,7},{8,10},{10,12},{12,14},{9,11},... | collective-permute-start | bytes 27656 | tf_op jit(solution)/shard_map/ppermute | solution.py:12
  20.6 4.6 %copy-start.3 = (f32[512]{0:T(512)S(1)}, f32[512]{0:T(512)}, u32[]{:S(2)}) copy-start(f32[512]{0:T(512)} %param.7) | copy-start | bytes 6148
  20.6 4.8 %collective-permute-start.3 = (bf16[256,18,1]{0,2,1:T(2,128)(2,1)S(1)}, bf16[256,18,1]{0,2,1:T(2,128)(2,1)S(1)}, u32[]{:S(2)}, u32[]{:S(2)}) collective-permute-start(bf16[256,18,1]{0,2,1:T(2,128)(2,1)S(1)} %get-tuple-element.140), channel_id=1, source_target_pairs={{2,0},{4,2},{6,4},{3,1},{5,3},{7,5},{10,8},{12,10},{14,12},{11,9},... | collective-permute-start | bytes 27656 | tf_op jit(solution)/shard_map/ppermute | solution.py:15
  25.2 2.0 %copy-start.4 = (pred[8,17]{0,1:T(8,128)(4,1)S(1)}, pred[8,17]{0,1:T(8,128)(4,1)}, u32[]{:S(2)}) copy-start(pred[8,17]{0,1:T(8,128)(4,1)} %constant.106) | copy-start | bytes 412
  27.2 50.7 %all-reduce.2.cloned.1.call-start = ((), (), s32[]{:S(2)}) async-start(), calls=%async_computation | async-start | bytes 2506752 | tf_op jit(solution)/shard_map/while/body/eval_jaxpr/psum | solution.py:22
  79.8 1.7 %copy-start.2 = (bf16[3,3,512,256]{3,2,1,0:T(8,128)(2,1)S(1)}, bf16[3,3,512,256]{3,2,1,0:T(8,128)(2,1)}, u32[]{:S(2)}) copy-start(bf16[3,3,512,256]{3,2,1,0:T(8,128)(2,1)} %get-tuple-element.193) | copy-start | bytes 7077892 | tf_op jit(solution)/shard_map/while
  84.5 1.6 %copy-start = (f32[256,16,128]{0,1,2:T(8,128)S(1)}, f32[256,16,128]{0,1,2:T(8,128)}, u32[]{:S(2)}) copy-start(f32[256,16,128]{0,1,2:T(8,128)} %get-tuple-element.180) | copy-start | bytes 6291460 | tf_op jit(solution)/shard_map/while
  86.8 1.3 copy-start.1
  88.1 47.9 %all-reduce.2.cloned.1.call-start = ((), (), s32[]{:S(2)}) async-start(), calls=%async_computation | async-start | bytes 2506752 | tf_op jit(solution)/shard_map/while/body/eval_jaxpr/psum | solution.py:22
  137.9 1.7 %copy-start.2 = (bf16[3,3,512,256]{3,2,1,0:T(8,128)(2,1)S(1)}, bf16[3,3,512,256]{3,2,1,0:T(8,128)(2,1)}, u32[]{:S(2)}) copy-start(bf16[3,3,512,256]{3,2,1,0:T(8,128)(2,1)} %get-tuple-element.193) | copy-start | bytes 7077892 | tf_op jit(solution)/shard_map/while
  142.6 1.6 %copy-start = (f32[256,16,128]{0,1,2:T(8,128)S(1)}, f32[256,16,128]{0,1,2:T(8,128)}, u32[]{:S(2)}) copy-start(f32[256,16,128]{0,1,2:T(8,128)} %get-tuple-element.180) | copy-start | bytes 6291460 | tf_op jit(solution)/shard_map/while
  144.9 1.3 copy-start.1
Sparse Core Ops, SparseCore 0:
  30.3 47.5 all-reduce.1
  91.3 44.6 all-reduce.1
where the time goes:
time: 157 us
  waiting for transfers between devices  100 us (64%)
  local copies, waits for them, and re-layouts  20.3 us (13%)
  between operations  13.5 us (9%)
  starting transfers between devices  8.81 us (6%)
  other arithmetic  8.11 us (5%)
  matrix products  6.04 us (4%)
    psum x2, waiting for transfers between devices, spread(): return lax.psum(kept, axis)  95 us
    while x12, local copies, waits for them, and re-layouts  6.91 us
    ppermute x2, starting transfers between devices, padded_2(): lax.ppermute(lax.slice_in_dim(block, block.shape[dim] - width, None, axis...  6.22 us
    conv_general_dilated x2, matrix products, convolve(): lax.conv_general_dilated(padded[None], weights, (1, 1), 'VALID', dimensio...  6.04 us
    ppermute x2, waiting for transfers between devices, padded_2(): lax.ppermute(lax.slice_in_dim(block, 0, width, axis=dim), axis, backward)  4.45 us
    broadcast_in_dim x2, other arithmetic, convolve(): padded[None]  3.58 us
    dynamic_slice x1, local copies, waits for them, and re-layouts, body(): lax.dynamic_slice_in_dim(kernel, owner * width_out, width_out, 3)  3.25 us
  transfers between devices with their start and end apart: 6, of which 5 were waited for; matrix products, arithmetic and copies ran while one was open for 2% of the time, Pallas kernels for 0%

commit v1 on v0

v1 whole, which is shorter than its diff:
```python
import functools

import jax
import jax.numpy as jnp
from jax import lax
from jax.experimental import pallas as pl
from jax.experimental.pallas import tpu as pltpu
from jax.sharding import PartitionSpec as P

BF16, F32 = jnp.bfloat16, jnp.float32
VMEM = pl.BlockSpec(memory_space=pltpu.VMEM)
ANY = pl.BlockSpec(memory_space=pl.ANY)
PARAMS = pltpu.CompilerParams(vmem_limit_bytes=24 << 20)
BLOCK = 4


def relayout_kernel(chunks, x_ref, rim_ref, *refs):
    outs, col_ref = refs[:-1], refs[-1]
    slab, rows, width = x_ref.shape
    for base in range(0, rows, 8):
        group = jnp.swapaxes(x_ref[:, base : base + 8, :].astype(F32), 0, 1)
        for h in range(base, base + 8):
            pixels = group[h - base].T
            col_ref[h : h + 1, :] = pixels[0:1, :]
            col_ref[rows + h : rows + h + 1, :] = pixels[width - 1 : width, :]
            pixels = pixels.astype(BF16)
            if h == 0:
                rim_ref[0:width, :] = pixels
            elif h == rows - 1:
                rim_ref[width : 2 * width, :] = pixels
            else:
                for out, (first, last) in zip(outs, chunks):
                    if first <= h < last:
                        out[h - first] = pixels
    rim_ref[2 * width :, :] = col_ref[...].astype(BF16)


def relayout(features, chunks):
    slab, rows, width = features.shape
    shapes = [(2 * width + 2 * rows, slab)] + [(last - first, width, slab) for first, last in chunks]
    return pl.pallas_call(
        functools.partial(relayout_kernel, chunks),
        out_shape=[jax.ShapeDtypeStruct(s, BF16) for s in shapes],
        in_specs=[VMEM],
        out_specs=[VMEM] * len(shapes),
        scratch_shapes=[pltpu.VMEM((2 * rows, slab), F32)],
        compiler_params=PARAMS,
        name="relayout",
    )(features)


def add_rows(spans, pieces, left_ref, right_ref, w_ref, total_ref, x_ref, written):
    height, width, _ = total_ref.shape
    slab = w_ref.shape[2]
    edge = lax.broadcasted_iota(jnp.int32, (16, slab), 0)
    at = 0
    for piece, local, row, count in spans:
        for start in range(0, count, BLOCK):
            size = min(BLOCK, count - start)
            for i in range(size):
                value = piece[local + start + i]
                r = row + start + i + 1
                x_ref[1, at + i] = value
                x_ref[0, at + i, 0 : width - 16, :] = value[0 : width - 16]
                last = value[width - 16 :].astype(F32)
                x_ref[0, at + i, width - 16 :, :] = jnp.where(edge == 15, left_ref[r : r + 1, :], last).astype(BF16)
                x_ref[2, at + i, 16:, :] = value[16:]
                lead = value[0:16].astype(F32)
                x_ref[2, at + i, 0:16, :] = jnp.where(edge == 0, right_ref[r : r + 1, :], lead).astype(BF16)
            for a in range(3):
                low = max(0, row + start + 1 - a)
                high = min(height, row + start + size + 1 - a)
                if high <= low:
                    continue
                skip = low - (row + start + 1 - a)
                n = high - low
                for b in range(3):
                    lhs = x_ref[b, at + skip : at + skip + n].reshape(n * width, slab)
                    part = jnp.dot(lhs, w_ref[a, b], preferred_element_type=F32).reshape(n, width, -1)
                    for i in range(n):
                        term = part[i] if b == 1 else pltpu.roll(part[i], 1 if b == 0 else width - 1, 0)
                        if low + i in written:
                            total_ref[low + i] += term
                        else:
                            total_ref[low + i] = term
                            written.add(low + i)
            at += size


def store_rows(total_ref, bias_ref, rows, out_ref):
    turned = jnp.stack([(total_ref[h] + bias_ref[...]).T for h in rows], 0)
    out_ref[...] = jnp.swapaxes(turned, 0, 1).astype(BF16)


def accumulate_kernel(spans, n, started, *refs):
    pieces = refs[:n]
    left_ref, right_ref, w_ref = refs[n : n + 3]
    total_ref, x_ref = refs[-2:]
    written = set(range(total_ref.shape[0])) if started else set()
    spans = [(pieces[p], local, row, count) for p, local, row, count in spans]
    add_rows(spans, pieces, left_ref, right_ref, w_ref, total_ref, x_ref, written)


def accumulate(spans, pieces, left, right, weights, total, shape):
    count = sum(s[3] for s in spans)
    width, slab = shape[1], weights.shape[2]
    operands = [*pieces, left, right, weights]
    aliases = {}
    if total is not None:
        aliases = {len(operands): 0}
        operands.append(total)
    flops = 2 * count * width * 9 * slab * shape[2]
    return pl.pallas_call(
        functools.partial(accumulate_kernel, spans, len(pieces), total is not None),
        out_shape=jax.ShapeDtypeStruct(shape, F32),
        in_specs=[VMEM] * len(operands),
        out_specs=VMEM,
        scratch_shapes=[pltpu.VMEM((3, count, width, slab), BF16)],
        input_output_aliases=aliases,
        compiler_params=PARAMS,
        cost_estimate=pl.CostEstimate(flops=flops, bytes_accessed=1 << 20, transcendentals=0),
        name="accumulate",
    )(*operands)


def upper_kernel(total_ref, bias_ref, out_ref):
    store_rows(total_ref, bias_ref, range(out_ref.shape[1]), out_ref)


def upper(total, bias, half):
    return pl.pallas_call(
        upper_kernel,
        out_shape=jax.ShapeDtypeStruct((total.shape[2], half, total.shape[1]), BF16),
        in_specs=[VMEM] * 2,
        out_specs=VMEM,
        compiler_params=PARAMS,
        name="upper",
    )(total, bias)


def last_kernel(span, piece, left_ref, right_ref, w_ref, total_in, bias_ref, upper_ref, out_ref, total_ref, x_ref, lower_ref, sems):
    half = upper_ref.shape[1]
    height = out_ref.shape[1]
    first = pltpu.make_async_copy(upper_ref, out_ref.at[:, 0:half, :], sems.at[0])
    first.start()
    total_ref[half:] = total_in[half:]
    add_rows([(piece, *span)], None, left_ref, right_ref, w_ref, total_ref, x_ref, set(range(height)))
    store_rows(total_ref, bias_ref, range(half, height), lower_ref)
    second = pltpu.make_async_copy(lower_ref, out_ref.at[:, half:height, :], sems.at[1])
    second.start()
    first.wait()
    second.wait()


def last(span, piece, left, right, weights, total, bias, top):
    height, width, outs = total.shape
    slab = weights.shape[2]
    half = top.shape[1]
    return pl.pallas_call(
        functools.partial(last_kernel, span),
        out_shape=jax.ShapeDtypeStruct((outs, height, width), BF16),
        in_specs=[VMEM] * 7,
        out_specs=ANY,
        scratch_shapes=[
            pltpu.VMEM(total.shape, F32),
            pltpu.VMEM((3, span[2], width, slab), BF16),
            pltpu.VMEM((outs, height - half, width), BF16),
            pltpu.SemaphoreType.DMA((2,)),
        ],
        compiler_params=PARAMS,
        name="last",
    )(piece, left, right, weights, total, bias, top)


def body(features, kernel, bias):
    groups = lax.axis_size("filt")
    owner = lax.axis_index("filt")
    slab, height, width = features.shape
    outs = kernel.shape[3] // groups
    half = height // 2
    chunks = ((1, half), (half, height - 3), (height - 3, height - 1))
    own_kernel = lax.dynamic_slice_in_dim(kernel, owner * outs, outs, 3)
    own_bias = lax.dynamic_slice_in_dim(bias, owner * outs, outs, 0)[None, :]

    parts = relayout(features, chunks)
    sets = [parts]
    for shift in range(1, groups):
        ring = [(i, (i + shift) % groups) for i in range(groups)]
        sets.append([lax.ppermute(part, "filt", ring) for part in parts])
    weights = [
        lax.dynamic_slice_in_dim(own_kernel, lax.rem(owner - shift + groups, groups) * slab, slab, 2)
        for shift in range(groups)
    ]

    rims = [s[0] for s in sets]
    count = lax.axis_size("row")
    forward = [(i, i + 1) for i in range(count - 1)]
    backward = [(t, s) for s, t in forward]
    above = lax.ppermute(jnp.stack([r[width : 2 * width] for r in rims]), "row", forward)
    below = lax.ppermute(jnp.stack([r[0:width] for r in rims]), "row", backward)
    count = lax.axis_size("col")
    forward = [(i, i + 1) for i in range(count - 1)]
    backward = [(t, s) for s, t in forward]
    inner = jnp.stack([r[2 * width :] for r in rims])
    first = jnp.concatenate([above[:, 0:1], inner[:, 0:height], below[:, 0:1]], 1)
    final = jnp.concatenate([above[:, width - 1 :], inner[:, height:], below[:, width - 1 :]], 1)
    left = lax.ppermute(final, "col", forward).astype(F32)
    right = lax.ppermute(first, "col", backward).astype(F32)

    shape = (height, width, outs)
    total = None
    for g in range(groups):
        rim, a, b, c = sets[g]
        halo = jnp.stack([above[g], rim[0:width], rim[width : 2 * width], below[g]])
        spans = [(0, 0, -1, 2), (0, 2, height - 1, 2)]
        args = left[g], right[g], weights[g]
        if g == 0:
            spans += [(1 + i, 0, first_, last_ - first_) for i, (first_, last_) in enumerate(chunks)]
            total = accumulate(spans, [halo, a, b, c], *args, None, shape)
            continue
        total = accumulate(spans, [halo], *args, total, shape)
        total = accumulate([(0, 0, chunks[0][0], a.shape[0])], [a], *args, total, shape)
        total = accumulate([(0, 0, chunks[1][0], b.shape[0])], [b], *args, total, shape)
        if g < groups - 1:
            total = accumulate([(0, 0, chunks[2][0], c.shape[0])], [c], *args, total, shape)
    top = upper(total, own_bias, half)
    return last((0, chunks[2][0], c.shape[0]), c, *args, total, own_bias, top)


def solution(mesh):
    return jax.shard_map(
        body,
        mesh=mesh,
        in_specs=(P("filt", "row", "col"), P(), P()),
        out_specs=P("filt", "row", "col"),
        check_vma=False,
    )
```

time: 157 us -> 37.2 us (0.24)
  the two profiles are of different devices: /device:TPU:0 before, /device:TPU:1 now
where the time goes in v1:
time: 37.2 us; the launch traced here: 36.9 us
  starting transfers between devices  16.2 us (44%)
  Pallas kernels  8.58 us (23%)
  local copies, waits for them, and re-layouts  6.34 us (17%)
  waiting for transfers between devices  5.45 us (15%)
    pallas_call x4, Pallas kernels, accumulate(): pl.pallas_call(functools.partial(accumulate_kernel, spans, len(pieces), t...  5.7 us
    ppermute x1, starting transfers between devices, body(): right = lax.ppermute(first, 'col', backward).astype(F32)  4.84 us
    dynamic_slice x1, local copies, waits for them, and re-layouts, body(): lax.dynamic_slice_in_dim(own_kernel, lax.rem(owner - shift + groups, grou...  4.28 us
    ppermute x1, waiting for transfers between devices, body(): below = lax.ppermute(jnp.stack([r[0:width] for r in rims]), 'row', backward)  4.1 us
    ppermute x4, starting transfers between devices, body(): sets.append([lax.ppermute(part, 'filt', ring) for part in parts])  3.68 us
    ppermute x1, starting transfers between devices, body(): lax.ppermute(jnp.stack([r[width:2 * width] for r in rims]), 'row', forward)  3.36 us
    ppermute x1, starting transfers between devices, body(): left = lax.ppermute(final, 'col', forward).astype(F32)  3.02 us
    pallas_call x1, Pallas kernels, last(): pl.pallas_call(functools.partial(last_kernel, span), out_shape=jax.ShapeD...  1.6 us
  transfers between devices with their start and end apart: 8, of which 3 were waited for; matrix products, arithmetic and copies ran while one was open for 14% of the time, Pallas kernels for 17%

profile of v1, /device:TPU:1, one launch (start us, length us, event | category | flops | bytes accessed | tf_op | source)
XLA Modules:
  0.0 36.9 jit_solution(3955236767328576147)
XLA Ops:
  0.0 0.0 copy-start
  0.0 1.2 %copy-done = bf16[256,16,128]{2,1,0:T(8,128)(2,1)S(1)} copy-done((bf16[256,16,128]{2,1,0:T(8,128)(2,1)S(1)}, bf16[256,16,128]{2,1,0:T(8,128)(2,1)}, u32[]{:S(2)}) %copy-start) | copy-done | bytes 1048600
  1.2 0.8 %relayout.1 = (bf16[288,256]{1,0:T(8,128)(2,1)S(1)}, bf16[7,128,256]{2,1,0:T(8,128)(2,1)S(1)}, bf16[5,128,256]{2,1,0:T(8,128)(2,1)S(1)}, bf16[2,128,256]{2,1,0:T(8,128)(2,1)S(1)}) custom-call(bf16[256,16,128]{2,1,0:T(8,128)(2,1)S(1)} %copy-done), custom_call_target="tpu_custom_call" | custom-call | tf_op jit(solution)/shard_map/relayout/pallas_call | solution.py:41
  2.0 2.1 %collective-permute-start.1 = (bf16[288,256]{1,0:T(8,128)(2,1)S(1)}, bf16[288,256]{1,0:T(8,128)(2,1)S(1)}, u32[]{:S(2)}, u32[]{:S(2)}) collective-permute-start(bf16[288,256]{1,0:T(8,128)(2,1)S(1)} %get-tuple-element.10), channel_id=1, source_target_pairs={{0,1},{1,0},{2,3},{3,2},{4,5},{5,4},{6,7},{7,6},{8,9},{9,8},{10,11... | collective-permute-start | bytes 442376 | tf_op jit(solution)/shard_map/ppermute | solution.py:189
  4.2 0.1 collective-permute-start.7
  4.3 1.4 %collective-permute-start.6 = (bf16[5,128,256]{2,1,0:T(8,128)(2,1)S(1)}, bf16[5,128,256]{2,1,0:T(8,128)(2,1)S(1)}, u32[]{:S(2)}, u32[]{:S(2)}) collective-permute-start(bf16[5,128,256]{2,1,0:T(8,128)(2,1)S(1)} %get-tuple-element.11.refs_2_), channel_id=1, source_target_pairs={{0,1},{1,0},{2,3},{3,2},{4,5},{5,4},{6,7},{7,6},{8,9},{9,8},{10,11... | collective-permute-start | bytes 983048 | tf_op jit(solution)/shard_map/ppermute | solution.py:189
  5.6 0.1 collective-permute-start
  5.8 0.8 %dynamic_slice.12 = f32[256]{0:T(256)S(1)} dynamic-slice(f32[512]{0:T(512)} %param.5, s32[]{:T(128)S(6)} %select_n.18), dynamic_slice_sizes={256} | dynamic-slice | bytes 2052 | tf_op jit(solution)/shard_map/dynamic_slice | solution.py:183
  6.5 4.3 %constant_dynamic-slice_fusion = (bf16[3,3,256,256]{3,2,1,0:T(8,128)(2,1)S(1)}, bf16[3,3,256,256]{3,2,1,0:T(8,128)(2,1)S(1)}) fusion(bf16[3,3,512,512]{3,2,1,0:T(8,128)(2,1)} %param.4, s32[]{:T(128)S(6)} %select_n.21, s32[]{:T(128)S(6)} %select_n.19, s32[]{:T(128)S(6)} %select_n.17), kind=kLoop, calls=%fused_computation.26 | loop fusion | bytes 4718604 | tf_op jit(solution)/shard_map/dynamic_slice | solution.py:191
  10.8 0.0 collective-permute-done.1
  10.9 3.4 %collective-permute-start.2 = (bf16[2,128,256]{2,1,0:T(8,128)(2,1)S(1)}, bf16[2,128,256]{2,1,0:T(8,128)(2,1)S(1)}, u32[]{:S(2)}, u32[]{:S(2)}) collective-permute-start(bf16[2,128,256]{2,1,0:T(8,128)(2,1)S(1)} %pad_maximum_fusion.2), channel_id=1, source_target_pairs={{0,8},{8,16},{16,24},{1,9},{9,17},{17,25},{2,10},{10,18},{18,26},{... | collective-permute-start | bytes 393224 | tf_op jit(solution)/shard_map/ppermute | solution.py:199
  14.3 1.3 %collective-permute-start.3 = (bf16[2,128,256]{2,1,0:T(8,128)(2,1)S(1)}, bf16[2,128,256]{2,1,0:T(8,128)(2,1)S(1)}, u32[]{:S(2)}, u32[]{:S(2)}) collective-permute-start(bf16[2,128,256]{2,1,0:T(8,128)(2,1)S(1)} %pad_maximum_fusion.3), channel_id=1, source_target_pairs={{8,0},{16,8},{24,16},{9,1},{17,9},{25,17},{10,2},{18,10},{26,18},{... | collective-permute-start | bytes 393224 | tf_op jit(solution)/shard_map/ppermute | solution.py:200
  15.6 0.6 %collective-permute-done.2 = bf16[2,128,256]{2,1,0:T(8,128)(2,1)S(1)} collective-permute-done((bf16[2,128,256]{2,1,0:T(8,128)(2,1)S(1)}, bf16[2,128,256]{2,1,0:T(8,128)(2,1)S(1)}, u32[]{:S(2)}, u32[]{:S(2)}) %collective-permute-start.2) | collective-permute-done | bytes 131104 | tf_op jit(solution)/shard_map/ppermute | solution.py:199
  16.2 4.1 %collective-permute-done.3 = bf16[2,128,256]{2,1,0:T(8,128)(2,1)S(1)} collective-permute-done((bf16[2,128,256]{2,1,0:T(8,128)(2,1)S(1)}, bf16[2,128,256]{2,1,0:T(8,128)(2,1)S(1)}, u32[]{:S(2)}, u32[]{:S(2)}) %collective-permute-start.3) | collective-permute-done | bytes 131104 | tf_op jit(solution)/shard_map/ppermute | solution.py:200
  20.3 4.8 %collective-permute-start.5 = (bf16[2,18,256]{2,1,0:T(8,128)(2,1)S(1)}, bf16[2,18,256]{2,1,0:T(8,128)(2,1)S(1)}, u32[]{:S(2)}, u32[]{:S(2)}) collective-permute-start(bf16[2,18,256]{2,1,0:T(8,128)(2,1)S(1)} %fusion.5), channel_id=1, source_target_pairs={{2,0},{4,2},{6,4},{3,1},{5,3},{7,5},{10,8},{12,10},{14,12},{11,9},... | collective-permute-start | bytes 55304 | tf_op jit(solution)/shard_map/ppermute | solution.py:208
  25.2 3.0 %collective-permute-start.4 = (bf16[2,18,256]{2,1,0:T(8,128)(2,1)S(1)}, bf16[2,18,256]{2,1,0:T(8,128)(2,1)S(1)}, u32[]{:S(2)}, u32[]{:S(2)}) collective-permute-start(bf16[2,18,256]{2,1,0:T(8,128)(2,1)S(1)} %pad_maximum_fusion.4), channel_id=1, source_target_pairs={{0,2},{2,4},{4,6},{1,3},{3,5},{5,7},{8,10},{10,12},{12,14},{9,11},... | collective-permute-start | bytes 55304 | tf_op jit(solution)/shard_map/ppermute | solution.py:207
  28.3 0.0 collective-permute-done.5
  28.3 0.8 %collective-permute-done.4 = bf16[2,18,256]{2,1,0:T(8,128)(2,1)S(1)} collective-permute-done((bf16[2,18,256]{2,1,0:T(8,128)(2,1)S(1)}, bf16[2,18,256]{2,1,0:T(8,128)(2,1)S(1)}, u32[]{:S(2)}, u32[]{:S(2)}) %collective-permute-start.4) | collective-permute-done | bytes 18464 | tf_op jit(solution)/shard_map/ppermute | solution.py:207
  29.1 2.8 %accumulate.4.refs_4_ = f32[16,128,256]{2,1,0:T(8,128)S(1)} custom-call(bf16[4,128,256]{2,1,0:T(8,128)(2,1)S(1)} %pad_maximum_fusion.1.refs_0_, bf16[7,128,256]{2,1,0:T(8,128)(2,1)S(1)} %get-tuple-element.12.refs_1_, bf16[5,128,256]{2,1,0:T(8,128)(2,1)S(1)} %get-tuple-element.11.refs_2_, bf16[2,128,256]{2,1,0:T(8,128)(2,1)S(1)} %get-tuple-element.9.refs_3_, ...), custom_call_target="tpu_custom_call" | custom-call | flops 2717908992 | bytes 1048576 | tf_op jit(solution)/shard_map/accumulate/pallas_call | solution.py:113
  32.0 0.5 %accumulate.5.refs_4_ = f32[16,128,256]{2,1,0:T(8,128)S(1)} custom-call(bf16[4,128,256]{2,1,0:T(8,128)(2,1)S(1)} %pad_maximum_fusion.refs_0_, f32[18,256]{1,0:T(8,128)S(1)} %get-tuple-element.30.refs_1_.left_ref, f32[18,256]{1,0:T(8,128)S(1)} %get-tuple-element.28.refs_2_.right_ref, ...), custom_call_target="tpu_custom_call", output_to_operand_aliasing={{}: (4, {})} | custom-call | flops 603979776 | bytes 1048576 | tf_op jit(solution)/shard_map/accumulate/pallas_call | solution.py:113
  32.5 0.0 collective-permute-done.7.refs_0_
  32.5 1.3 %accumulate.6.refs_4_ = f32[16,128,256]{2,1,0:T(8,128)S(1)} custom-call(bf16[7,128,256]{2,1,0:T(8,128)(2,1)S(1)} %collective-permute-done.7.refs_0_, f32[18,256]{1,0:T(8,128)S(1)} %get-tuple-element.30.refs_1_.left_ref, f32[18,256]{1,0:T(8,128)S(1)} %get-tuple-element.28.refs_2_.right_ref, ...), custom_call_target="tpu_custom_call", output_to_operand_aliasing={{}: (4, {})} | custom-call | flops 1056964608 | bytes 1048576 | tf_op jit(solution)/shard_map/accumulate/pallas_call | solution.py:113
  33.8 0.0 collective-permute-done.6.refs_0_
  33.9 1.0 %accumulate.7.total_ref.total_in = f32[16,128,256]{2,1,0:T(8,128)S(1)} custom-call(bf16[5,128,256]{2,1,0:T(8,128)(2,1)S(1)} %collective-permute-done.6.refs_0_, f32[18,256]{1,0:T(8,128)S(1)} %get-tuple-element.30.refs_1_.left_ref, f32[18,256]{1,0:T(8,128)S(1)} %get-tuple-element.28.refs_2_.right_ref, ...), custom_call_target="tpu_custom_call", output_to_operand_aliasing={{}: (4, {})} | custom-call | flops 754974720 | bytes 1048576 | tf_op jit(solution)/shard_map/accumulate/pallas_call | solution.py:113
  34.9 0.5 %upper.1.upper_ref = bf16[256,8,128]{2,1,0:T(8,128)(2,1)S(1)} custom-call(f32[16,128,256]{2,1,0:T(8,128)S(1)} %accumulate.7.total_ref.total_in, f32[1,256]{1,0:T(1,128)S(1)} %bitcast.21), custom_call_target="tpu_custom_call" | custom-call | tf_op jit(solution)/shard_map/upper/pallas_call | solution.py:131
  35.3 0.0 collective-permute-done.piece
  35.3 1.6 %last.1 = bf16[256,16,128]{2,1,0:T(8,128)(2,1)} custom-call(bf16[2,128,256]{2,1,0:T(8,128)(2,1)S(1)} %collective-permute-done.piece, f32[18,256]{1,0:T(8,128)S(1)} %get-tuple-element.30.refs_1_.left_ref, f32[18,256]{1,0:T(8,128)S(1)} %get-tuple-element.28.refs_2_.right_ref, bf16[3,3,256,256]{3,2,1,0:T(8,128)(2,1)S(1)} %get-tuple-element.14.refs_3_.w_ref, ...), custom_call_target="tpu_custom_call" | custom-call | tf_op jit(solution)/shard_map/last/pallas_call | solution.py:159
  (19 shorter events, 0.2 us)
Async XLA Ops:
  0.0 1.2 %copy-start = (bf16[256,16,128]{2,1,0:T(8,128)(2,1)S(1)}, bf16[256,16,128]{2,1,0:T(8,128)(2,1)}, u32[]{:S(2)}) copy-start(bf16[256,16,128]{2,1,0:T(8,128)(2,1)} %x_ref.1) | copy-start | bytes 3145732
  2.0 8.8 %collective-permute-start.1 = (bf16[288,256]{1,0:T(8,128)(2,1)S(1)}, bf16[288,256]{1,0:T(8,128)(2,1)S(1)}, u32[]{:S(2)}, u32[]{:S(2)}) collective-permute-start(bf16[288,256]{1,0:T(8,128)(2,1)S(1)} %get-tuple-element.10), channel_id=1, source_target_pairs={{0,1},{1,0},{2,3},{3,2},{4,5},{5,4},{6,7},{7,6},{8,9},{9,8},{10,11... | collective-permute-start | bytes 442376 | tf_op jit(solution)/shard_map/ppermute | solution.py:189
  4.2 28.3 %collective-permute-start.7 = (bf16[7,128,256]{2,1,0:T(8,128)(2,1)S(1)}, bf16[7,128,256]{2,1,0:T(8,128)(2,1)S(1)}, u32[]{:S(2)}, u32[]{:S(2)}) collective-permute-start(bf16[7,128,256]{2,1,0:T(8,128)(2,1)S(1)} %get-tuple-element.12.refs_1_), channel_id=1, source_target_pairs={{0,1},{1,0},{2,3},{3,2},{4,5},{5,4},{6,7},{7,6},{8,9},{9,8},{10,11... | collective-permute-start | bytes 1376264 | tf_op jit(solution)/shard_map/ppermute | solution.py:189
  4.3 29.6 %collective-permute-start.6 = (bf16[5,128,256]{2,1,0:T(8,128)(2,1)S(1)}, bf16[5,128,256]{2,1,0:T(8,128)(2,1)S(1)}, u32[]{:S(2)}, u32[]{:S(2)}) collective-permute-start(bf16[5,128,256]{2,1,0:T(8,128)(2,1)S(1)} %get-tuple-element.11.refs_2_), channel_id=1, source_target_pairs={{0,1},{1,0},{2,3},{3,2},{4,5},{5,4},{6,7},{7,6},{8,9},{9,8},{10,11... | collective-permute-start | bytes 983048 | tf_op jit(solution)/shard_map/ppermute | solution.py:189
  5.6 29.7 %collective-permute-start = (bf16[2,128,256]{2,1,0:T(8,128)(2,1)S(1)}, bf16[2,128,256]{2,1,0:T(8,128)(2,1)S(1)}, u32[]{:S(2)}, u32[]{:S(2)}) collective-permute-start(bf16[2,128,256]{2,1,0:T(8,128)(2,1)S(1)} %get-tuple-element.9.refs_3_), channel_id=1, source_target_pairs={{0,1},{1,0},{2,3},{3,2},{4,5},{5,4},{6,7},{7,6},{8,9},{9,8},{10,11... | collective-permute-start | bytes 393224 | tf_op jit(solution)/shard_map/ppermute | solution.py:189
  10.9 5.3 %collective-permute-start.2 = (bf16[2,128,256]{2,1,0:T(8,128)(2,1)S(1)}, bf16[2,128,256]{2,1,0:T(8,128)(2,1)S(1)}, u32[]{:S(2)}, u32[]{:S(2)}) collective-permute-start(bf16[2,128,256]{2,1,0:T(8,128)(2,1)S(1)} %pad_maximum_fusion.2), channel_id=1, source_target_pairs={{0,8},{8,16},{16,24},{1,9},{9,17},{17,25},{2,10},{10,18},{18,26},{... | collective-permute-start | bytes 393224 | tf_op jit(solution)/shard_map/ppermute | solution.py:199
  14.3 6.0 %collective-permute-start.3 = (bf16[2,128,256]{2,1,0:T(8,128)(2,1)S(1)}, bf16[2,128,256]{2,1,0:T(8,128)(2,1)S(1)}, u32[]{:S(2)}, u32[]{:S(2)}) collective-permute-start(bf16[2,128,256]{2,1,0:T(8,128)(2,1)S(1)} %pad_maximum_fusion.3), channel_id=1, source_target_pairs={{8,0},{16,8},{24,16},{9,1},{17,9},{25,17},{10,2},{18,10},{26,18},{... | collective-permute-start | bytes 393224 | tf_op jit(solution)/shard_map/ppermute | solution.py:200
  20.3 8.0 %collective-permute-start.5 = (bf16[2,18,256]{2,1,0:T(8,128)(2,1)S(1)}, bf16[2,18,256]{2,1,0:T(8,128)(2,1)S(1)}, u32[]{:S(2)}, u32[]{:S(2)}) collective-permute-start(bf16[2,18,256]{2,1,0:T(8,128)(2,1)S(1)} %fusion.5), channel_id=1, source_target_pairs={{2,0},{4,2},{6,4},{3,1},{5,3},{7,5},{10,8},{12,10},{14,12},{11,9},... | collective-permute-start | bytes 55304 | tf_op jit(solution)/shard_map/ppermute | solution.py:208
  25.2 3.9 %collective-permute-start.4 = (bf16[2,18,256]{2,1,0:T(8,128)(2,1)S(1)}, bf16[2,18,256]{2,1,0:T(8,128)(2,1)S(1)}, u32[]{:S(2)}, u32[]{:S(2)}) collective-permute-start(bf16[2,18,256]{2,1,0:T(8,128)(2,1)S(1)} %pad_maximum_fusion.4), channel_id=1, source_target_pairs={{0,2},{2,4},{4,6},{1,3},{3,5},{5,7},{8,10},{10,12},{12,14},{9,11},... | collective-permute-start | bytes 55304 | tf_op jit(solution)/shard_map/ppermute | solution.py:207

commit v2 on v1

v2 whole, which is shorter than its diff:
```python
import functools

import jax
import jax.numpy as jnp
from jax import lax
from jax.experimental import pallas as pl
from jax.experimental.pallas import tpu as pltpu
from jax.sharding import PartitionSpec as P

BF16, F32 = jnp.bfloat16, jnp.float32
VMEM = pl.BlockSpec(memory_space=pltpu.VMEM)
ANY = pl.BlockSpec(memory_space=pl.ANY)
PARAMS = pltpu.CompilerParams(vmem_limit_bytes=24 << 20)
BLOCK = 4


def relayout_kernel(chunks, x_ref, rim_ref, *refs):
    outs, col_ref = refs[:-1], refs[-1]
    slab, rows, width = x_ref.shape
    for base in range(0, rows, 8):
        group = jnp.swapaxes(x_ref[:, base : base + 8, :].astype(F32), 0, 1)
        for h in range(base, base + 8):
            pixels = group[h - base].T
            col_ref[h : h + 1, :] = pixels[0:1, :]
            col_ref[rows + h : rows + h + 1, :] = pixels[width - 1 : width, :]
            pixels = pixels.astype(BF16)
            if h == 0:
                rim_ref[0:width, :] = pixels
            elif h == rows - 1:
                rim_ref[width : 2 * width, :] = pixels
            else:
                for out, (first, last) in zip(outs, chunks):
                    if first <= h < last:
                        out[h - first] = pixels
    rim_ref[2 * width :, :] = col_ref[...].astype(BF16)


def relayout(features, chunks):
    slab, rows, width = features.shape
    shapes = [(2 * width + 2 * rows, slab)] + [(last - first, width, slab) for first, last in chunks]
    return pl.pallas_call(
        functools.partial(relayout_kernel, chunks),
        out_shape=[jax.ShapeDtypeStruct(s, BF16) for s in shapes],
        in_specs=[VMEM],
        out_specs=[VMEM] * len(shapes),
        scratch_shapes=[pltpu.VMEM((2 * rows, slab), F32)],
        compiler_params=PARAMS,
        name="relayout",
    )(features)


def put_row(x_ref, at, value):
    width, slab = value.shape
    edge = lax.broadcasted_iota(jnp.int32, (16, slab), 0)
    x_ref[1, at] = value
    x_ref[0, at, 0 : width - 16, :] = value[0 : width - 16]
    x_ref[0, at, width - 16 :, :] = jnp.where(edge == 15, 0, value[width - 16 :].astype(F32)).astype(BF16)
    x_ref[2, at, 16:, :] = value[16:]
    x_ref[2, at, 0:16, :] = jnp.where(edge == 0, 0, value[0:16].astype(F32)).astype(BF16)


def turn(part, b):
    return part if b == 1 else pltpu.roll(part, 1 if b == 0 else part.shape[0] - 1, 0)


def add_rows(spans, w_ref, total_ref, x_ref, written):
    height, width, _ = total_ref.shape
    slab = w_ref.shape[2]
    at = 0
    for piece, local, row, count in spans:
        for start in range(0, count, BLOCK):
            size = min(BLOCK, count - start)
            for i in range(size):
                put_row(x_ref, at + i, piece[local + start + i])
            for a in range(3):
                low = max(0, row + start + 1 - a)
                high = min(height, row + start + size + 1 - a)
                if high <= low:
                    continue
                skip = low - (row + start + 1 - a)
                n = high - low
                for b in range(3):
                    lhs = x_ref[b, at + skip : at + skip + n].reshape(n * width, slab)
                    part = jnp.dot(lhs, w_ref[a, b], preferred_element_type=F32).reshape(n, width, -1)
                    for i in range(n):
                        term = turn(part[i], b)
                        if low + i in written:
                            total_ref[low + i] += term
                        else:
                            total_ref[low + i] = term
                            written.add(low + i)
            at += size


def accumulate_kernel(spans, n, started, *refs):
    pieces, w_ref, total_ref, x_ref = refs[:n], refs[n], refs[-2], refs[-1]
    written = set(range(total_ref.shape[0])) if started else set()
    spans = [(pieces[p], local, row, count) for p, local, row, count in spans]
    add_rows(spans, w_ref, total_ref, x_ref, written)


def accumulate(spans, pieces, weights, total, shape):
    count = sum(s[3] for s in spans)
    width, slab = shape[1], weights.shape[2]
    operands = [*pieces, weights]
    aliases = {}
    if total is not None:
        aliases = {len(operands): 0}
        operands.append(total)
    return pl.pallas_call(
        functools.partial(accumulate_kernel, spans, len(pieces), total is not None),
        out_shape=jax.ShapeDtypeStruct(shape, F32),
        in_specs=[VMEM] * len(operands),
        out_specs=VMEM,
        scratch_shapes=[pltpu.VMEM((3, count, width, slab), BF16)],
        input_output_aliases=aliases,
        compiler_params=PARAMS,
        cost_estimate=cost(count * width * 9, slab, shape[2]),
        name="accumulate",
    )(*operands)


def cost(pixels, slab, outs):
    return pl.CostEstimate(flops=2 * pixels * slab * outs, bytes_accessed=1 << 20, transcendentals=0)


def outer_rows_kernel(groups, above_ref, below_ref, *refs):
    w_refs, fix_ref, x_ref = refs[:groups], refs[-2], refs[-1]
    for i, (ref, a) in enumerate(((above_ref, 0), (below_ref, 2))):
        fix = None
        for g in range(groups):
            put_row(x_ref, 0, ref[g])
            for b in range(3):
                part = turn(jnp.dot(x_ref[b, 0], w_refs[g][a, b], preferred_element_type=F32), b)
                fix = part if fix is None else fix + part
        fix_ref[i] = fix


def outer_cols_kernel(groups, left_ref, right_ref, *refs):
    w_refs, fix_ref = refs[:groups], refs[-1]
    height = fix_ref.shape[1]
    for i, (ref, b) in enumerate(((left_ref, 0), (right_ref, 2))):
        fix = None
        for g in range(groups):
            pixels = ref[g]
            for a in range(3):
                part = jnp.dot(pixels, w_refs[g][a, b], preferred_element_type=F32)[a : a + height]
                fix = part if fix is None else fix + part
        fix_ref[i] = fix


def finish_row(total_ref, h, bias_ref, rows_ref, cols_ref):
    height, width = cols_ref.shape[1], total_ref.shape[1]
    value = total_ref[h] + bias_ref[...]
    if h == 0:
        value += rows_ref[0]
    if h == height - 1:
        value += rows_ref[1]
    edge = lax.broadcasted_iota(jnp.int32, (8, value.shape[1]), 0)
    first = value[0:8] + jnp.where(edge == 0, cols_ref[0, h : h + 1, :], 0)
    final = value[width - 8 :] + jnp.where(edge == 7, cols_ref[1, h : h + 1, :], 0)
    return jnp.concatenate([first, value[8 : width - 8], final], 0)


def store_rows(total_ref, bias_ref, rows_ref, cols_ref, rows, out_ref):
    turned = jnp.stack([finish_row(total_ref, h, bias_ref, rows_ref, cols_ref).T for h in rows], 0)
    out_ref[...] = jnp.swapaxes(turned, 0, 1).astype(BF16)


def upper_kernel(total_ref, bias_ref, rows_ref, cols_ref, out_ref):
    store_rows(total_ref, bias_ref, rows_ref, cols_ref, range(out_ref.shape[1]), out_ref)


def last_kernel(span, piece, w_ref, total_in, bias_ref, rows_ref, cols_ref, upper_ref, out_ref, total_ref, x_ref, lower_ref, sems):
    half = upper_ref.shape[1]
    height = out_ref.shape[1]
    first = pltpu.make_async_copy(upper_ref, out_ref.at[:, 0:half, :], sems.at[0])
    first.start()
    total_ref[half:] = total_in[half:]
    add_rows([(piece, *span)], w_ref, total_ref, x_ref, set(range(height)))
    store_rows(total_ref, bias_ref, rows_ref, cols_ref, range(half, height), lower_ref)
    second = pltpu.make_async_copy(lower_ref, out_ref.at[:, half:height, :], sems.at[1])
    second.start()
    first.wait()
    second.wait()


def call(kernel, name, shape, dtype, operands, estimate, scratch=(), out=VMEM):
    return pl.pallas_call(
        kernel,
        out_shape=jax.ShapeDtypeStruct(shape, dtype),
        in_specs=[VMEM] * len(operands),
        out_specs=out,
        scratch_shapes=scratch,
        compiler_params=PARAMS,
        cost_estimate=estimate,
        name=name,
    )(*operands)


def weights_kernel(groups, kernel_ref, *refs):
    outs, sems = refs[:-1], refs[-1]
    slab, width = outs[0].shape[2:]
    owner = lax.axis_index("filt")
    copies = []
    for shift, out in enumerate(outs):
        group = lax.rem(owner - shift + groups, groups)
        source = kernel_ref.at[:, :, pl.ds(pl.multiple_of(group * slab, slab), slab), pl.ds(pl.multiple_of(owner * width, width), width)]
        copies.append(pltpu.make_async_copy(source, out, sems.at[shift]))
    for copy in copies:
        copy.start()
    for copy in copies:
        copy.wait()


def split_weights(kernel, groups, slab, outs):
    if outs % 128 == 0 and slab % 128 == 0:
        return pl.pallas_call(
            functools.partial(weights_kernel, groups),
            out_shape=[jax.ShapeDtypeStruct((3, 3, slab, outs), BF16)] * groups,
            in_specs=[ANY],
            out_specs=[VMEM] * groups,
            scratch_shapes=[pltpu.SemaphoreType.DMA((groups,))],
            compiler_params=PARAMS,
            name="split_weights",
        )(kernel)
    owner = lax.axis_index("filt")
    own = lax.dynamic_slice_in_dim(kernel, owner * outs, outs, 3)
    order = [lax.rem(owner - shift + groups, groups) for shift in range(groups)]
    return [lax.dynamic_slice_in_dim(own, group * slab, slab, 2) for group in order]


def body(features, kernel, bias):
    groups = lax.axis_size("filt")
    owner = lax.axis_index("filt")
    slab, height, width = features.shape
    outs = kernel.shape[3] // groups
    half = height // 2
    chunks = ((1, half), (half, height - 3), (height - 3, height - 1))
    own_bias = lax.dynamic_slice_in_dim(bias, owner * outs, outs, 0)[None, :]

    parts = relayout(features, chunks)
    sets = [parts]
    for shift in range(1, groups):
        ring = [(i, (i + shift) % groups) for i in range(groups)]
        sets.append([lax.ppermute(part, "filt", ring) for part in parts])
    weights = split_weights(kernel, groups, slab, outs)

    rims = [s[0] for s in sets]
    count = lax.axis_size("row")
    forward = [(i, i + 1) for i in range(count - 1)]
    backward = [(t, s) for s, t in forward]
    above = lax.ppermute(jnp.stack([r[width : 2 * width] for r in rims]), "row", forward)
    below = lax.ppermute(jnp.stack([r[0:width] for r in rims]), "row", backward)
    count = lax.axis_size("col")
    forward = [(i, i + 1) for i in range(count - 1)]
    backward = [(t, s) for s, t in forward]
    inner = jnp.stack([r[2 * width :] for r in rims])
    first = jnp.concatenate([above[:, 0:1], inner[:, 0:height], below[:, 0:1]], 1)
    final = jnp.concatenate([above[:, width - 1 :], inner[:, height:], below[:, width - 1 :]], 1)
    left = lax.ppermute(final, "col", forward)
    right = lax.ppermute(first, "col", backward)

    rows_fix = call(
        functools.partial(outer_rows_kernel, groups), "outer_rows", (2, width, outs), F32,
        [above, below, *weights], cost(6 * width * groups, slab, outs), [pltpu.VMEM((3, 1, width, slab), BF16)],
    )
    cols_fix = call(
        functools.partial(outer_cols_kernel, groups), "outer_cols", (2, height, outs), F32,
        [left, right, *weights], cost(6 * 256 * groups, slab, outs),
    )

    shape = (height, width, outs)
    total = None
    for g in range(groups):
        rim, a, b, c = sets[g]
        rim = rim[0 : 2 * width].reshape(2, width, slab)
        spans = [(0, 0, 0, 1), (0, 1, height - 1, 1)]
        if g == 0:
            spans += [(1 + i, 0, first_, last_ - first_) for i, (first_, last_) in enumerate(chunks)]
            total = accumulate(spans, [rim, a, b, c], weights[g], None, shape)
            continue
        total = accumulate(spans, [rim], weights[g], total, shape)
        total = accumulate([(0, 0, chunks[0][0], a.shape[0])], [a], weights[g], total, shape)
        total = accumulate([(0, 0, chunks[1][0], b.shape[0])], [b], weights[g], total, shape)
        if g < groups - 1:
            total = accumulate([(0, 0, chunks[2][0], c.shape[0])], [c], weights[g], total, shape)
    top = call(upper_kernel, "upper", (outs, half, width), BF16, [total, own_bias, rows_fix, cols_fix], cost(256, slab, outs))
    scratch = [
        pltpu.VMEM(shape, F32),
        pltpu.VMEM((3, c.shape[0], width, slab), BF16),
        pltpu.VMEM((outs, height - half, width), BF16),
        pltpu.SemaphoreType.DMA((2,)),
    ]
    span = (0, chunks[2][0], c.shape[0])
    return call(
        functools.partial(last_kernel, span), "last", (outs, height, width), BF16,
        [c, weights[-1], total, own_bias, rows_fix, cols_fix, top], cost(9 * 256, slab, outs), scratch, ANY,
    )


def solution(mesh):
    return jax.shard_map(
        body,
        mesh=mesh,
        in_specs=(P("filt", "row", "col"), P(), P()),
        out_specs=P("filt", "row", "col"),
        check_vma=False,
    )
```

time: 37.2 us -> 40.9 us (1.099)
  Pallas kernels: 8.58 us -> 11 us
  local copies, waits for them, and re-layouts: 6.34 us -> 7.54 us
    dynamic_slice x1 -> x0, local copies, waits for them, and re-layouts: 4.28 us -> none  [body(): lax.dynamic_slice_in_dim(own_kernel, lax.rem(owner - shift + groups, grou...]
    unnamed x2 -> x8, local copies, waits for them, and re-layouts: 1.22 us -> 3.57 us
    ppermute x2, waiting for transfers between devices: 0.76 us -> 2.82 us  [the longest x1 2.82 us: body(): right = lax.ppermute(first, 'col', backward)]
    another operation x2, local copies, waits for them, and re-layouts: 0.02 us -> 1.55 us  [body(): below = lax.ppermute(jnp.stack([r[0:width] for r in rims]), 'row', backward)]
    ppermute x1, waiting for transfers between devices: 4.1 us -> 2.64 us  [body(): below = lax.ppermute(jnp.stack([r[0:width] for r in rims]), 'row', backward)]
    pallas_call x2 -> x5, Pallas kernels: 2.06 us -> 2.98 us  [the longest x4 2.81 us: call(): pl.pallas_call(kernel, out_shape=jax.ShapeDtypeStruct(shape, dtype), in_s...]
    slice x2, local copies, waits for them, and re-layouts: 0.02 us -> 0.92 us  [body(): rim = rim[0:2 * width].reshape(2, width, slab)]
    pallas_call x4, Pallas kernels: 5.7 us -> 6.57 us  [accumulate(): pl.pallas_call(functools.partial(accumulate_kernel, spans, len(pieces), t...]
  transfers between devices with their start and end apart: 8 -> 8, of which waited for: 3 -> 2; matrix products, arithmetic and copies ran while one was open for 14% -> 10% of each run, Pallas kernels for 17% -> 20%
where the time goes in v2:
time: 40.9 us; the launch traced here: 40.4 us
  starting transfers between devices  16.1 us (39%)
  Pallas kernels  11 us (27%)
  local copies, waits for them, and re-layouts  7.54 us (18%)
  waiting for transfers between devices  5.49 us (13%)
    pallas_call x4, Pallas kernels, accumulate(): pl.pallas_call(functools.partial(accumulate_kernel, spans, len(pieces), t...  6.57 us
    ppermute x1, starting transfers between devices, body(): left = lax.ppermute(final, 'col', forward)  5.94 us
    ppermute x4, starting transfers between devices, body(): sets.append([lax.ppermute(part, 'filt', ring) for part in parts])  3.58 us
    unnamed x8, local copies, waits for them, and re-layouts  3.57 us
    ppermute x1, starting transfers between devices, body(): lax.ppermute(jnp.stack([r[width:2 * width] for r in rims]), 'row', forward)  3.39 us
    ppermute x1, waiting for transfers between devices, body(): right = lax.ppermute(first, 'col', backward)  2.82 us
    pallas_call x4, Pallas kernels, call(): pl.pallas_call(kernel, out_shape=jax.ShapeDtypeStruct(shape, dtype), in_s...  2.81 us
    ppermute x1, waiting for transfers between devices, body(): below = lax.ppermute(jnp.stack([r[0:width] for r in rims]), 'row', backward)  2.64 us
  transfers between devices with their start and end apart: 8, of which 2 were waited for; matrix products, arithmetic and copies ran while one was open for 10% of the time, Pallas kernels for 20%

profile of v2, /device:TPU:1, one launch (start us, length us, event | category | flops | bytes accessed | tf_op | source)
XLA Modules:
  0.0 40.4 jit_solution(4327184160031212914)
XLA Ops:
  0.0 0.0 copy-start.1
  0.0 1.2 %copy-done.1 = bf16[256,16,128]{2,1,0:T(8,128)(2,1)S(1)} copy-done((bf16[256,16,128]{2,1,0:T(8,128)(2,1)S(1)}, bf16[256,16,128]{2,1,0:T(8,128)(2,1)}, u32[]{:S(2)}) %copy-start.1) | copy-done | bytes 1048600
  1.2 1.5 %relayout.1 = (bf16[288,256]{1,0:T(8,128)(2,1)S(1)}, bf16[7,128,256]{2,1,0:T(8,128)(2,1)}, bf16[5,128,256]{2,1,0:T(8,128)(2,1)}, bf16[2,128,256]{2,1,0:T(8,128)(2,1)}) custom-call(bf16[256,16,128]{2,1,0:T(8,128)(2,1)S(1)} %copy-done.1), custom_call_target="tpu_custom_call" | custom-call | tf_op jit(solution)/shard_map/relayout/pallas_call | solution.py:41
  2.7 2.1 %collective-permute-start = (bf16[2,128,256]{2,1,0:T(8,128)(2,1)}, bf16[2,128,256]{2,1,0:T(8,128)(2,1)S(1)}, u32[]{:S(2)}, u32[]{:S(2)}) collective-permute-start(bf16[2,128,256]{2,1,0:T(8,128)(2,1)} %get-tuple-element.11.refs_3_), channel_id=1, source_target_pairs={{0,1},{1,0},{2,3},{3,2},{4,5},{5,4},{6,7},{7,6},{8,9},{9,8},{10,11... | collective-permute-start | bytes 393224 | tf_op jit(solution)/shard_map/ppermute | solution.py:246
  4.8 0.0 collective-permute-start.3
  4.8 1.4 %collective-permute-start.1 = (bf16[5,128,256]{2,1,0:T(8,128)(2,1)}, bf16[5,128,256]{2,1,0:T(8,128)(2,1)S(1)}, u32[]{:S(2)}, u32[]{:S(2)}) collective-permute-start(bf16[5,128,256]{2,1,0:T(8,128)(2,1)} %get-tuple-element.13.refs_2_), channel_id=1, source_target_pairs={{0,1},{1,0},{2,3},{3,2},{4,5},{5,4},{6,7},{7,6},{8,9},{9,8},{10,11... | collective-permute-start | bytes 983048 | tf_op jit(solution)/shard_map/ppermute | solution.py:246
  6.2 0.0 collective-permute-start.2
  6.3 0.7 %slice_bitcast_fusion.2 = (bf16[1,128,256]{2,1,0:T(8,128)(2,1)}, bf16[1,128,256]{2,1,0:T(8,128)(2,1)}) fusion(bf16[288,256]{1,0:T(8,128)(2,1)S(1)} %get-tuple-element.15), kind=kLoop, calls=%fused_computation.6 | loop fusion | bytes 262144 | tf_op jit(solution)/shard_map/stack | solution.py:254
  7.0 0.0 copy-start
  7.0 2.3 %copy-done = bf16[3,3,512,512]{3,2,1,0:T(8,128)(2,1)S(1)} copy-done((bf16[3,3,512,512]{3,2,1,0:T(8,128)(2,1)S(1)}, bf16[3,3,512,512]{3,2,1,0:T(8,128)(2,1)}, u32[]{:S(2)}) %copy-start) | copy-done | bytes 4718616
  9.3 0.2 split_weights.1
  9.5 0.8 %dynamic_slice.3 = f32[256]{0:T(256)S(1)} dynamic-slice(f32[512]{0:T(512)} %param.5, s32[]{:T(128)S(6)} %select_n.3), dynamic_slice_sizes={256} | dynamic-slice | bytes 2052 | tf_op jit(solution)/shard_map/dynamic_slice | solution.py:240
  10.2 0.0 copy-start.3
  10.2 0.0 copy-start.2
  10.2 3.9 %accumulate.4.refs_2_ = f32[16,128,256]{2,1,0:T(8,128)S(1)} custom-call(bf16[2,128,256]{2,1,0:T(8,128)(2,1)S(1)} %bitcast.16, bf16[7,128,256]{2,1,0:T(8,128)(2,1)} %get-tuple-element.14.refs_1_, bf16[5,128,256]{2,1,0:T(8,128)(2,1)} %get-tuple-element.13.refs_2_, bf16[2,128,256]{2,1,0:T(8,128)(2,1)} %get-tuple-element.11.refs_3_, ...), custom_call_target="tpu_custom_call" | custom-call | flops 2415919104 | bytes 1048576 | tf_op jit(solution)/shard_map/accumulate/pallas_call | solution.py:110
  14.1 0.0 collective-permute-done.3
  14.2 0.9 %slice_bitcast_fusion = (bf16[1,128,256]{2,1,0:T(8,128)(2,1)S(1)}, bf16[1,128,256]{2,1,0:T(8,128)(2,1)S(1)}) fusion(bf16[288,256]{1,0:T(8,128)(2,1)} %collective-permute-done.3), kind=kLoop, calls=%fused_computation.4 | loop fusion | bytes 262144 | tf_op jit(solution)/shard_map/stack | solution.py:254
  15.0 0.0 copy-done.3
  15.1 3.4 %collective-permute-start.4 = (bf16[2,128,256]{2,1,0:T(8,128)(2,1)S(1)}, bf16[2,128,256]{2,1,0:T(8,128)(2,1)S(1)}, u32[]{:S(2)}, u32[]{:S(2)}) collective-permute-start(bf16[2,128,256]{2,1,0:T(8,128)(2,1)S(1)} %pad_maximum_fusion), channel_id=1, source_target_pairs={{0,8},{8,16},{16,24},{1,9},{9,17},{17,25},{2,10},{10,18},{18,26},{... | collective-permute-start | bytes 393224 | tf_op jit(solution)/shard_map/ppermute | solution.py:253
  18.5 0.0 copy-done.2
  18.5 1.3 %collective-permute-start.5 = (bf16[2,128,256]{2,1,0:T(8,128)(2,1)S(1)}, bf16[2,128,256]{2,1,0:T(8,128)(2,1)S(1)}, u32[]{:S(2)}, u32[]{:S(2)}) collective-permute-start(bf16[2,128,256]{2,1,0:T(8,128)(2,1)S(1)} %pad_maximum_fusion.1), channel_id=1, source_target_pairs={{8,0},{16,8},{24,16},{9,1},{17,9},{25,17},{10,2},{18,10},{26,18},{... | collective-permute-start | bytes 393224 | tf_op jit(solution)/shard_map/ppermute | solution.py:254
  19.8 0.7 %slice_bitcast_fusion.4 = bf16[1,32,256]{2,1,0:T(8,128)(2,1)S(1)} fusion(bf16[288,256]{1,0:T(8,128)(2,1)} %collective-permute-done.3), kind=kLoop, calls=%fused_computation.18 | loop fusion | bytes 32768 | tf_op jit(solution)/shard_map/stack | solution.py:258
  20.5 0.9 %slice.56 = bf16[256,256]{1,0:T(8,128)(2,1)S(1)} slice(bf16[288,256]{1,0:T(8,128)(2,1)} %collective-permute-done.3), slice={[0:256], [0:256]} | slice | bytes 262144 | tf_op jit(solution)/shard_map/slice | solution.py:277
  21.4 0.4 accumulate.5.refs_2_
  21.8 0.0 collective-permute-done.4.above_ref
  21.9 2.6 %collective-permute-done.5.below_ref = bf16[2,128,256]{2,1,0:T(8,128)(2,1)S(1)} collective-permute-done((bf16[2,128,256]{2,1,0:T(8,128)(2,1)S(1)}, bf16[2,128,256]{2,1,0:T(8,128)(2,1)S(1)}, u32[]{:S(2)}, u32[]{:S(2)}) %collective-permute-start.5) | collective-permute-done | bytes 131104 | tf_op jit(solution)/shard_map/ppermute | solution.py:254
  24.5 5.9 %collective-permute-start.6 = (bf16[2,18,256]{2,1,0:T(8,128)(2,1)S(1)}, bf16[2,18,256]{2,1,0:T(8,128)(2,1)S(1)}, u32[]{:S(2)}, u32[]{:S(2)}) collective-permute-start(bf16[2,18,256]{2,1,0:T(8,128)(2,1)S(1)} %pad_maximum_fusion.2), channel_id=1, source_target_pairs={{0,2},{2,4},{4,6},{1,3},{3,5},{5,7},{8,10},{10,12},{12,14},{9,11},... | collective-permute-start | bytes 55304 | tf_op jit(solution)/shard_map/ppermute | solution.py:261
  30.5 1.9 %collective-permute-start.7 = (bf16[2,18,256]{2,1,0:T(8,128)(2,1)S(1)}, bf16[2,18,256]{2,1,0:T(8,128)(2,1)S(1)}, u32[]{:S(2)}, u32[]{:S(2)}) collective-permute-start(bf16[2,18,256]{2,1,0:T(8,128)(2,1)S(1)} %fusion.5), channel_id=1, source_target_pairs={{2,0},{4,2},{6,4},{3,1},{5,3},{7,5},{10,8},{12,10},{14,12},{11,9},... | collective-permute-start | bytes 55304 | tf_op jit(solution)/shard_map/ppermute | solution.py:262
  32.4 0.4 outer_rows.1.rows_ref
  32.8 0.0 collective-permute-done.6.left_ref
  32.8 2.8 %collective-permute-done.7.right_ref = bf16[2,18,256]{2,1,0:T(8,128)(2,1)S(1)} collective-permute-done((bf16[2,18,256]{2,1,0:T(8,128)(2,1)S(1)}, bf16[2,18,256]{2,1,0:T(8,128)(2,1)S(1)}, u32[]{:S(2)}, u32[]{:S(2)}) %collective-permute-start.7) | collective-permute-done | bytes 18464 | tf_op jit(solution)/shard_map/ppermute | solution.py:262
  35.7 0.4 outer_cols.1.cols_ref
  36.0 0.0 collective-permute-done.2.refs_0_
  36.0 1.3 %accumulate.6.refs_2_ = f32[16,128,256]{2,1,0:T(8,128)S(1)} custom-call(bf16[7,128,256]{2,1,0:T(8,128)(2,1)S(1)} %collective-permute-done.2.refs_0_, bf16[3,3,256,256]{3,2,1,0:T(8,128)(2,1)S(1)} %get-tuple-element.12.refs_1_.w_ref, f32[16,128,256]{2,1,0:T(8,128)S(1)} %accumulate.5.refs_2_), custom_call_target="tpu_custom_call", output_to_operand_aliasing={{}: (2, {})} | custom-call | flops 1056964608 | bytes 1048576 | tf_op jit(solution)/shard_map/accumulate/pallas_call | solution.py:110
  37.3 0.0 collective-permute-done.1.refs_0_
  37.4 1.0 %accumulate.7.total_ref.total_in = f32[16,128,256]{2,1,0:T(8,128)S(1)} custom-call(bf16[5,128,256]{2,1,0:T(8,128)(2,1)S(1)} %collective-permute-done.1.refs_0_, bf16[3,3,256,256]{3,2,1,0:T(8,128)(2,1)S(1)} %get-tuple-element.12.refs_1_.w_ref, f32[16,128,256]{2,1,0:T(8,128)S(1)} %accumulate.6.refs_2_), custom_call_target="tpu_custom_call", output_to_operand_aliasing={{}: (2, {})} | custom-call | flops 754974720 | bytes 1048576 | tf_op jit(solution)/shard_map/accumulate/pallas_call | solution.py:110
  38.4 0.5 %upper.1.upper_ref = bf16[256,8,128]{2,1,0:T(8,128)(2,1)S(1)} custom-call(f32[16,128,256]{2,1,0:T(8,128)S(1)} %accumulate.7.total_ref.total_in, f32[1,256]{1,0:T(1,128)S(1)} %bitcast.17, f32[2,128,256]{2,1,0:T(8,128)S(1)} %outer_rows.1.rows_ref, f32[2,16,256]{2,1,0:T(8,128)S(1)} %outer_cols.1.cols_ref), custom_call_target="tpu_custom_call" | custom-call | flops 33554432 | bytes 1048576 | tf_op jit(solution)/shard_map/upper/pallas_call | solution.py:189
  38.8 0.0 collective-permute-done.piece
  38.8 1.6 %last.1 = bf16[256,16,128]{2,1,0:T(8,128)(2,1)} custom-call(bf16[2,128,256]{2,1,0:T(8,128)(2,1)S(1)} %collective-permute-done.piece, bf16[3,3,256,256]{3,2,1,0:T(8,128)(2,1)S(1)} %get-tuple-element.12.refs_1_.w_ref, f32[16,128,256]{2,1,0:T(8,128)S(1)} %accumulate.7.total_ref.total_in, f32[1,256]{1,0:T(1,128)S(1)} %bitcast.18, ...), custom_call_target="tpu_custom_call" | custom-call | flops 301989888 | bytes 1048576 | tf_op jit(solution)/shard_map/last/pallas_call | solution.py:189
  (9 shorter events, 0.1 us)
Async XLA Ops:
  0.0 1.2 %copy-start.1 = (bf16[256,16,128]{2,1,0:T(8,128)(2,1)S(1)}, bf16[256,16,128]{2,1,0:T(8,128)(2,1)}, u32[]{:S(2)}) copy-start(bf16[256,16,128]{2,1,0:T(8,128)(2,1)} %x_ref.1) | copy-start | bytes 3145732
  2.7 36.1 %collective-permute-start = (bf16[2,128,256]{2,1,0:T(8,128)(2,1)}, bf16[2,128,256]{2,1,0:T(8,128)(2,1)S(1)}, u32[]{:S(2)}, u32[]{:S(2)}) collective-permute-start(bf16[2,128,256]{2,1,0:T(8,128)(2,1)} %get-tuple-element.11.refs_3_), channel_id=1, source_target_pairs={{0,1},{1,0},{2,3},{3,2},{4,5},{5,4},{6,7},{7,6},{8,9},{9,8},{10,11... | collective-permute-start | bytes 393224 | tf_op jit(solution)/shard_map/ppermute | solution.py:246
  4.8 9.4 %collective-permute-start.3 = (bf16[288,256]{1,0:T(8,128)(2,1)S(1)}, bf16[288,256]{1,0:T(8,128)(2,1)}, u32[]{:S(2)}, u32[]{:S(2)}) collective-permute-start(bf16[288,256]{1,0:T(8,128)(2,1)S(1)} %get-tuple-element.15), channel_id=1, source_target_pairs={{0,1},{1,0},{2,3},{3,2},{4,5},{5,4},{6,7},{7,6},{8,9},{9,8},{10,11... | collective-permute-start | bytes 442376 | tf_op jit(solution)/shard_map/ppermute | solution.py:246
  4.8 32.6 %collective-permute-start.1 = (bf16[5,128,256]{2,1,0:T(8,128)(2,1)}, bf16[5,128,256]{2,1,0:T(8,128)(2,1)S(1)}, u32[]{:S(2)}, u32[]{:S(2)}) collective-permute-start(bf16[5,128,256]{2,1,0:T(8,128)(2,1)} %get-tuple-element.13.refs_2_), channel_id=1, source_target_pairs={{0,1},{1,0},{2,3},{3,2},{4,5},{5,4},{6,7},{7,6},{8,9},{9,8},{10,11... | collective-permute-start | bytes 983048 | tf_op jit(solution)/shard_map/ppermute | solution.py:246
  6.2 29.8 %collective-permute-start.2 = (bf16[7,128,256]{2,1,0:T(8,128)(2,1)}, bf16[7,128,256]{2,1,0:T(8,128)(2,1)S(1)}, u32[]{:S(2)}, u32[]{:S(2)}) collective-permute-start(bf16[7,128,256]{2,1,0:T(8,128)(2,1)} %get-tuple-element.14.refs_1_), channel_id=1, source_target_pairs={{0,1},{1,0},{2,3},{3,2},{4,5},{5,4},{6,7},{7,6},{8,9},{9,8},{10,11... | collective-permute-start | bytes 1376264 | tf_op jit(solution)/shard_map/ppermute | solution.py:246
  7.0 2.3 %copy-start = (bf16[3,3,512,512]{3,2,1,0:T(8,128)(2,1)S(1)}, bf16[3,3,512,512]{3,2,1,0:T(8,128)(2,1)}, u32[]{:S(2)}) copy-start(bf16[3,3,512,512]{3,2,1,0:T(8,128)(2,1)} %kernel_ref.1) | copy-start | bytes 14155780
  10.2 4.8 %copy-start.3 = (bf16[1,128,256]{2,1,0:T(8,128)(2,1)S(1)}, bf16[1,128,256]{2,1,0:T(8,128)(2,1)}, u32[]{:S(2)}) copy-start(bf16[1,128,256]{2,1,0:T(8,128)(2,1)} %get-tuple-element.18) | copy-start | bytes 196612
  10.2 8.2 %copy-start.2 = (bf16[1,128,256]{2,1,0:T(8,128)(2,1)S(1)}, bf16[1,128,256]{2,1,0:T(8,128)(2,1)}, u32[]{:S(2)}) copy-start(bf16[1,128,256]{2,1,0:T(8,128)(2,1)} %get-tuple-element.17) | copy-start | bytes 196612
  15.1 6.8 %collective-permute-start.4 = (bf16[2,128,256]{2,1,0:T(8,128)(2,1)S(1)}, bf16[2,128,256]{2,1,0:T(8,128)(2,1)S(1)}, u32[]{:S(2)}, u32[]{:S(2)}) collective-permute-start(bf16[2,128,256]{2,1,0:T(8,128)(2,1)S(1)} %pad_maximum_fusion), channel_id=1, source_target_pairs={{0,8},{8,16},{16,24},{1,9},{9,17},{17,25},{2,10},{10,18},{18,26},{... | collective-permute-start | bytes 393224 | tf_op jit(solution)/shard_map/ppermute | solution.py:253
  18.5 6.0 %collective-permute-start.5 = (bf16[2,128,256]{2,1,0:T(8,128)(2,1)S(1)}, bf16[2,128,256]{2,1,0:T(8,128)(2,1)S(1)}, u32[]{:S(2)}, u32[]{:S(2)}) collective-permute-start(bf16[2,128,256]{2,1,0:T(8,128)(2,1)S(1)} %pad_maximum_fusion.1), channel_id=1, source_target_pairs={{8,0},{16,8},{24,16},{9,1},{17,9},{25,17},{10,2},{18,10},{26,18},{... | collective-permute-start | bytes 393224 | tf_op jit(solution)/shard_map/ppermute | solution.py:254
  24.5 8.3 %collective-permute-start.6 = (bf16[2,18,256]{2,1,0:T(8,128)(2,1)S(1)}, bf16[2,18,256]{2,1,0:T(8,128)(2,1)S(1)}, u32[]{:S(2)}, u32[]{:S(2)}) collective-permute-start(bf16[2,18,256]{2,1,0:T(8,128)(2,1)S(1)} %pad_maximum_fusion.2), channel_id=1, source_target_pairs={{0,2},{2,4},{4,6},{1,3},{3,5},{5,7},{8,10},{10,12},{12,14},{9,11},... | collective-permute-start | bytes 55304 | tf_op jit(solution)/shard_map/ppermute | solution.py:261
  30.5 5.1 %collective-permute-start.7 = (bf16[2,18,256]{2,1,0:T(8,128)(2,1)S(1)}, bf16[2,18,256]{2,1,0:T(8,128)(2,1)S(1)}, u32[]{:S(2)}, u32[]{:S(2)}) collective-permute-start(bf16[2,18,256]{2,1,0:T(8,128)(2,1)S(1)} %fusion.5), channel_id=1, source_target_pairs={{2,0},{4,2},{6,4},{3,1},{5,3},{7,5},{10,8},{12,10},{14,12},{11,9},... | collective-permute-start | bytes 55304 | tf_op jit(solution)/shard_map/ppermute | solution.py:262

commit v3 on v2

--- a/solution.py
+++ b/solution.py
@@ -9,8 +9,8 @@
 
 BF16, F32 = jnp.bfloat16, jnp.float32
 VMEM = pl.BlockSpec(memory_space=pltpu.VMEM)
-ANY = pl.BlockSpec(memory_space=pl.ANY)
-PARAMS = pltpu.CompilerParams(vmem_limit_bytes=24 << 20)
+HBM = pl.BlockSpec(memory_space=pltpu.HBM)
+PARAMS = pltpu.CompilerParams(vmem_limit_bytes=10 << 20)
 BLOCK = 4
 
 
@@ -99,7 +99,7 @@
     add_rows(spans, w_ref, total_ref, x_ref, written)
 
 
-def accumulate(spans, pieces, weights, total, shape):
+def accumulate(spans, pieces, weights, total, shape, after=None):
     count = sum(s[3] for s in spans)
     width, slab = shape[1], weights.shape[2]
     operands = [*pieces, weights]
@@ -107,6 +107,8 @@
     if total is not None:
         aliases = {len(operands): 0}
         operands.append(total)
+    if after is not None:
+        operands.append(after)
     return pl.pallas_call(
         functools.partial(accumulate_kernel, spans, len(pieces), total is not None),
         out_shape=jax.ShapeDtypeStruct(shape, F32),
@@ -120,6 +122,15 @@
     )(*operands)
 
 
+def pick_kernel(low, high, rows_ref, after_ref, out_ref):
+    out_ref[...] = rows_ref[low:high]
+
+
+def pick(rows, low, high, after):
+    shape = (high - low, *rows.shape[1:])
+    return call(functools.partial(pick_kernel, low, high), "pick", shape, BF16, [rows, after], cost(1, 1, 1))
+
+
 def cost(pixels, slab, outs):
     return pl.CostEstimate(flops=2 * pixels * slab * outs, bytes_accessed=1 << 20, transcendentals=0)
 
@@ -151,7 +162,7 @@
 
 def finish_row(total_ref, h, bias_ref, rows_ref, cols_ref):
     height, width = cols_ref.shape[1], total_ref.shape[1]
-    value = total_ref[h] + bias_ref[...]
+    value = total_ref[h] + bias_ref[pl.ds(lax.axis_index("filt"), 1), :]
     if h == 0:
         value += rows_ref[0]
     if h == height - 1:
@@ -218,7 +229,7 @@
         return pl.pallas_call(
             functools.partial(weights_kernel, groups),
             out_shape=[jax.ShapeDtypeStruct((3, 3, slab, outs), BF16)] * groups,
-            in_specs=[ANY],
+            in_specs=[HBM],
             out_specs=[VMEM] * groups,
             scratch_shapes=[pltpu.SemaphoreType.DMA((groups,))],
             compiler_params=PARAMS,
@@ -232,26 +243,30 @@
 
 def body(features, kernel, bias):
     groups = lax.axis_size("filt")
-    owner = lax.axis_index("filt")
     slab, height, width = features.shape
     outs = kernel.shape[3] // groups
     half = height // 2
     chunks = ((1, half), (half, height - 3), (height - 3, height - 1))
-    own_bias = lax.dynamic_slice_in_dim(bias, owner * outs, outs, 0)[None, :]
-
-    parts = relayout(features, chunks)
-    sets = [parts]
-    for shift in range(1, groups):
-        ring = [(i, (i + shift) % groups) for i in range(groups)]
-        sets.append([lax.ppermute(part, "filt", ring) for part in parts])
+    bias = bias.reshape(groups, outs)
+
+    rim, upper_rows, lower_rows = relayout(features, ((1, half), (half, height - 1)))
     weights = split_weights(kernel, groups, slab, outs)
-
-    rims = [s[0] for s in sets]
+    rings = [[(i, (i + shift) % groups) for i in range(groups)] for shift in range(1, groups)]
+    rims = [rim] + [lax.ppermute(rim, "filt", ring) for ring in rings]
+    sets = [[lax.ppermute(upper_rows, "filt", ring)] for ring in rings]
+    second = pick(lower_rows, 0, chunks[1][1] - half, rims[-1])
+    for received, ring in zip(sets, rings):
+        received.append(lax.ppermute(second, "filt", ring))
+
     count = lax.axis_size("row")
     forward = [(i, i + 1) for i in range(count - 1)]
     backward = [(t, s) for s, t in forward]
+    below = lax.ppermute(jnp.stack([r[0:width] for r in rims]), "row", backward)
     above = lax.ppermute(jnp.stack([r[width : 2 * width] for r in rims]), "row", forward)
-    below = lax.ppermute(jnp.stack([r[0:width] for r in rims]), "row", backward)
+    third = pick(lower_rows, chunks[2][0] - half, chunks[2][1] - half, below)
+    for received, ring in zip(sets, rings):
+        received.append(lax.ppermute(third, "filt", ring))
+
     count = lax.axis_size("col")
     forward = [(i, i + 1) for i in range(count - 1)]
     backward = [(t, s) for s, t in forward]
@@ -273,19 +288,19 @@
     shape = (height, width, outs)
     total = None
     for g in range(groups):
-        rim, a, b, c = sets[g]
-        rim = rim[0 : 2 * width].reshape(2, width, slab)
+        rim = rims[g][0 : 2 * width].reshape(2, width, slab)
         spans = [(0, 0, 0, 1), (0, 1, height - 1, 1)]
         if g == 0:
-            spans += [(1 + i, 0, first_, last_ - first_) for i, (first_, last_) in enumerate(chunks)]
-            total = accumulate(spans, [rim, a, b, c], weights[g], None, shape)
+            spans += [(1, 0, 1, half - 1), (2, 0, half, half - 1)]
+            total = accumulate(spans, [rim, upper_rows, lower_rows], weights[g], None, shape, rims[-1])
             continue
+        a, b, c = sets[g - 1]
         total = accumulate(spans, [rim], weights[g], total, shape)
         total = accumulate([(0, 0, chunks[0][0], a.shape[0])], [a], weights[g], total, shape)
         total = accumulate([(0, 0, chunks[1][0], b.shape[0])], [b], weights[g], total, shape)
         if g < groups - 1:
             total = accumulate([(0, 0, chunks[2][0], c.shape[0])], [c], weights[g], total, shape)
-    top = call(upper_kernel, "upper", (outs, half, width), BF16, [total, own_bias, rows_fix, cols_fix], cost(256, slab, outs))
+    top = call(upper_kernel, "upper", (outs, half, width), BF16, [total, bias, rows_fix, cols_fix], cost(256, slab, outs))
     scratch = [
         pltpu.VMEM(shape, F32),
         pltpu.VMEM((3, c.shape[0], width, slab), BF16),
@@ -295,7 +310,7 @@
     span = (0, chunks[2][0], c.shape[0])
     return call(
         functools.partial(last_kernel, span), "last", (outs, height, width), BF16,
-        [c, weights[-1], total, own_bias, rows_fix, cols_fix, top], cost(9 * 256, slab, outs), scratch, ANY,
+        [c, weights[-1], total, bias, rows_fix, cols_fix, top], cost(9 * 256, slab, outs), scratch, HBM,
     )
 
 

time: 40.9 us -> 34.8 us (0.85)
  local copies, waits for them, and re-layouts: 7.54 us -> 4.32 us
  waiting for transfers between devices: 5.49 us -> 3.07 us
  Pallas kernels: 11 us -> 9.1 us
  starting transfers between devices: 16.1 us -> 17.7 us
    ppermute x1, waiting for transfers between devices: 2.64 us -> 0.01 us  [body(): below = lax.ppermute(jnp.stack([r[0:width] for r in rims]), 'row', backward)]
    another operation x2, local copies, waits for them, and re-layouts: 1.55 us -> 0.02 us  [body(): jnp.stack([r[width:2 * width] for r in rims])]
    pallas_call x4, Pallas kernels: 6.57 us -> 5.23 us  [accumulate(): pl.pallas_call(functools.partial(accumulate_kernel, spans, len(pieces), t...]
    slice x2, local copies, waits for them, and re-layouts: 0.92 us -> 0.02 us  [body(): rim = rims[g][0:2 * width].reshape(2, width, slab)]
    ppermute x1, starting transfers between devices: 5.94 us -> 6.72 us  [body(): left = lax.ppermute(final, 'col', forward)]
    dynamic_slice x1 -> x0, local copies, waits for them, and re-layouts: 0.76 us -> none  [body(): own_bias = lax.dynamic_slice_in_dim(bias, owner * outs, outs, 0)[None, :]]
    another operation x2, local copies, waits for them, and re-layouts: 0.72 us -> 0.01 us  [body(): inner = jnp.stack([r[2 * width:] for r in rims])]
    reshape x0 -> x1, local copies, waits for them, and re-layouts: none -> 0.7 us  [body(): bias = bias.reshape(groups, outs)]
  transfers between devices with their start and end apart: 8 -> 8, of which waited for: 2 -> 2; matrix products, arithmetic and copies ran while one was open for 10% -> 2% of each run, Pallas kernels for 20% -> 19%
where the time goes in v3:
time: 34.8 us; the launch traced here: 34.5 us
  starting transfers between devices  17.7 us (51%)
  Pallas kernels  9.1 us (26%)
  local copies, waits for them, and re-layouts  4.32 us (12%)
  waiting for transfers between devices  3.07 us (9%)
    ppermute x1, starting transfers between devices, body(): left = lax.ppermute(final, 'col', forward)  6.72 us
    pallas_call x4, Pallas kernels, accumulate(): pl.pallas_call(functools.partial(accumulate_kernel, spans, len(pieces), t...  5.23 us
    ppermute x1, starting transfers between devices, body(): lax.ppermute(jnp.stack([r[width:2 * width] for r in rims]), 'row', forward)  3.99 us
    unnamed x4, local copies, waits for them, and re-layouts  3.56 us
    pallas_call x6, Pallas kernels, call(): pl.pallas_call(kernel, out_shape=jax.ShapeDtypeStruct(shape, dtype), in_s...  2.87 us
    ppermute x1, waiting for transfers between devices, body(): right = lax.ppermute(first, 'col', backward)  2.81 us
    ppermute x1, starting transfers between devices, body(): rims = [rim] + [lax.ppermute(rim, 'filt', ring) for ring in rings]  2.13 us
    ppermute x1, starting transfers between devices, body(): right = lax.ppermute(first, 'col', backward)  1.92 us
  transfers between devices with their start and end apart: 8, of which 2 were waited for; matrix products, arithmetic and copies ran while one was open for 2% of the time, Pallas kernels for 19%

profile of v3, /device:TPU:1, one launch (start us, length us, event | category | flops | bytes accessed | tf_op | source)
XLA Modules:
  0.0 34.5 jit_solution(17887628569657522113)
XLA Ops:
  0.0 0.0 copy-start.1
  0.0 1.2 %copy-done.1 = bf16[256,16,128]{2,1,0:T(8,128)(2,1)S(1)} copy-done((bf16[256,16,128]{2,1,0:T(8,128)(2,1)S(1)}, bf16[256,16,128]{2,1,0:T(8,128)(2,1)}, u32[]{:S(2)}) %copy-start.1) | copy-done | bytes 1048600
  1.2 0.8 %relayout.1 = (bf16[288,256]{1,0:T(8,128)(2,1)S(1)}, bf16[7,128,256]{2,1,0:T(8,128)(2,1)S(1)}, bf16[7,128,256]{2,1,0:T(8,128)(2,1)S(1)}) custom-call(bf16[256,16,128]{2,1,0:T(8,128)(2,1)S(1)} %copy-done.1), custom_call_target="tpu_custom_call" | custom-call | tf_op jit(solution)/shard_map/relayout/pallas_call | solution.py:41
  2.0 2.1 %collective-permute-start = (bf16[288,256]{1,0:T(8,128)(2,1)S(1)}, bf16[288,256]{1,0:T(8,128)(2,1)S(1)}, u32[]{:S(2)}, u32[]{:S(2)}) collective-permute-start(bf16[288,256]{1,0:T(8,128)(2,1)S(1)} %get-tuple-element.11), channel_id=1, source_target_pairs={{0,1},{1,0},{2,3},{3,2},{4,5},{5,4},{6,7},{7,6},{8,9},{9,8},{10,11... | collective-permute-start | bytes 442376 | tf_op jit(solution)/shard_map/ppermute | solution.py:255
  4.2 0.1 collective-permute-start.4
  4.3 0.7 %reshape.11.bias_ref = f32[2,256]{1,0:T(2,128)S(1)} reshape(f32[512]{0:T(512)} %param.5) | data formatting | bytes 4096 | tf_op jit(solution)/shard_map/reshape | solution.py:250
  5.0 0.0 copy-start
  5.0 2.3 %copy-done = bf16[3,3,512,512]{3,2,1,0:T(8,128)(2,1)S(1)} copy-done((bf16[3,3,512,512]{3,2,1,0:T(8,128)(2,1)S(1)}, bf16[3,3,512,512]{3,2,1,0:T(8,128)(2,1)}, u32[]{:S(2)}) %copy-start) | copy-done | bytes 4718616
  7.3 0.2 split_weights.1
  7.5 0.2 collective-permute-done.after_ref.refs_4_
  7.8 1.3 %collective-permute-start.1 = (bf16[2,128,256]{2,1,0:T(8,128)(2,1)S(1)}, bf16[2,128,256]{2,1,0:T(8,128)(2,1)S(1)}, u32[]{:S(2)}, u32[]{:S(2)}) collective-permute-start(bf16[2,128,256]{2,1,0:T(8,128)(2,1)S(1)} %pad_maximum_fusion), channel_id=1, source_target_pairs={{8,0},{16,8},{24,16},{9,1},{17,9},{25,17},{10,2},{18,10},{26,18},{... | collective-permute-start | bytes 393224 | tf_op jit(solution)/shard_map/ppermute | solution.py:264
  9.1 4.0 %collective-permute-start.5 = (bf16[2,128,256]{2,1,0:T(8,128)(2,1)S(1)}, bf16[2,128,256]{2,1,0:T(8,128)(2,1)S(1)}, u32[]{:S(2)}, u32[]{:S(2)}) collective-permute-start(bf16[2,128,256]{2,1,0:T(8,128)(2,1)S(1)} %pad_maximum_fusion.1), channel_id=1, source_target_pairs={{0,8},{8,16},{16,24},{1,9},{9,17},{17,25},{2,10},{10,18},{18,26},{... | collective-permute-start | bytes 393224 | tf_op jit(solution)/shard_map/ppermute | solution.py:265
  13.2 1.2 %collective-permute-start.3 = (bf16[5,128,256]{2,1,0:T(8,128)(2,1)S(1)}, bf16[5,128,256]{2,1,0:T(8,128)(2,1)S(1)}, u32[]{:S(2)}, u32[]{:S(2)}) collective-permute-start(bf16[5,128,256]{2,1,0:T(8,128)(2,1)S(1)} %pick.3), channel_id=1, source_target_pairs={{0,1},{1,0},{2,3},{3,2},{4,5},{5,4},{6,7},{7,6},{8,9},{9,8},{10,11... | collective-permute-start | bytes 983048 | tf_op jit(solution)/shard_map/ppermute | solution.py:259
  14.4 2.6 %accumulate.4.refs_2_ = f32[16,128,256]{2,1,0:T(8,128)S(1)} custom-call(bf16[2,128,256]{2,1,0:T(8,128)(2,1)S(1)} %bitcast.15, bf16[7,128,256]{2,1,0:T(8,128)(2,1)S(1)} %get-tuple-element.13.refs_1_, bf16[7,128,256]{2,1,0:T(8,128)(2,1)S(1)} %get-tuple-element.10.rows_ref.refs_2_, bf16[3,3,256,256]{3,2,1,0:T(8,128)(2,1)S(1)} %get-tuple-element.14.refs_3_.refs_0_, ...), custom_call_target="tpu_custom_call" | custom-call | flops 2415919104 | bytes 1048576 | tf_op jit(solution)/shard_map/accumulate/pallas_call | solution.py:112
  17.0 0.4 %accumulate.5.refs_2_ = f32[16,128,256]{2,1,0:T(8,128)S(1)} custom-call(bf16[2,128,256]{2,1,0:T(8,128)(2,1)S(1)} %bitcast.14, bf16[3,3,256,256]{3,2,1,0:T(8,128)(2,1)S(1)} %get-tuple-element.12.refs_1_.w_ref, f32[16,128,256]{2,1,0:T(8,128)S(1)} %accumulate.4.refs_2_), custom_call_target="tpu_custom_call", output_to_operand_aliasing={{}: (2, {})} | custom-call | flops 301989888 | bytes 1048576 | tf_op jit(solution)/shard_map/accumulate/pallas_call | solution.py:112
  17.4 0.0 collective-permute-done.1.after_ref.below_ref
  17.4 0.3 %collective-permute-start.2 = (bf16[2,128,256]{2,1,0:T(8,128)(2,1)S(1)}, bf16[2,128,256]{2,1,0:T(8,128)(2,1)S(1)}, u32[]{:S(2)}, u32[]{:S(2)}) collective-permute-start(bf16[2,128,256]{2,1,0:T(8,128)(2,1)S(1)} %pick.2), channel_id=1, source_target_pairs={{0,1},{1,0},{2,3},{3,2},{4,5},{5,4},{6,7},{7,6},{8,9},{9,8},{10,11... | collective-permute-start | bytes 393224 | tf_op jit(solution)/shard_map/ppermute | solution.py:268
  17.8 0.0 collective-permute-done.5.above_ref
  17.8 6.7 %collective-permute-start.6 = (bf16[2,18,256]{2,1,0:T(8,128)(2,1)S(1)}, bf16[2,18,256]{2,1,0:T(8,128)(2,1)S(1)}, u32[]{:S(2)}, u32[]{:S(2)}) collective-permute-start(bf16[2,18,256]{2,1,0:T(8,128)(2,1)S(1)} %pad_maximum_fusion.2), channel_id=1, source_target_pairs={{0,2},{2,4},{4,6},{1,3},{3,5},{5,7},{8,10},{10,12},{12,14},{9,11},... | collective-permute-start | bytes 55304 | tf_op jit(solution)/shard_map/ppermute | solution.py:276
  24.6 1.9 %collective-permute-start.7 = (bf16[2,18,256]{2,1,0:T(8,128)(2,1)S(1)}, bf16[2,18,256]{2,1,0:T(8,128)(2,1)S(1)}, u32[]{:S(2)}, u32[]{:S(2)}) collective-permute-start(bf16[2,18,256]{2,1,0:T(8,128)(2,1)S(1)} %fusion.5), channel_id=1, source_target_pairs={{2,0},{4,2},{6,4},{3,1},{5,3},{7,5},{10,8},{12,10},{14,12},{11,9},... | collective-permute-start | bytes 55304 | tf_op jit(solution)/shard_map/ppermute | solution.py:277
  26.5 0.4 %outer_rows.1.rows_ref = f32[2,128,256]{2,1,0:T(8,128)S(1)} custom-call(bf16[2,128,256]{2,1,0:T(8,128)(2,1)S(1)} %collective-permute-done.5.above_ref, bf16[2,128,256]{2,1,0:T(8,128)(2,1)S(1)} %collective-permute-done.1.after_ref.below_ref, bf16[3,3,256,256]{3,2,1,0:T(8,128)(2,1)S(1)} %get-tuple-element.14.refs_3_.refs_0_, ...), custom_call_target="tpu_custom_call" | custom-call | flops 201326592 | bytes 1048576 | tf_op jit(solution)/shard_map/outer_rows/pallas_call | solution.py:200
  26.9 0.0 collective-permute-done.6.left_ref
  26.9 2.8 %collective-permute-done.7.right_ref = bf16[2,18,256]{2,1,0:T(8,128)(2,1)S(1)} collective-permute-done((bf16[2,18,256]{2,1,0:T(8,128)(2,1)S(1)}, bf16[2,18,256]{2,1,0:T(8,128)(2,1)S(1)}, u32[]{:S(2)}, u32[]{:S(2)}) %collective-permute-start.7) | collective-permute-done | bytes 18464 | tf_op jit(solution)/shard_map/ppermute | solution.py:277
  29.7 0.4 %outer_cols.1.cols_ref = f32[2,16,256]{2,1,0:T(8,128)S(1)} custom-call(bf16[2,18,256]{2,1,0:T(8,128)(2,1)S(1)} %collective-permute-done.6.left_ref, bf16[2,18,256]{2,1,0:T(8,128)(2,1)S(1)} %collective-permute-done.7.right_ref, bf16[3,3,256,256]{3,2,1,0:T(8,128)(2,1)S(1)} %get-tuple-element.14.refs_3_.refs_0_, ...), custom_call_target="tpu_custom_call" | custom-call | flops 402653184 | bytes 1048576 | tf_op jit(solution)/shard_map/outer_cols/pallas_call | solution.py:200
  30.1 0.0 collective-permute-done.4.refs_0_
  30.1 1.3 %accumulate.6.refs_2_ = f32[16,128,256]{2,1,0:T(8,128)S(1)} custom-call(bf16[7,128,256]{2,1,0:T(8,128)(2,1)S(1)} %collective-permute-done.4.refs_0_, bf16[3,3,256,256]{3,2,1,0:T(8,128)(2,1)S(1)} %get-tuple-element.12.refs_1_.w_ref, f32[16,128,256]{2,1,0:T(8,128)S(1)} %accumulate.5.refs_2_), custom_call_target="tpu_custom_call", output_to_operand_aliasing={{}: (2, {})} | custom-call | flops 1056964608 | bytes 1048576 | tf_op jit(solution)/shard_map/accumulate/pallas_call | solution.py:112
  31.4 0.0 collective-permute-done.3.refs_0_
  31.4 1.0 %accumulate.7.total_ref.total_in = f32[16,128,256]{2,1,0:T(8,128)S(1)} custom-call(bf16[5,128,256]{2,1,0:T(8,128)(2,1)S(1)} %collective-permute-done.3.refs_0_, bf16[3,3,256,256]{3,2,1,0:T(8,128)(2,1)S(1)} %get-tuple-element.12.refs_1_.w_ref, f32[16,128,256]{2,1,0:T(8,128)S(1)} %accumulate.6.refs_2_), custom_call_target="tpu_custom_call", output_to_operand_aliasing={{}: (2, {})} | custom-call | flops 754974720 | bytes 1048576 | tf_op jit(solution)/shard_map/accumulate/pallas_call | solution.py:112
  32.4 0.5 %upper.1.upper_ref = bf16[256,8,128]{2,1,0:T(8,128)(2,1)S(1)} custom-call(f32[16,128,256]{2,1,0:T(8,128)S(1)} %accumulate.7.total_ref.total_in, f32[2,256]{1,0:T(2,128)S(1)} %reshape.11.bias_ref, f32[2,128,256]{2,1,0:T(8,128)S(1)} %outer_rows.1.rows_ref, f32[2,16,256]{2,1,0:T(8,128)S(1)} %outer_cols.1.cols_ref), custom_call_target="tpu_custom_call" | custom-call | flops 33554432 | bytes 1048576 | tf_op jit(solution)/shard_map/upper/pallas_call | solution.py:200
  32.9 0.0 collective-permute-done.2.piece
  32.9 1.6 %last.1 = bf16[256,16,128]{2,1,0:T(8,128)(2,1)} custom-call(bf16[2,128,256]{2,1,0:T(8,128)(2,1)S(1)} %collective-permute-done.2.piece, bf16[3,3,256,256]{3,2,1,0:T(8,128)(2,1)S(1)} %get-tuple-element.12.refs_1_.w_ref, f32[16,128,256]{2,1,0:T(8,128)S(1)} %accumulate.7.total_ref.total_in, f32[2,256]{1,0:T(2,128)S(1)} %reshape.11.bias_ref, ...), custom_call_target="tpu_custom_call" | custom-call | flops 301989888 | bytes 1048576 | tf_op jit(solution)/shard_map/last/pallas_call | solution.py:200
  (15 shorter events, 0.2 us)
Async XLA Ops:
  0.0 1.2 %copy-start.1 = (bf16[256,16,128]{2,1,0:T(8,128)(2,1)S(1)}, bf16[256,16,128]{2,1,0:T(8,128)(2,1)}, u32[]{:S(2)}) copy-start(bf16[256,16,128]{2,1,0:T(8,128)(2,1)} %x_ref.1) | copy-start | bytes 3145732
  2.0 5.7 %collective-permute-start = (bf16[288,256]{1,0:T(8,128)(2,1)S(1)}, bf16[288,256]{1,0:T(8,128)(2,1)S(1)}, u32[]{:S(2)}, u32[]{:S(2)}) collective-permute-start(bf16[288,256]{1,0:T(8,128)(2,1)S(1)} %get-tuple-element.11), channel_id=1, source_target_pairs={{0,1},{1,0},{2,3},{3,2},{4,5},{5,4},{6,7},{7,6},{8,9},{9,8},{10,11... | collective-permute-start | bytes 442376 | tf_op jit(solution)/shard_map/ppermute | solution.py:255
  4.2 25.9 %collective-permute-start.4 = (bf16[7,128,256]{2,1,0:T(8,128)(2,1)S(1)}, bf16[7,128,256]{2,1,0:T(8,128)(2,1)S(1)}, u32[]{:S(2)}, u32[]{:S(2)}) collective-permute-start(bf16[7,128,256]{2,1,0:T(8,128)(2,1)S(1)} %get-tuple-element.13.refs_1_), channel_id=1, source_target_pairs={{0,1},{1,0},{2,3},{3,2},{4,5},{5,4},{6,7},{7,6},{8,9},{9,8},{10,11... | collective-permute-start | bytes 1376264 | tf_op jit(solution)/shard_map/ppermute | solution.py:256
  5.0 2.3 %copy-start = (bf16[3,3,512,512]{3,2,1,0:T(8,128)(2,1)S(1)}, bf16[3,3,512,512]{3,2,1,0:T(8,128)(2,1)}, u32[]{:S(2)}) copy-start(bf16[3,3,512,512]{3,2,1,0:T(8,128)(2,1)} %kernel_ref.1) | copy-start | bytes 14155780
  7.8 9.6 %collective-permute-start.1 = (bf16[2,128,256]{2,1,0:T(8,128)(2,1)S(1)}, bf16[2,128,256]{2,1,0:T(8,128)(2,1)S(1)}, u32[]{:S(2)}, u32[]{:S(2)}) collective-permute-start(bf16[2,128,256]{2,1,0:T(8,128)(2,1)S(1)} %pad_maximum_fusion), channel_id=1, source_target_pairs={{8,0},{16,8},{24,16},{9,1},{17,9},{25,17},{10,2},{18,10},{26,18},{... | collective-permute-start | bytes 393224 | tf_op jit(solution)/shard_map/ppermute | solution.py:264
  9.1 8.7 %collective-permute-start.5 = (bf16[2,128,256]{2,1,0:T(8,128)(2,1)S(1)}, bf16[2,128,256]{2,1,0:T(8,128)(2,1)S(1)}, u32[]{:S(2)}, u32[]{:S(2)}) collective-permute-start(bf16[2,128,256]{2,1,0:T(8,128)(2,1)S(1)} %pad_maximum_fusion.1), channel_id=1, source_target_pairs={{0,8},{8,16},{16,24},{1,9},{9,17},{17,25},{2,10},{10,18},{18,26},{... | collective-permute-start | bytes 393224 | tf_op jit(solution)/shard_map/ppermute | solution.py:265
  13.2 18.3 %collective-permute-start.3 = (bf16[5,128,256]{2,1,0:T(8,128)(2,1)S(1)}, bf16[5,128,256]{2,1,0:T(8,128)(2,1)S(1)}, u32[]{:S(2)}, u32[]{:S(2)}) collective-permute-start(bf16[5,128,256]{2,1,0:T(8,128)(2,1)S(1)} %pick.3), channel_id=1, source_target_pairs={{0,1},{1,0},{2,3},{3,2},{4,5},{5,4},{6,7},{7,6},{8,9},{9,8},{10,11... | collective-permute-start | bytes 983048 | tf_op jit(solution)/shard_map/ppermute | solution.py:259
  17.4 15.4 %collective-permute-start.2 = (bf16[2,128,256]{2,1,0:T(8,128)(2,1)S(1)}, bf16[2,128,256]{2,1,0:T(8,128)(2,1)S(1)}, u32[]{:S(2)}, u32[]{:S(2)}) collective-permute-start(bf16[2,128,256]{2,1,0:T(8,128)(2,1)S(1)} %pick.2), channel_id=1, source_target_pairs={{0,1},{1,0},{2,3},{3,2},{4,5},{5,4},{6,7},{7,6},{8,9},{9,8},{10,11... | collective-permute-start | bytes 393224 | tf_op jit(solution)/shard_map/ppermute | solution.py:268
  17.8 9.1 %collective-permute-start.6 = (bf16[2,18,256]{2,1,0:T(8,128)(2,1)S(1)}, bf16[2,18,256]{2,1,0:T(8,128)(2,1)S(1)}, u32[]{:S(2)}, u32[]{:S(2)}) collective-permute-start(bf16[2,18,256]{2,1,0:T(8,128)(2,1)S(1)} %pad_maximum_fusion.2), channel_id=1, source_target_pairs={{0,2},{2,4},{4,6},{1,3},{3,5},{5,7},{8,10},{10,12},{12,14},{9,11},... | collective-permute-start | bytes 55304 | tf_op jit(solution)/shard_map/ppermute | solution.py:276
  24.6 5.1 %collective-permute-start.7 = (bf16[2,18,256]{2,1,0:T(8,128)(2,1)S(1)}, bf16[2,18,256]{2,1,0:T(8,128)(2,1)S(1)}, u32[]{:S(2)}, u32[]{:S(2)}) collective-permute-start(bf16[2,18,256]{2,1,0:T(8,128)(2,1)S(1)} %fusion.5), channel_id=1, source_target_pairs={{2,0},{4,2},{6,4},{3,1},{5,3},{7,5},{10,8},{12,10},{14,12},{11,9},... | collective-permute-start | bytes 55304 | tf_op jit(solution)/shard_map/ppermute | solution.py:277

commit v4 on v3

--- a/solution.py
+++ b/solution.py
@@ -162,7 +162,7 @@
 
 def finish_row(total_ref, h, bias_ref, rows_ref, cols_ref):
     height, width = cols_ref.shape[1], total_ref.shape[1]
-    value = total_ref[h] + bias_ref[pl.ds(lax.axis_index("filt"), 1), :]
+    value = total_ref[h] + bias_ref[...]
     if h == 0:
         value += rows_ref[0]
     if h == height - 1:
@@ -209,36 +209,40 @@
     )(*operands)
 
 
-def weights_kernel(groups, kernel_ref, *refs):
-    outs, sems = refs[:-1], refs[-1]
+def weights_kernel(groups, kernel_ref, bias_ref, *refs):
+    outs, own_bias_ref, sems = refs[:-2], refs[-2], refs[-1]
     slab, width = outs[0].shape[2:]
     owner = lax.axis_index("filt")
+    own = pl.ds(pl.multiple_of(owner * width, width), width)
     copies = []
     for shift, out in enumerate(outs):
         group = lax.rem(owner - shift + groups, groups)
-        source = kernel_ref.at[:, :, pl.ds(pl.multiple_of(group * slab, slab), slab), pl.ds(pl.multiple_of(owner * width, width), width)]
+        source = kernel_ref.at[:, :, pl.ds(pl.multiple_of(group * slab, slab), slab), own]
         copies.append(pltpu.make_async_copy(source, out, sems.at[shift]))
     for copy in copies:
         copy.start()
+    own_bias_ref[...] = bias_ref[:, own]
     for copy in copies:
         copy.wait()
 
 
-def split_weights(kernel, groups, slab, outs):
+def split_weights(kernel, bias, groups, slab, outs):
     if outs % 128 == 0 and slab % 128 == 0:
+        shapes = [jax.ShapeDtypeStruct((3, 3, slab, outs), BF16)] * groups
         return pl.pallas_call(
             functools.partial(weights_kernel, groups),
-            out_shape=[jax.ShapeDtypeStruct((3, 3, slab, outs), BF16)] * groups,
-            in_specs=[HBM],
-            out_specs=[VMEM] * groups,
+            out_shape=[*shapes, jax.ShapeDtypeStruct((1, outs), F32)],
+            in_specs=[HBM, VMEM],
+            out_specs=[VMEM] * (groups + 1),
             scratch_shapes=[pltpu.SemaphoreType.DMA((groups,))],
             compiler_params=PARAMS,
             name="split_weights",
-        )(kernel)
+        )(kernel, bias)
     owner = lax.axis_index("filt")
     own = lax.dynamic_slice_in_dim(kernel, owner * outs, outs, 3)
     order = [lax.rem(owner - shift + groups, groups) for shift in range(groups)]
-    return [lax.dynamic_slice_in_dim(own, group * slab, slab, 2) for group in order]
+    weights = [lax.dynamic_slice_in_dim(own, group * slab, slab, 2) for group in order]
+    return [*weights, lax.dynamic_slice_in_dim(bias, owner * outs, outs, 1)]
 
 
 def body(features, kernel, bias):
@@ -247,14 +251,13 @@
     outs = kernel.shape[3] // groups
     half = height // 2
     chunks = ((1, half), (half, height - 3), (height - 3, height - 1))
-    bias = bias.reshape(groups, outs)
 
     rim, upper_rows, lower_rows = relayout(features, ((1, half), (half, height - 1)))
-    weights = split_weights(kernel, groups, slab, outs)
+    *weights, bias = split_weights(kernel, bias[None, :], groups, slab, outs)
     rings = [[(i, (i + shift) % groups) for i in range(groups)] for shift in range(1, groups)]
     rims = [rim] + [lax.ppermute(rim, "filt", ring) for ring in rings]
     sets = [[lax.ppermute(upper_rows, "filt", ring)] for ring in rings]
-    second = pick(lower_rows, 0, chunks[1][1] - half, rims[-1])
+    second = pick(lower_rows, 0, chunks[1][1] - half, weights[0])
     for received, ring in zip(sets, rings):
         received.append(lax.ppermute(second, "filt", ring))
 
@@ -263,10 +266,6 @@
     backward = [(t, s) for s, t in forward]
     below = lax.ppermute(jnp.stack([r[0:width] for r in rims]), "row", backward)
     above = lax.ppermute(jnp.stack([r[width : 2 * width] for r in rims]), "row", forward)
-    third = pick(lower_rows, chunks[2][0] - half, chunks[2][1] - half, below)
-    for received, ring in zip(sets, rings):
-        received.append(lax.ppermute(third, "filt", ring))
-
     count = lax.axis_size("col")
     forward = [(i, i + 1) for i in range(count - 1)]
     backward = [(t, s) for s, t in forward]
@@ -276,27 +275,27 @@
     left = lax.ppermute(final, "col", forward)
     right = lax.ppermute(first, "col", backward)
 
+    shape = (height, width, outs)
+    pairs = [r[0 : 2 * width].reshape(2, width, slab) for r in rims]
+    outer = [(0, 0, 0, 1), (0, 1, height - 1, 1)]
+    spans = [*outer, (1, 0, 1, half - 1), (2, 0, half, half - 1)]
+    total = accumulate(spans, [pairs[0], upper_rows, lower_rows], weights[0], None, shape, rims[-1])
+    third = pick(lower_rows, chunks[2][0] - half, chunks[2][1] - half, sets[-1][0])
+    for received, ring in zip(sets, rings):
+        received.append(lax.ppermute(third, "filt", ring))
     rows_fix = call(
         functools.partial(outer_rows_kernel, groups), "outer_rows", (2, width, outs), F32,
         [above, below, *weights], cost(6 * width * groups, slab, outs), [pltpu.VMEM((3, 1, width, slab), BF16)],
     )
+    for g in range(1, groups):
+        total = accumulate(outer, [pairs[g]], weights[g], total, shape, rows_fix)
+        total = accumulate([(0, 0, chunks[0][0], half - 1)], [sets[g - 1][0]], weights[g], total, shape)
     cols_fix = call(
         functools.partial(outer_cols_kernel, groups), "outer_cols", (2, height, outs), F32,
-        [left, right, *weights], cost(6 * 256 * groups, slab, outs),
+        [left, right, *weights, total], cost(6 * 256 * groups, slab, outs),
     )
-
-    shape = (height, width, outs)
-    total = None
-    for g in range(groups):
-        rim = rims[g][0 : 2 * width].reshape(2, width, slab)
-        spans = [(0, 0, 0, 1), (0, 1, height - 1, 1)]
-        if g == 0:
-            spans += [(1, 0, 1, half - 1), (2, 0, half, half - 1)]
-            total = accumulate(spans, [rim, upper_rows, lower_rows], weights[g], None, shape, rims[-1])
-            continue
-        a, b, c = sets[g - 1]
-        total = accumulate(spans, [rim], weights[g], total, shape)
-        total = accumulate([(0, 0, chunks[0][0], a.shape[0])], [a], weights[g], total, shape)
+    for g in range(1, groups):
+        b, c = sets[g - 1][1:]
         total = accumulate([(0, 0, chunks[1][0], b.shape[0])], [b], weights[g], total, shape)
         if g < groups - 1:
             total = accumulate([(0, 0, chunks[2][0], c.shape[0])], [c], weights[g], total, shape)

time: 34.8 us -> 33.1 us (0.951)
  waiting for transfers between devices: 3.07 us -> 1.9 us
  starting transfers between devices: 17.7 us -> 16.9 us
    ppermute x1, waiting for transfers between devices: 2.81 us -> 0.01 us  [body(): right = lax.ppermute(first, 'col', backward)]
    ppermute x1, waiting for transfers between devices: 0.01 us -> 1.88 us  [body(): below = lax.ppermute(jnp.stack([r[0:width] for r in rims]), 'row', backward)]
    ppermute x1, starting transfers between devices: 6.72 us -> 5.65 us  [body(): left = lax.ppermute(final, 'col', forward)]
    ppermute x1, starting transfers between devices: 3.99 us -> 3.21 us  [body(): lax.ppermute(jnp.stack([r[width:2 * width] for r in rims]), 'row', forward)]
    ppermute x1, starting transfers between devices: 0.35 us -> 1.12 us  [body(): received.append(lax.ppermute(third, 'filt', ring))]
    reshape x1 -> x0, local copies, waits for them, and re-layouts: 0.7 us -> none  [body(): bias = bias.reshape(groups, outs)]
    unnamed x4 -> x6, local copies, waits for them, and re-layouts: 3.56 us -> 4.24 us
  transfers between devices with their start and end apart: 8 -> 8, of which waited for: 2 -> 1; matrix products, arithmetic and copies ran while one was open for 2% -> 0% of each run, Pallas kernels for 19% -> 21%
where the time goes in v4:
time: 33.1 us; the launch traced here: 32.8 us
  starting transfers between devices  16.9 us (51%)
  Pallas kernels  9.38 us (28%)
  local copies, waits for them, and re-layouts  4.3 us (13%)
  waiting for transfers between devices  1.9 us (6%)
    ppermute x1, starting transfers between devices, body(): left = lax.ppermute(final, 'col', forward)  5.65 us
    pallas_call x4, Pallas kernels, accumulate(): pl.pallas_call(functools.partial(accumulate_kernel, spans, len(pieces), t...  5.51 us
    unnamed x6, local copies, waits for them, and re-layouts  4.24 us
    ppermute x1, starting transfers between devices, body(): lax.ppermute(jnp.stack([r[width:2 * width] for r in rims]), 'row', forward)  3.21 us
    pallas_call x6, Pallas kernels, call(): pl.pallas_call(kernel, out_shape=jax.ShapeDtypeStruct(shape, dtype), in_s...  2.87 us
    ppermute x1, starting transfers between devices, body(): rims = [rim] + [lax.ppermute(rim, 'filt', ring) for ring in rings]  2.13 us
    ppermute x1, starting transfers between devices, body(): right = lax.ppermute(first, 'col', backward)  1.92 us
    ppermute x1, waiting for transfers between devices, body(): below = lax.ppermute(jnp.stack([r[0:width] for r in rims]), 'row', backward)  1.88 us
  transfers between devices with their start and end apart: 8, of which 1 were waited for; matrix products, arithmetic and copies ran while one was open for 0% of the time, Pallas kernels for 21%

profile of v4, /device:TPU:1, one launch (start us, length us, event | category | flops | bytes accessed | tf_op | source)
XLA Modules:
  0.0 32.8 jit_solution(11085394330292717554)
XLA Ops:
  0.0 0.0 copy-start.1
  0.0 1.2 %copy-done.1 = bf16[256,16,128]{2,1,0:T(8,128)(2,1)S(1)} copy-done((bf16[256,16,128]{2,1,0:T(8,128)(2,1)S(1)}, bf16[256,16,128]{2,1,0:T(8,128)(2,1)}, u32[]{:S(2)}) %copy-start.1) | copy-done | bytes 1048600
  1.2 0.8 %relayout.1 = (bf16[288,256]{1,0:T(8,128)(2,1)S(1)}, bf16[7,128,256]{2,1,0:T(8,128)(2,1)S(1)}, bf16[7,128,256]{2,1,0:T(8,128)(2,1)S(1)}) custom-call(bf16[256,16,128]{2,1,0:T(8,128)(2,1)S(1)} %copy-done.1), custom_call_target="tpu_custom_call" | custom-call | tf_op jit(solution)/shard_map/relayout/pallas_call | solution.py:41
  2.0 2.1 %collective-permute-start.3 = (bf16[288,256]{1,0:T(8,128)(2,1)S(1)}, bf16[288,256]{1,0:T(8,128)(2,1)S(1)}, u32[]{:S(2)}, u32[]{:S(2)}) collective-permute-start(bf16[288,256]{1,0:T(8,128)(2,1)S(1)} %get-tuple-element.15), channel_id=1, source_target_pairs={{0,1},{1,0},{2,3},{3,2},{4,5},{5,4},{6,7},{7,6},{8,9},{9,8},{10,11... | collective-permute-start | bytes 442376 | tf_op jit(solution)/shard_map/ppermute | solution.py:258
  4.2 0.1 collective-permute-start
  4.3 0.0 copy-start
  4.3 2.3 %copy-done = bf16[3,3,512,512]{3,2,1,0:T(8,128)(2,1)S(1)} copy-done((bf16[3,3,512,512]{3,2,1,0:T(8,128)(2,1)S(1)}, bf16[3,3,512,512]{3,2,1,0:T(8,128)(2,1)}, u32[]{:S(2)}) %copy-start) | copy-done | bytes 4718616
  6.6 0.0 copy-start.2
  6.6 0.7 %copy-done.2 = f32[512]{0:T(512)S(1)} copy-done((f32[512]{0:T(512)S(1)}, f32[512]{0:T(512)}, u32[]{:S(2)}) %copy-start.2) | copy-done | bytes 2072
  7.3 0.2 split_weights.1
  7.5 1.5 %collective-permute-start.2 = (bf16[5,128,256]{2,1,0:T(8,128)(2,1)S(1)}, bf16[5,128,256]{2,1,0:T(8,128)(2,1)S(1)}, u32[]{:S(2)}, u32[]{:S(2)}) collective-permute-start(bf16[5,128,256]{2,1,0:T(8,128)(2,1)S(1)} %pick.3), channel_id=1, source_target_pairs={{0,1},{1,0},{2,3},{3,2},{4,5},{5,4},{6,7},{7,6},{8,9},{9,8},{10,11... | collective-permute-start | bytes 983048 | tf_op jit(solution)/shard_map/ppermute | solution.py:262
  9.0 0.0 collective-permute-done.3.refs_4_
  9.0 3.2 %collective-permute-start.4 = (bf16[2,128,256]{2,1,0:T(8,128)(2,1)S(1)}, bf16[2,128,256]{2,1,0:T(8,128)(2,1)S(1)}, u32[]{:S(2)}, u32[]{:S(2)}) collective-permute-start(bf16[2,128,256]{2,1,0:T(8,128)(2,1)S(1)} %pad_maximum_fusion), channel_id=1, source_target_pairs={{0,8},{8,16},{16,24},{1,9},{9,17},{17,25},{2,10},{10,18},{18,26},{... | collective-permute-start | bytes 393224 | tf_op jit(solution)/shard_map/ppermute | solution.py:268
  12.3 1.3 %collective-permute-start.5 = (bf16[2,128,256]{2,1,0:T(8,128)(2,1)S(1)}, bf16[2,128,256]{2,1,0:T(8,128)(2,1)S(1)}, u32[]{:S(2)}, u32[]{:S(2)}) collective-permute-start(bf16[2,128,256]{2,1,0:T(8,128)(2,1)S(1)} %pad_maximum_fusion.1), channel_id=1, source_target_pairs={{8,0},{16,8},{24,16},{9,1},{17,9},{25,17},{10,2},{18,10},{26,18},{... | collective-permute-start | bytes 393224 | tf_op jit(solution)/shard_map/ppermute | solution.py:267
  13.6 2.8 %accumulate.4.refs_2_ = f32[16,128,256]{2,1,0:T(8,128)S(1)} custom-call(bf16[2,128,256]{2,1,0:T(8,128)(2,1)S(1)} %bitcast.16, bf16[7,128,256]{2,1,0:T(8,128)(2,1)S(1)} %get-tuple-element.12.refs_1_, bf16[7,128,256]{2,1,0:T(8,128)(2,1)S(1)} %get-tuple-element.11.rows_ref.refs_2_, bf16[3,3,256,256]{3,2,1,0:T(8,128)(2,1)S(1)} %get-tuple-element.14.after_ref.refs_3_.refs_0_, ...), custom_call_target="tpu_custom_call" | custom-call | flops 2415919104 | bytes 1048576 | tf_op jit(solution)/shard_map/accumulate/pallas_call | solution.py:112
  16.4 0.0 collective-permute-done.4.above_ref
  16.4 1.9 %collective-permute-done.5.below_ref = bf16[2,128,256]{2,1,0:T(8,128)(2,1)S(1)} collective-permute-done((bf16[2,128,256]{2,1,0:T(8,128)(2,1)S(1)}, bf16[2,128,256]{2,1,0:T(8,128)(2,1)S(1)}, u32[]{:S(2)}, u32[]{:S(2)}) %collective-permute-start.5) | collective-permute-done | bytes 131104 | tf_op jit(solution)/shard_map/ppermute | solution.py:267
  18.3 5.7 %collective-permute-start.6 = (bf16[2,18,256]{2,1,0:T(8,128)(2,1)S(1)}, bf16[2,18,256]{2,1,0:T(8,128)(2,1)S(1)}, u32[]{:S(2)}, u32[]{:S(2)}) collective-permute-start(bf16[2,18,256]{2,1,0:T(8,128)(2,1)S(1)} %pad_maximum_fusion.2), channel_id=1, source_target_pairs={{0,2},{2,4},{4,6},{1,3},{3,5},{5,7},{8,10},{10,12},{12,14},{9,11},... | collective-permute-start | bytes 55304 | tf_op jit(solution)/shard_map/ppermute | solution.py:275
  24.0 1.9 %collective-permute-start.7 = (bf16[2,18,256]{2,1,0:T(8,128)(2,1)S(1)}, bf16[2,18,256]{2,1,0:T(8,128)(2,1)S(1)}, u32[]{:S(2)}, u32[]{:S(2)}) collective-permute-start(bf16[2,18,256]{2,1,0:T(8,128)(2,1)S(1)} %fusion.5), channel_id=1, source_target_pairs={{2,0},{4,2},{6,4},{3,1},{5,3},{7,5},{10,8},{12,10},{14,12},{11,9},... | collective-permute-start | bytes 55304 | tf_op jit(solution)/shard_map/ppermute | solution.py:276
  25.9 0.4 %outer_rows.1.refs_3_.rows_ref = f32[2,128,256]{2,1,0:T(8,128)S(1)} custom-call(bf16[2,128,256]{2,1,0:T(8,128)(2,1)S(1)} %collective-permute-done.4.above_ref, bf16[2,128,256]{2,1,0:T(8,128)(2,1)S(1)} %collective-permute-done.5.below_ref, bf16[3,3,256,256]{3,2,1,0:T(8,128)(2,1)S(1)} %get-tuple-element.14.after_ref.refs_3_.refs_0_, ...), custom_call_target="tpu_custom_call" | custom-call | flops 201326592 | bytes 1048576 | tf_op jit(solution)/shard_map/outer_rows/pallas_call | solution.py:200
  26.3 0.4 %accumulate.5.refs_2_ = f32[16,128,256]{2,1,0:T(8,128)S(1)} custom-call(bf16[2,128,256]{2,1,0:T(8,128)(2,1)S(1)} %bitcast.15, bf16[3,3,256,256]{3,2,1,0:T(8,128)(2,1)S(1)} %get-tuple-element.13.refs_1_.w_ref, f32[16,128,256]{2,1,0:T(8,128)S(1)} %accumulate.4.refs_2_, f32[2,128,256]{2,1,0:T(8,128)S(1)} %outer_rows.1.refs_3_.rows_ref), custom_call_target="tpu_custom_call", output_to_operand_aliasing={{}: (2, {})} | custom-call | flops 301989888 | bytes 1048576 | tf_op jit(solution)/shard_map/accumulate/pallas_call | solution.py:112
  26.7 0.0 collective-permute-done.after_ref.refs_0_
  26.8 1.1 %collective-permute-start.1 = (bf16[2,128,256]{2,1,0:T(8,128)(2,1)S(1)}, bf16[2,128,256]{2,1,0:T(8,128)(2,1)S(1)}, u32[]{:S(2)}, u32[]{:S(2)}) collective-permute-start(bf16[2,128,256]{2,1,0:T(8,128)(2,1)S(1)} %pick.2), channel_id=1, source_target_pairs={{0,1},{1,0},{2,3},{3,2},{4,5},{5,4},{6,7},{7,6},{8,9},{9,8},{10,11... | collective-permute-start | bytes 393224 | tf_op jit(solution)/shard_map/ppermute | solution.py:285
  27.9 1.3 %accumulate.6.refs_2_ = f32[16,128,256]{2,1,0:T(8,128)S(1)} custom-call(bf16[7,128,256]{2,1,0:T(8,128)(2,1)S(1)} %collective-permute-done.after_ref.refs_0_, bf16[3,3,256,256]{3,2,1,0:T(8,128)(2,1)S(1)} %get-tuple-element.13.refs_1_.w_ref, f32[16,128,256]{2,1,0:T(8,128)S(1)} %accumulate.5.refs_2_), custom_call_target="tpu_custom_call", output_to_operand_aliasing={{}: (2, {})} | custom-call | flops 1056964608 | bytes 1048576 | tf_op jit(solution)/shard_map/accumulate/pallas_call | solution.py:112
  29.2 0.0 collective-permute-done.6.left_ref
  29.3 0.0 collective-permute-done.7.right_ref
  29.3 0.4 %outer_cols.1.cols_ref = f32[2,16,256]{2,1,0:T(8,128)S(1)} custom-call(bf16[2,18,256]{2,1,0:T(8,128)(2,1)S(1)} %collective-permute-done.6.left_ref, bf16[2,18,256]{2,1,0:T(8,128)(2,1)S(1)} %collective-permute-done.7.right_ref, bf16[3,3,256,256]{3,2,1,0:T(8,128)(2,1)S(1)} %get-tuple-element.14.after_ref.refs_3_.refs_0_, ...), custom_call_target="tpu_custom_call" | custom-call | flops 402653184 | bytes 1048576 | tf_op jit(solution)/shard_map/outer_cols/pallas_call | solution.py:200
  29.6 0.0 collective-permute-done.2.refs_0_
  29.7 1.0 %accumulate.7.total_ref.total_in = f32[16,128,256]{2,1,0:T(8,128)S(1)} custom-call(bf16[5,128,256]{2,1,0:T(8,128)(2,1)S(1)} %collective-permute-done.2.refs_0_, bf16[3,3,256,256]{3,2,1,0:T(8,128)(2,1)S(1)} %get-tuple-element.13.refs_1_.w_ref, f32[16,128,256]{2,1,0:T(8,128)S(1)} %accumulate.6.refs_2_), custom_call_target="tpu_custom_call", output_to_operand_aliasing={{}: (2, {})} | custom-call | flops 754974720 | bytes 1048576 | tf_op jit(solution)/shard_map/accumulate/pallas_call | solution.py:112
  30.7 0.5 %upper.1.upper_ref = bf16[256,8,128]{2,1,0:T(8,128)(2,1)S(1)} custom-call(f32[16,128,256]{2,1,0:T(8,128)S(1)} %accumulate.7.total_ref.total_in, f32[1,256]{1,0:T(1,128)S(1)} %get-tuple-element.16.bias_ref, f32[2,128,256]{2,1,0:T(8,128)S(1)} %outer_rows.1.refs_3_.rows_ref, f32[2,16,256]{2,1,0:T(8,128)S(1)} %outer_cols.1.cols_ref), custom_call_target="tpu_custom_call" | custom-call | flops 33554432 | bytes 1048576 | tf_op jit(solution)/shard_map/upper/pallas_call | solution.py:200
  31.1 0.0 collective-permute-done.1.piece
  31.2 1.6 %last.1 = bf16[256,16,128]{2,1,0:T(8,128)(2,1)} custom-call(bf16[2,128,256]{2,1,0:T(8,128)(2,1)S(1)} %collective-permute-done.1.piece, bf16[3,3,256,256]{3,2,1,0:T(8,128)(2,1)S(1)} %get-tuple-element.13.refs_1_.w_ref, f32[16,128,256]{2,1,0:T(8,128)S(1)} %accumulate.7.total_ref.total_in, f32[1,256]{1,0:T(1,128)S(1)} %get-tuple-element.16.bias_ref, ...), custom_call_target="tpu_custom_call" | custom-call | flops 301989888 | bytes 1048576 | tf_op jit(solution)/shard_map/last/pallas_call | solution.py:200
  (15 shorter events, 0.2 us)
Async XLA Ops:
  0.0 1.2 %copy-start.1 = (bf16[256,16,128]{2,1,0:T(8,128)(2,1)S(1)}, bf16[256,16,128]{2,1,0:T(8,128)(2,1)}, u32[]{:S(2)}) copy-start(bf16[256,16,128]{2,1,0:T(8,128)(2,1)} %x_ref.1) | copy-start | bytes 3145732
  2.0 7.0 %collective-permute-start.3 = (bf16[288,256]{1,0:T(8,128)(2,1)S(1)}, bf16[288,256]{1,0:T(8,128)(2,1)S(1)}, u32[]{:S(2)}, u32[]{:S(2)}) collective-permute-start(bf16[288,256]{1,0:T(8,128)(2,1)S(1)} %get-tuple-element.15), channel_id=1, source_target_pairs={{0,1},{1,0},{2,3},{3,2},{4,5},{5,4},{6,7},{7,6},{8,9},{9,8},{10,11... | collective-permute-start | bytes 442376 | tf_op jit(solution)/shard_map/ppermute | solution.py:258
  4.2 22.6 %collective-permute-start = (bf16[7,128,256]{2,1,0:T(8,128)(2,1)S(1)}, bf16[7,128,256]{2,1,0:T(8,128)(2,1)S(1)}, u32[]{:S(2)}, u32[]{:S(2)}) collective-permute-start(bf16[7,128,256]{2,1,0:T(8,128)(2,1)S(1)} %get-tuple-element.12.refs_1_), channel_id=1, source_target_pairs={{0,1},{1,0},{2,3},{3,2},{4,5},{5,4},{6,7},{7,6},{8,9},{9,8},{10,11... | collective-permute-start | bytes 1376264 | tf_op jit(solution)/shard_map/ppermute | solution.py:259
  4.3 2.3 %copy-start = (bf16[3,3,512,512]{3,2,1,0:T(8,128)(2,1)S(1)}, bf16[3,3,512,512]{3,2,1,0:T(8,128)(2,1)}, u32[]{:S(2)}) copy-start(bf16[3,3,512,512]{3,2,1,0:T(8,128)(2,1)} %kernel_ref.1) | copy-start | bytes 14155780
  6.6 0.7 %copy-start.2 = (f32[512]{0:T(512)S(1)}, f32[512]{0:T(512)}, u32[]{:S(2)}) copy-start(f32[512]{0:T(512)} %param.5) | copy-start | bytes 6148
  7.5 22.1 %collective-permute-start.2 = (bf16[5,128,256]{2,1,0:T(8,128)(2,1)S(1)}, bf16[5,128,256]{2,1,0:T(8,128)(2,1)S(1)}, u32[]{:S(2)}, u32[]{:S(2)}) collective-permute-start(bf16[5,128,256]{2,1,0:T(8,128)(2,1)S(1)} %pick.3), channel_id=1, source_target_pairs={{0,1},{1,0},{2,3},{3,2},{4,5},{5,4},{6,7},{7,6},{8,9},{9,8},{10,11... | collective-permute-start | bytes 983048 | tf_op jit(solution)/shard_map/ppermute | solution.py:262
  9.0 7.3 %collective-permute-start.4 = (bf16[2,128,256]{2,1,0:T(8,128)(2,1)S(1)}, bf16[2,128,256]{2,1,0:T(8,128)(2,1)S(1)}, u32[]{:S(2)}, u32[]{:S(2)}) collective-permute-start(bf16[2,128,256]{2,1,0:T(8,128)(2,1)S(1)} %pad_maximum_fusion), channel_id=1, source_target_pairs={{0,8},{8,16},{16,24},{1,9},{9,17},{17,25},{2,10},{10,18},{18,26},{... | collective-permute-start | bytes 393224 | tf_op jit(solution)/shard_map/ppermute | solution.py:268
  12.3 6.0 %collective-permute-start.5 = (bf16[2,128,256]{2,1,0:T(8,128)(2,1)S(1)}, bf16[2,128,256]{2,1,0:T(8,128)(2,1)S(1)}, u32[]{:S(2)}, u32[]{:S(2)}) collective-permute-start(bf16[2,128,256]{2,1,0:T(8,128)(2,1)S(1)} %pad_maximum_fusion.1), channel_id=1, source_target_pairs={{8,0},{16,8},{24,16},{9,1},{17,9},{25,17},{10,2},{18,10},{26,18},{... | collective-permute-start | bytes 393224 | tf_op jit(solution)/shard_map/ppermute | solution.py:267
  18.3 10.9 %collective-permute-start.6 = (bf16[2,18,256]{2,1,0:T(8,128)(2,1)S(1)}, bf16[2,18,256]{2,1,0:T(8,128)(2,1)S(1)}, u32[]{:S(2)}, u32[]{:S(2)}) collective-permute-start(bf16[2,18,256]{2,1,0:T(8,128)(2,1)S(1)} %pad_maximum_fusion.2), channel_id=1, source_target_pairs={{0,2},{2,4},{4,6},{1,3},{3,5},{5,7},{8,10},{10,12},{12,14},{9,11},... | collective-permute-start | bytes 55304 | tf_op jit(solution)/shard_map/ppermute | solution.py:275
  24.0 5.2 %collective-permute-start.7 = (bf16[2,18,256]{2,1,0:T(8,128)(2,1)S(1)}, bf16[2,18,256]{2,1,0:T(8,128)(2,1)S(1)}, u32[]{:S(2)}, u32[]{:S(2)}) collective-permute-start(bf16[2,18,256]{2,1,0:T(8,128)(2,1)S(1)} %fusion.5), channel_id=1, source_target_pairs={{2,0},{4,2},{6,4},{3,1},{5,3},{7,5},{10,8},{12,10},{14,12},{11,9},... | collective-permute-start | bytes 55304 | tf_op jit(solution)/shard_map/ppermute | solution.py:276
  26.8 4.4 %collective-permute-start.1 = (bf16[2,128,256]{2,1,0:T(8,128)(2,1)S(1)}, bf16[2,128,256]{2,1,0:T(8,128)(2,1)S(1)}, u32[]{:S(2)}, u32[]{:S(2)}) collective-permute-start(bf16[2,128,256]{2,1,0:T(8,128)(2,1)S(1)} %pick.2), channel_id=1, source_target_pairs={{0,1},{1,0},{2,3},{3,2},{4,5},{5,4},{6,7},{7,6},{8,9},{9,8},{10,11... | collective-permute-start | bytes 393224 | tf_op jit(solution)/shard_map/ppermute | solution.py:285

commit v5 on v4

--- a/solution.py
+++ b/solution.py
@@ -99,7 +99,7 @@
     add_rows(spans, w_ref, total_ref, x_ref, written)
 
 
-def accumulate(spans, pieces, weights, total, shape, after=None):
+def accumulate(spans, pieces, weights, total, shape, after=None, estimate=None):
     count = sum(s[3] for s in spans)
     width, slab = shape[1], weights.shape[2]
     operands = [*pieces, weights]
@@ -117,7 +117,7 @@
         scratch_shapes=[pltpu.VMEM((3, count, width, slab), BF16)],
         input_output_aliases=aliases,
         compiler_params=PARAMS,
-        cost_estimate=cost(count * width * 9, slab, shape[2]),
+        cost_estimate=estimate or cost(count * width * 9, slab, shape[2]),
         name="accumulate",
     )(*operands)
 
@@ -133,6 +133,22 @@
 
 def cost(pixels, slab, outs):
     return pl.CostEstimate(flops=2 * pixels * slab * outs, bytes_accessed=1 << 20, transcendentals=0)
+
+
+def edges_kernel(groups, *refs):
+    rims, (above_ref, below_ref), outs, col_ref = refs[:groups], refs[groups : groups + 2], refs[-3:-1], refs[-1]
+    width = above_ref.shape[1]
+    height = col_ref.shape[0] - 2
+    for side, out_ref in enumerate(outs):
+        for g in range(groups):
+            rows = rims[g][2 * width + side * height : 2 * width + (side + 1) * height, :].astype(F32)
+            col_ref[1 : height + 1, :] = rows
+            for row, ref in ((0, above_ref), (height + 1, below_ref)):
+                if side:
+                    col_ref[row : row + 1, :] = ref[g, width - 16 :, :].astype(F32)[15:16, :]
+                else:
+                    col_ref[row : row + 1, :] = ref[g, 0:16, :].astype(F32)[0:1, :]
+            out_ref[g] = col_ref[...].astype(BF16)
 
 
 def outer_rows_kernel(groups, above_ref, below_ref, *refs):
@@ -235,7 +251,7 @@
             in_specs=[HBM, VMEM],
             out_specs=[VMEM] * (groups + 1),
             scratch_shapes=[pltpu.SemaphoreType.DMA((groups,))],
-            compiler_params=PARAMS,
+            compiler_params=pltpu.CompilerParams(vmem_limit_bytes=48 << 20),
             name="split_weights",
         )(kernel, bias)
     owner = lax.axis_index("filt")
@@ -253,10 +269,16 @@
     chunks = ((1, half), (half, height - 3), (height - 3, height - 1))
 
     rim, upper_rows, lower_rows = relayout(features, ((1, half), (half, height - 1)))
-    *weights, bias = split_weights(kernel, bias[None, :], groups, slab, outs)
     rings = [[(i, (i + shift) % groups) for i in range(groups)] for shift in range(1, groups)]
     rims = [rim] + [lax.ppermute(rim, "filt", ring) for ring in rings]
     sets = [[lax.ppermute(upper_rows, "filt", ring)] for ring in rings]
+    pairs = [r[0 : 2 * width].reshape(2, width, slab) for r in rims]
+    outer = [(0, 0, 0, 1), (0, 1, height - 1, 1)]
+    shape = (height, width, outs)
+
+    *weights, bias = split_weights(kernel, bias[None, :], groups, slab, outs)
+    spans = [*outer, (1, 0, 1, half - 1), (2, 0, half, half - 1)]
+    total = accumulate(spans, [pairs[0], upper_rows, lower_rows], weights[0], None, shape)
     second = pick(lower_rows, 0, chunks[1][1] - half, weights[0])
     for received, ring in zip(sets, rings):
         received.append(lax.ppermute(second, "filt", ring))
@@ -266,39 +288,42 @@
     backward = [(t, s) for s, t in forward]
     below = lax.ppermute(jnp.stack([r[0:width] for r in rims]), "row", backward)
     above = lax.ppermute(jnp.stack([r[width : 2 * width] for r in rims]), "row", forward)
+    for g in range(1, groups):
+        total = accumulate(outer, [pairs[g]], weights[g], total, shape)
+        total = accumulate([(0, 0, chunks[0][0], half - 1)], [sets[g - 1][0]], weights[g], total, shape)
+    third = pick(lower_rows, chunks[2][0] - half, chunks[2][1] - half, total)
+    for received, ring in zip(sets, rings):
+        received.append(lax.ppermute(third, "filt", ring))
     count = lax.axis_size("col")
     forward = [(i, i + 1) for i in range(count - 1)]
     backward = [(t, s) for s, t in forward]
-    inner = jnp.stack([r[2 * width :] for r in rims])
-    first = jnp.concatenate([above[:, 0:1], inner[:, 0:height], below[:, 0:1]], 1)
-    final = jnp.concatenate([above[:, width - 1 :], inner[:, height:], below[:, width - 1 :]], 1)
+    columns = [jax.ShapeDtypeStruct((groups, height + 2, slab), BF16)] * 2
+    first, final = pl.pallas_call(
+        functools.partial(edges_kernel, groups),
+        out_shape=columns,
+        in_specs=[VMEM] * (groups + 3),
+        out_specs=[VMEM] * 2,
+        scratch_shapes=[pltpu.VMEM((height + 2, slab), F32)],
+        compiler_params=PARAMS,
+        cost_estimate=cost(1, 1, 1),
+        name="edges",
+    )(*rims, above, below, total)
     left = lax.ppermute(final, "col", forward)
     right = lax.ppermute(first, "col", backward)
 
-    shape = (height, width, outs)
-    pairs = [r[0 : 2 * width].reshape(2, width, slab) for r in rims]
-    outer = [(0, 0, 0, 1), (0, 1, height - 1, 1)]
-    spans = [*outer, (1, 0, 1, half - 1), (2, 0, half, half - 1)]
-    total = accumulate(spans, [pairs[0], upper_rows, lower_rows], weights[0], None, shape, rims[-1])
-    third = pick(lower_rows, chunks[2][0] - half, chunks[2][1] - half, sets[-1][0])
-    for received, ring in zip(sets, rings):
-        received.append(lax.ppermute(third, "filt", ring))
     rows_fix = call(
         functools.partial(outer_rows_kernel, groups), "outer_rows", (2, width, outs), F32,
-        [above, below, *weights], cost(6 * width * groups, slab, outs), [pltpu.VMEM((3, 1, width, slab), BF16)],
+        [above, below, *weights, first], cost(6 * width * groups, slab, outs), [pltpu.VMEM((3, 1, width, slab), BF16)],
     )
     for g in range(1, groups):
-        total = accumulate(outer, [pairs[g]], weights[g], total, shape, rows_fix)
-        total = accumulate([(0, 0, chunks[0][0], half - 1)], [sets[g - 1][0]], weights[g], total, shape)
+        b, c = sets[g - 1][1:]
+        total = accumulate([(0, 0, chunks[1][0], b.shape[0])], [b], weights[g], total, shape, rows_fix)
+        if g < groups - 1:
+            total = accumulate([(0, 0, chunks[2][0], c.shape[0])], [c], weights[g], total, shape)
     cols_fix = call(
         functools.partial(outer_cols_kernel, groups), "outer_cols", (2, height, outs), F32,
         [left, right, *weights, total], cost(6 * 256 * groups, slab, outs),
     )
-    for g in range(1, groups):
-        b, c = sets[g - 1][1:]
-        total = accumulate([(0, 0, chunks[1][0], b.shape[0])], [b], weights[g], total, shape)
-        if g < groups - 1:
-            total = accumulate([(0, 0, chunks[2][0], c.shape[0])], [c], weights[g], total, shape)
     top = call(upper_kernel, "upper", (outs, half, width), BF16, [total, bias, rows_fix, cols_fix], cost(256, slab, outs))
     scratch = [
         pltpu.VMEM(shape, F32),

time: 33.1 us -> 34 us (1.027)
  local copies, waits for them, and re-layouts: 4.3 us -> 1.95 us
  waiting for transfers between devices: 1.9 us -> 3.5 us
  Pallas kernels: 9.38 us -> 10.8 us
  starting transfers between devices: 16.9 us -> 17.3 us
    unnamed x6 -> x4, local copies, waits for them, and re-layouts: 4.24 us -> 1.91 us
    ppermute x1, waiting for transfers between devices: 1.88 us -> 0.01 us  [body(): below = lax.ppermute(jnp.stack([r[0:width] for r in rims]), 'row', backward)]
    ppermute x1, waiting for transfers between devices: 0.01 us -> 1.79 us  [body(): right = lax.ppermute(first, 'col', backward)]
    ppermute x1, waiting for transfers between devices: 0.01 us -> 1.69 us  [body(): sets = [[lax.ppermute(upper_rows, 'filt', ring)] for ring in rings]]
    pallas_call x1, Pallas kernels: 0.18 us -> 1.69 us  [split_weights(): pl.pallas_call(functools.partial(weights_kernel, groups), out_shape=[*sha...]
  transfers between devices with their start and end apart: 8 -> 8, of which waited for: 1 -> 2; matrix products, arithmetic and copies ran while one was open for 0% -> 0% of each run, Pallas kernels for 21% -> 25%
where the time goes in v5:
time: 34 us; the launch traced here: 33.8 us
  starting transfers between devices  17.3 us (51%)
  Pallas kernels  10.8 us (32%)
  waiting for transfers between devices  3.5 us (10%)
  local copies, waits for them, and re-layouts  1.95 us (6%)
    ppermute x1, starting transfers between devices, body(): left = lax.ppermute(final, 'col', forward)  5.98 us
    pallas_call x4, Pallas kernels, accumulate(): pl.pallas_call(functools.partial(accumulate_kernel, spans, len(pieces), t...  5.43 us
    ppermute x1, starting transfers between devices, body(): lax.ppermute(jnp.stack([r[width:2 * width] for r in rims]), 'row', forward)  3.21 us
    pallas_call x6, Pallas kernels, call(): pl.pallas_call(kernel, out_shape=jax.ShapeDtypeStruct(shape, dtype), in_s...  2.86 us
    ppermute x1, starting transfers between devices, body(): rims = [rim] + [lax.ppermute(rim, 'filt', ring) for ring in rings]  2.13 us
    ppermute x1, starting transfers between devices, body(): right = lax.ppermute(first, 'col', backward)  1.92 us
    unnamed x4, local copies, waits for them, and re-layouts  1.91 us
    ppermute x1, waiting for transfers between devices, body(): right = lax.ppermute(first, 'col', backward)  1.79 us
  transfers between devices with their start and end apart: 8, of which 2 were waited for; matrix products, arithmetic and copies ran while one was open for 0% of the time, Pallas kernels for 25%

profile of v5, /device:TPU:1, one launch (start us, length us, event | category | flops | bytes accessed | tf_op | source)
XLA Modules:
  0.0 33.8 jit_solution(10469521381010020591)
XLA Ops:
  0.0 0.0 copy-start
  0.0 1.2 %copy-done = bf16[256,16,128]{2,1,0:T(8,128)(2,1)S(1)} copy-done((bf16[256,16,128]{2,1,0:T(8,128)(2,1)S(1)}, bf16[256,16,128]{2,1,0:T(8,128)(2,1)}, u32[]{:S(2)}) %copy-start) | copy-done | bytes 1048600
  1.2 0.8 %relayout.1 = (bf16[288,256]{1,0:T(8,128)(2,1)S(1)}, bf16[7,128,256]{2,1,0:T(8,128)(2,1)S(1)}, bf16[7,128,256]{2,1,0:T(8,128)(2,1)S(1)}) custom-call(bf16[256,16,128]{2,1,0:T(8,128)(2,1)S(1)} %copy-done), custom_call_target="tpu_custom_call" | custom-call | tf_op jit(solution)/shard_map/relayout/pallas_call | solution.py:41
  2.0 2.1 %collective-permute-start.1 = (bf16[288,256]{1,0:T(8,128)(2,1)S(1)}, bf16[288,256]{1,0:T(8,128)(2,1)S(1)}, u32[]{:S(2)}, u32[]{:S(2)}) collective-permute-start(bf16[288,256]{1,0:T(8,128)(2,1)S(1)} %get-tuple-element.16.refs_0_), channel_id=1, source_target_pairs={{0,1},{1,0},{2,3},{3,2},{4,5},{5,4},{6,7},{7,6},{8,9},{9,8},{10,11... | collective-permute-start | bytes 442376 | tf_op jit(solution)/shard_map/ppermute | solution.py:273
  4.2 0.1 collective-permute-start
  4.3 0.0 copy-start.1
  4.3 0.7 %copy-done.1 = f32[512]{0:T(512)S(1)} copy-done((f32[512]{0:T(512)S(1)}, f32[512]{0:T(512)}, u32[]{:S(2)}) %copy-start.1) | copy-done | bytes 2072
  4.9 1.7 %split_weights.1 = (bf16[3,3,256,256]{3,2,1,0:T(8,128)(2,1)S(1)}, bf16[3,3,256,256]{3,2,1,0:T(8,128)(2,1)S(1)}, f32[1,256]{1,0:T(1,128)S(1)}) custom-call(bf16[3,3,512,512]{3,2,1,0:T(8,128)(2,1)} %kernel_ref.1, f32[1,512]{1,0:T(1,128)S(1)} %bitcast.13), custom_call_target="tpu_custom_call" | custom-call | tf_op jit(solution)/shard_map/split_weights/pallas_call | solution.py:248
  6.7 1.5 %collective-permute-start.3 = (bf16[5,128,256]{2,1,0:T(8,128)(2,1)S(1)}, bf16[5,128,256]{2,1,0:T(8,128)(2,1)S(1)}, u32[]{:S(2)}, u32[]{:S(2)}) collective-permute-start(bf16[5,128,256]{2,1,0:T(8,128)(2,1)S(1)} %pick.3), channel_id=1, source_target_pairs={{0,1},{1,0},{2,3},{3,2},{4,5},{5,4},{6,7},{7,6},{8,9},{9,8},{10,11... | collective-permute-start | bytes 983048 | tf_op jit(solution)/shard_map/ppermute | solution.py:284
  8.2 0.0 collective-permute-done.1.refs_1_
  8.2 3.2 %collective-permute-start.4 = (bf16[2,128,256]{2,1,0:T(8,128)(2,1)S(1)}, bf16[2,128,256]{2,1,0:T(8,128)(2,1)S(1)}, u32[]{:S(2)}, u32[]{:S(2)}) collective-permute-start(bf16[2,128,256]{2,1,0:T(8,128)(2,1)S(1)} %pad_maximum_fusion), channel_id=1, source_target_pairs={{0,8},{8,16},{16,24},{1,9},{9,17},{17,25},{2,10},{10,18},{18,26},{... | collective-permute-start | bytes 393224 | tf_op jit(solution)/shard_map/ppermute | solution.py:290
  11.5 1.3 %collective-permute-start.5 = (bf16[2,128,256]{2,1,0:T(8,128)(2,1)S(1)}, bf16[2,128,256]{2,1,0:T(8,128)(2,1)S(1)}, u32[]{:S(2)}, u32[]{:S(2)}) collective-permute-start(bf16[2,128,256]{2,1,0:T(8,128)(2,1)S(1)} %pad_maximum_fusion.1), channel_id=1, source_target_pairs={{8,0},{16,8},{24,16},{9,1},{17,9},{25,17},{10,2},{18,10},{26,18},{... | collective-permute-start | bytes 393224 | tf_op jit(solution)/shard_map/ppermute | solution.py:289
  12.8 2.7 %accumulate.4.refs_2_ = f32[16,128,256]{2,1,0:T(8,128)S(1)} custom-call(bf16[2,128,256]{2,1,0:T(8,128)(2,1)S(1)} %bitcast.12, bf16[7,128,256]{2,1,0:T(8,128)(2,1)S(1)} %get-tuple-element.14.refs_1_, bf16[7,128,256]{2,1,0:T(8,128)(2,1)S(1)} %get-tuple-element.13.refs_2_.rows_ref, bf16[3,3,256,256]{3,2,1,0:T(8,128)(2,1)S(1)} %get-tuple-element.17.refs_3_.after_ref.refs_0_), custom_call_target="tpu_custom_call" | custom-call | flops 2415919104 | bytes 1048576 | tf_op jit(solution)/shard_map/accumulate/pallas_call | solution.py:112
  15.5 0.4 %accumulate.5.refs_2_ = f32[16,128,256]{2,1,0:T(8,128)S(1)} custom-call(bf16[2,128,256]{2,1,0:T(8,128)(2,1)S(1)} %bitcast.11, bf16[3,3,256,256]{3,2,1,0:T(8,128)(2,1)S(1)} %get-tuple-element.15.refs_1_.w_ref, f32[16,128,256]{2,1,0:T(8,128)S(1)} %accumulate.4.refs_2_), custom_call_target="tpu_custom_call", output_to_operand_aliasing={{}: (2, {})} | custom-call | flops 301989888 | bytes 1048576 | tf_op jit(solution)/shard_map/accumulate/pallas_call | solution.py:112
  15.9 1.7 %collective-permute-done.refs_0_ = bf16[7,128,256]{2,1,0:T(8,128)(2,1)S(1)} collective-permute-done((bf16[7,128,256]{2,1,0:T(8,128)(2,1)S(1)}, bf16[7,128,256]{2,1,0:T(8,128)(2,1)S(1)}, u32[]{:S(2)}, u32[]{:S(2)}) %collective-permute-start) | collective-permute-done | bytes 458784 | tf_op jit(solution)/shard_map/ppermute | solution.py:274
  17.6 1.3 %accumulate.6.after_ref.refs_4_.refs_2_ = f32[16,128,256]{2,1,0:T(8,128)S(1)} custom-call(bf16[7,128,256]{2,1,0:T(8,128)(2,1)S(1)} %collective-permute-done.refs_0_, bf16[3,3,256,256]{3,2,1,0:T(8,128)(2,1)S(1)} %get-tuple-element.15.refs_1_.w_ref, f32[16,128,256]{2,1,0:T(8,128)S(1)} %accumulate.5.refs_2_), custom_call_target="tpu_custom_call", output_to_operand_aliasing={{}: (2, {})} | custom-call | flops 1056964608 | bytes 1048576 | tf_op jit(solution)/shard_map/accumulate/pallas_call | solution.py:112
  18.9 1.2 %collective-permute-start.2 = (bf16[2,128,256]{2,1,0:T(8,128)(2,1)S(1)}, bf16[2,128,256]{2,1,0:T(8,128)(2,1)S(1)}, u32[]{:S(2)}, u32[]{:S(2)}) collective-permute-start(bf16[2,128,256]{2,1,0:T(8,128)(2,1)S(1)} %pick.2), channel_id=1, source_target_pairs={{0,1},{1,0},{2,3},{3,2},{4,5},{5,4},{6,7},{7,6},{8,9},{9,8},{10,11... | collective-permute-start | bytes 393224 | tf_op jit(solution)/shard_map/ppermute | solution.py:296
  20.1 0.0 collective-permute-done.4.refs_2_.above_ref
  20.2 0.0 collective-permute-done.5.refs_3_.below_ref
  20.2 6.0 %collective-permute-start.6 = (bf16[2,18,256]{2,1,0:T(8,128)(2,1)S(1)}, bf16[2,18,256]{2,1,0:T(8,128)(2,1)S(1)}, u32[]{:S(2)}, u32[]{:S(2)}) collective-permute-start(bf16[2,18,256]{2,1,0:T(8,128)(2,1)S(1)} %get-tuple-element.20), channel_id=1, source_target_pairs={{0,2},{2,4},{4,6},{1,3},{3,5},{5,7},{8,10},{10,12},{12,14},{9,11},... | collective-permute-start | bytes 55304 | tf_op jit(solution)/shard_map/ppermute | solution.py:311
  26.2 1.9 %collective-permute-start.7 = (bf16[2,18,256]{2,1,0:T(8,128)(2,1)S(1)}, bf16[2,18,256]{2,1,0:T(8,128)(2,1)S(1)}, u32[]{:S(2)}, u32[]{:S(2)}) collective-permute-start(bf16[2,18,256]{2,1,0:T(8,128)(2,1)S(1)} %get-tuple-element.18.refs_2_), channel_id=1, source_target_pairs={{2,0},{4,2},{6,4},{3,1},{5,3},{7,5},{10,8},{12,10},{14,12},{11,9},... | collective-permute-start | bytes 55304 | tf_op jit(solution)/shard_map/ppermute | solution.py:312
  28.1 0.4 %outer_rows.1.refs_3_.rows_ref = f32[2,128,256]{2,1,0:T(8,128)S(1)} custom-call(bf16[2,128,256]{2,1,0:T(8,128)(2,1)S(1)} %collective-permute-done.4.refs_2_.above_ref, bf16[2,128,256]{2,1,0:T(8,128)(2,1)S(1)} %collective-permute-done.5.refs_3_.below_ref, bf16[3,3,256,256]{3,2,1,0:T(8,128)(2,1)S(1)} %get-tuple-element.17.refs_3_.after_ref.refs_0_, ...), custom_call_target="tpu_custom_call" | custom-call | flops 201326592 | bytes 1048576 | tf_op jit(solution)/shard_map/outer_rows/pallas_call | solution.py:216
  28.5 0.0 collective-permute-done.3.refs_0_
  28.5 1.0 %accumulate.7.refs_2_.total_ref.total_in = f32[16,128,256]{2,1,0:T(8,128)S(1)} custom-call(bf16[5,128,256]{2,1,0:T(8,128)(2,1)S(1)} %collective-permute-done.3.refs_0_, bf16[3,3,256,256]{3,2,1,0:T(8,128)(2,1)S(1)} %get-tuple-element.15.refs_1_.w_ref, f32[16,128,256]{2,1,0:T(8,128)S(1)} %accumulate.6.after_ref.refs_4_.refs_2_, ...), custom_call_target="tpu_custom_call", output_to_operand_aliasing={{}: (2, {})} | custom-call | flops 754974720 | bytes 1048576 | tf_op jit(solution)/shard_map/accumulate/pallas_call | solution.py:112
  29.5 0.0 collective-permute-done.6.left_ref
  29.5 1.8 %collective-permute-done.7.right_ref = bf16[2,18,256]{2,1,0:T(8,128)(2,1)S(1)} collective-permute-done((bf16[2,18,256]{2,1,0:T(8,128)(2,1)S(1)}, bf16[2,18,256]{2,1,0:T(8,128)(2,1)S(1)}, u32[]{:S(2)}, u32[]{:S(2)}) %collective-permute-start.7) | collective-permute-done | bytes 18464 | tf_op jit(solution)/shard_map/ppermute | solution.py:312
  31.3 0.4 %outer_cols.1.cols_ref = f32[2,16,256]{2,1,0:T(8,128)S(1)} custom-call(bf16[2,18,256]{2,1,0:T(8,128)(2,1)S(1)} %collective-permute-done.6.left_ref, bf16[2,18,256]{2,1,0:T(8,128)(2,1)S(1)} %collective-permute-done.7.right_ref, bf16[3,3,256,256]{3,2,1,0:T(8,128)(2,1)S(1)} %get-tuple-element.17.refs_3_.after_ref.refs_0_, ...), custom_call_target="tpu_custom_call" | custom-call | flops 402653184 | bytes 1048576 | tf_op jit(solution)/shard_map/outer_cols/pallas_call | solution.py:216
  31.7 0.5 %upper.1.upper_ref = bf16[256,8,128]{2,1,0:T(8,128)(2,1)S(1)} custom-call(f32[16,128,256]{2,1,0:T(8,128)S(1)} %accumulate.7.refs_2_.total_ref.total_in, f32[1,256]{1,0:T(1,128)S(1)} %get-tuple-element.19.bias_ref, f32[2,128,256]{2,1,0:T(8,128)S(1)} %outer_rows.1.refs_3_.rows_ref, f32[2,16,256]{2,1,0:T(8,128)S(1)} %outer_cols.1.cols_ref), custom_call_target="tpu_custom_call" | custom-call | flops 33554432 | bytes 1048576 | tf_op jit(solution)/shard_map/upper/pallas_call | solution.py:216
  32.2 0.0 collective-permute-done.2.piece
  32.2 1.6 %last.1 = bf16[256,16,128]{2,1,0:T(8,128)(2,1)} custom-call(bf16[2,128,256]{2,1,0:T(8,128)(2,1)S(1)} %collective-permute-done.2.piece, bf16[3,3,256,256]{3,2,1,0:T(8,128)(2,1)S(1)} %get-tuple-element.15.refs_1_.w_ref, f32[16,128,256]{2,1,0:T(8,128)S(1)} %accumulate.7.refs_2_.total_ref.total_in, f32[1,256]{1,0:T(1,128)S(1)} %get-tuple-element.19.bias_ref, ...), custom_call_target="tpu_custom_call" | custom-call | flops 301989888 | bytes 1048576 | tf_op jit(solution)/shard_map/last/pallas_call | solution.py:216
  (9 shorter events, 0.1 us)
Async XLA Ops:
  0.0 1.2 %copy-start = (bf16[256,16,128]{2,1,0:T(8,128)(2,1)S(1)}, bf16[256,16,128]{2,1,0:T(8,128)(2,1)}, u32[]{:S(2)}) copy-start(bf16[256,16,128]{2,1,0:T(8,128)(2,1)} %x_ref.1) | copy-start | bytes 3145732
  2.0 6.1 %collective-permute-start.1 = (bf16[288,256]{1,0:T(8,128)(2,1)S(1)}, bf16[288,256]{1,0:T(8,128)(2,1)S(1)}, u32[]{:S(2)}, u32[]{:S(2)}) collective-permute-start(bf16[288,256]{1,0:T(8,128)(2,1)S(1)} %get-tuple-element.16.refs_0_), channel_id=1, source_target_pairs={{0,1},{1,0},{2,3},{3,2},{4,5},{5,4},{6,7},{7,6},{8,9},{9,8},{10,11... | collective-permute-start | bytes 442376 | tf_op jit(solution)/shard_map/ppermute | solution.py:273
  4.2 13.4 %collective-permute-start = (bf16[7,128,256]{2,1,0:T(8,128)(2,1)S(1)}, bf16[7,128,256]{2,1,0:T(8,128)(2,1)S(1)}, u32[]{:S(2)}, u32[]{:S(2)}) collective-permute-start(bf16[7,128,256]{2,1,0:T(8,128)(2,1)S(1)} %get-tuple-element.14.refs_1_), channel_id=1, source_target_pairs={{0,1},{1,0},{2,3},{3,2},{4,5},{5,4},{6,7},{7,6},{8,9},{9,8},{10,11... | collective-permute-start | bytes 1376264 | tf_op jit(solution)/shard_map/ppermute | solution.py:274
  4.3 0.7 %copy-start.1 = (f32[512]{0:T(512)S(1)}, f32[512]{0:T(512)}, u32[]{:S(2)}) copy-start(f32[512]{0:T(512)} %param.5) | copy-start | bytes 6148
  6.7 21.8 %collective-permute-start.3 = (bf16[5,128,256]{2,1,0:T(8,128)(2,1)S(1)}, bf16[5,128,256]{2,1,0:T(8,128)(2,1)S(1)}, u32[]{:S(2)}, u32[]{:S(2)}) collective-permute-start(bf16[5,128,256]{2,1,0:T(8,128)(2,1)S(1)} %pick.3), channel_id=1, source_target_pairs={{0,1},{1,0},{2,3},{3,2},{4,5},{5,4},{6,7},{7,6},{8,9},{9,8},{10,11... | collective-permute-start | bytes 983048 | tf_op jit(solution)/shard_map/ppermute | solution.py:284
  8.2 11.9 %collective-permute-start.4 = (bf16[2,128,256]{2,1,0:T(8,128)(2,1)S(1)}, bf16[2,128,256]{2,1,0:T(8,128)(2,1)S(1)}, u32[]{:S(2)}, u32[]{:S(2)}) collective-permute-start(bf16[2,128,256]{2,1,0:T(8,128)(2,1)S(1)} %pad_maximum_fusion), channel_id=1, source_target_pairs={{0,8},{8,16},{16,24},{1,9},{9,17},{17,25},{2,10},{10,18},{18,26},{... | collective-permute-start | bytes 393224 | tf_op jit(solution)/shard_map/ppermute | solution.py:290
  11.5 8.7 %collective-permute-start.5 = (bf16[2,128,256]{2,1,0:T(8,128)(2,1)S(1)}, bf16[2,128,256]{2,1,0:T(8,128)(2,1)S(1)}, u32[]{:S(2)}, u32[]{:S(2)}) collective-permute-start(bf16[2,128,256]{2,1,0:T(8,128)(2,1)S(1)} %pad_maximum_fusion.1), channel_id=1, source_target_pairs={{8,0},{16,8},{24,16},{9,1},{17,9},{25,17},{10,2},{18,10},{26,18},{... | collective-permute-start | bytes 393224 | tf_op jit(solution)/shard_map/ppermute | solution.py:289
  18.9 13.2 %collective-permute-start.2 = (bf16[2,128,256]{2,1,0:T(8,128)(2,1)S(1)}, bf16[2,128,256]{2,1,0:T(8,128)(2,1)S(1)}, u32[]{:S(2)}, u32[]{:S(2)}) collective-permute-start(bf16[2,128,256]{2,1,0:T(8,128)(2,1)S(1)} %pick.2), channel_id=1, source_target_pairs={{0,1},{1,0},{2,3},{3,2},{4,5},{5,4},{6,7},{7,6},{8,9},{9,8},{10,11... | collective-permute-start | bytes 393224 | tf_op jit(solution)/shard_map/ppermute | solution.py:296
  20.2 9.3 %collective-permute-start.6 = (bf16[2,18,256]{2,1,0:T(8,128)(2,1)S(1)}, bf16[2,18,256]{2,1,0:T(8,128)(2,1)S(1)}, u32[]{:S(2)}, u32[]{:S(2)}) collective-permute-start(bf16[2,18,256]{2,1,0:T(8,128)(2,1)S(1)} %get-tuple-element.20), channel_id=1, source_target_pairs={{0,2},{2,4},{4,6},{1,3},{3,5},{5,7},{8,10},{10,12},{12,14},{9,11},... | collective-permute-start | bytes 55304 | tf_op jit(solution)/shard_map/ppermute | solution.py:311
  26.2 5.1 %collective-permute-start.7 = (bf16[2,18,256]{2,1,0:T(8,128)(2,1)S(1)}, bf16[2,18,256]{2,1,0:T(8,128)(2,1)S(1)}, u32[]{:S(2)}, u32[]{:S(2)}) collective-permute-start(bf16[2,18,256]{2,1,0:T(8,128)(2,1)S(1)} %get-tuple-element.18.refs_2_), channel_id=1, source_target_pairs={{2,0},{4,2},{6,4},{3,1},{5,3},{7,5},{10,8},{12,10},{14,12},{11,9},... | collective-permute-start | bytes 55304 | tf_op jit(solution)/shard_map/ppermute | solution.py:312

commit v6 on v3

--- a/solution.py
+++ b/solution.py
@@ -11,6 +11,7 @@
 VMEM = pl.BlockSpec(memory_space=pltpu.VMEM)
 HBM = pl.BlockSpec(memory_space=pltpu.HBM)
 PARAMS = pltpu.CompilerParams(vmem_limit_bytes=10 << 20)
+WAIT = pl.CostEstimate(flops=6 * 10**9, bytes_accessed=1 << 20, transcendentals=0)
 BLOCK = 4
 
 
@@ -99,7 +100,7 @@
     add_rows(spans, w_ref, total_ref, x_ref, written)
 
 
-def accumulate(spans, pieces, weights, total, shape, after=None):
+def accumulate(spans, pieces, weights, total, shape, after=None, estimate=None):
     count = sum(s[3] for s in spans)
     width, slab = shape[1], weights.shape[2]
     operands = [*pieces, weights]
@@ -117,7 +118,7 @@
         scratch_shapes=[pltpu.VMEM((3, count, width, slab), BF16)],
         input_output_aliases=aliases,
         compiler_params=PARAMS,
-        cost_estimate=cost(count * width * 9, slab, shape[2]),
+        cost_estimate=estimate or cost(count * width * 9, slab, shape[2]),
         name="accumulate",
     )(*operands)
 
@@ -135,25 +136,62 @@
     return pl.CostEstimate(flops=2 * pixels * slab * outs, bytes_accessed=1 << 20, transcendentals=0)
 
 
-def outer_rows_kernel(groups, above_ref, below_ref, *refs):
-    w_refs, fix_ref, x_ref = refs[:groups], refs[-2], refs[-1]
-    for i, (ref, a) in enumerate(((above_ref, 0), (below_ref, 2))):
+def parity(axis):
+    return lax.rem(lax.axis_index(axis), 2)
+
+
+def swap_pairs(axis):
+    count = lax.axis_size(axis)
+    return [[p for i in range(start, count - 1, 2) for p in ((i, i + 1), (i + 1, i))] for start in (1, 0)]
+
+
+def outermost_kernel(groups, *refs):
+    rims, outs = refs[:groups], refs[-2:]
+    width = outs[0].shape[1]
+    odd = parity("row")
+    for swap, out_ref in enumerate(outs):
+        start = pl.multiple_of((odd if swap == 0 else 1 - odd) * width, width)
+        for g in range(groups):
+            out_ref[g] = rims[g][pl.ds(start, width), :]
+
+
+def edges_kernel(groups, *refs):
+    rims, swapped, outs, col_ref = refs[:groups], refs[groups : groups + 2], refs[-3:-1], refs[-1]
+    width = swapped[0].shape[1]
+    height = outs[0].shape[1] - 2
+    odd_row, odd_col = parity("row") == 1, parity("col") == 1
+    for g in range(groups):
+        for side, at in enumerate((0, width - 16)):
+            pixels = [ref[g, at : at + 16, :].astype(F32)[side * 15 : side * 15 + 1, :] for ref in swapped]
+            start = 2 * width + side * height
+            col_ref[side, 0:1, :] = jnp.where(odd_row, pixels[1], pixels[0])
+            col_ref[side, 1 : height + 1, :] = rims[g][start : start + height, :].astype(F32)
+            col_ref[side, height + 1 :, :] = jnp.where(odd_row, pixels[0], pixels[1])
+        outs[0][g] = jnp.where(odd_col, col_ref[1], col_ref[0]).astype(BF16)
+        outs[1][g] = jnp.where(odd_col, col_ref[0], col_ref[1]).astype(BF16)
+
+
+def outer_rows_kernel(groups, *refs):
+    swapped, w_refs, fix_ref, x_ref = refs[:2], refs[2 : 2 + groups], refs[-2], refs[-1]
+    odd = parity("row") == 1
+    for i, a in enumerate((0, 2)):
         fix = None
         for g in range(groups):
-            put_row(x_ref, 0, ref[g])
+            put_row(x_ref, 0, jnp.where(odd, swapped[1 - i][g], swapped[i][g]))
             for b in range(3):
                 part = turn(jnp.dot(x_ref[b, 0], w_refs[g][a, b], preferred_element_type=F32), b)
                 fix = part if fix is None else fix + part
         fix_ref[i] = fix
 
 
-def outer_cols_kernel(groups, left_ref, right_ref, *refs):
-    w_refs, fix_ref = refs[:groups], refs[-1]
+def outer_cols_kernel(groups, *refs):
+    swapped, w_refs, fix_ref = refs[:2], refs[2 : 2 + groups], refs[-1]
     height = fix_ref.shape[1]
-    for i, (ref, b) in enumerate(((left_ref, 0), (right_ref, 2))):
+    odd = parity("col") == 1
+    for i, b in enumerate((0, 2)):
         fix = None
         for g in range(groups):
-            pixels = ref[g]
+            pixels = jnp.where(odd, swapped[1 - i][g], swapped[i][g])
             for a in range(3):
                 part = jnp.dot(pixels, w_refs[g][a, b], preferred_element_type=F32)[a : a + height]
                 fix = part if fix is None else fix + part
@@ -162,7 +200,12 @@
 
 def finish_row(total_ref, h, bias_ref, rows_ref, cols_ref):
     height, width = cols_ref.shape[1], total_ref.shape[1]
-    value = total_ref[h] + bias_ref[pl.ds(lax.axis_index("filt"), 1), :]
+    outs = total_ref.shape[2]
+    if bias_ref.shape[1] == outs:
+        bias = bias_ref[...]
+    else:
+        bias = bias_ref[:, pl.ds(pl.multiple_of(lax.axis_index("filt") * outs, outs), outs)]
+    value = total_ref[h] + bias
     if h == 0:
         value += rows_ref[0]
     if h == height - 1:
@@ -209,15 +252,29 @@
     )(*operands)
 
 
+def calls(kernel, name, shapes, operands, scratch=(), estimate=None):
+    return pl.pallas_call(
+        kernel,
+        out_shape=[jax.ShapeDtypeStruct(shape, BF16) for shape in shapes],
+        in_specs=[VMEM] * len(operands),
+        out_specs=[VMEM] * len(shapes),
+        scratch_shapes=scratch,
+        compiler_params=PARAMS,
+        cost_estimate=estimate or cost(1, 1, 1),
+        name=name,
+    )(*operands)
+
+
 def weights_kernel(groups, kernel_ref, *refs):
     outs, sems = refs[:-1], refs[-1]
     slab, width = outs[0].shape[2:]
     owner = lax.axis_index("filt")
+    own = pl.ds(pl.multiple_of(owner * width, width), width)
     copies = []
     for shift, out in enumerate(outs):
-        group = lax.rem(owner - shift + groups, groups)
-        source = kernel_ref.at[:, :, pl.ds(pl.multiple_of(group * slab, slab), slab), pl.ds(pl.multiple_of(owner * width, width), width)]
-        copies.append(pltpu.make_async_copy(source, out, sems.at[shift]))
+        group = pl.ds(pl.multiple_of(lax.rem(owner - shift + groups, groups) * slab, slab), slab)
+        for a in range(3):
+            copies.append(pltpu.make_async_copy(kernel_ref.at[a, :, group, own], out.at[a], sems.at[shift, a]))
     for copy in copies:
         copy.start()
     for copy in copies:
@@ -231,8 +288,8 @@
             out_shape=[jax.ShapeDtypeStruct((3, 3, slab, outs), BF16)] * groups,
             in_specs=[HBM],
             out_specs=[VMEM] * groups,
-            scratch_shapes=[pltpu.SemaphoreType.DMA((groups,))],
-            compiler_params=PARAMS,
+            scratch_shapes=[pltpu.SemaphoreType.DMA((groups, 3))],
+            compiler_params=pltpu.CompilerParams(vmem_limit_bytes=48 << 20),
             name="split_weights",
         )(kernel)
     owner = lax.axis_index("filt")
@@ -247,59 +304,51 @@
     outs = kernel.shape[3] // groups
     half = height // 2
     chunks = ((1, half), (half, height - 3), (height - 3, height - 1))
-    bias = bias.reshape(groups, outs)
 
     rim, upper_rows, lower_rows = relayout(features, ((1, half), (half, height - 1)))
-    weights = split_weights(kernel, groups, slab, outs)
     rings = [[(i, (i + shift) % groups) for i in range(groups)] for shift in range(1, groups)]
     rims = [rim] + [lax.ppermute(rim, "filt", ring) for ring in rings]
     sets = [[lax.ppermute(upper_rows, "filt", ring)] for ring in rings]
-    second = pick(lower_rows, 0, chunks[1][1] - half, rims[-1])
+    pairs = [r[0 : 2 * width].reshape(2, width, slab) for r in rims]
+    outer = [(0, 0, 0, 1), (0, 1, height - 1, 1)]
+    shape = (height, width, outs)
+
+    weights = split_weights(kernel, groups, slab, outs)
+    bias = bias[None, :]
+    if outs % 128 != 0:
+        bias = lax.dynamic_slice_in_dim(bias, lax.axis_index("filt") * outs, outs, 1)
+    spans = [*outer, (1, 0, 1, half - 1), (2, 0, half, half - 1)]
+    second = pick(lower_rows, 0, chunks[1][1] - half, weights[0])
     for received, ring in zip(sets, rings):
         received.append(lax.ppermute(second, "filt", ring))
 
-    count = lax.axis_size("row")
-    forward = [(i, i + 1) for i in range(count - 1)]
-    backward = [(t, s) for s, t in forward]
-    below = lax.ppermute(jnp.stack([r[0:width] for r in rims]), "row", backward)
-    above = lax.ppermute(jnp.stack([r[width : 2 * width] for r in rims]), "row", forward)
-    third = pick(lower_rows, chunks[2][0] - half, chunks[2][1] - half, below)
+    row_pairs, col_pairs = swap_pairs("row"), swap_pairs("col")
+    sent = calls(functools.partial(outermost_kernel, groups), "outermost", [(groups, width, slab)] * 2, rims, estimate=WAIT)
+    outer_rows = [lax.ppermute(v, "row", p) for v, p in zip(sent, row_pairs)]
+    total = accumulate(spans, [pairs[0], upper_rows, lower_rows], weights[0], None, shape, rims[-1])
+    for g in range(1, groups):
+        total = accumulate(outer, [pairs[g]], weights[g], total, shape)
+    third = pick(lower_rows, chunks[2][0] - half, chunks[2][1] - half, total)
     for received, ring in zip(sets, rings):
         received.append(lax.ppermute(third, "filt", ring))
 
-    count = lax.axis_size("col")
-    forward = [(i, i + 1) for i in range(count - 1)]
-    backward = [(t, s) for s, t in forward]
-    inner = jnp.stack([r[2 * width :] for r in rims])
-    first = jnp.concatenate([above[:, 0:1], inner[:, 0:height], below[:, 0:1]], 1)
-    final = jnp.concatenate([above[:, width - 1 :], inner[:, height:], below[:, width - 1 :]], 1)
-    left = lax.ppermute(final, "col", forward)
-    right = lax.ppermute(first, "col", backward)
-
+    edge = pltpu.VMEM((2, height + 2, slab), F32)
+    sent = calls(functools.partial(edges_kernel, groups), "edges", [(groups, height + 2, slab)] * 2, [*rims, *outer_rows, third], [edge])
+    outer_cols = [lax.ppermute(v, "col", p) for v, p in zip(sent, col_pairs)]
     rows_fix = call(
         functools.partial(outer_rows_kernel, groups), "outer_rows", (2, width, outs), F32,
-        [above, below, *weights], cost(6 * width * groups, slab, outs), [pltpu.VMEM((3, 1, width, slab), BF16)],
+        [*outer_rows, *weights, *sent], cost(6 * width * groups, slab, outs), [pltpu.VMEM((3, 1, width, slab), BF16)],
     )
-    cols_fix = call(
-        functools.partial(outer_cols_kernel, groups), "outer_cols", (2, height, outs), F32,
-        [left, right, *weights], cost(6 * 256 * groups, slab, outs),
-    )
-
-    shape = (height, width, outs)
-    total = None
-    for g in range(groups):
-        rim = rims[g][0 : 2 * width].reshape(2, width, slab)
-        spans = [(0, 0, 0, 1), (0, 1, height - 1, 1)]
-        if g == 0:
-            spans += [(1, 0, 1, half - 1), (2, 0, half, half - 1)]
-            total = accumulate(spans, [rim, upper_rows, lower_rows], weights[g], None, shape, rims[-1])
-            continue
+    for g in range(1, groups):
         a, b, c = sets[g - 1]
-        total = accumulate(spans, [rim], weights[g], total, shape)
-        total = accumulate([(0, 0, chunks[0][0], a.shape[0])], [a], weights[g], total, shape)
+        total = accumulate([(0, 0, chunks[0][0], half - 1)], [a], weights[g], total, shape, rows_fix)
         total = accumulate([(0, 0, chunks[1][0], b.shape[0])], [b], weights[g], total, shape)
         if g < groups - 1:
             total = accumulate([(0, 0, chunks[2][0], c.shape[0])], [c], weights[g], total, shape)
+    cols_fix = call(
+        functools.partial(outer_cols_kernel, groups), "outer_cols", (2, height, outs), F32,
+        [*outer_cols, *weights, total], cost(6 * 256 * groups, slab, outs),
+    )
     top = call(upper_kernel, "upper", (outs, half, width), BF16, [total, bias, rows_fix, cols_fix], cost(256, slab, outs))
     scratch = [
         pltpu.VMEM(shape, F32),

time: 34.8 us -> 32.5 us (0.934)
  the two profiles are of different devices: /device:TPU:1 before, /device:TPU:0 now
where the time goes in v6:
time: 32.5 us; the launch traced here: 32.2 us
  starting transfers between devices  16.4 us (50%)
  Pallas kernels  10.5 us (32%)
  waiting for transfers between devices  3.67 us (11%)
  local copies, waits for them, and re-layouts  1.53 us (5%)
    ppermute x2, starting transfers between devices, body(): outer_rows = [lax.ppermute(v, 'row', p) for v, p in zip(sent, row_pairs)]  5.15 us
    pallas_call x4, Pallas kernels, accumulate(): pl.pallas_call(functools.partial(accumulate_kernel, spans, len(pieces), t...  5.11 us
    ppermute x2, starting transfers between devices, body(): outer_cols = [lax.ppermute(v, 'col', p) for v, p in zip(sent, col_pairs)]  3.58 us
    ppermute x1, waiting for transfers between devices, body(): sets = [[lax.ppermute(upper_rows, 'filt', ring)] for ring in rings]  3.23 us
    ppermute x1, starting transfers between devices, body(): rims = [rim] + [lax.ppermute(rim, 'filt', ring) for ring in rings]  3.03 us
    pallas_call x6, Pallas kernels, call(): pl.pallas_call(kernel, out_shape=jax.ShapeDtypeStruct(shape, dtype), in_s...  2.83 us
    ppermute x1, starting transfers between devices, body(): received.append(lax.ppermute(third, 'filt', ring))  2.54 us
    ppermute x1, starting transfers between devices, body(): sets = [[lax.ppermute(upper_rows, 'filt', ring)] for ring in rings]  2 us
  transfers between devices with their start and end apart: 8, of which 2 were waited for; matrix products, arithmetic and copies ran while one was open for 0% of the time, Pallas kernels for 25%

profile of v6, /device:TPU:0, one launch (start us, length us, event | category | flops | bytes accessed | tf_op | source)
XLA Modules:
  0.0 32.2 jit_solution(17462095880325206258)
XLA Ops:
  0.0 0.0 copy-start
  0.0 1.2 %copy-done = bf16[256,16,128]{2,1,0:T(8,128)(2,1)S(1)} copy-done((bf16[256,16,128]{2,1,0:T(8,128)(2,1)S(1)}, bf16[256,16,128]{2,1,0:T(8,128)(2,1)}, u32[]{:S(2)}) %copy-start) | copy-done | bytes 1048600
  1.2 0.8 %relayout.1 = (bf16[288,256]{1,0:T(8,128)(2,1)S(1)}, bf16[7,128,256]{2,1,0:T(8,128)(2,1)S(1)}, bf16[7,128,256]{2,1,0:T(8,128)(2,1)S(1)}) custom-call(bf16[256,16,128]{2,1,0:T(8,128)(2,1)S(1)} %copy-done), custom_call_target="tpu_custom_call" | custom-call | tf_op jit(solution)/shard_map/relayout/pallas_call | solution.py:42
  2.0 3.0 %collective-permute-start = (bf16[288,256]{1,0:T(8,128)(2,1)S(1)}, bf16[288,256]{1,0:T(8,128)(2,1)S(1)}, u32[]{:S(2)}, u32[]{:S(2)}) collective-permute-start(bf16[288,256]{1,0:T(8,128)(2,1)S(1)} %get-tuple-element.15.refs_0_), channel_id=1, source_target_pairs={{0,1},{1,0},{2,3},{3,2},{4,5},{5,4},{6,7},{7,6},{8,9},{9,8},{10,11... | collective-permute-start | bytes 442376 | tf_op jit(solution)/shard_map/ppermute | solution.py:310
  5.1 1.7 %split_weights.1 = (bf16[3,3,256,256]{3,2,1,0:T(8,128)(2,1)S(1)}, bf16[3,3,256,256]{3,2,1,0:T(8,128)(2,1)S(1)}) custom-call(bf16[3,3,512,512]{3,2,1,0:T(8,128)(2,1)} %kernel_ref.1), custom_call_target="tpu_custom_call" | custom-call | tf_op jit(solution)/shard_map/split_weights/pallas_call | solution.py:286
  6.8 0.1 collective-permute-start.2
  6.9 2.0 %collective-permute-start.3 = (bf16[7,128,256]{2,1,0:T(8,128)(2,1)S(1)}, bf16[7,128,256]{2,1,0:T(8,128)(2,1)S(1)}, u32[]{:S(2)}, u32[]{:S(2)}) collective-permute-start(bf16[7,128,256]{2,1,0:T(8,128)(2,1)S(1)} %get-tuple-element.17.refs_1_), channel_id=1, source_target_pairs={{0,1},{1,0},{2,3},{3,2},{4,5},{5,4},{6,7},{7,6},{8,9},{9,8},{10,11... | collective-permute-start | bytes 1376264 | tf_op jit(solution)/shard_map/ppermute | solution.py:311
  8.9 0.4 %collective-permute-done.refs_4_.refs_1_ = bf16[288,256]{1,0:T(8,128)(2,1)S(1)} collective-permute-done((bf16[288,256]{1,0:T(8,128)(2,1)S(1)}, bf16[288,256]{1,0:T(8,128)(2,1)S(1)}, u32[]{:S(2)}, u32[]{:S(2)}) %collective-permute-start) | collective-permute-done | bytes 147488 | tf_op jit(solution)/shard_map/ppermute | solution.py:310
  9.4 0.7 %collective-permute-start.4 = (bf16[2,128,256]{2,1,0:T(8,128)(2,1)S(1)}, bf16[2,128,256]{2,1,0:T(8,128)(2,1)S(1)}, u32[]{:S(2)}, u32[]{:S(2)}) collective-permute-start(bf16[2,128,256]{2,1,0:T(8,128)(2,1)S(1)} %get-tuple-element.19), channel_id=1, source_target_pairs={{8,16},{16,8},{9,17},{17,9},{10,18},{18,10},{11,19},{19,11},{12,20... | collective-permute-start | bytes 393224 | tf_op jit(solution)/shard_map/ppermute | solution.py:327
  10.0 4.5 %collective-permute-start.5 = (bf16[2,128,256]{2,1,0:T(8,128)(2,1)S(1)}, bf16[2,128,256]{2,1,0:T(8,128)(2,1)S(1)}, u32[]{:S(2)}, u32[]{:S(2)}) collective-permute-start(bf16[2,128,256]{2,1,0:T(8,128)(2,1)S(1)} %get-tuple-element.20), channel_id=1, source_target_pairs={{0,8},{8,0},{16,24},{24,16},{1,9},{9,1},{17,25},{25,17},{2,10},{10... | collective-permute-start | bytes 393224 | tf_op jit(solution)/shard_map/ppermute | solution.py:327
  14.5 2.5 %accumulate.4.refs_2_ = f32[16,128,256]{2,1,0:T(8,128)S(1)} custom-call(bf16[2,128,256]{2,1,0:T(8,128)(2,1)S(1)} %bitcast.4, bf16[7,128,256]{2,1,0:T(8,128)(2,1)S(1)} %get-tuple-element.17.refs_1_, bf16[7,128,256]{2,1,0:T(8,128)(2,1)S(1)} %get-tuple-element.14.refs_2_.rows_ref, bf16[3,3,256,256]{3,2,1,0:T(8,128)(2,1)S(1)} %get-tuple-element.18.refs_3_.after_ref.refs_2_, ...), custom_call_target="tpu_custom_call" | custom-call | flops 2415919104 | bytes 1048576 | tf_op jit(solution)/shard_map/accumulate/pallas_call | solution.py:113
  17.1 0.4 %accumulate.5.after_ref.refs_2_ = f32[16,128,256]{2,1,0:T(8,128)S(1)} custom-call(bf16[2,128,256]{2,1,0:T(8,128)(2,1)S(1)} %bitcast.3, bf16[3,3,256,256]{3,2,1,0:T(8,128)(2,1)S(1)} %get-tuple-element.16.refs_1_.refs_3_.w_ref, f32[16,128,256]{2,1,0:T(8,128)S(1)} %accumulate.4.refs_2_), custom_call_target="tpu_custom_call", output_to_operand_aliasing={{}: (2, {})} | custom-call | flops 301989888 | bytes 1048576 | tf_op jit(solution)/shard_map/accumulate/pallas_call | solution.py:113
  17.5 2.5 %collective-permute-start.1 = (bf16[2,128,256]{2,1,0:T(8,128)(2,1)S(1)}, bf16[2,128,256]{2,1,0:T(8,128)(2,1)S(1)}, u32[]{:S(2)}, u32[]{:S(2)}) collective-permute-start(bf16[2,128,256]{2,1,0:T(8,128)(2,1)S(1)} %pick.2.refs_4_), channel_id=1, source_target_pairs={{0,1},{1,0},{2,3},{3,2},{4,5},{5,4},{6,7},{7,6},{8,9},{9,8},{10,11... | collective-permute-start | bytes 393224 | tf_op jit(solution)/shard_map/ppermute | solution.py:333
  20.0 0.0 collective-permute-done.4.refs_2_.refs_0_
  20.0 0.0 collective-permute-done.5.refs_3_.refs_1_
  20.1 0.7 %collective-permute-start.6 = (bf16[2,18,256]{2,1,0:T(8,128)(2,1)S(1)}, bf16[2,18,256]{2,1,0:T(8,128)(2,1)S(1)}, u32[]{:S(2)}, u32[]{:S(2)}) collective-permute-start(bf16[2,18,256]{2,1,0:T(8,128)(2,1)S(1)} %get-tuple-element.21.refs_4_), channel_id=1, source_target_pairs={{2,4},{4,2},{3,5},{5,3},{10,12},{12,10},{11,13},{13,11},{18,20},{2... | collective-permute-start | bytes 55304 | tf_op jit(solution)/shard_map/ppermute | solution.py:337
  20.7 2.9 %collective-permute-start.7 = (bf16[2,18,256]{2,1,0:T(8,128)(2,1)S(1)}, bf16[2,18,256]{2,1,0:T(8,128)(2,1)S(1)}, u32[]{:S(2)}, u32[]{:S(2)}) collective-permute-start(bf16[2,18,256]{2,1,0:T(8,128)(2,1)S(1)} %get-tuple-element.22.refs_5_), channel_id=1, source_target_pairs={{0,2},{2,0},{4,6},{6,4},{1,3},{3,1},{5,7},{7,5},{8,10},{10,8},{12,... | collective-permute-start | bytes 55304 | tf_op jit(solution)/shard_map/ppermute | solution.py:337
  23.7 0.4 %outer_rows.1.refs_3_.rows_ref = f32[2,128,256]{2,1,0:T(8,128)S(1)} custom-call(bf16[2,128,256]{2,1,0:T(8,128)(2,1)S(1)} %collective-permute-done.4.refs_2_.refs_0_, bf16[2,128,256]{2,1,0:T(8,128)(2,1)S(1)} %collective-permute-done.5.refs_3_.refs_1_, bf16[3,3,256,256]{3,2,1,0:T(8,128)(2,1)S(1)} %get-tuple-element.18.refs_3_.after_ref.refs_2_, ...), custom_call_target="tpu_custom_call" | custom-call | flops 201326592 | bytes 1048576 | tf_op jit(solution)/shard_map/outer_rows/pallas_call | solution.py:243
  24.0 3.2 %collective-permute-done.3.refs_0_ = bf16[7,128,256]{2,1,0:T(8,128)(2,1)S(1)} collective-permute-done((bf16[7,128,256]{2,1,0:T(8,128)(2,1)S(1)}, bf16[7,128,256]{2,1,0:T(8,128)(2,1)S(1)}, u32[]{:S(2)}, u32[]{:S(2)}) %collective-permute-start.3) | collective-permute-done | bytes 458784 | tf_op jit(solution)/shard_map/ppermute | solution.py:311
  27.3 1.2 %accumulate.6.refs_2_ = f32[16,128,256]{2,1,0:T(8,128)S(1)} custom-call(bf16[7,128,256]{2,1,0:T(8,128)(2,1)S(1)} %collective-permute-done.3.refs_0_, bf16[3,3,256,256]{3,2,1,0:T(8,128)(2,1)S(1)} %get-tuple-element.16.refs_1_.refs_3_.w_ref, f32[16,128,256]{2,1,0:T(8,128)S(1)} %accumulate.5.after_ref.refs_2_, ...), custom_call_target="tpu_custom_call", output_to_operand_aliasing={{}: (2, {})} | custom-call | flops 1056964608 | bytes 1048576 | tf_op jit(solution)/shard_map/accumulate/pallas_call | solution.py:113
  28.5 0.0 collective-permute-done.2.refs_0_
  28.5 0.9 %accumulate.7.refs_4_.total_ref.total_in = f32[16,128,256]{2,1,0:T(8,128)S(1)} custom-call(bf16[5,128,256]{2,1,0:T(8,128)(2,1)S(1)} %collective-permute-done.2.refs_0_, bf16[3,3,256,256]{3,2,1,0:T(8,128)(2,1)S(1)} %get-tuple-element.16.refs_1_.refs_3_.w_ref, f32[16,128,256]{2,1,0:T(8,128)S(1)} %accumulate.6.refs_2_), custom_call_target="tpu_custom_call", output_to_operand_aliasing={{}: (2, {})} | custom-call | flops 754974720 | bytes 1048576 | tf_op jit(solution)/shard_map/accumulate/pallas_call | solution.py:113
  29.5 0.0 copy-start.1
  29.5 0.0 collective-permute-done.6.refs_0_
  29.5 0.0 collective-permute-done.7.refs_1_
  29.5 0.4 %outer_cols.1.cols_ref = f32[2,16,256]{2,1,0:T(8,128)S(1)} custom-call(bf16[2,18,256]{2,1,0:T(8,128)(2,1)S(1)} %collective-permute-done.6.refs_0_, bf16[2,18,256]{2,1,0:T(8,128)(2,1)S(1)} %collective-permute-done.7.refs_1_, bf16[3,3,256,256]{3,2,1,0:T(8,128)(2,1)S(1)} %get-tuple-element.18.refs_3_.after_ref.refs_2_, ...), custom_call_target="tpu_custom_call" | custom-call | flops 402653184 | bytes 1048576 | tf_op jit(solution)/shard_map/outer_cols/pallas_call | solution.py:243
  29.9 0.3 copy-done.1
  30.2 0.5 %upper.1.upper_ref = bf16[256,8,128]{2,1,0:T(8,128)(2,1)S(1)} custom-call(f32[16,128,256]{2,1,0:T(8,128)S(1)} %accumulate.7.refs_4_.total_ref.total_in, f32[1,512]{1,0:T(1,128)S(1)} %bitcast.5, f32[2,128,256]{2,1,0:T(8,128)S(1)} %outer_rows.1.refs_3_.rows_ref, f32[2,16,256]{2,1,0:T(8,128)S(1)} %outer_cols.1.cols_ref), custom_call_target="tpu_custom_call" | custom-call | flops 33554432 | bytes 1048576 | tf_op jit(solution)/shard_map/upper/pallas_call | solution.py:243
  30.6 0.0 collective-permute-done.1.piece
  30.7 1.6 %last.1 = bf16[256,16,128]{2,1,0:T(8,128)(2,1)} custom-call(bf16[2,128,256]{2,1,0:T(8,128)(2,1)S(1)} %collective-permute-done.1.piece, bf16[3,3,256,256]{3,2,1,0:T(8,128)(2,1)S(1)} %get-tuple-element.16.refs_1_.refs_3_.w_ref, f32[16,128,256]{2,1,0:T(8,128)S(1)} %accumulate.7.refs_4_.total_ref.total_in, f32[1,512]{1,0:T(1,128)S(1)} %bitcast.6, ...), custom_call_target="tpu_custom_call" | custom-call | flops 301989888 | bytes 1048576 | tf_op jit(solution)/shard_map/last/pallas_call | solution.py:243
  (6 shorter events, 0.1 us)
Async XLA Ops:
  0.0 1.2 %copy-start = (bf16[256,16,128]{2,1,0:T(8,128)(2,1)S(1)}, bf16[256,16,128]{2,1,0:T(8,128)(2,1)}, u32[]{:S(2)}) copy-start(bf16[256,16,128]{2,1,0:T(8,128)(2,1)} %x_ref.1) | copy-start | bytes 3145732
  2.0 7.3 %collective-permute-start = (bf16[288,256]{1,0:T(8,128)(2,1)S(1)}, bf16[288,256]{1,0:T(8,128)(2,1)S(1)}, u32[]{:S(2)}, u32[]{:S(2)}) collective-permute-start(bf16[288,256]{1,0:T(8,128)(2,1)S(1)} %get-tuple-element.15.refs_0_), channel_id=1, source_target_pairs={{0,1},{1,0},{2,3},{3,2},{4,5},{5,4},{6,7},{7,6},{8,9},{9,8},{10,11... | collective-permute-start | bytes 442376 | tf_op jit(solution)/shard_map/ppermute | solution.py:310
  6.8 21.7 %collective-permute-start.2 = (bf16[5,128,256]{2,1,0:T(8,128)(2,1)S(1)}, bf16[5,128,256]{2,1,0:T(8,128)(2,1)S(1)}, u32[]{:S(2)}, u32[]{:S(2)}) collective-permute-start(bf16[5,128,256]{2,1,0:T(8,128)(2,1)S(1)} %pick.3), channel_id=1, source_target_pairs={{0,1},{1,0},{2,3},{3,2},{4,5},{5,4},{6,7},{7,6},{8,9},{9,8},{10,11... | collective-permute-start | bytes 983048 | tf_op jit(solution)/shard_map/ppermute | solution.py:323
  6.9 20.4 %collective-permute-start.3 = (bf16[7,128,256]{2,1,0:T(8,128)(2,1)S(1)}, bf16[7,128,256]{2,1,0:T(8,128)(2,1)S(1)}, u32[]{:S(2)}, u32[]{:S(2)}) collective-permute-start(bf16[7,128,256]{2,1,0:T(8,128)(2,1)S(1)} %get-tuple-element.17.refs_1_), channel_id=1, source_target_pairs={{0,1},{1,0},{2,3},{3,2},{4,5},{5,4},{6,7},{7,6},{8,9},{9,8},{10,11... | collective-permute-start | bytes 1376264 | tf_op jit(solution)/shard_map/ppermute | solution.py:311
  9.4 10.7 %collective-permute-start.4 = (bf16[2,128,256]{2,1,0:T(8,128)(2,1)S(1)}, bf16[2,128,256]{2,1,0:T(8,128)(2,1)S(1)}, u32[]{:S(2)}, u32[]{:S(2)}) collective-permute-start(bf16[2,128,256]{2,1,0:T(8,128)(2,1)S(1)} %get-tuple-element.19), channel_id=1, source_target_pairs={{8,16},{16,8},{9,17},{17,9},{10,18},{18,10},{11,19},{19,11},{12,20... | collective-permute-start | bytes 393224 | tf_op jit(solution)/shard_map/ppermute | solution.py:327
  10.0 10.0 %collective-permute-start.5 = (bf16[2,128,256]{2,1,0:T(8,128)(2,1)S(1)}, bf16[2,128,256]{2,1,0:T(8,128)(2,1)S(1)}, u32[]{:S(2)}, u32[]{:S(2)}) collective-permute-start(bf16[2,128,256]{2,1,0:T(8,128)(2,1)S(1)} %get-tuple-element.20), channel_id=1, source_target_pairs={{0,8},{8,0},{16,24},{24,16},{1,9},{9,1},{17,25},{25,17},{2,10},{10... | collective-permute-start | bytes 393224 | tf_op jit(solution)/shard_map/ppermute | solution.py:327
  17.5 13.2 %collective-permute-start.1 = (bf16[2,128,256]{2,1,0:T(8,128)(2,1)S(1)}, bf16[2,128,256]{2,1,0:T(8,128)(2,1)S(1)}, u32[]{:S(2)}, u32[]{:S(2)}) collective-permute-start(bf16[2,128,256]{2,1,0:T(8,128)(2,1)S(1)} %pick.2.refs_4_), channel_id=1, source_target_pairs={{0,1},{1,0},{2,3},{3,2},{4,5},{5,4},{6,7},{7,6},{8,9},{9,8},{10,11... | collective-permute-start | bytes 393224 | tf_op jit(solution)/shard_map/ppermute | solution.py:333
  20.1 9.4 %collective-permute-start.6 = (bf16[2,18,256]{2,1,0:T(8,128)(2,1)S(1)}, bf16[2,18,256]{2,1,0:T(8,128)(2,1)S(1)}, u32[]{:S(2)}, u32[]{:S(2)}) collective-permute-start(bf16[2,18,256]{2,1,0:T(8,128)(2,1)S(1)} %get-tuple-element.21.refs_4_), channel_id=1, source_target_pairs={{2,4},{4,2},{3,5},{5,3},{10,12},{12,10},{11,13},{13,11},{18,20},{2... | collective-permute-start | bytes 55304 | tf_op jit(solution)/shard_map/ppermute | solution.py:337
  20.7 8.8 %collective-permute-start.7 = (bf16[2,18,256]{2,1,0:T(8,128)(2,1)S(1)}, bf16[2,18,256]{2,1,0:T(8,128)(2,1)S(1)}, u32[]{:S(2)}, u32[]{:S(2)}) collective-permute-start(bf16[2,18,256]{2,1,0:T(8,128)(2,1)S(1)} %get-tuple-element.22.refs_5_), channel_id=1, source_target_pairs={{0,2},{2,0},{4,6},{6,4},{1,3},{3,1},{5,7},{7,5},{8,10},{10,8},{12,... | collective-permute-start | bytes 55304 | tf_op jit(solution)/shard_map/ppermute | solution.py:337
  29.5 0.7 %copy-start.1 = (f32[512]{0:T(512)S(1)}, f32[512]{0:T(512)}, u32[]{:S(2)}) copy-start(f32[512]{0:T(512)} %param.5) | copy-start | bytes 6148

commit v7 on v6

--- a/solution.py
+++ b/solution.py
@@ -11,7 +11,7 @@
 VMEM = pl.BlockSpec(memory_space=pltpu.VMEM)
 HBM = pl.BlockSpec(memory_space=pltpu.HBM)
 PARAMS = pltpu.CompilerParams(vmem_limit_bytes=10 << 20)
-WAIT = pl.CostEstimate(flops=6 * 10**9, bytes_accessed=1 << 20, transcendentals=0)
+WAIT = pl.CostEstimate(flops=4 * 10**9, bytes_accessed=1 << 20, transcendentals=0)
 BLOCK = 4
 
 
@@ -64,7 +64,7 @@
     return part if b == 1 else pltpu.roll(part, 1 if b == 0 else part.shape[0] - 1, 0)
 
 
-def add_rows(spans, w_ref, total_ref, x_ref, written):
+def add_rows(spans, w_ref, total_ref, x_ref, written, initial=None):
     height, width, _ = total_ref.shape
     slab = w_ref.shape[2]
     at = 0
@@ -88,7 +88,7 @@
                         if low + i in written:
                             total_ref[low + i] += term
                         else:
-                            total_ref[low + i] = term
+                            total_ref[low + i] = term + initial
                             written.add(low + i)
             at += size
 
@@ -97,10 +97,16 @@
     pieces, w_ref, total_ref, x_ref = refs[:n], refs[n], refs[-2], refs[-1]
     written = set(range(total_ref.shape[0])) if started else set()
     spans = [(pieces[p], local, row, count) for p, local, row, count in spans]
-    add_rows(spans, w_ref, total_ref, x_ref, written)
-
-
-def accumulate(spans, pieces, weights, total, shape, after=None, estimate=None):
+    add_rows(spans, w_ref, total_ref, x_ref, written, None if started else own_bias(refs[n + 1], total_ref.shape[2]))
+
+
+def own_bias(bias_ref, outs):
+    if bias_ref.shape[1] == outs:
+        return bias_ref[...]
+    return bias_ref[:, pl.ds(pl.multiple_of(lax.axis_index("filt") * outs, outs), outs)]
+
+
+def accumulate(spans, pieces, weights, total, shape, after=None, bias=None):
     count = sum(s[3] for s in spans)
     width, slab = shape[1], weights.shape[2]
     operands = [*pieces, weights]
@@ -108,6 +114,8 @@
     if total is not None:
         aliases = {len(operands): 0}
         operands.append(total)
+    else:
+        operands.append(bias)
     if after is not None:
         operands.append(after)
     return pl.pallas_call(
@@ -118,7 +126,7 @@
         scratch_shapes=[pltpu.VMEM((3, count, width, slab), BF16)],
         input_output_aliases=aliases,
         compiler_params=PARAMS,
-        cost_estimate=estimate or cost(count * width * 9, slab, shape[2]),
+        cost_estimate=cost(count * width * 9, slab, shape[2]),
         name="accumulate",
     )(*operands)
 
@@ -198,14 +206,9 @@
         fix_ref[i] = fix
 
 
-def finish_row(total_ref, h, bias_ref, rows_ref, cols_ref):
+def finish_row(total_ref, h, rows_ref, cols_ref):
     height, width = cols_ref.shape[1], total_ref.shape[1]
-    outs = total_ref.shape[2]
-    if bias_ref.shape[1] == outs:
-        bias = bias_ref[...]
-    else:
-        bias = bias_ref[:, pl.ds(pl.multiple_of(lax.axis_index("filt") * outs, outs), outs)]
-    value = total_ref[h] + bias
+    value = total_ref[h]
     if h == 0:
         value += rows_ref[0]
     if h == height - 1:
@@ -216,23 +219,23 @@
     return jnp.concatenate([first, value[8 : width - 8], final], 0)
 
 
-def store_rows(total_ref, bias_ref, rows_ref, cols_ref, rows, out_ref):
-    turned = jnp.stack([finish_row(total_ref, h, bias_ref, rows_ref, cols_ref).T for h in rows], 0)
+def store_rows(total_ref, rows_ref, cols_ref, rows, out_ref):
+    turned = jnp.stack([finish_row(total_ref, h, rows_ref, cols_ref).T for h in rows], 0)
     out_ref[...] = jnp.swapaxes(turned, 0, 1).astype(BF16)
 
 
-def upper_kernel(total_ref, bias_ref, rows_ref, cols_ref, out_ref):
-    store_rows(total_ref, bias_ref, rows_ref, cols_ref, range(out_ref.shape[1]), out_ref)
-
-
-def last_kernel(span, piece, w_ref, total_in, bias_ref, rows_ref, cols_ref, upper_ref, out_ref, total_ref, x_ref, lower_ref, sems):
+def upper_kernel(total_ref, rows_ref, cols_ref, out_ref):
+    store_rows(total_ref, rows_ref, cols_ref, range(out_ref.shape[1]), out_ref)
+
+
+def last_kernel(span, piece, w_ref, total_in, rows_ref, cols_ref, upper_ref, out_ref, total_ref, x_ref, lower_ref, sems):
     half = upper_ref.shape[1]
     height = out_ref.shape[1]
     first = pltpu.make_async_copy(upper_ref, out_ref.at[:, 0:half, :], sems.at[0])
     first.start()
     total_ref[half:] = total_in[half:]
     add_rows([(piece, *span)], w_ref, total_ref, x_ref, set(range(height)))
-    store_rows(total_ref, bias_ref, rows_ref, cols_ref, range(half, height), lower_ref)
+    store_rows(total_ref, rows_ref, cols_ref, range(half, height), lower_ref)
     second = pltpu.make_async_copy(lower_ref, out_ref.at[:, half:height, :], sems.at[1])
     second.start()
     first.wait()
@@ -325,15 +328,14 @@
     row_pairs, col_pairs = swap_pairs("row"), swap_pairs("col")
     sent = calls(functools.partial(outermost_kernel, groups), "outermost", [(groups, width, slab)] * 2, rims, estimate=WAIT)
     outer_rows = [lax.ppermute(v, "row", p) for v, p in zip(sent, row_pairs)]
-    total = accumulate(spans, [pairs[0], upper_rows, lower_rows], weights[0], None, shape, rims[-1])
+    total = accumulate(spans, [pairs[0], upper_rows, lower_rows], weights[0], None, shape, rims[-1], bias)
     for g in range(1, groups):
         total = accumulate(outer, [pairs[g]], weights[g], total, shape)
-    third = pick(lower_rows, chunks[2][0] - half, chunks[2][1] - half, total)
+    edge = pltpu.VMEM((2, height + 2, slab), F32)
+    sent = calls(functools.partial(edges_kernel, groups), "edges", [(groups, height + 2, slab)] * 2, [*rims, *outer_rows], [edge])
+    third = pick(lower_rows, chunks[2][0] - half, chunks[2][1] - half, sent[0])
     for received, ring in zip(sets, rings):
         received.append(lax.ppermute(third, "filt", ring))
-
-    edge = pltpu.VMEM((2, height + 2, slab), F32)
-    sent = calls(functools.partial(edges_kernel, groups), "edges", [(groups, height + 2, slab)] * 2, [*rims, *outer_rows, third], [edge])
     outer_cols = [lax.ppermute(v, "col", p) for v, p in zip(sent, col_pairs)]
     rows_fix = call(
         functools.partial(outer_rows_kernel, groups), "outer_rows", (2, width, outs), F32,
@@ -349,7 +351,7 @@
         functools.partial(outer_cols_kernel, groups), "outer_cols", (2, height, outs), F32,
         [*outer_cols, *weights, total], cost(6 * 256 * groups, slab, outs),
     )
-    top = call(upper_kernel, "upper", (outs, half, width), BF16, [total, bias, rows_fix, cols_fix], cost(256, slab, outs))
+    top = call(upper_kernel, "upper", (outs, half, width), BF16, [total, rows_fix, cols_fix], cost(256, slab, outs))
     scratch = [
         pltpu.VMEM(shape, F32),
         pltpu.VMEM((3, c.shape[0], width, slab), BF16),
@@ -359,7 +361,7 @@
     span = (0, chunks[2][0], c.shape[0])
     return call(
         functools.partial(last_kernel, span), "last", (outs, height, width), BF16,
-        [c, weights[-1], total, bias, rows_fix, cols_fix, top], cost(9 * 256, slab, outs), scratch, HBM,
+        [c, weights[-1], total, rows_fix, cols_fix, top], cost(9 * 256, slab, outs), scratch, HBM,
     )
 
 

time: 32.5 us -> 30.4 us (0.935)
  waiting for transfers between devices: 3.67 us -> 2.35 us
  starting transfers between devices: 16.4 us -> 15.9 us
    ppermute x1, waiting for transfers between devices: 3.23 us -> 0.01 us  [body(): sets = [[lax.ppermute(upper_rows, 'filt', ring)] for ring in rings]]
    ppermute x1, starting transfers between devices: 0.1 us -> 2.01 us  [body(): received.append(lax.ppermute(second, 'filt', ring))]
    ppermute x1, starting transfers between devices: 2 us -> 0.08 us  [body(): sets = [[lax.ppermute(upper_rows, 'filt', ring)] for ring in rings]]
    ppermute x1, waiting for transfers between devices: 0.01 us -> 1.34 us  [body(): received.append(lax.ppermute(second, 'filt', ring))]
    ppermute x1, starting transfers between devices: 2.54 us -> 1.52 us  [body(): received.append(lax.ppermute(third, 'filt', ring))]
    ppermute x2, starting transfers between devices: 5.15 us -> 5.67 us  [body(): outer_rows = [lax.ppermute(v, 'row', p) for v, p in zip(sent, row_pairs)]]
    ppermute x1, waiting for transfers between devices: 0.43 us -> 0.84 us  [body(): rims = [rim] + [lax.ppermute(rim, 'filt', ring) for ring in rings]]
  transfers between devices with their start and end apart: 8 -> 8, of which waited for: 2 -> 3; matrix products, arithmetic and copies ran while one was open for 0% -> 0% of each run, Pallas kernels for 25% -> 27%
where the time goes in v7:
time: 30.4 us; the launch traced here: 30.2 us
  starting transfers between devices  15.9 us (52%)
  Pallas kernels  10.5 us (35%)
  waiting for transfers between devices  2.35 us (8%)
  local copies, waits for them, and re-layouts  1.25 us (4%)
    ppermute x2, starting transfers between devices, body(): outer_rows = [lax.ppermute(v, 'row', p) for v, p in zip(sent, row_pairs)]  5.67 us
    pallas_call x4, Pallas kernels, accumulate(): pl.pallas_call(functools.partial(accumulate_kernel, spans, len(pieces), t...  5.11 us
    ppermute x2, starting transfers between devices, body(): outer_cols = [lax.ppermute(v, 'col', p) for v, p in zip(sent, col_pairs)]  3.58 us
    ppermute x1, starting transfers between devices, body(): rims = [rim] + [lax.ppermute(rim, 'filt', ring) for ring in rings]  3.03 us
    pallas_call x6, Pallas kernels, call(): pl.pallas_call(kernel, out_shape=jax.ShapeDtypeStruct(shape, dtype), in_s...  2.83 us
    ppermute x1, starting transfers between devices, body(): received.append(lax.ppermute(second, 'filt', ring))  2.01 us
    pallas_call x1, Pallas kernels, split_weights(): pl.pallas_call(functools.partial(weights_kernel, groups), out_shape=[jax....  1.68 us
    ppermute x1, starting transfers between devices, body(): received.append(lax.ppermute(third, 'filt', ring))  1.52 us
  transfers between devices with their start and end apart: 8, of which 3 were waited for; matrix products, arithmetic and copies ran while one was open for 0% of the time, Pallas kernels for 27%

profile of v7, /device:TPU:0, one launch (start us, length us, event | category | flops | bytes accessed | tf_op | source)
XLA Modules:
  0.0 30.2 jit_solution(13679624712160082196)
XLA Ops:
  0.0 0.0 copy-start
  0.0 1.2 %copy-done = bf16[256,16,128]{2,1,0:T(8,128)(2,1)S(1)} copy-done((bf16[256,16,128]{2,1,0:T(8,128)(2,1)S(1)}, bf16[256,16,128]{2,1,0:T(8,128)(2,1)}, u32[]{:S(2)}) %copy-start) | copy-done | bytes 1048600
  1.2 0.8 %relayout.1 = (bf16[288,256]{1,0:T(8,128)(2,1)S(1)}, bf16[7,128,256]{2,1,0:T(8,128)(2,1)S(1)}, bf16[7,128,256]{2,1,0:T(8,128)(2,1)S(1)}) custom-call(bf16[256,16,128]{2,1,0:T(8,128)(2,1)S(1)} %copy-done), custom_call_target="tpu_custom_call" | custom-call | tf_op jit(solution)/shard_map/relayout/pallas_call | solution.py:42
  2.0 3.0 %collective-permute-start = (bf16[288,256]{1,0:T(8,128)(2,1)S(1)}, bf16[288,256]{1,0:T(8,128)(2,1)S(1)}, u32[]{:S(2)}, u32[]{:S(2)}) collective-permute-start(bf16[288,256]{1,0:T(8,128)(2,1)S(1)} %get-tuple-element.15.refs_0_), channel_id=1, source_target_pairs={{0,1},{1,0},{2,3},{3,2},{4,5},{5,4},{6,7},{7,6},{8,9},{9,8},{10,11... | collective-permute-start | bytes 442376 | tf_op jit(solution)/shard_map/ppermute | solution.py:313
  5.1 0.1 collective-permute-start.5
  5.2 1.7 %split_weights.1 = (bf16[3,3,256,256]{3,2,1,0:T(8,128)(2,1)S(1)}, bf16[3,3,256,256]{3,2,1,0:T(8,128)(2,1)S(1)}) custom-call(bf16[3,3,512,512]{3,2,1,0:T(8,128)(2,1)} %kernel_ref.1), custom_call_target="tpu_custom_call" | custom-call | tf_op jit(solution)/shard_map/split_weights/pallas_call | solution.py:289
  6.9 2.0 %collective-permute-start.4 = (bf16[5,128,256]{2,1,0:T(8,128)(2,1)S(1)}, bf16[5,128,256]{2,1,0:T(8,128)(2,1)S(1)}, u32[]{:S(2)}, u32[]{:S(2)}) collective-permute-start(bf16[5,128,256]{2,1,0:T(8,128)(2,1)S(1)} %pick.3), channel_id=1, source_target_pairs={{0,1},{1,0},{2,3},{3,2},{4,5},{5,4},{6,7},{7,6},{8,9},{9,8},{10,11... | collective-permute-start | bytes 983048 | tf_op jit(solution)/shard_map/ppermute | solution.py:326
  8.9 0.0 copy-start.1
  8.9 0.8 %collective-permute-done.refs_1_.refs_5_ = bf16[288,256]{1,0:T(8,128)(2,1)S(1)} collective-permute-done((bf16[288,256]{1,0:T(8,128)(2,1)S(1)}, bf16[288,256]{1,0:T(8,128)(2,1)S(1)}, u32[]{:S(2)}, u32[]{:S(2)}) %collective-permute-start) | collective-permute-done | bytes 147488 | tf_op jit(solution)/shard_map/ppermute | solution.py:313
  9.8 0.7 %collective-permute-start.1 = (bf16[2,128,256]{2,1,0:T(8,128)(2,1)S(1)}, bf16[2,128,256]{2,1,0:T(8,128)(2,1)S(1)}, u32[]{:S(2)}, u32[]{:S(2)}) collective-permute-start(bf16[2,128,256]{2,1,0:T(8,128)(2,1)S(1)} %get-tuple-element.16), channel_id=1, source_target_pairs={{8,16},{16,8},{9,17},{17,9},{10,18},{18,10},{11,19},{19,11},{12,20... | collective-permute-start | bytes 393224 | tf_op jit(solution)/shard_map/ppermute | solution.py:330
  10.5 5.0 %collective-permute-start.2 = (bf16[2,128,256]{2,1,0:T(8,128)(2,1)S(1)}, bf16[2,128,256]{2,1,0:T(8,128)(2,1)S(1)}, u32[]{:S(2)}, u32[]{:S(2)}) collective-permute-start(bf16[2,128,256]{2,1,0:T(8,128)(2,1)S(1)} %get-tuple-element.17), channel_id=1, source_target_pairs={{0,8},{8,0},{16,24},{24,16},{1,9},{9,1},{17,25},{25,17},{2,10},{10... | collective-permute-start | bytes 393224 | tf_op jit(solution)/shard_map/ppermute | solution.py:330
  15.5 0.0 copy-done.1
  15.5 2.5 %accumulate.4.refs_2_ = f32[16,128,256]{2,1,0:T(8,128)S(1)} custom-call(bf16[2,128,256]{2,1,0:T(8,128)(2,1)S(1)} %bitcast.4, bf16[7,128,256]{2,1,0:T(8,128)(2,1)S(1)} %get-tuple-element.21.refs_1_, bf16[7,128,256]{2,1,0:T(8,128)(2,1)S(1)} %get-tuple-element.14.rows_ref.refs_2_, bf16[3,3,256,256]{3,2,1,0:T(8,128)(2,1)S(1)} %get-tuple-element.20.after_ref.refs_3_.refs_2_, ...), custom_call_target="tpu_custom_call" | custom-call | flops 2415919104 | bytes 1048576 | tf_op jit(solution)/shard_map/accumulate/pallas_call | solution.py:121
  18.0 0.4 %accumulate.5.refs_2_ = f32[16,128,256]{2,1,0:T(8,128)S(1)} custom-call(bf16[2,128,256]{2,1,0:T(8,128)(2,1)S(1)} %bitcast.3, bf16[3,3,256,256]{3,2,1,0:T(8,128)(2,1)S(1)} %get-tuple-element.19.refs_1_.refs_3_.w_ref, f32[16,128,256]{2,1,0:T(8,128)S(1)} %accumulate.4.refs_2_), custom_call_target="tpu_custom_call", output_to_operand_aliasing={{}: (2, {})} | custom-call | flops 301989888 | bytes 1048576 | tf_op jit(solution)/shard_map/accumulate/pallas_call | solution.py:121
  18.4 0.0 collective-permute-done.1.refs_2_.refs_0_
  18.4 0.0 collective-permute-done.2.refs_3_.refs_1_
  18.5 0.7 %collective-permute-start.6 = (bf16[2,18,256]{2,1,0:T(8,128)(2,1)S(1)}, bf16[2,18,256]{2,1,0:T(8,128)(2,1)S(1)}, u32[]{:S(2)}, u32[]{:S(2)}) collective-permute-start(bf16[2,18,256]{2,1,0:T(8,128)(2,1)S(1)} %get-tuple-element.18.after_ref.refs_4_), channel_id=1, source_target_pairs={{2,4},{4,2},{3,5},{5,3},{10,12},{12,10},{11,13},{13,11},{18,20},{2... | collective-permute-start | bytes 55304 | tf_op jit(solution)/shard_map/ppermute | solution.py:339
  19.2 2.9 %collective-permute-start.7 = (bf16[2,18,256]{2,1,0:T(8,128)(2,1)S(1)}, bf16[2,18,256]{2,1,0:T(8,128)(2,1)S(1)}, u32[]{:S(2)}, u32[]{:S(2)}) collective-permute-start(bf16[2,18,256]{2,1,0:T(8,128)(2,1)S(1)} %get-tuple-element.22.refs_5_), channel_id=1, source_target_pairs={{0,2},{2,0},{4,6},{6,4},{1,3},{3,1},{5,7},{7,5},{8,10},{10,8},{12,... | collective-permute-start | bytes 55304 | tf_op jit(solution)/shard_map/ppermute | solution.py:339
  22.1 1.5 %collective-permute-start.3 = (bf16[2,128,256]{2,1,0:T(8,128)(2,1)S(1)}, bf16[2,128,256]{2,1,0:T(8,128)(2,1)S(1)}, u32[]{:S(2)}, u32[]{:S(2)}) collective-permute-start(bf16[2,128,256]{2,1,0:T(8,128)(2,1)S(1)} %pick.2), channel_id=1, source_target_pairs={{0,1},{1,0},{2,3},{3,2},{4,5},{5,4},{6,7},{7,6},{8,9},{9,8},{10,11... | collective-permute-start | bytes 393224 | tf_op jit(solution)/shard_map/ppermute | solution.py:338
  23.6 0.4 %outer_rows.1.refs_3_.rows_ref = f32[2,128,256]{2,1,0:T(8,128)S(1)} custom-call(bf16[2,128,256]{2,1,0:T(8,128)(2,1)S(1)} %collective-permute-done.1.refs_2_.refs_0_, bf16[2,128,256]{2,1,0:T(8,128)(2,1)S(1)} %collective-permute-done.2.refs_3_.refs_1_, bf16[3,3,256,256]{3,2,1,0:T(8,128)(2,1)S(1)} %get-tuple-element.20.after_ref.refs_3_.refs_2_, ...), custom_call_target="tpu_custom_call" | custom-call | flops 201326592 | bytes 1048576 | tf_op jit(solution)/shard_map/outer_rows/pallas_call | solution.py:246
  24.0 0.0 collective-permute-done.5.refs_0_
  24.0 1.2 %accumulate.6.refs_2_ = f32[16,128,256]{2,1,0:T(8,128)S(1)} custom-call(bf16[7,128,256]{2,1,0:T(8,128)(2,1)S(1)} %collective-permute-done.5.refs_0_, bf16[3,3,256,256]{3,2,1,0:T(8,128)(2,1)S(1)} %get-tuple-element.19.refs_1_.refs_3_.w_ref, f32[16,128,256]{2,1,0:T(8,128)S(1)} %accumulate.5.refs_2_, ...), custom_call_target="tpu_custom_call", output_to_operand_aliasing={{}: (2, {})} | custom-call | flops 1056964608 | bytes 1048576 | tf_op jit(solution)/shard_map/accumulate/pallas_call | solution.py:121
  25.3 1.3 %collective-permute-done.4.refs_0_ = bf16[5,128,256]{2,1,0:T(8,128)(2,1)S(1)} collective-permute-done((bf16[5,128,256]{2,1,0:T(8,128)(2,1)S(1)}, bf16[5,128,256]{2,1,0:T(8,128)(2,1)S(1)}, u32[]{:S(2)}, u32[]{:S(2)}) %collective-permute-start.4) | collective-permute-done | bytes 327712 | tf_op jit(solution)/shard_map/ppermute | solution.py:326
  26.6 0.9 %accumulate.7.refs_4_.total_ref.total_in = f32[16,128,256]{2,1,0:T(8,128)S(1)} custom-call(bf16[5,128,256]{2,1,0:T(8,128)(2,1)S(1)} %collective-permute-done.4.refs_0_, bf16[3,3,256,256]{3,2,1,0:T(8,128)(2,1)S(1)} %get-tuple-element.19.refs_1_.refs_3_.w_ref, f32[16,128,256]{2,1,0:T(8,128)S(1)} %accumulate.6.refs_2_), custom_call_target="tpu_custom_call", output_to_operand_aliasing={{}: (2, {})} | custom-call | flops 754974720 | bytes 1048576 | tf_op jit(solution)/shard_map/accumulate/pallas_call | solution.py:121
  27.6 0.0 collective-permute-done.7.refs_1_
  27.6 0.0 collective-permute-done.6.refs_0_
  27.6 0.4 %outer_cols.1.cols_ref = f32[2,16,256]{2,1,0:T(8,128)S(1)} custom-call(bf16[2,18,256]{2,1,0:T(8,128)(2,1)S(1)} %collective-permute-done.6.refs_0_, bf16[2,18,256]{2,1,0:T(8,128)(2,1)S(1)} %collective-permute-done.7.refs_1_, bf16[3,3,256,256]{3,2,1,0:T(8,128)(2,1)S(1)} %get-tuple-element.20.after_ref.refs_3_.refs_2_, ...), custom_call_target="tpu_custom_call" | custom-call | flops 402653184 | bytes 1048576 | tf_op jit(solution)/shard_map/outer_cols/pallas_call | solution.py:246
  27.9 0.5 %upper.1.upper_ref = bf16[256,8,128]{2,1,0:T(8,128)(2,1)S(1)} custom-call(f32[16,128,256]{2,1,0:T(8,128)S(1)} %accumulate.7.refs_4_.total_ref.total_in, f32[2,128,256]{2,1,0:T(8,128)S(1)} %outer_rows.1.refs_3_.rows_ref, f32[2,16,256]{2,1,0:T(8,128)S(1)} %outer_cols.1.cols_ref), custom_call_target="tpu_custom_call" | custom-call | flops 33554432 | bytes 1048576 | tf_op jit(solution)/shard_map/upper/pallas_call | solution.py:246
  28.4 0.2 collective-permute-done.3.piece
  28.6 1.6 %last.1 = bf16[256,16,128]{2,1,0:T(8,128)(2,1)} custom-call(bf16[2,128,256]{2,1,0:T(8,128)(2,1)S(1)} %collective-permute-done.3.piece, bf16[3,3,256,256]{3,2,1,0:T(8,128)(2,1)S(1)} %get-tuple-element.19.refs_1_.refs_3_.w_ref, f32[16,128,256]{2,1,0:T(8,128)S(1)} %accumulate.7.refs_4_.total_ref.total_in, f32[2,128,256]{2,1,0:T(8,128)S(1)} %outer_rows.1.refs_3_.rows_ref, ...), custom_call_target="tpu_custom_call" | custom-call | flops 301989888 | bytes 1048576 | tf_op jit(solution)/shard_map/last/pallas_call | solution.py:246
  (6 shorter events, 0.1 us)
Async XLA Ops:
  0.0 1.2 %copy-start = (bf16[256,16,128]{2,1,0:T(8,128)(2,1)S(1)}, bf16[256,16,128]{2,1,0:T(8,128)(2,1)}, u32[]{:S(2)}) copy-start(bf16[256,16,128]{2,1,0:T(8,128)(2,1)} %x_ref.1) | copy-start | bytes 3145732
  2.0 7.7 %collective-permute-start = (bf16[288,256]{1,0:T(8,128)(2,1)S(1)}, bf16[288,256]{1,0:T(8,128)(2,1)S(1)}, u32[]{:S(2)}, u32[]{:S(2)}) collective-permute-start(bf16[288,256]{1,0:T(8,128)(2,1)S(1)} %get-tuple-element.15.refs_0_), channel_id=1, source_target_pairs={{0,1},{1,0},{2,3},{3,2},{4,5},{5,4},{6,7},{7,6},{8,9},{9,8},{10,11... | collective-permute-start | bytes 442376 | tf_op jit(solution)/shard_map/ppermute | solution.py:313
  5.1 18.9 %collective-permute-start.5 = (bf16[7,128,256]{2,1,0:T(8,128)(2,1)S(1)}, bf16[7,128,256]{2,1,0:T(8,128)(2,1)S(1)}, u32[]{:S(2)}, u32[]{:S(2)}) collective-permute-start(bf16[7,128,256]{2,1,0:T(8,128)(2,1)S(1)} %get-tuple-element.21.refs_1_), channel_id=1, source_target_pairs={{0,1},{1,0},{2,3},{3,2},{4,5},{5,4},{6,7},{7,6},{8,9},{9,8},{10,11... | collective-permute-start | bytes 1376264 | tf_op jit(solution)/shard_map/ppermute | solution.py:314
  6.9 19.7 %collective-permute-start.4 = (bf16[5,128,256]{2,1,0:T(8,128)(2,1)S(1)}, bf16[5,128,256]{2,1,0:T(8,128)(2,1)S(1)}, u32[]{:S(2)}, u32[]{:S(2)}) collective-permute-start(bf16[5,128,256]{2,1,0:T(8,128)(2,1)S(1)} %pick.3), channel_id=1, source_target_pairs={{0,1},{1,0},{2,3},{3,2},{4,5},{5,4},{6,7},{7,6},{8,9},{9,8},{10,11... | collective-permute-start | bytes 983048 | tf_op jit(solution)/shard_map/ppermute | solution.py:326
  8.9 6.5 %copy-start.1 = (f32[512]{0:T(512)S(1)}, f32[512]{0:T(512)}, u32[]{:S(2)}) copy-start(f32[512]{0:T(512)} %param.5) | copy-start | bytes 6148
  9.8 8.6 %collective-permute-start.1 = (bf16[2,128,256]{2,1,0:T(8,128)(2,1)S(1)}, bf16[2,128,256]{2,1,0:T(8,128)(2,1)S(1)}, u32[]{:S(2)}, u32[]{:S(2)}) collective-permute-start(bf16[2,128,256]{2,1,0:T(8,128)(2,1)S(1)} %get-tuple-element.16), channel_id=1, source_target_pairs={{8,16},{16,8},{9,17},{17,9},{10,18},{18,10},{11,19},{19,11},{12,20... | collective-permute-start | bytes 393224 | tf_op jit(solution)/shard_map/ppermute | solution.py:330
  10.5 8.0 %collective-permute-start.2 = (bf16[2,128,256]{2,1,0:T(8,128)(2,1)S(1)}, bf16[2,128,256]{2,1,0:T(8,128)(2,1)S(1)}, u32[]{:S(2)}, u32[]{:S(2)}) collective-permute-start(bf16[2,128,256]{2,1,0:T(8,128)(2,1)S(1)} %get-tuple-element.17), channel_id=1, source_target_pairs={{0,8},{8,0},{16,24},{24,16},{1,9},{9,1},{17,25},{25,17},{2,10},{10... | collective-permute-start | bytes 393224 | tf_op jit(solution)/shard_map/ppermute | solution.py:330
  18.5 9.1 %collective-permute-start.6 = (bf16[2,18,256]{2,1,0:T(8,128)(2,1)S(1)}, bf16[2,18,256]{2,1,0:T(8,128)(2,1)S(1)}, u32[]{:S(2)}, u32[]{:S(2)}) collective-permute-start(bf16[2,18,256]{2,1,0:T(8,128)(2,1)S(1)} %get-tuple-element.18.after_ref.refs_4_), channel_id=1, source_target_pairs={{2,4},{4,2},{3,5},{5,3},{10,12},{12,10},{11,13},{13,11},{18,20},{2... | collective-permute-start | bytes 55304 | tf_op jit(solution)/shard_map/ppermute | solution.py:339
  19.2 8.4 %collective-permute-start.7 = (bf16[2,18,256]{2,1,0:T(8,128)(2,1)S(1)}, bf16[2,18,256]{2,1,0:T(8,128)(2,1)S(1)}, u32[]{:S(2)}, u32[]{:S(2)}) collective-permute-start(bf16[2,18,256]{2,1,0:T(8,128)(2,1)S(1)} %get-tuple-element.22.refs_5_), channel_id=1, source_target_pairs={{0,2},{2,0},{4,6},{6,4},{1,3},{3,1},{5,7},{7,5},{8,10},{10,8},{12,... | collective-permute-start | bytes 55304 | tf_op jit(solution)/shard_map/ppermute | solution.py:339
  22.1 6.5 %collective-permute-start.3 = (bf16[2,128,256]{2,1,0:T(8,128)(2,1)S(1)}, bf16[2,128,256]{2,1,0:T(8,128)(2,1)S(1)}, u32[]{:S(2)}, u32[]{:S(2)}) collective-permute-start(bf16[2,128,256]{2,1,0:T(8,128)(2,1)S(1)} %pick.2), channel_id=1, source_target_pairs={{0,1},{1,0},{2,3},{3,2},{4,5},{5,4},{6,7},{7,6},{8,9},{9,8},{10,11... | collective-permute-start | bytes 393224 | tf_op jit(solution)/shard_map/ppermute | solution.py:338

commit v8 on v7

--- a/solution.py
+++ b/solution.py
@@ -268,6 +268,10 @@
     )(*operands)
 
 
+def greeting_kernel(out_ref):
+    out_ref[...] = jnp.zeros_like(out_ref)
+
+
 def weights_kernel(groups, kernel_ref, *refs):
     outs, sems = refs[:-1], refs[-1]
     slab, width = outs[0].shape[2:]
@@ -308,8 +312,11 @@
     half = height // 2
     chunks = ((1, half), (half, height - 3), (height - 3, height - 1))
 
+    rings = [[(i, (i + shift) % groups) for i in range(groups)] for shift in range(1, groups)]
+    greeting = call(greeting_kernel, "greeting", (8, 128), F32, [], WAIT)
+    greeting = lax.ppermute(greeting, "filt", rings[0])
     rim, upper_rows, lower_rows = relayout(features, ((1, half), (half, height - 1)))
-    rings = [[(i, (i + shift) % groups) for i in range(groups)] for shift in range(1, groups)]
+    rim = pick(rim, 0, rim.shape[0], greeting)
     rims = [rim] + [lax.ppermute(rim, "filt", ring) for ring in rings]
     sets = [[lax.ppermute(upper_rows, "filt", ring)] for ring in rings]
     pairs = [r[0 : 2 * width].reshape(2, width, slab) for r in rims]

time: 30.4 us -> 31 us (1.020)
  starting transfers between devices: 15.9 us -> 17.9 us
  local copies, waits for them, and re-layouts: 1.25 us -> 0.03 us
    ppermute x0 -> x1, starting transfers between devices: none -> 2.97 us  [body(): greeting = lax.ppermute(greeting, 'filt', rings[0])]
    ppermute x1, waiting for transfers between devices: 1.34 us -> 0.01 us  [body(): received.append(lax.ppermute(second, 'filt', ring))]
    unnamed x4, local copies, waits for them, and re-layouts: 1.23 us -> 0.01 us
    ppermute x1, starting transfers between devices: 3.03 us -> 2.09 us  [body(): rims = [rim] + [lax.ppermute(rim, 'filt', ring) for ring in rings]]
    ppermute x0 -> x1, waiting for transfers between devices: none -> 0.76 us  [body(): greeting = lax.ppermute(greeting, 'filt', rings[0])]
    ppermute x1, waiting for transfers between devices: 0.16 us -> 0.47 us  [body(): received.append(lax.ppermute(third, 'filt', ring))]
    pallas_call x6 -> x8, Pallas kernels: 2.83 us -> 2.84 us  [call(): pl.pallas_call(kernel, out_shape=jax.ShapeDtypeStruct(shape, dtype), in_s...]
  transfers between devices with their start and end apart: 8 -> 9, of which waited for: 3 -> 3; matrix products, arithmetic and copies ran while one was open for 0% -> 0% of each run, Pallas kernels for 27% -> 29%
where the time goes in v8:
time: 31 us; the launch traced here: 30.8 us
  starting transfers between devices  17.9 us (58%)
  Pallas kernels  10.5 us (34%)
  waiting for transfers between devices  2.17 us (7%)
    ppermute x2, starting transfers between devices, body(): outer_rows = [lax.ppermute(v, 'row', p) for v, p in zip(sent, row_pairs)]  5.63 us
    pallas_call x4, Pallas kernels, accumulate(): pl.pallas_call(functools.partial(accumulate_kernel, spans, len(pieces), t...  5.12 us
    ppermute x2, starting transfers between devices, body(): outer_cols = [lax.ppermute(v, 'col', p) for v, p in zip(sent, col_pairs)]  3.58 us
    ppermute x1, starting transfers between devices, body(): greeting = lax.ppermute(greeting, 'filt', rings[0])  2.97 us
    pallas_call x8, Pallas kernels, call(): pl.pallas_call(kernel, out_shape=jax.ShapeDtypeStruct(shape, dtype), in_s...  2.84 us
    ppermute x1, starting transfers between devices, body(): rims = [rim] + [lax.ppermute(rim, 'filt', ring) for ring in rings]  2.09 us
    ppermute x1, starting transfers between devices, body(): received.append(lax.ppermute(second, 'filt', ring))  2.01 us
    pallas_call x1, Pallas kernels, split_weights(): pl.pallas_call(functools.partial(weights_kernel, groups), out_shape=[jax....  1.68 us
  transfers between devices with their start and end apart: 9, of which 3 were waited for; matrix products, arithmetic and copies ran while one was open for 0% of the time, Pallas kernels for 29%

profile of v8, /device:TPU:0, one launch (start us, length us, event | category | flops | bytes accessed | tf_op | source)
XLA Modules:
  0.0 30.8 jit_solution(2275599728313047679)
XLA Ops:
  0.0 0.0 copy-start
  0.0 3.0 %collective-permute-start = (f32[8,128]{1,0:T(8,128)S(1)}, f32[8,128]{1,0:T(8,128)S(1)}, u32[]{:S(2)}, u32[]{:S(2)}) collective-permute-start(f32[8,128]{1,0:T(8,128)S(1)} %greeting.1), channel_id=1, source_target_pairs={{0,1},{1,0},{2,3},{3,2},{4,5},{5,4},{6,7},{7,6},{8,9},{9,8},{10,11... | collective-permute-start | bytes 12296 | tf_op jit(solution)/shard_map/ppermute | solution.py:317
  3.0 0.0 copy-done
  3.0 0.8 %relayout.1 = (bf16[288,256]{1,0:T(8,128)(2,1)S(1)}, bf16[7,128,256]{2,1,0:T(8,128)(2,1)S(1)}, bf16[7,128,256]{2,1,0:T(8,128)(2,1)S(1)}) custom-call(bf16[256,16,128]{2,1,0:T(8,128)(2,1)S(1)} %copy-done), custom_call_target="tpu_custom_call" | custom-call | tf_op jit(solution)/shard_map/relayout/pallas_call | solution.py:42
  3.8 0.8 %collective-permute-done.after_ref = f32[8,128]{1,0:T(8,128)S(1)} collective-permute-done((f32[8,128]{1,0:T(8,128)S(1)}, f32[8,128]{1,0:T(8,128)S(1)}, u32[]{:S(2)}, u32[]{:S(2)}) %collective-permute-start) | collective-permute-done | bytes 4128 | tf_op jit(solution)/shard_map/ppermute | solution.py:317
  4.6 2.1 %collective-permute-start.1 = (bf16[288,256]{1,0:T(8,128)(2,1)S(1)}, bf16[288,256]{1,0:T(8,128)(2,1)S(1)}, u32[]{:S(2)}, u32[]{:S(2)}) collective-permute-start(bf16[288,256]{1,0:T(8,128)(2,1)S(1)} %pick.3.refs_0_), channel_id=1, source_target_pairs={{0,1},{1,0},{2,3},{3,2},{4,5},{5,4},{6,7},{7,6},{8,9},{9,8},{10,11... | collective-permute-start | bytes 442376 | tf_op jit(solution)/shard_map/ppermute | solution.py:320
  6.7 0.1 collective-permute-start.6
  6.7 1.7 %split_weights.1 = (bf16[3,3,256,256]{3,2,1,0:T(8,128)(2,1)S(1)}, bf16[3,3,256,256]{3,2,1,0:T(8,128)(2,1)S(1)}) custom-call(bf16[3,3,512,512]{3,2,1,0:T(8,128)(2,1)} %kernel_ref.1), custom_call_target="tpu_custom_call" | custom-call | tf_op jit(solution)/shard_map/split_weights/pallas_call | solution.py:293
  8.5 2.0 %collective-permute-start.5 = (bf16[5,128,256]{2,1,0:T(8,128)(2,1)S(1)}, bf16[5,128,256]{2,1,0:T(8,128)(2,1)S(1)}, u32[]{:S(2)}, u32[]{:S(2)}) collective-permute-start(bf16[5,128,256]{2,1,0:T(8,128)(2,1)S(1)} %pick.5), channel_id=1, source_target_pairs={{0,1},{1,0},{2,3},{3,2},{4,5},{5,4},{6,7},{7,6},{8,9},{9,8},{10,11... | collective-permute-start | bytes 983048 | tf_op jit(solution)/shard_map/ppermute | solution.py:333
  10.5 0.0 copy-start.1
  10.5 0.9 %collective-permute-done.1.refs_1_.refs_5_ = bf16[288,256]{1,0:T(8,128)(2,1)S(1)} collective-permute-done((bf16[288,256]{1,0:T(8,128)(2,1)S(1)}, bf16[288,256]{1,0:T(8,128)(2,1)S(1)}, u32[]{:S(2)}, u32[]{:S(2)}) %collective-permute-start.1) | collective-permute-done | bytes 147488 | tf_op jit(solution)/shard_map/ppermute | solution.py:320
  11.4 0.7 %collective-permute-start.2 = (bf16[2,128,256]{2,1,0:T(8,128)(2,1)S(1)}, bf16[2,128,256]{2,1,0:T(8,128)(2,1)S(1)}, u32[]{:S(2)}, u32[]{:S(2)}) collective-permute-start(bf16[2,128,256]{2,1,0:T(8,128)(2,1)S(1)} %get-tuple-element.16), channel_id=1, source_target_pairs={{8,16},{16,8},{9,17},{17,9},{10,18},{18,10},{11,19},{19,11},{12,20... | collective-permute-start | bytes 393224 | tf_op jit(solution)/shard_map/ppermute | solution.py:337
  12.1 5.0 %collective-permute-start.3 = (bf16[2,128,256]{2,1,0:T(8,128)(2,1)S(1)}, bf16[2,128,256]{2,1,0:T(8,128)(2,1)S(1)}, u32[]{:S(2)}, u32[]{:S(2)}) collective-permute-start(bf16[2,128,256]{2,1,0:T(8,128)(2,1)S(1)} %get-tuple-element.17), channel_id=1, source_target_pairs={{0,8},{8,0},{16,24},{24,16},{1,9},{9,1},{17,25},{25,17},{2,10},{10... | collective-permute-start | bytes 393224 | tf_op jit(solution)/shard_map/ppermute | solution.py:337
  17.1 0.0 copy-done.1
  17.1 2.5 %accumulate.4.refs_2_ = f32[16,128,256]{2,1,0:T(8,128)S(1)} custom-call(bf16[2,128,256]{2,1,0:T(8,128)(2,1)S(1)} %bitcast.4, bf16[7,128,256]{2,1,0:T(8,128)(2,1)S(1)} %get-tuple-element.21.refs_1_, bf16[7,128,256]{2,1,0:T(8,128)(2,1)S(1)} %get-tuple-element.14.rows_ref.refs_2_, bf16[3,3,256,256]{3,2,1,0:T(8,128)(2,1)S(1)} %get-tuple-element.20.after_ref.refs_3_.refs_2_, ...), custom_call_target="tpu_custom_call" | custom-call | flops 2415919104 | bytes 1048576 | tf_op jit(solution)/shard_map/accumulate/pallas_call | solution.py:121
  19.7 0.4 %accumulate.5.refs_2_ = f32[16,128,256]{2,1,0:T(8,128)S(1)} custom-call(bf16[2,128,256]{2,1,0:T(8,128)(2,1)S(1)} %bitcast.3, bf16[3,3,256,256]{3,2,1,0:T(8,128)(2,1)S(1)} %get-tuple-element.19.refs_1_.refs_3_.w_ref, f32[16,128,256]{2,1,0:T(8,128)S(1)} %accumulate.4.refs_2_), custom_call_target="tpu_custom_call", output_to_operand_aliasing={{}: (2, {})} | custom-call | flops 301989888 | bytes 1048576 | tf_op jit(solution)/shard_map/accumulate/pallas_call | solution.py:121
  20.0 0.0 collective-permute-done.2.refs_2_.refs_0_
  20.1 0.0 collective-permute-done.3.refs_3_.refs_1_
  20.1 0.7 %collective-permute-start.7 = (bf16[2,18,256]{2,1,0:T(8,128)(2,1)S(1)}, bf16[2,18,256]{2,1,0:T(8,128)(2,1)S(1)}, u32[]{:S(2)}, u32[]{:S(2)}) collective-permute-start(bf16[2,18,256]{2,1,0:T(8,128)(2,1)S(1)} %get-tuple-element.18.after_ref.refs_4_), channel_id=1, source_target_pairs={{2,4},{4,2},{3,5},{5,3},{10,12},{12,10},{11,13},{13,11},{18,20},{2... | collective-permute-start | bytes 55304 | tf_op jit(solution)/shard_map/ppermute | solution.py:346
  20.8 2.9 %collective-permute-start.8 = (bf16[2,18,256]{2,1,0:T(8,128)(2,1)S(1)}, bf16[2,18,256]{2,1,0:T(8,128)(2,1)S(1)}, u32[]{:S(2)}, u32[]{:S(2)}) collective-permute-start(bf16[2,18,256]{2,1,0:T(8,128)(2,1)S(1)} %get-tuple-element.22.refs_5_), channel_id=1, source_target_pairs={{0,2},{2,0},{4,6},{6,4},{1,3},{3,1},{5,7},{7,5},{8,10},{10,8},{12,... | collective-permute-start | bytes 55304 | tf_op jit(solution)/shard_map/ppermute | solution.py:346
  23.7 1.5 %collective-permute-start.4 = (bf16[2,128,256]{2,1,0:T(8,128)(2,1)S(1)}, bf16[2,128,256]{2,1,0:T(8,128)(2,1)S(1)}, u32[]{:S(2)}, u32[]{:S(2)}) collective-permute-start(bf16[2,128,256]{2,1,0:T(8,128)(2,1)S(1)} %pick.4), channel_id=1, source_target_pairs={{0,1},{1,0},{2,3},{3,2},{4,5},{5,4},{6,7},{7,6},{8,9},{9,8},{10,11... | collective-permute-start | bytes 393224 | tf_op jit(solution)/shard_map/ppermute | solution.py:345
  25.2 0.4 %outer_rows.1.refs_3_.rows_ref = f32[2,128,256]{2,1,0:T(8,128)S(1)} custom-call(bf16[2,128,256]{2,1,0:T(8,128)(2,1)S(1)} %collective-permute-done.2.refs_2_.refs_0_, bf16[2,128,256]{2,1,0:T(8,128)(2,1)S(1)} %collective-permute-done.3.refs_3_.refs_1_, bf16[3,3,256,256]{3,2,1,0:T(8,128)(2,1)S(1)} %get-tuple-element.20.after_ref.refs_3_.refs_2_, ...), custom_call_target="tpu_custom_call" | custom-call | flops 201326592 | bytes 1048576 | tf_op jit(solution)/shard_map/outer_rows/pallas_call | solution.py:246
  25.6 0.0 collective-permute-done.6.refs_0_
  25.6 1.2 %accumulate.6.refs_2_ = f32[16,128,256]{2,1,0:T(8,128)S(1)} custom-call(bf16[7,128,256]{2,1,0:T(8,128)(2,1)S(1)} %collective-permute-done.6.refs_0_, bf16[3,3,256,256]{3,2,1,0:T(8,128)(2,1)S(1)} %get-tuple-element.19.refs_1_.refs_3_.w_ref, f32[16,128,256]{2,1,0:T(8,128)S(1)} %accumulate.5.refs_2_, ...), custom_call_target="tpu_custom_call", output_to_operand_aliasing={{}: (2, {})} | custom-call | flops 1056964608 | bytes 1048576 | tf_op jit(solution)/shard_map/accumulate/pallas_call | solution.py:121
  26.9 0.0 collective-permute-done.5.refs_0_
  26.9 0.9 %accumulate.7.refs_4_.total_ref.total_in = f32[16,128,256]{2,1,0:T(8,128)S(1)} custom-call(bf16[5,128,256]{2,1,0:T(8,128)(2,1)S(1)} %collective-permute-done.5.refs_0_, bf16[3,3,256,256]{3,2,1,0:T(8,128)(2,1)S(1)} %get-tuple-element.19.refs_1_.refs_3_.w_ref, f32[16,128,256]{2,1,0:T(8,128)S(1)} %accumulate.6.refs_2_), custom_call_target="tpu_custom_call", output_to_operand_aliasing={{}: (2, {})} | custom-call | flops 754974720 | bytes 1048576 | tf_op jit(solution)/shard_map/accumulate/pallas_call | solution.py:121
  27.9 0.0 collective-permute-done.8.refs_1_
  27.9 0.0 collective-permute-done.7.refs_0_
  27.9 0.4 %outer_cols.1.cols_ref = f32[2,16,256]{2,1,0:T(8,128)S(1)} custom-call(bf16[2,18,256]{2,1,0:T(8,128)(2,1)S(1)} %collective-permute-done.7.refs_0_, bf16[2,18,256]{2,1,0:T(8,128)(2,1)S(1)} %collective-permute-done.8.refs_1_, bf16[3,3,256,256]{3,2,1,0:T(8,128)(2,1)S(1)} %get-tuple-element.20.after_ref.refs_3_.refs_2_, ...), custom_call_target="tpu_custom_call" | custom-call | flops 402653184 | bytes 1048576 | tf_op jit(solution)/shard_map/outer_cols/pallas_call | solution.py:246
  28.2 0.5 %upper.1.upper_ref = bf16[256,8,128]{2,1,0:T(8,128)(2,1)S(1)} custom-call(f32[16,128,256]{2,1,0:T(8,128)S(1)} %accumulate.7.refs_4_.total_ref.total_in, f32[2,128,256]{2,1,0:T(8,128)S(1)} %outer_rows.1.refs_3_.rows_ref, f32[2,16,256]{2,1,0:T(8,128)S(1)} %outer_cols.1.cols_ref), custom_call_target="tpu_custom_call" | custom-call | flops 33554432 | bytes 1048576 | tf_op jit(solution)/shard_map/upper/pallas_call | solution.py:246
  28.7 0.5 %collective-permute-done.4.piece = bf16[2,128,256]{2,1,0:T(8,128)(2,1)S(1)} collective-permute-done((bf16[2,128,256]{2,1,0:T(8,128)(2,1)S(1)}, bf16[2,128,256]{2,1,0:T(8,128)(2,1)S(1)}, u32[]{:S(2)}, u32[]{:S(2)}) %collective-permute-start.4) | collective-permute-done | bytes 131104 | tf_op jit(solution)/shard_map/ppermute | solution.py:345
  29.2 1.6 %last.1 = bf16[256,16,128]{2,1,0:T(8,128)(2,1)} custom-call(bf16[2,128,256]{2,1,0:T(8,128)(2,1)S(1)} %collective-permute-done.4.piece, bf16[3,3,256,256]{3,2,1,0:T(8,128)(2,1)S(1)} %get-tuple-element.19.refs_1_.refs_3_.w_ref, f32[16,128,256]{2,1,0:T(8,128)S(1)} %accumulate.7.refs_4_.total_ref.total_in, f32[2,128,256]{2,1,0:T(8,128)S(1)} %outer_rows.1.refs_3_.rows_ref, ...), custom_call_target="tpu_custom_call" | custom-call | flops 301989888 | bytes 1048576 | tf_op jit(solution)/shard_map/last/pallas_call | solution.py:246
  (8 shorter events, 0.1 us)
Async XLA Ops:
  0.0 3.0 %copy-start = (bf16[256,16,128]{2,1,0:T(8,128)(2,1)S(1)}, bf16[256,16,128]{2,1,0:T(8,128)(2,1)}, u32[]{:S(2)}) copy-start(bf16[256,16,128]{2,1,0:T(8,128)(2,1)} %x_ref.1) | copy-start | bytes 3145732
  0.0 4.6 %collective-permute-start = (f32[8,128]{1,0:T(8,128)S(1)}, f32[8,128]{1,0:T(8,128)S(1)}, u32[]{:S(2)}, u32[]{:S(2)}) collective-permute-start(f32[8,128]{1,0:T(8,128)S(1)} %greeting.1), channel_id=1, source_target_pairs={{0,1},{1,0},{2,3},{3,2},{4,5},{5,4},{6,7},{7,6},{8,9},{9,8},{10,11... | collective-permute-start | bytes 12296 | tf_op jit(solution)/shard_map/ppermute | solution.py:317
  4.6 6.9 %collective-permute-start.1 = (bf16[288,256]{1,0:T(8,128)(2,1)S(1)}, bf16[288,256]{1,0:T(8,128)(2,1)S(1)}, u32[]{:S(2)}, u32[]{:S(2)}) collective-permute-start(bf16[288,256]{1,0:T(8,128)(2,1)S(1)} %pick.3.refs_0_), channel_id=1, source_target_pairs={{0,1},{1,0},{2,3},{3,2},{4,5},{5,4},{6,7},{7,6},{8,9},{9,8},{10,11... | collective-permute-start | bytes 442376 | tf_op jit(solution)/shard_map/ppermute | solution.py:320
  6.7 19.0 %collective-permute-start.6 = (bf16[7,128,256]{2,1,0:T(8,128)(2,1)S(1)}, bf16[7,128,256]{2,1,0:T(8,128)(2,1)S(1)}, u32[]{:S(2)}, u32[]{:S(2)}) collective-permute-start(bf16[7,128,256]{2,1,0:T(8,128)(2,1)S(1)} %get-tuple-element.21.refs_1_), channel_id=1, source_target_pairs={{0,1},{1,0},{2,3},{3,2},{4,5},{5,4},{6,7},{7,6},{8,9},{9,8},{10,11... | collective-permute-start | bytes 1376264 | tf_op jit(solution)/shard_map/ppermute | solution.py:321
  8.5 18.4 %collective-permute-start.5 = (bf16[5,128,256]{2,1,0:T(8,128)(2,1)S(1)}, bf16[5,128,256]{2,1,0:T(8,128)(2,1)S(1)}, u32[]{:S(2)}, u32[]{:S(2)}) collective-permute-start(bf16[5,128,256]{2,1,0:T(8,128)(2,1)S(1)} %pick.5), channel_id=1, source_target_pairs={{0,1},{1,0},{2,3},{3,2},{4,5},{5,4},{6,7},{7,6},{8,9},{9,8},{10,11... | collective-permute-start | bytes 983048 | tf_op jit(solution)/shard_map/ppermute | solution.py:333
  10.5 6.6 %copy-start.1 = (f32[512]{0:T(512)S(1)}, f32[512]{0:T(512)}, u32[]{:S(2)}) copy-start(f32[512]{0:T(512)} %param.5) | copy-start | bytes 6148
  11.4 8.6 %collective-permute-start.2 = (bf16[2,128,256]{2,1,0:T(8,128)(2,1)S(1)}, bf16[2,128,256]{2,1,0:T(8,128)(2,1)S(1)}, u32[]{:S(2)}, u32[]{:S(2)}) collective-permute-start(bf16[2,128,256]{2,1,0:T(8,128)(2,1)S(1)} %get-tuple-element.16), channel_id=1, source_target_pairs={{8,16},{16,8},{9,17},{17,9},{10,18},{18,10},{11,19},{19,11},{12,20... | collective-permute-start | bytes 393224 | tf_op jit(solution)/shard_map/ppermute | solution.py:337
  12.1 7.9 %collective-permute-start.3 = (bf16[2,128,256]{2,1,0:T(8,128)(2,1)S(1)}, bf16[2,128,256]{2,1,0:T(8,128)(2,1)S(1)}, u32[]{:S(2)}, u32[]{:S(2)}) collective-permute-start(bf16[2,128,256]{2,1,0:T(8,128)(2,1)S(1)} %get-tuple-element.17), channel_id=1, source_target_pairs={{0,8},{8,0},{16,24},{24,16},{1,9},{9,1},{17,25},{25,17},{2,10},{10... | collective-permute-start | bytes 393224 | tf_op jit(solution)/shard_map/ppermute | solution.py:337
  20.1 7.8 %collective-permute-start.7 = (bf16[2,18,256]{2,1,0:T(8,128)(2,1)S(1)}, bf16[2,18,256]{2,1,0:T(8,128)(2,1)S(1)}, u32[]{:S(2)}, u32[]{:S(2)}) collective-permute-start(bf16[2,18,256]{2,1,0:T(8,128)(2,1)S(1)} %get-tuple-element.18.after_ref.refs_4_), channel_id=1, source_target_pairs={{2,4},{4,2},{3,5},{5,3},{10,12},{12,10},{11,13},{13,11},{18,20},{2... | collective-permute-start | bytes 55304 | tf_op jit(solution)/shard_map/ppermute | solution.py:346
  20.8 7.1 %collective-permute-start.8 = (bf16[2,18,256]{2,1,0:T(8,128)(2,1)S(1)}, bf16[2,18,256]{2,1,0:T(8,128)(2,1)S(1)}, u32[]{:S(2)}, u32[]{:S(2)}) collective-permute-start(bf16[2,18,256]{2,1,0:T(8,128)(2,1)S(1)} %get-tuple-element.22.refs_5_), channel_id=1, source_target_pairs={{0,2},{2,0},{4,6},{6,4},{1,3},{3,1},{5,7},{7,5},{8,10},{10,8},{12,... | collective-permute-start | bytes 55304 | tf_op jit(solution)/shard_map/ppermute | solution.py:346
  23.7 5.5 %collective-permute-start.4 = (bf16[2,128,256]{2,1,0:T(8,128)(2,1)S(1)}, bf16[2,128,256]{2,1,0:T(8,128)(2,1)S(1)}, u32[]{:S(2)}, u32[]{:S(2)}) collective-permute-start(bf16[2,128,256]{2,1,0:T(8,128)(2,1)S(1)} %pick.4), channel_id=1, source_target_pairs={{0,1},{1,0},{2,3},{3,2},{4,5},{5,4},{6,7},{7,6},{8,9},{9,8},{10,11... | collective-permute-start | bytes 393224 | tf_op jit(solution)/shard_map/ppermute | solution.py:345

commit v9 on v7

--- a/solution.py
+++ b/solution.py
@@ -15,24 +15,32 @@
 BLOCK = 4
 
 
-def relayout_kernel(chunks, x_ref, rim_ref, *refs):
-    outs, col_ref = refs[:-1], refs[-1]
+def relayout_kernel(chunks, x_hbm, rim_ref, *refs):
+    outs, (x_ref, col_ref, sems) = refs[:-3], refs[-3:]
     slab, rows, width = x_ref.shape
-    for base in range(0, rows, 8):
-        group = jnp.swapaxes(x_ref[:, base : base + 8, :].astype(F32), 0, 1)
-        for h in range(base, base + 8):
-            pixels = group[h - base].T
-            col_ref[h : h + 1, :] = pixels[0:1, :]
-            col_ref[rows + h : rows + h + 1, :] = pixels[width - 1 : width, :]
-            pixels = pixels.astype(BF16)
-            if h == 0:
-                rim_ref[0:width, :] = pixels
-            elif h == rows - 1:
-                rim_ref[width : 2 * width, :] = pixels
-            else:
-                for out, (first, last) in zip(outs, chunks):
-                    if first <= h < last:
-                        out[h - first] = pixels
+    parts = 2 if slab % 256 == 0 else 1
+    step = slab // parts
+    copies = [pltpu.make_async_copy(x_hbm.at[q * step : (q + 1) * step], x_ref.at[q * step : (q + 1) * step], sems.at[q]) for q in range(parts)]
+    for copy in copies:
+        copy.start()
+    for q, copy in enumerate(copies):
+        copy.wait()
+        lanes = slice(q * step, (q + 1) * step)
+        for base in range(0, rows, 8):
+            group = jnp.swapaxes(x_ref[lanes, base : base + 8, :].astype(F32), 0, 1)
+            for h in range(base, base + 8):
+                pixels = group[h - base].T
+                col_ref[h : h + 1, lanes] = pixels[0:1, :]
+                col_ref[rows + h : rows + h + 1, lanes] = pixels[width - 1 : width, :]
+                pixels = pixels.astype(BF16)
+                if h == 0:
+                    rim_ref[0:width, lanes] = pixels
+                elif h == rows - 1:
+                    rim_ref[width : 2 * width, lanes] = pixels
+                else:
+                    for out, (first, last) in zip(outs, chunks):
+                        if first <= h < last:
+                            out[h - first, :, lanes] = pixels
     rim_ref[2 * width :, :] = col_ref[...].astype(BF16)
 
 
@@ -42,12 +50,12 @@
     return pl.pallas_call(
         functools.partial(relayout_kernel, chunks),
         out_shape=[jax.ShapeDtypeStruct(s, BF16) for s in shapes],
-        in_specs=[VMEM],
+        in_specs=[HBM],
         out_specs=[VMEM] * len(shapes),
-        scratch_shapes=[pltpu.VMEM((2 * rows, slab), F32)],
+        scratch_shapes=[pltpu.VMEM(features.shape, BF16), pltpu.VMEM((2 * rows, slab), F32), pltpu.SemaphoreType.DMA((2,))],
         compiler_params=PARAMS,
         name="relayout",
-    )(features)
+    )(pltpu.with_memory_space_constraint(features, pltpu.HBM))
 
 
 def put_row(x_ref, at, value):
@@ -206,9 +214,8 @@
         fix_ref[i] = fix
 
 
-def finish_row(total_ref, h, rows_ref, cols_ref):
-    height, width = cols_ref.shape[1], total_ref.shape[1]
-    value = total_ref[h]
+def finish_row(value, h, rows_ref, cols_ref):
+    height, width = cols_ref.shape[1], value.shape[0]
     if h == 0:
         value += rows_ref[0]
     if h == height - 1:
@@ -216,26 +223,36 @@
     edge = lax.broadcasted_iota(jnp.int32, (8, value.shape[1]), 0)
     first = value[0:8] + jnp.where(edge == 0, cols_ref[0, h : h + 1, :], 0)
     final = value[width - 8 :] + jnp.where(edge == 7, cols_ref[1, h : h + 1, :], 0)
-    return jnp.concatenate([first, value[8 : width - 8], final], 0)
-
-
-def store_rows(total_ref, rows_ref, cols_ref, rows, out_ref):
-    turned = jnp.stack([finish_row(total_ref, h, rows_ref, cols_ref).T for h in rows], 0)
-    out_ref[...] = jnp.swapaxes(turned, 0, 1).astype(BF16)
+    return jnp.concatenate([first, value[8 : width - 8], final], 0).T
 
 
 def upper_kernel(total_ref, rows_ref, cols_ref, out_ref):
-    store_rows(total_ref, rows_ref, cols_ref, range(out_ref.shape[1]), out_ref)
-
-
-def last_kernel(span, piece, w_ref, total_in, rows_ref, cols_ref, upper_ref, out_ref, total_ref, x_ref, lower_ref, sems):
-    half = upper_ref.shape[1]
-    height = out_ref.shape[1]
+    turned = [finish_row(total_ref[h], h, rows_ref, cols_ref) for h in range(out_ref.shape[1])]
+    out_ref[...] = jnp.swapaxes(jnp.stack(turned, 0), 0, 1).astype(BF16)
+
+
+def middle_kernel(start, total_ref, rows_ref, cols_ref, out_ref):
+    for i in range(out_ref.shape[0]):
+        out_ref[i] = finish_row(total_ref[start + i], start + i, rows_ref, cols_ref)
+
+
+def last_kernel(piece, w_ref, total_ref, rows_ref, cols_ref, upper_ref, middle_ref, out_ref, x_ref, lower_ref, sems):
+    outs, height, width = out_ref.shape
+    half, done = upper_ref.shape[1], middle_ref.shape[0]
     first = pltpu.make_async_copy(upper_ref, out_ref.at[:, 0:half, :], sems.at[0])
     first.start()
-    total_ref[half:] = total_in[half:]
-    add_rows([(piece, *span)], w_ref, total_ref, x_ref, set(range(height)))
-    store_rows(total_ref, rows_ref, cols_ref, range(half, height), lower_ref)
+    count = piece.shape[0]
+    for i in range(count):
+        put_row(x_ref, i, piece[i])
+    values = [total_ref[h] for h in range(half + done, height)]
+    for a in range(3):
+        for b in range(3):
+            part = jnp.dot(x_ref[b].reshape(count * width, -1), w_ref[a, b], preferred_element_type=F32).reshape(count, width, outs)
+            for i in range(count):
+                values[i + 2 - a] += turn(part[i], b)
+    turned = [middle_ref[i] for i in range(done)]
+    turned += [finish_row(value, half + done + i, rows_ref, cols_ref) for i, value in enumerate(values)]
+    lower_ref[...] = jnp.swapaxes(jnp.stack(turned, 0), 0, 1).astype(BF16)
     second = pltpu.make_async_copy(lower_ref, out_ref.at[:, half:height, :], sems.at[1])
     second.start()
     first.wait()
@@ -306,9 +323,9 @@
     slab, height, width = features.shape
     outs = kernel.shape[3] // groups
     half = height // 2
-    chunks = ((1, half), (half, height - 3), (height - 3, height - 1))
-
-    rim, upper_rows, lower_rows = relayout(features, ((1, half), (half, height - 1)))
+    chunks = ((1, half + 1), (half + 1, height - 2), (height - 2, height - 1))
+
+    rim, upper_rows, lower_rows = relayout(features, (chunks[0], (half + 1, height - 1)))
     rings = [[(i, (i + shift) % groups) for i in range(groups)] for shift in range(1, groups)]
     rims = [rim] + [lax.ppermute(rim, "filt", ring) for ring in rings]
     sets = [[lax.ppermute(upper_rows, "filt", ring)] for ring in rings]
@@ -320,8 +337,8 @@
     bias = bias[None, :]
     if outs % 128 != 0:
         bias = lax.dynamic_slice_in_dim(bias, lax.axis_index("filt") * outs, outs, 1)
-    spans = [*outer, (1, 0, 1, half - 1), (2, 0, half, half - 1)]
-    second = pick(lower_rows, 0, chunks[1][1] - half, weights[0])
+    spans = [*outer, (1, 0, 1, half), (2, 0, half + 1, height - half - 2)]
+    second = pick(lower_rows, 0, chunks[1][1] - half - 1, weights[0])
     for received, ring in zip(sets, rings):
         received.append(lax.ppermute(second, "filt", ring))
 
@@ -333,7 +350,7 @@
         total = accumulate(outer, [pairs[g]], weights[g], total, shape)
     edge = pltpu.VMEM((2, height + 2, slab), F32)
     sent = calls(functools.partial(edges_kernel, groups), "edges", [(groups, height + 2, slab)] * 2, [*rims, *outer_rows], [edge])
-    third = pick(lower_rows, chunks[2][0] - half, chunks[2][1] - half, sent[0])
+    third = pick(lower_rows, chunks[2][0] - half - 1, chunks[2][1] - half - 1, sent[0])
     for received, ring in zip(sets, rings):
         received.append(lax.ppermute(third, "filt", ring))
     outer_cols = [lax.ppermute(v, "col", p) for v, p in zip(sent, col_pairs)]
@@ -343,25 +360,26 @@
     )
     for g in range(1, groups):
         a, b, c = sets[g - 1]
-        total = accumulate([(0, 0, chunks[0][0], half - 1)], [a], weights[g], total, shape, rows_fix)
-        total = accumulate([(0, 0, chunks[1][0], b.shape[0])], [b], weights[g], total, shape)
+        total = accumulate([(0, 0, chunks[0][0], a.shape[0])], [a], weights[g], total, shape, rows_fix)
         if g < groups - 1:
+            total = accumulate([(0, 0, chunks[1][0], b.shape[0])], [b], weights[g], total, shape)
             total = accumulate([(0, 0, chunks[2][0], c.shape[0])], [c], weights[g], total, shape)
     cols_fix = call(
         functools.partial(outer_cols_kernel, groups), "outer_cols", (2, height, outs), F32,
         [*outer_cols, *weights, total], cost(6 * 256 * groups, slab, outs),
     )
     top = call(upper_kernel, "upper", (outs, half, width), BF16, [total, rows_fix, cols_fix], cost(256, slab, outs))
+    total = accumulate([(0, 0, chunks[1][0], b.shape[0])], [b], weights[-1], total, shape, top)
+    done = chunks[2][0] - 1 - half
+    middle = call(functools.partial(middle_kernel, half), "middle", (done, outs, width), F32, [total, rows_fix, cols_fix], cost(1, 1, 1))
     scratch = [
-        pltpu.VMEM(shape, F32),
         pltpu.VMEM((3, c.shape[0], width, slab), BF16),
         pltpu.VMEM((outs, height - half, width), BF16),
         pltpu.SemaphoreType.DMA((2,)),
     ]
-    span = (0, chunks[2][0], c.shape[0])
     return call(
-        functools.partial(last_kernel, span), "last", (outs, height, width), BF16,
-        [c, weights[-1], total, rows_fix, cols_fix, top], cost(9 * 256, slab, outs), scratch, HBM,
+        last_kernel, "last", (outs, height, width), BF16,
+        [c, weights[-1], total, rows_fix, cols_fix, top, middle], cost(9 * 256, slab, outs), scratch, HBM,
     )
 
 

time: 30.4 us -> 30.4 us (level)
  local copies, waits for them, and re-layouts: 1.25 us -> 0.03 us
  Pallas kernels: 10.5 us -> 11.7 us
    unnamed x4 -> x2, local copies, waits for them, and re-layouts: 1.23 us -> 0.01 us
    pallas_call x1, Pallas kernels: 0.82 us -> 1.83 us  [relayout(): pl.pallas_call(functools.partial(relayout_kernel, chunks), out_shape=[jax...]
    pallas_call x6 -> x7, Pallas kernels: 2.83 us -> 2.86 us  [call(): pl.pallas_call(kernel, out_shape=jax.ShapeDtypeStruct(shape, dtype), in_s...]
  transfers between devices with their start and end apart: 8 -> 8, of which waited for: 3 -> 2; matrix products, arithmetic and copies ran while one was open for 0% -> 0% of each run, Pallas kernels for 27% -> 28%
where the time goes in v9:
time: 30.4 us; the launch traced here: 30.2 us
  starting transfers between devices  15.9 us (52%)
  Pallas kernels  11.7 us (38%)
  waiting for transfers between devices  2.46 us (8%)
    ppermute x2, starting transfers between devices, body(): outer_rows = [lax.ppermute(v, 'row', p) for v, p in zip(sent, row_pairs)]  5.67 us
    pallas_call x4, Pallas kernels, accumulate(): pl.pallas_call(functools.partial(accumulate_kernel, spans, len(pieces), t...  5.26 us
    ppermute x2, starting transfers between devices, body(): outer_cols = [lax.ppermute(v, 'col', p) for v, p in zip(sent, col_pairs)]  3.58 us
    ppermute x1, starting transfers between devices, body(): rims = [rim] + [lax.ppermute(rim, 'filt', ring) for ring in rings]  3.03 us
    pallas_call x7, Pallas kernels, call(): pl.pallas_call(kernel, out_shape=jax.ShapeDtypeStruct(shape, dtype), in_s...  2.86 us
    ppermute x1, starting transfers between devices, body(): received.append(lax.ppermute(second, 'filt', ring))  2.01 us
    pallas_call x1, Pallas kernels, relayout(): pl.pallas_call(functools.partial(relayout_kernel, chunks), out_shape=[jax...  1.83 us
    pallas_call x1, Pallas kernels, split_weights(): pl.pallas_call(functools.partial(weights_kernel, groups), out_shape=[jax....  1.68 us
  transfers between devices with their start and end apart: 8, of which 2 were waited for; matrix products, arithmetic and copies ran while one was open for 0% of the time, Pallas kernels for 28%

profile of v9, /device:TPU:0, one launch (start us, length us, event | category | flops | bytes accessed | tf_op | source)
XLA Modules:
  0.0 30.2 jit_solution(1521814997031879626)
XLA Ops:
  0.0 1.8 %relayout.1 = (bf16[288,256]{1,0:T(8,128)(2,1)S(1)}, bf16[8,128,256]{2,1,0:T(8,128)(2,1)S(1)}, bf16[6,128,256]{2,1,0:T(8,128)(2,1)S(1)}) custom-call(bf16[256,16,128]{2,1,0:T(8,128)(2,1)} %x_hbm.1), custom_call_target="tpu_custom_call" | custom-call | tf_op jit(solution)/shard_map/relayout/pallas_call | solution.py:50
  1.8 3.0 %collective-permute-start = (bf16[288,256]{1,0:T(8,128)(2,1)S(1)}, bf16[288,256]{1,0:T(8,128)(2,1)S(1)}, u32[]{:S(2)}, u32[]{:S(2)}) collective-permute-start(bf16[288,256]{1,0:T(8,128)(2,1)S(1)} %get-tuple-element.15.refs_0_), channel_id=1, source_target_pairs={{0,1},{1,0},{2,3},{3,2},{4,5},{5,4},{6,7},{7,6},{8,9},{9,8},{10,11... | collective-permute-start | bytes 442376 | tf_op jit(solution)/shard_map/ppermute | solution.py:330
  4.9 0.1 collective-permute-start.5
  4.9 1.7 %split_weights.1 = (bf16[3,3,256,256]{3,2,1,0:T(8,128)(2,1)S(1)}, bf16[3,3,256,256]{3,2,1,0:T(8,128)(2,1)S(1)}) custom-call(bf16[3,3,512,512]{3,2,1,0:T(8,128)(2,1)} %kernel_ref.1), custom_call_target="tpu_custom_call" | custom-call | tf_op jit(solution)/shard_map/split_weights/pallas_call | solution.py:306
  6.7 2.0 %collective-permute-start.4 = (bf16[5,128,256]{2,1,0:T(8,128)(2,1)S(1)}, bf16[5,128,256]{2,1,0:T(8,128)(2,1)S(1)}, u32[]{:S(2)}, u32[]{:S(2)}) collective-permute-start(bf16[5,128,256]{2,1,0:T(8,128)(2,1)S(1)} %pick.3), channel_id=1, source_target_pairs={{0,1},{1,0},{2,3},{3,2},{4,5},{5,4},{6,7},{7,6},{8,9},{9,8},{10,11... | collective-permute-start | bytes 983048 | tf_op jit(solution)/shard_map/ppermute | solution.py:343
  8.7 0.0 copy-start
  8.7 0.8 %collective-permute-done.refs_1_.refs_5_ = bf16[288,256]{1,0:T(8,128)(2,1)S(1)} collective-permute-done((bf16[288,256]{1,0:T(8,128)(2,1)S(1)}, bf16[288,256]{1,0:T(8,128)(2,1)S(1)}, u32[]{:S(2)}, u32[]{:S(2)}) %collective-permute-start) | collective-permute-done | bytes 147488 | tf_op jit(solution)/shard_map/ppermute | solution.py:330
  9.6 0.7 %collective-permute-start.1 = (bf16[2,128,256]{2,1,0:T(8,128)(2,1)S(1)}, bf16[2,128,256]{2,1,0:T(8,128)(2,1)S(1)}, u32[]{:S(2)}, u32[]{:S(2)}) collective-permute-start(bf16[2,128,256]{2,1,0:T(8,128)(2,1)S(1)} %get-tuple-element.16), channel_id=1, source_target_pairs={{8,16},{16,8},{9,17},{17,9},{10,18},{18,10},{11,19},{19,11},{12,20... | collective-permute-start | bytes 393224 | tf_op jit(solution)/shard_map/ppermute | solution.py:347
  10.2 5.0 %collective-permute-start.2 = (bf16[2,128,256]{2,1,0:T(8,128)(2,1)S(1)}, bf16[2,128,256]{2,1,0:T(8,128)(2,1)S(1)}, u32[]{:S(2)}, u32[]{:S(2)}) collective-permute-start(bf16[2,128,256]{2,1,0:T(8,128)(2,1)S(1)} %get-tuple-element.17), channel_id=1, source_target_pairs={{0,8},{8,0},{16,24},{24,16},{1,9},{9,1},{17,25},{25,17},{2,10},{10... | collective-permute-start | bytes 393224 | tf_op jit(solution)/shard_map/ppermute | solution.py:347
  15.2 0.0 copy-done
  15.2 2.5 %accumulate.4.refs_2_ = f32[16,128,256]{2,1,0:T(8,128)S(1)} custom-call(bf16[2,128,256]{2,1,0:T(8,128)(2,1)S(1)} %bitcast.4, bf16[8,128,256]{2,1,0:T(8,128)(2,1)S(1)} %get-tuple-element.21.refs_1_, bf16[6,128,256]{2,1,0:T(8,128)(2,1)S(1)} %get-tuple-element.14.rows_ref.refs_2_, bf16[3,3,256,256]{3,2,1,0:T(8,128)(2,1)S(1)} %get-tuple-element.20.after_ref.refs_3_.refs_2_, ...), custom_call_target="tpu_custom_call" | custom-call | flops 2415919104 | bytes 1048576 | tf_op jit(solution)/shard_map/accumulate/pallas_call | solution.py:129
  17.8 0.4 %accumulate.5.refs_2_ = f32[16,128,256]{2,1,0:T(8,128)S(1)} custom-call(bf16[2,128,256]{2,1,0:T(8,128)(2,1)S(1)} %bitcast.3, bf16[3,3,256,256]{3,2,1,0:T(8,128)(2,1)S(1)} %get-tuple-element.19.refs_1_.refs_3_.w_ref, f32[16,128,256]{2,1,0:T(8,128)S(1)} %accumulate.4.refs_2_), custom_call_target="tpu_custom_call", output_to_operand_aliasing={{}: (2, {})} | custom-call | flops 301989888 | bytes 1048576 | tf_op jit(solution)/shard_map/accumulate/pallas_call | solution.py:129
  18.2 0.0 collective-permute-done.1.refs_2_.refs_0_
  18.2 0.0 collective-permute-done.2.refs_3_.refs_1_
  18.3 0.7 %collective-permute-start.6 = (bf16[2,18,256]{2,1,0:T(8,128)(2,1)S(1)}, bf16[2,18,256]{2,1,0:T(8,128)(2,1)S(1)}, u32[]{:S(2)}, u32[]{:S(2)}) collective-permute-start(bf16[2,18,256]{2,1,0:T(8,128)(2,1)S(1)} %get-tuple-element.18.after_ref.refs_4_), channel_id=1, source_target_pairs={{2,4},{4,2},{3,5},{5,3},{10,12},{12,10},{11,13},{13,11},{18,20},{2... | collective-permute-start | bytes 55304 | tf_op jit(solution)/shard_map/ppermute | solution.py:356
  19.0 2.9 %collective-permute-start.7 = (bf16[2,18,256]{2,1,0:T(8,128)(2,1)S(1)}, bf16[2,18,256]{2,1,0:T(8,128)(2,1)S(1)}, u32[]{:S(2)}, u32[]{:S(2)}) collective-permute-start(bf16[2,18,256]{2,1,0:T(8,128)(2,1)S(1)} %get-tuple-element.22.refs_5_), channel_id=1, source_target_pairs={{0,2},{2,0},{4,6},{6,4},{1,3},{3,1},{5,7},{7,5},{8,10},{10,8},{12,... | collective-permute-start | bytes 55304 | tf_op jit(solution)/shard_map/ppermute | solution.py:356
  21.9 1.5 %collective-permute-start.3 = (bf16[1,128,256]{2,1,0:T(8,128)(2,1)S(1)}, bf16[1,128,256]{2,1,0:T(8,128)(2,1)S(1)}, u32[]{:S(2)}, u32[]{:S(2)}) collective-permute-start(bf16[1,128,256]{2,1,0:T(8,128)(2,1)S(1)} %pick.2), channel_id=1, source_target_pairs={{0,1},{1,0},{2,3},{3,2},{4,5},{5,4},{6,7},{7,6},{8,9},{9,8},{10,11... | collective-permute-start | bytes 196616 | tf_op jit(solution)/shard_map/ppermute | solution.py:355
  23.4 0.4 %outer_rows.1.refs_3_.rows_ref = f32[2,128,256]{2,1,0:T(8,128)S(1)} custom-call(bf16[2,128,256]{2,1,0:T(8,128)(2,1)S(1)} %collective-permute-done.1.refs_2_.refs_0_, bf16[2,128,256]{2,1,0:T(8,128)(2,1)S(1)} %collective-permute-done.2.refs_3_.refs_1_, bf16[3,3,256,256]{3,2,1,0:T(8,128)(2,1)S(1)} %get-tuple-element.20.after_ref.refs_3_.refs_2_, ...), custom_call_target="tpu_custom_call" | custom-call | flops 201326592 | bytes 1048576 | tf_op jit(solution)/shard_map/outer_rows/pallas_call | solution.py:263
  23.8 0.0 collective-permute-done.5.refs_0_
  23.8 1.4 %accumulate.6.refs_4_.total_ref.refs_2_ = f32[16,128,256]{2,1,0:T(8,128)S(1)} custom-call(bf16[8,128,256]{2,1,0:T(8,128)(2,1)S(1)} %collective-permute-done.5.refs_0_, bf16[3,3,256,256]{3,2,1,0:T(8,128)(2,1)S(1)} %get-tuple-element.19.refs_1_.refs_3_.w_ref, f32[16,128,256]{2,1,0:T(8,128)S(1)} %accumulate.5.refs_2_, ...), custom_call_target="tpu_custom_call", output_to_operand_aliasing={{}: (2, {})} | custom-call | flops 1207959552 | bytes 1048576 | tf_op jit(solution)/shard_map/accumulate/pallas_call | solution.py:129
  25.2 0.0 collective-permute-done.7.refs_1_
  25.2 0.0 collective-permute-done.6.refs_0_
  25.2 0.4 %outer_cols.1.cols_ref = f32[2,16,256]{2,1,0:T(8,128)S(1)} custom-call(bf16[2,18,256]{2,1,0:T(8,128)(2,1)S(1)} %collective-permute-done.6.refs_0_, bf16[2,18,256]{2,1,0:T(8,128)(2,1)S(1)} %collective-permute-done.7.refs_1_, bf16[3,3,256,256]{3,2,1,0:T(8,128)(2,1)S(1)} %get-tuple-element.20.after_ref.refs_3_.refs_2_, ...), custom_call_target="tpu_custom_call" | custom-call | flops 402653184 | bytes 1048576 | tf_op jit(solution)/shard_map/outer_cols/pallas_call | solution.py:263
  25.6 0.5 %upper.1.refs_3_.upper_ref = bf16[256,8,128]{2,1,0:T(8,128)(2,1)S(1)} custom-call(f32[16,128,256]{2,1,0:T(8,128)S(1)} %accumulate.6.refs_4_.total_ref.refs_2_, f32[2,128,256]{2,1,0:T(8,128)S(1)} %outer_rows.1.refs_3_.rows_ref, f32[2,16,256]{2,1,0:T(8,128)S(1)} %outer_cols.1.cols_ref), custom_call_target="tpu_custom_call" | custom-call | flops 33554432 | bytes 1048576 | tf_op jit(solution)/shard_map/upper/pallas_call | solution.py:263
  26.1 1.6 %collective-permute-done.4.refs_0_ = bf16[5,128,256]{2,1,0:T(8,128)(2,1)S(1)} collective-permute-done((bf16[5,128,256]{2,1,0:T(8,128)(2,1)S(1)}, bf16[5,128,256]{2,1,0:T(8,128)(2,1)S(1)}, u32[]{:S(2)}, u32[]{:S(2)}) %collective-permute-start.4) | collective-permute-done | bytes 327712 | tf_op jit(solution)/shard_map/ppermute | solution.py:343
  27.7 0.9 %accumulate.7.total_ref = f32[16,128,256]{2,1,0:T(8,128)S(1)} custom-call(bf16[5,128,256]{2,1,0:T(8,128)(2,1)S(1)} %collective-permute-done.4.refs_0_, bf16[3,3,256,256]{3,2,1,0:T(8,128)(2,1)S(1)} %get-tuple-element.19.refs_1_.refs_3_.w_ref, f32[16,128,256]{2,1,0:T(8,128)S(1)} %accumulate.6.refs_4_.total_ref.refs_2_, ...), custom_call_target="tpu_custom_call", output_to_operand_aliasing={{}: (2, {})} | custom-call | flops 754974720 | bytes 1048576 | tf_op jit(solution)/shard_map/accumulate/pallas_call | solution.py:129
  28.6 0.2 middle.1.middle_ref
  28.9 0.0 collective-permute-done.3.piece
  28.9 1.4 %last.1 = bf16[256,16,128]{2,1,0:T(8,128)(2,1)} custom-call(bf16[1,128,256]{2,1,0:T(8,128)(2,1)S(1)} %collective-permute-done.3.piece, bf16[3,3,256,256]{3,2,1,0:T(8,128)(2,1)S(1)} %get-tuple-element.19.refs_1_.refs_3_.w_ref, f32[16,128,256]{2,1,0:T(8,128)S(1)} %accumulate.7.total_ref, f32[2,128,256]{2,1,0:T(8,128)S(1)} %outer_rows.1.refs_3_.rows_ref, ...), custom_call_target="tpu_custom_call" | custom-call | flops 301989888 | bytes 1048576 | tf_op jit(solution)/shard_map/last/pallas_call | solution.py:263
  (6 shorter events, 0.1 us)
Async XLA Ops:
  1.8 7.7 %collective-permute-start = (bf16[288,256]{1,0:T(8,128)(2,1)S(1)}, bf16[288,256]{1,0:T(8,128)(2,1)S(1)}, u32[]{:S(2)}, u32[]{:S(2)}) collective-permute-start(bf16[288,256]{1,0:T(8,128)(2,1)S(1)} %get-tuple-element.15.refs_0_), channel_id=1, source_target_pairs={{0,1},{1,0},{2,3},{3,2},{4,5},{5,4},{6,7},{7,6},{8,9},{9,8},{10,11... | collective-permute-start | bytes 442376 | tf_op jit(solution)/shard_map/ppermute | solution.py:330
  4.9 18.9 %collective-permute-start.5 = (bf16[8,128,256]{2,1,0:T(8,128)(2,1)S(1)}, bf16[8,128,256]{2,1,0:T(8,128)(2,1)S(1)}, u32[]{:S(2)}, u32[]{:S(2)}) collective-permute-start(bf16[8,128,256]{2,1,0:T(8,128)(2,1)S(1)} %get-tuple-element.21.refs_1_), channel_id=1, source_target_pairs={{0,1},{1,0},{2,3},{3,2},{4,5},{5,4},{6,7},{7,6},{8,9},{9,8},{10,11... | collective-permute-start | bytes 1572872 | tf_op jit(solution)/shard_map/ppermute | solution.py:331
  6.7 21.0 %collective-permute-start.4 = (bf16[5,128,256]{2,1,0:T(8,128)(2,1)S(1)}, bf16[5,128,256]{2,1,0:T(8,128)(2,1)S(1)}, u32[]{:S(2)}, u32[]{:S(2)}) collective-permute-start(bf16[5,128,256]{2,1,0:T(8,128)(2,1)S(1)} %pick.3), channel_id=1, source_target_pairs={{0,1},{1,0},{2,3},{3,2},{4,5},{5,4},{6,7},{7,6},{8,9},{9,8},{10,11... | collective-permute-start | bytes 983048 | tf_op jit(solution)/shard_map/ppermute | solution.py:343
  8.7 6.5 %copy-start = (f32[512]{0:T(512)S(1)}, f32[512]{0:T(512)}, u32[]{:S(2)}) copy-start(f32[512]{0:T(512)} %param.5) | copy-start | bytes 6148
  9.6 8.6 %collective-permute-start.1 = (bf16[2,128,256]{2,1,0:T(8,128)(2,1)S(1)}, bf16[2,128,256]{2,1,0:T(8,128)(2,1)S(1)}, u32[]{:S(2)}, u32[]{:S(2)}) collective-permute-start(bf16[2,128,256]{2,1,0:T(8,128)(2,1)S(1)} %get-tuple-element.16), channel_id=1, source_target_pairs={{8,16},{16,8},{9,17},{17,9},{10,18},{18,10},{11,19},{19,11},{12,20... | collective-permute-start | bytes 393224 | tf_op jit(solution)/shard_map/ppermute | solution.py:347
  10.2 8.0 %collective-permute-start.2 = (bf16[2,128,256]{2,1,0:T(8,128)(2,1)S(1)}, bf16[2,128,256]{2,1,0:T(8,128)(2,1)S(1)}, u32[]{:S(2)}, u32[]{:S(2)}) collective-permute-start(bf16[2,128,256]{2,1,0:T(8,128)(2,1)S(1)} %get-tuple-element.17), channel_id=1, source_target_pairs={{0,8},{8,0},{16,24},{24,16},{1,9},{9,1},{17,25},{25,17},{2,10},{10... | collective-permute-start | bytes 393224 | tf_op jit(solution)/shard_map/ppermute | solution.py:347
  18.3 6.9 %collective-permute-start.6 = (bf16[2,18,256]{2,1,0:T(8,128)(2,1)S(1)}, bf16[2,18,256]{2,1,0:T(8,128)(2,1)S(1)}, u32[]{:S(2)}, u32[]{:S(2)}) collective-permute-start(bf16[2,18,256]{2,1,0:T(8,128)(2,1)S(1)} %get-tuple-element.18.after_ref.refs_4_), channel_id=1, source_target_pairs={{2,4},{4,2},{3,5},{5,3},{10,12},{12,10},{11,13},{13,11},{18,20},{2... | collective-permute-start | bytes 55304 | tf_op jit(solution)/shard_map/ppermute | solution.py:356
  19.0 6.2 %collective-permute-start.7 = (bf16[2,18,256]{2,1,0:T(8,128)(2,1)S(1)}, bf16[2,18,256]{2,1,0:T(8,128)(2,1)S(1)}, u32[]{:S(2)}, u32[]{:S(2)}) collective-permute-start(bf16[2,18,256]{2,1,0:T(8,128)(2,1)S(1)} %get-tuple-element.22.refs_5_), channel_id=1, source_target_pairs={{0,2},{2,0},{4,6},{6,4},{1,3},{3,1},{5,7},{7,5},{8,10},{10,8},{12,... | collective-permute-start | bytes 55304 | tf_op jit(solution)/shard_map/ppermute | solution.py:356
  21.9 7.0 %collective-permute-start.3 = (bf16[1,128,256]{2,1,0:T(8,128)(2,1)S(1)}, bf16[1,128,256]{2,1,0:T(8,128)(2,1)S(1)}, u32[]{:S(2)}, u32[]{:S(2)}) collective-permute-start(bf16[1,128,256]{2,1,0:T(8,128)(2,1)S(1)} %pick.2), channel_id=1, source_target_pairs={{0,1},{1,0},{2,3},{3,2},{4,5},{5,4},{6,7},{7,6},{8,9},{9,8},{10,11... | collective-permute-start | bytes 196616 | tf_op jit(solution)/shard_map/ppermute | solution.py:355

commit v10 on v9

--- a/solution.py
+++ b/solution.py
@@ -26,21 +26,19 @@
     for q, copy in enumerate(copies):
         copy.wait()
         lanes = slice(q * step, (q + 1) * step)
-        for base in range(0, rows, 8):
-            group = jnp.swapaxes(x_ref[lanes, base : base + 8, :].astype(F32), 0, 1)
-            for h in range(base, base + 8):
-                pixels = group[h - base].T
-                col_ref[h : h + 1, lanes] = pixels[0:1, :]
-                col_ref[rows + h : rows + h + 1, lanes] = pixels[width - 1 : width, :]
-                pixels = pixels.astype(BF16)
-                if h == 0:
-                    rim_ref[0:width, lanes] = pixels
-                elif h == rows - 1:
-                    rim_ref[width : 2 * width, lanes] = pixels
-                else:
-                    for out, (first, last) in zip(outs, chunks):
-                        if first <= h < last:
-                            out[h - first, :, lanes] = pixels
+        group = jnp.swapaxes(x_ref[lanes], 0, 1)
+        for h in range(rows):
+            pixels = group[h].T
+            col_ref[h : h + 1, lanes] = pixels[0:16].astype(F32)[0:1, :]
+            col_ref[rows + h : rows + h + 1, lanes] = pixels[width - 16 :].astype(F32)[15:16, :]
+            if h == 0:
+                rim_ref[0:width, lanes] = pixels
+            elif h == rows - 1:
+                rim_ref[width : 2 * width, lanes] = pixels
+            else:
+                for out, (first, last) in zip(outs, chunks):
+                    if first <= h < last:
+                        out[h - first, :, lanes] = pixels
     rim_ref[2 * width :, :] = col_ref[...].astype(BF16)
 
 
@@ -223,12 +221,12 @@
     edge = lax.broadcasted_iota(jnp.int32, (8, value.shape[1]), 0)
     first = value[0:8] + jnp.where(edge == 0, cols_ref[0, h : h + 1, :], 0)
     final = value[width - 8 :] + jnp.where(edge == 7, cols_ref[1, h : h + 1, :], 0)
-    return jnp.concatenate([first, value[8 : width - 8], final], 0).T
+    return jnp.concatenate([first, value[8 : width - 8], final], 0).astype(BF16).T
 
 
 def upper_kernel(total_ref, rows_ref, cols_ref, out_ref):
     turned = [finish_row(total_ref[h], h, rows_ref, cols_ref) for h in range(out_ref.shape[1])]
-    out_ref[...] = jnp.swapaxes(jnp.stack(turned, 0), 0, 1).astype(BF16)
+    out_ref[...] = jnp.swapaxes(jnp.stack(turned, 0), 0, 1)
 
 
 def middle_kernel(start, total_ref, rows_ref, cols_ref, out_ref):
@@ -252,7 +250,7 @@
                 values[i + 2 - a] += turn(part[i], b)
     turned = [middle_ref[i] for i in range(done)]
     turned += [finish_row(value, half + done + i, rows_ref, cols_ref) for i, value in enumerate(values)]
-    lower_ref[...] = jnp.swapaxes(jnp.stack(turned, 0), 0, 1).astype(BF16)
+    lower_ref[...] = jnp.swapaxes(jnp.stack(turned, 0), 0, 1)
     second = pltpu.make_async_copy(lower_ref, out_ref.at[:, half:height, :], sems.at[1])
     second.start()
     first.wait()
@@ -323,9 +321,9 @@
     slab, height, width = features.shape
     outs = kernel.shape[3] // groups
     half = height // 2
-    chunks = ((1, half + 1), (half + 1, height - 2), (height - 2, height - 1))
-
-    rim, upper_rows, lower_rows = relayout(features, (chunks[0], (half + 1, height - 1)))
+    chunks = ((1, half + 2), (half + 2, height - 2), (height - 2, height - 1))
+
+    rim, upper_rows, lower_rows = relayout(features, (chunks[0], (chunks[0][1], height - 1)))
     rings = [[(i, (i + shift) % groups) for i in range(groups)] for shift in range(1, groups)]
     rims = [rim] + [lax.ppermute(rim, "filt", ring) for ring in rings]
     sets = [[lax.ppermute(upper_rows, "filt", ring)] for ring in rings]
@@ -337,8 +335,8 @@
     bias = bias[None, :]
     if outs % 128 != 0:
         bias = lax.dynamic_slice_in_dim(bias, lax.axis_index("filt") * outs, outs, 1)
-    spans = [*outer, (1, 0, 1, half), (2, 0, half + 1, height - half - 2)]
-    second = pick(lower_rows, 0, chunks[1][1] - half - 1, weights[0])
+    spans = [*outer, (1, 0, 1, half + 1), (2, 0, half + 2, height - half - 3)]
+    second = pick(lower_rows, 0, chunks[1][1] - chunks[1][0], weights[0])
     for received, ring in zip(sets, rings):
         received.append(lax.ppermute(second, "filt", ring))
 
@@ -350,7 +348,7 @@
         total = accumulate(outer, [pairs[g]], weights[g], total, shape)
     edge = pltpu.VMEM((2, height + 2, slab), F32)
     sent = calls(functools.partial(edges_kernel, groups), "edges", [(groups, height + 2, slab)] * 2, [*rims, *outer_rows], [edge])
-    third = pick(lower_rows, chunks[2][0] - half - 1, chunks[2][1] - half - 1, sent[0])
+    third = pick(lower_rows, chunks[2][0] - chunks[1][0], chunks[2][1] - chunks[1][0], sent[0])
     for received, ring in zip(sets, rings):
         received.append(lax.ppermute(third, "filt", ring))
     outer_cols = [lax.ppermute(v, "col", p) for v, p in zip(sent, col_pairs)]
@@ -371,7 +369,7 @@
     top = call(upper_kernel, "upper", (outs, half, width), BF16, [total, rows_fix, cols_fix], cost(256, slab, outs))
     total = accumulate([(0, 0, chunks[1][0], b.shape[0])], [b], weights[-1], total, shape, top)
     done = chunks[2][0] - 1 - half
-    middle = call(functools.partial(middle_kernel, half), "middle", (done, outs, width), F32, [total, rows_fix, cols_fix], cost(1, 1, 1))
+    middle = call(functools.partial(middle_kernel, half), "middle", (done, outs, width), BF16, [total, rows_fix, cols_fix], cost(1, 1, 1))
     scratch = [
         pltpu.VMEM((3, c.shape[0], width, slab), BF16),
         pltpu.VMEM((outs, height - half, width), BF16),

time: 30.4 us -> 29.9 us (0.984)
  Pallas kernels: 11.7 us -> 11 us
    pallas_call x7, Pallas kernels: 2.86 us -> 2.43 us  [call(): pl.pallas_call(kernel, out_shape=jax.ShapeDtypeStruct(shape, dtype), in_s...]
  transfers between devices with their start and end apart: 8 -> 8, of which waited for: 2 -> 2; matrix products, arithmetic and copies ran while one was open for 0% -> 0% of each run, Pallas kernels for 28% -> 27%
where the time goes in v10:
time: 29.9 us; the launch traced here: 29.7 us
  starting transfers between devices  15.9 us (53%)
  Pallas kernels  11 us (37%)
  waiting for transfers between devices  2.55 us (9%)
    ppermute x2, starting transfers between devices, body(): outer_rows = [lax.ppermute(v, 'row', p) for v, p in zip(sent, row_pairs)]  5.67 us
    pallas_call x4, Pallas kernels, accumulate(): pl.pallas_call(functools.partial(accumulate_kernel, spans, len(pieces), t...  5.28 us
    ppermute x2, starting transfers between devices, body(): outer_cols = [lax.ppermute(v, 'col', p) for v, p in zip(sent, col_pairs)]  3.58 us
    ppermute x1, starting transfers between devices, body(): rims = [rim] + [lax.ppermute(rim, 'filt', ring) for ring in rings]  3.03 us
    pallas_call x7, Pallas kernels, call(): pl.pallas_call(kernel, out_shape=jax.ShapeDtypeStruct(shape, dtype), in_s...  2.43 us
    ppermute x1, starting transfers between devices, body(): received.append(lax.ppermute(second, 'filt', ring))  2.01 us
    ppermute x1, waiting for transfers between devices, body(): received.append(lax.ppermute(second, 'filt', ring))  1.69 us
    pallas_call x1, Pallas kernels, split_weights(): pl.pallas_call(functools.partial(weights_kernel, groups), out_shape=[jax....  1.68 us
  transfers between devices with their start and end apart: 8, of which 2 were waited for; matrix products, arithmetic and copies ran while one was open for 0% of the time, Pallas kernels for 27%

profile of v10, /device:TPU:0, one launch (start us, length us, event | category | flops | bytes accessed | tf_op | source)
XLA Modules:
  0.0 29.7 jit_solution(15320289417964695635)
XLA Ops:
  0.0 1.6 %relayout.1 = (bf16[288,256]{1,0:T(8,128)(2,1)S(1)}, bf16[9,128,256]{2,1,0:T(8,128)(2,1)S(1)}, bf16[5,128,256]{2,1,0:T(8,128)(2,1)S(1)}) custom-call(bf16[256,16,128]{2,1,0:T(8,128)(2,1)} %x_hbm.1), custom_call_target="tpu_custom_call" | custom-call | tf_op jit(solution)/shard_map/relayout/pallas_call | solution.py:48
  1.6 3.0 %collective-permute-start = (bf16[288,256]{1,0:T(8,128)(2,1)S(1)}, bf16[288,256]{1,0:T(8,128)(2,1)S(1)}, u32[]{:S(2)}, u32[]{:S(2)}) collective-permute-start(bf16[288,256]{1,0:T(8,128)(2,1)S(1)} %get-tuple-element.15.refs_0_), channel_id=1, source_target_pairs={{0,1},{1,0},{2,3},{3,2},{4,5},{5,4},{6,7},{7,6},{8,9},{9,8},{10,11... | collective-permute-start | bytes 442376 | tf_op jit(solution)/shard_map/ppermute | solution.py:328
  4.6 0.1 collective-permute-start.5
  4.7 1.7 %split_weights.1 = (bf16[3,3,256,256]{3,2,1,0:T(8,128)(2,1)S(1)}, bf16[3,3,256,256]{3,2,1,0:T(8,128)(2,1)S(1)}) custom-call(bf16[3,3,512,512]{3,2,1,0:T(8,128)(2,1)} %kernel_ref.1), custom_call_target="tpu_custom_call" | custom-call | tf_op jit(solution)/shard_map/split_weights/pallas_call | solution.py:304
  6.4 2.0 %collective-permute-start.4 = (bf16[4,128,256]{2,1,0:T(8,128)(2,1)S(1)}, bf16[4,128,256]{2,1,0:T(8,128)(2,1)S(1)}, u32[]{:S(2)}, u32[]{:S(2)}) collective-permute-start(bf16[4,128,256]{2,1,0:T(8,128)(2,1)S(1)} %pick.3), channel_id=1, source_target_pairs={{0,1},{1,0},{2,3},{3,2},{4,5},{5,4},{6,7},{7,6},{8,9},{9,8},{10,11... | collective-permute-start | bytes 786440 | tf_op jit(solution)/shard_map/ppermute | solution.py:341
  8.5 0.0 copy-start
  8.5 0.8 %collective-permute-done.refs_1_.refs_5_ = bf16[288,256]{1,0:T(8,128)(2,1)S(1)} collective-permute-done((bf16[288,256]{1,0:T(8,128)(2,1)S(1)}, bf16[288,256]{1,0:T(8,128)(2,1)S(1)}, u32[]{:S(2)}, u32[]{:S(2)}) %collective-permute-start) | collective-permute-done | bytes 147488 | tf_op jit(solution)/shard_map/ppermute | solution.py:328
  9.3 0.7 %collective-permute-start.1 = (bf16[2,128,256]{2,1,0:T(8,128)(2,1)S(1)}, bf16[2,128,256]{2,1,0:T(8,128)(2,1)S(1)}, u32[]{:S(2)}, u32[]{:S(2)}) collective-permute-start(bf16[2,128,256]{2,1,0:T(8,128)(2,1)S(1)} %get-tuple-element.16), channel_id=1, source_target_pairs={{8,16},{16,8},{9,17},{17,9},{10,18},{18,10},{11,19},{19,11},{12,20... | collective-permute-start | bytes 393224 | tf_op jit(solution)/shard_map/ppermute | solution.py:345
  10.0 5.0 %collective-permute-start.2 = (bf16[2,128,256]{2,1,0:T(8,128)(2,1)S(1)}, bf16[2,128,256]{2,1,0:T(8,128)(2,1)S(1)}, u32[]{:S(2)}, u32[]{:S(2)}) collective-permute-start(bf16[2,128,256]{2,1,0:T(8,128)(2,1)S(1)} %get-tuple-element.17), channel_id=1, source_target_pairs={{0,8},{8,0},{16,24},{24,16},{1,9},{9,1},{17,25},{25,17},{2,10},{10... | collective-permute-start | bytes 393224 | tf_op jit(solution)/shard_map/ppermute | solution.py:345
  15.0 0.0 copy-done
  15.0 2.5 %accumulate.4.refs_2_ = f32[16,128,256]{2,1,0:T(8,128)S(1)} custom-call(bf16[2,128,256]{2,1,0:T(8,128)(2,1)S(1)} %bitcast.4, bf16[9,128,256]{2,1,0:T(8,128)(2,1)S(1)} %get-tuple-element.21.refs_1_, bf16[5,128,256]{2,1,0:T(8,128)(2,1)S(1)} %get-tuple-element.14.rows_ref.refs_2_, bf16[3,3,256,256]{3,2,1,0:T(8,128)(2,1)S(1)} %get-tuple-element.20.after_ref.refs_3_.refs_2_, ...), custom_call_target="tpu_custom_call" | custom-call | flops 2415919104 | bytes 1048576 | tf_op jit(solution)/shard_map/accumulate/pallas_call | solution.py:127
  17.6 0.4 %accumulate.5.refs_2_ = f32[16,128,256]{2,1,0:T(8,128)S(1)} custom-call(bf16[2,128,256]{2,1,0:T(8,128)(2,1)S(1)} %bitcast.3, bf16[3,3,256,256]{3,2,1,0:T(8,128)(2,1)S(1)} %get-tuple-element.19.refs_1_.refs_3_.w_ref, f32[16,128,256]{2,1,0:T(8,128)S(1)} %accumulate.4.refs_2_), custom_call_target="tpu_custom_call", output_to_operand_aliasing={{}: (2, {})} | custom-call | flops 301989888 | bytes 1048576 | tf_op jit(solution)/shard_map/accumulate/pallas_call | solution.py:127
  18.0 0.0 collective-permute-done.1.refs_2_.refs_0_
  18.0 0.0 collective-permute-done.2.refs_3_.refs_1_
  18.0 0.7 %collective-permute-start.6 = (bf16[2,18,256]{2,1,0:T(8,128)(2,1)S(1)}, bf16[2,18,256]{2,1,0:T(8,128)(2,1)S(1)}, u32[]{:S(2)}, u32[]{:S(2)}) collective-permute-start(bf16[2,18,256]{2,1,0:T(8,128)(2,1)S(1)} %get-tuple-element.18.after_ref.refs_4_), channel_id=1, source_target_pairs={{2,4},{4,2},{3,5},{5,3},{10,12},{12,10},{11,13},{13,11},{18,20},{2... | collective-permute-start | bytes 55304 | tf_op jit(solution)/shard_map/ppermute | solution.py:354
  18.7 2.9 %collective-permute-start.7 = (bf16[2,18,256]{2,1,0:T(8,128)(2,1)S(1)}, bf16[2,18,256]{2,1,0:T(8,128)(2,1)S(1)}, u32[]{:S(2)}, u32[]{:S(2)}) collective-permute-start(bf16[2,18,256]{2,1,0:T(8,128)(2,1)S(1)} %get-tuple-element.22.refs_5_), channel_id=1, source_target_pairs={{0,2},{2,0},{4,6},{6,4},{1,3},{3,1},{5,7},{7,5},{8,10},{10,8},{12,... | collective-permute-start | bytes 55304 | tf_op jit(solution)/shard_map/ppermute | solution.py:354
  21.6 1.5 %collective-permute-start.3 = (bf16[1,128,256]{2,1,0:T(8,128)(2,1)S(1)}, bf16[1,128,256]{2,1,0:T(8,128)(2,1)S(1)}, u32[]{:S(2)}, u32[]{:S(2)}) collective-permute-start(bf16[1,128,256]{2,1,0:T(8,128)(2,1)S(1)} %pick.2), channel_id=1, source_target_pairs={{0,1},{1,0},{2,3},{3,2},{4,5},{5,4},{6,7},{7,6},{8,9},{9,8},{10,11... | collective-permute-start | bytes 196616 | tf_op jit(solution)/shard_map/ppermute | solution.py:353
  23.2 0.4 %outer_rows.1.refs_3_.rows_ref = f32[2,128,256]{2,1,0:T(8,128)S(1)} custom-call(bf16[2,128,256]{2,1,0:T(8,128)(2,1)S(1)} %collective-permute-done.1.refs_2_.refs_0_, bf16[2,128,256]{2,1,0:T(8,128)(2,1)S(1)} %collective-permute-done.2.refs_3_.refs_1_, bf16[3,3,256,256]{3,2,1,0:T(8,128)(2,1)S(1)} %get-tuple-element.20.after_ref.refs_3_.refs_2_, ...), custom_call_target="tpu_custom_call" | custom-call | flops 201326592 | bytes 1048576 | tf_op jit(solution)/shard_map/outer_rows/pallas_call | solution.py:261
  23.5 0.0 collective-permute-done.5.refs_0_
  23.6 1.6 %accumulate.6.refs_4_.total_ref.refs_2_ = f32[16,128,256]{2,1,0:T(8,128)S(1)} custom-call(bf16[9,128,256]{2,1,0:T(8,128)(2,1)S(1)} %collective-permute-done.5.refs_0_, bf16[3,3,256,256]{3,2,1,0:T(8,128)(2,1)S(1)} %get-tuple-element.19.refs_1_.refs_3_.w_ref, f32[16,128,256]{2,1,0:T(8,128)S(1)} %accumulate.5.refs_2_, ...), custom_call_target="tpu_custom_call", output_to_operand_aliasing={{}: (2, {})} | custom-call | flops 1358954496 | bytes 1048576 | tf_op jit(solution)/shard_map/accumulate/pallas_call | solution.py:127
  25.1 0.0 collective-permute-done.7.refs_1_
  25.2 0.0 collective-permute-done.6.refs_0_
  25.2 0.4 %outer_cols.1.cols_ref = f32[2,16,256]{2,1,0:T(8,128)S(1)} custom-call(bf16[2,18,256]{2,1,0:T(8,128)(2,1)S(1)} %collective-permute-done.6.refs_0_, bf16[2,18,256]{2,1,0:T(8,128)(2,1)S(1)} %collective-permute-done.7.refs_1_, bf16[3,3,256,256]{3,2,1,0:T(8,128)(2,1)S(1)} %get-tuple-element.20.after_ref.refs_3_.refs_2_, ...), custom_call_target="tpu_custom_call" | custom-call | flops 402653184 | bytes 1048576 | tf_op jit(solution)/shard_map/outer_cols/pallas_call | solution.py:261
  25.5 0.2 upper.1.refs_3_.upper_ref
  25.8 1.7 %collective-permute-done.4.refs_0_ = bf16[4,128,256]{2,1,0:T(8,128)(2,1)S(1)} collective-permute-done((bf16[4,128,256]{2,1,0:T(8,128)(2,1)S(1)}, bf16[4,128,256]{2,1,0:T(8,128)(2,1)S(1)}, u32[]{:S(2)}, u32[]{:S(2)}) %collective-permute-start.4) | collective-permute-done | bytes 262176 | tf_op jit(solution)/shard_map/ppermute | solution.py:341
  27.4 0.8 %accumulate.7.total_ref = f32[16,128,256]{2,1,0:T(8,128)S(1)} custom-call(bf16[4,128,256]{2,1,0:T(8,128)(2,1)S(1)} %collective-permute-done.4.refs_0_, bf16[3,3,256,256]{3,2,1,0:T(8,128)(2,1)S(1)} %get-tuple-element.19.refs_1_.refs_3_.w_ref, f32[16,128,256]{2,1,0:T(8,128)S(1)} %accumulate.6.refs_4_.total_ref.refs_2_, ...), custom_call_target="tpu_custom_call", output_to_operand_aliasing={{}: (2, {})} | custom-call | flops 603979776 | bytes 1048576 | tf_op jit(solution)/shard_map/accumulate/pallas_call | solution.py:127
  28.2 0.1 middle.1.middle_ref
  28.4 0.0 collective-permute-done.3.piece
  28.4 1.3 %last.1 = bf16[256,16,128]{2,1,0:T(8,128)(2,1)} custom-call(bf16[1,128,256]{2,1,0:T(8,128)(2,1)S(1)} %collective-permute-done.3.piece, bf16[3,3,256,256]{3,2,1,0:T(8,128)(2,1)S(1)} %get-tuple-element.19.refs_1_.refs_3_.w_ref, f32[16,128,256]{2,1,0:T(8,128)S(1)} %accumulate.7.total_ref, f32[2,128,256]{2,1,0:T(8,128)S(1)} %outer_rows.1.refs_3_.rows_ref, ...), custom_call_target="tpu_custom_call" | custom-call | flops 301989888 | bytes 1048576 | tf_op jit(solution)/shard_map/last/pallas_call | solution.py:261
  (6 shorter events, 0.1 us)
Async XLA Ops:
  1.6 7.7 %collective-permute-start = (bf16[288,256]{1,0:T(8,128)(2,1)S(1)}, bf16[288,256]{1,0:T(8,128)(2,1)S(1)}, u32[]{:S(2)}, u32[]{:S(2)}) collective-permute-start(bf16[288,256]{1,0:T(8,128)(2,1)S(1)} %get-tuple-element.15.refs_0_), channel_id=1, source_target_pairs={{0,1},{1,0},{2,3},{3,2},{4,5},{5,4},{6,7},{7,6},{8,9},{9,8},{10,11... | collective-permute-start | bytes 442376 | tf_op jit(solution)/shard_map/ppermute | solution.py:328
  4.6 18.9 %collective-permute-start.5 = (bf16[9,128,256]{2,1,0:T(8,128)(2,1)S(1)}, bf16[9,128,256]{2,1,0:T(8,128)(2,1)S(1)}, u32[]{:S(2)}, u32[]{:S(2)}) collective-permute-start(bf16[9,128,256]{2,1,0:T(8,128)(2,1)S(1)} %get-tuple-element.21.refs_1_), channel_id=1, source_target_pairs={{0,1},{1,0},{2,3},{3,2},{4,5},{5,4},{6,7},{7,6},{8,9},{9,8},{10,11... | collective-permute-start | bytes 1769480 | tf_op jit(solution)/shard_map/ppermute | solution.py:329
  6.4 21.0 %collective-permute-start.4 = (bf16[4,128,256]{2,1,0:T(8,128)(2,1)S(1)}, bf16[4,128,256]{2,1,0:T(8,128)(2,1)S(1)}, u32[]{:S(2)}, u32[]{:S(2)}) collective-permute-start(bf16[4,128,256]{2,1,0:T(8,128)(2,1)S(1)} %pick.3), channel_id=1, source_target_pairs={{0,1},{1,0},{2,3},{3,2},{4,5},{5,4},{6,7},{7,6},{8,9},{9,8},{10,11... | collective-permute-start | bytes 786440 | tf_op jit(solution)/shard_map/ppermute | solution.py:341
  8.5 6.6 %copy-start = (f32[512]{0:T(512)S(1)}, f32[512]{0:T(512)}, u32[]{:S(2)}) copy-start(f32[512]{0:T(512)} %param.5) | copy-start | bytes 6148
  9.3 8.6 %collective-permute-start.1 = (bf16[2,128,256]{2,1,0:T(8,128)(2,1)S(1)}, bf16[2,128,256]{2,1,0:T(8,128)(2,1)S(1)}, u32[]{:S(2)}, u32[]{:S(2)}) collective-permute-start(bf16[2,128,256]{2,1,0:T(8,128)(2,1)S(1)} %get-tuple-element.16), channel_id=1, source_target_pairs={{8,16},{16,8},{9,17},{17,9},{10,18},{18,10},{11,19},{19,11},{12,20... | collective-permute-start | bytes 393224 | tf_op jit(solution)/shard_map/ppermute | solution.py:345
  10.0 8.0 %collective-permute-start.2 = (bf16[2,128,256]{2,1,0:T(8,128)(2,1)S(1)}, bf16[2,128,256]{2,1,0:T(8,128)(2,1)S(1)}, u32[]{:S(2)}, u32[]{:S(2)}) collective-permute-start(bf16[2,128,256]{2,1,0:T(8,128)(2,1)S(1)} %get-tuple-element.17), channel_id=1, source_target_pairs={{0,8},{8,0},{16,24},{24,16},{1,9},{9,1},{17,25},{25,17},{2,10},{10... | collective-permute-start | bytes 393224 | tf_op jit(solution)/shard_map/ppermute | solution.py:345
  18.0 7.1 %collective-permute-start.6 = (bf16[2,18,256]{2,1,0:T(8,128)(2,1)S(1)}, bf16[2,18,256]{2,1,0:T(8,128)(2,1)S(1)}, u32[]{:S(2)}, u32[]{:S(2)}) collective-permute-start(bf16[2,18,256]{2,1,0:T(8,128)(2,1)S(1)} %get-tuple-element.18.after_ref.refs_4_), channel_id=1, source_target_pairs={{2,4},{4,2},{3,5},{5,3},{10,12},{12,10},{11,13},{13,11},{18,20},{2... | collective-permute-start | bytes 55304 | tf_op jit(solution)/shard_map/ppermute | solution.py:354
  18.7 6.4 %collective-permute-start.7 = (bf16[2,18,256]{2,1,0:T(8,128)(2,1)S(1)}, bf16[2,18,256]{2,1,0:T(8,128)(2,1)S(1)}, u32[]{:S(2)}, u32[]{:S(2)}) collective-permute-start(bf16[2,18,256]{2,1,0:T(8,128)(2,1)S(1)} %get-tuple-element.22.refs_5_), channel_id=1, source_target_pairs={{0,2},{2,0},{4,6},{6,4},{1,3},{3,1},{5,7},{7,5},{8,10},{10,8},{12,... | collective-permute-start | bytes 55304 | tf_op jit(solution)/shard_map/ppermute | solution.py:354
  21.6 6.7 %collective-permute-start.3 = (bf16[1,128,256]{2,1,0:T(8,128)(2,1)S(1)}, bf16[1,128,256]{2,1,0:T(8,128)(2,1)S(1)}, u32[]{:S(2)}, u32[]{:S(2)}) collective-permute-start(bf16[1,128,256]{2,1,0:T(8,128)(2,1)S(1)} %pick.2), channel_id=1, source_target_pairs={{0,1},{1,0},{2,3},{3,2},{4,5},{5,4},{6,7},{7,6},{8,9},{9,8},{10,11... | collective-permute-start | bytes 196616 | tf_op jit(solution)/shard_map/ppermute | solution.py:353

commit v11 on v10

--- a/solution.py
+++ b/solution.py
@@ -15,17 +15,39 @@
 BLOCK = 4
 
 
-def relayout_kernel(chunks, x_hbm, rim_ref, *refs):
-    outs, (x_ref, col_ref, sems) = refs[:-3], refs[-3:]
-    slab, rows, width = x_ref.shape
-    parts = 2 if slab % 256 == 0 else 1
-    step = slab // parts
-    copies = [pltpu.make_async_copy(x_hbm.at[q * step : (q + 1) * step], x_ref.at[q * step : (q + 1) * step], sems.at[q]) for q in range(parts)]
+def early_kernel(x_hbm, out_ref, x_ref, sems):
+    slab = x_ref.shape[0]
+    step = slab // 2 if slab % 256 == 0 else slab
+    parts = [slice(at, at + step) for at in range(0, slab, step)]
+    copies = [pltpu.make_async_copy(x_hbm.at[part, 0:8, :], x_ref.at[part], sems.at[i]) for i, part in enumerate(parts)]
     for copy in copies:
         copy.start()
-    for q, copy in enumerate(copies):
+    for copy, part in zip(copies, parts):
         copy.wait()
-        lanes = slice(q * step, (q + 1) * step)
+        group = jnp.swapaxes(x_ref[part], 0, 1)
+        for h in range(out_ref.shape[0]):
+            out_ref[h, :, part] = group[h + 1].T
+
+
+def early(features, count):
+    slab, _, width = features.shape
+    return pl.pallas_call(
+        early_kernel,
+        out_shape=jax.ShapeDtypeStruct((count, width, slab), BF16),
+        in_specs=[HBM],
+        out_specs=VMEM,
+        scratch_shapes=[pltpu.VMEM((slab, 8, width), BF16), pltpu.SemaphoreType.DMA((2,))],
+        compiler_params=PARAMS,
+        cost_estimate=WAIT,
+        name="early",
+    )(pltpu.with_memory_space_constraint(features, pltpu.HBM))
+
+
+def relayout_kernel(chunks, x_ref, rim_ref, *refs):
+    outs, col_ref = refs[:-1], refs[-1]
+    slab, rows, width = x_ref.shape
+    step = slab // 2 if slab % 256 == 0 else slab
+    for lanes in [slice(at, at + step) for at in range(0, slab, step)]:
         group = jnp.swapaxes(x_ref[lanes], 0, 1)
         for h in range(rows):
             pixels = group[h].T
@@ -45,15 +67,7 @@
 def relayout(features, chunks):
     slab, rows, width = features.shape
     shapes = [(2 * width + 2 * rows, slab)] + [(last - first, width, slab) for first, last in chunks]
-    return pl.pallas_call(
-        functools.partial(relayout_kernel, chunks),
-        out_shape=[jax.ShapeDtypeStruct(s, BF16) for s in shapes],
-        in_specs=[HBM],
-        out_specs=[VMEM] * len(shapes),
-        scratch_shapes=[pltpu.VMEM(features.shape, BF16), pltpu.VMEM((2 * rows, slab), F32), pltpu.SemaphoreType.DMA((2,))],
-        compiler_params=PARAMS,
-        name="relayout",
-    )(pltpu.with_memory_space_constraint(features, pltpu.HBM))
+    return calls(functools.partial(relayout_kernel, chunks), "relayout", shapes, [features], [pltpu.VMEM((2 * rows, slab), F32)])
 
 
 def put_row(x_ref, at, value):
@@ -283,7 +297,7 @@
     )(*operands)
 
 
-def weights_kernel(groups, kernel_ref, *refs):
+def weights_kernel(groups, kernel_ref, after_ref, *refs):
     outs, sems = refs[:-1], refs[-1]
     slab, width = outs[0].shape[2:]
     owner = lax.axis_index("filt")
@@ -299,17 +313,18 @@
         copy.wait()
 
 
-def split_weights(kernel, groups, slab, outs):
+def split_weights(kernel, groups, slab, outs, after):
     if outs % 128 == 0 and slab % 128 == 0:
         return pl.pallas_call(
             functools.partial(weights_kernel, groups),
             out_shape=[jax.ShapeDtypeStruct((3, 3, slab, outs), BF16)] * groups,
-            in_specs=[HBM],
+            in_specs=[HBM, VMEM],
             out_specs=[VMEM] * groups,
             scratch_shapes=[pltpu.SemaphoreType.DMA((groups, 3))],
             compiler_params=pltpu.CompilerParams(vmem_limit_bytes=48 << 20),
+            cost_estimate=pl.CostEstimate(flops=2 * 10**9, bytes_accessed=1 << 20, transcendentals=0),
             name="split_weights",
-        )(kernel)
+        )(kernel, after)
     owner = lax.axis_index("filt")
     own = lax.dynamic_slice_in_dim(kernel, owner * outs, outs, 3)
     order = [lax.rem(owner - shift + groups, groups) for shift in range(groups)]
@@ -321,21 +336,23 @@
     slab, height, width = features.shape
     outs = kernel.shape[3] // groups
     half = height // 2
-    chunks = ((1, half + 2), (half + 2, height - 2), (height - 2, height - 1))
-
+    chunks = ((3, half + 2), (half + 2, height - 2), (height - 2, height - 1))
+
+    rings = [[(i, (i + shift) % groups) for i in range(groups)] for shift in range(1, groups)]
+    soon = early(features, chunks[0][0] - 1)
+    soons = [lax.ppermute(soon, "filt", ring) for ring in rings]
     rim, upper_rows, lower_rows = relayout(features, (chunks[0], (chunks[0][1], height - 1)))
-    rings = [[(i, (i + shift) % groups) for i in range(groups)] for shift in range(1, groups)]
     rims = [rim] + [lax.ppermute(rim, "filt", ring) for ring in rings]
     sets = [[lax.ppermute(upper_rows, "filt", ring)] for ring in rings]
     pairs = [r[0 : 2 * width].reshape(2, width, slab) for r in rims]
     outer = [(0, 0, 0, 1), (0, 1, height - 1, 1)]
     shape = (height, width, outs)
 
-    weights = split_weights(kernel, groups, slab, outs)
+    weights = split_weights(kernel, groups, slab, outs, soons[0])
     bias = bias[None, :]
     if outs % 128 != 0:
         bias = lax.dynamic_slice_in_dim(bias, lax.axis_index("filt") * outs, outs, 1)
-    spans = [*outer, (1, 0, 1, half + 1), (2, 0, half + 2, height - half - 3)]
+    spans = [*outer, (1, 0, 1, soon.shape[0]), (2, 0, chunks[0][0], upper_rows.shape[0]), (3, 0, chunks[0][1], lower_rows.shape[0])]
     second = pick(lower_rows, 0, chunks[1][1] - chunks[1][0], weights[0])
     for received, ring in zip(sets, rings):
         received.append(lax.ppermute(second, "filt", ring))
@@ -343,7 +360,7 @@
     row_pairs, col_pairs = swap_pairs("row"), swap_pairs("col")
     sent = calls(functools.partial(outermost_kernel, groups), "outermost", [(groups, width, slab)] * 2, rims, estimate=WAIT)
     outer_rows = [lax.ppermute(v, "row", p) for v, p in zip(sent, row_pairs)]
-    total = accumulate(spans, [pairs[0], upper_rows, lower_rows], weights[0], None, shape, rims[-1], bias)
+    total = accumulate(spans, [pairs[0], soon, upper_rows, lower_rows], weights[0], None, shape, rims[-1], bias)
     for g in range(1, groups):
         total = accumulate(outer, [pairs[g]], weights[g], total, shape)
     edge = pltpu.VMEM((2, height + 2, slab), F32)
@@ -358,7 +375,8 @@
     )
     for g in range(1, groups):
         a, b, c = sets[g - 1]
-        total = accumulate([(0, 0, chunks[0][0], a.shape[0])], [a], weights[g], total, shape, rows_fix)
+        spans = [(0, 0, 1, soon.shape[0]), (1, 0, chunks[0][0], a.shape[0])]
+        total = accumulate(spans, [soons[g - 1], a], weights[g], total, shape, rows_fix)
         if g < groups - 1:
             total = accumulate([(0, 0, chunks[1][0], b.shape[0])], [b], weights[g], total, shape)
             total = accumulate([(0, 0, chunks[2][0], c.shape[0])], [c], weights[g], total, shape)

time: 29.9 us -> 30.6 us (1.023)
  starting transfers between devices: 15.9 us -> 17.4 us
  waiting for transfers between devices: 2.55 us -> 1.7 us
    ppermute x0 -> x1, starting transfers between devices: none -> 3.03 us  [body(): soons = [lax.ppermute(soon, 'filt', ring) for ring in rings]]
    ppermute x1, starting transfers between devices: 3.03 us -> 0.12 us  [body(): rims = [rim] + [lax.ppermute(rim, 'filt', ring) for ring in rings]]
    ppermute x1, starting transfers between devices: 0.08 us -> 1.96 us  [body(): sets = [[lax.ppermute(upper_rows, 'filt', ring)] for ring in rings]]
    ppermute x1, waiting for transfers between devices: 1.69 us -> 0.01 us  [body(): received.append(lax.ppermute(second, 'filt', ring))]
    ppermute x0 -> x1, waiting for transfers between devices: none -> 1.68 us  [body(): soons = [lax.ppermute(soon, 'filt', ring) for ring in rings]]
    ppermute x1, waiting for transfers between devices: 0.84 us -> 0.01 us  [body(): rims = [rim] + [lax.ppermute(rim, 'filt', ring) for ring in rings]]
    ppermute x2, starting transfers between devices: 5.67 us -> 5.13 us  [body(): outer_rows = [lax.ppermute(v, 'row', p) for v, p in zip(sent, row_pairs)]]
    pallas_call x2 -> x3, Pallas kernels: 0.06 us -> 0.54 us  [calls(): pl.pallas_call(kernel, out_shape=[jax.ShapeDtypeStruct(shape, BF16) for s...]
  transfers between devices with their start and end apart: 8 -> 9, of which waited for: 2 -> 1; matrix products, arithmetic and copies ran while one was open for 0% -> 0% of each run, Pallas kernels for 27% -> 28%
where the time goes in v11:
time: 30.6 us; the launch traced here: 30.4 us
  starting transfers between devices  17.4 us (57%)
  Pallas kernels  11.2 us (37%)
  waiting for transfers between devices  1.7 us (6%)
    pallas_call x4, Pallas kernels, accumulate(): pl.pallas_call(functools.partial(accumulate_kernel, spans, len(pieces), t...  5.27 us
    ppermute x2, starting transfers between devices, body(): outer_rows = [lax.ppermute(v, 'row', p) for v, p in zip(sent, row_pairs)]  5.13 us
    ppermute x2, starting transfers between devices, body(): outer_cols = [lax.ppermute(v, 'col', p) for v, p in zip(sent, col_pairs)]  3.58 us
    ppermute x1, starting transfers between devices, body(): soons = [lax.ppermute(soon, 'filt', ring) for ring in rings]  3.03 us
    pallas_call x7, Pallas kernels, call(): pl.pallas_call(kernel, out_shape=jax.ShapeDtypeStruct(shape, dtype), in_s...  2.42 us
    ppermute x1, starting transfers between devices, body(): received.append(lax.ppermute(second, 'filt', ring))  2.18 us
    ppermute x1, starting transfers between devices, body(): sets = [[lax.ppermute(upper_rows, 'filt', ring)] for ring in rings]  1.96 us
    pallas_call x1, Pallas kernels, split_weights(): pl.pallas_call(functools.partial(weights_kernel, groups), out_shape=[jax....  1.68 us
  transfers between devices with their start and end apart: 9, of which 1 were waited for; matrix products, arithmetic and copies ran while one was open for 0% of the time, Pallas kernels for 28%

profile of v11, /device:TPU:0, one launch (start us, length us, event | category | flops | bytes accessed | tf_op | source)
XLA Modules:
  0.0 30.4 jit_solution(14077953768776292251)
XLA Ops:
  0.0 0.0 copy-start
  0.0 1.2 %early.1.refs_1_ = bf16[2,128,256]{2,1,0:T(8,128)(2,1)S(1)} custom-call(bf16[256,16,128]{2,1,0:T(8,128)(2,1)} %x_hbm.1), custom_call_target="tpu_custom_call" | custom-call | flops 4000000000 | bytes 1048576 | tf_op jit(solution)/shard_map/early/pallas_call | solution.py:34
  1.3 3.0 %collective-permute-start.4 = (bf16[2,128,256]{2,1,0:T(8,128)(2,1)S(1)}, bf16[2,128,256]{2,1,0:T(8,128)(2,1)S(1)}, u32[]{:S(2)}, u32[]{:S(2)}) collective-permute-start(bf16[2,128,256]{2,1,0:T(8,128)(2,1)S(1)} %early.1.refs_1_), channel_id=1, source_target_pairs={{0,1},{1,0},{2,3},{3,2},{4,5},{5,4},{6,7},{7,6},{8,9},{9,8},{10,11... | collective-permute-start | bytes 393224 | tf_op jit(solution)/shard_map/ppermute | solution.py:343
  4.3 0.0 copy-done
  4.3 0.5 %relayout.1 = (bf16[288,256]{1,0:T(8,128)(2,1)S(1)}, bf16[7,128,256]{2,1,0:T(8,128)(2,1)S(1)}, bf16[5,128,256]{2,1,0:T(8,128)(2,1)S(1)}) custom-call(bf16[256,16,128]{2,1,0:T(8,128)(2,1)S(1)} %copy-done), custom_call_target="tpu_custom_call" | custom-call | flops 2 | bytes 1048576 | tf_op jit(solution)/shard_map/relayout/pallas_call | solution.py:288
  4.8 0.1 collective-permute-start
  4.9 2.0 %collective-permute-start.6 = (bf16[7,128,256]{2,1,0:T(8,128)(2,1)S(1)}, bf16[7,128,256]{2,1,0:T(8,128)(2,1)S(1)}, u32[]{:S(2)}, u32[]{:S(2)}) collective-permute-start(bf16[7,128,256]{2,1,0:T(8,128)(2,1)S(1)} %get-tuple-element.21.refs_2_), channel_id=1, source_target_pairs={{0,1},{1,0},{2,3},{3,2},{4,5},{5,4},{6,7},{7,6},{8,9},{9,8},{10,11... | collective-permute-start | bytes 1376264 | tf_op jit(solution)/shard_map/ppermute | solution.py:346
  6.9 1.7 %collective-permute-done.4.after_ref.refs_0_ = bf16[2,128,256]{2,1,0:T(8,128)(2,1)S(1)} collective-permute-done((bf16[2,128,256]{2,1,0:T(8,128)(2,1)S(1)}, bf16[2,128,256]{2,1,0:T(8,128)(2,1)S(1)}, u32[]{:S(2)}, u32[]{:S(2)}) %collective-permute-start.4) | collective-permute-done | bytes 131104 | tf_op jit(solution)/shard_map/ppermute | solution.py:343
  8.6 1.7 %split_weights.1 = (bf16[3,3,256,256]{3,2,1,0:T(8,128)(2,1)S(1)}, bf16[3,3,256,256]{3,2,1,0:T(8,128)(2,1)S(1)}) custom-call(bf16[3,3,512,512]{3,2,1,0:T(8,128)(2,1)} %kernel_ref.1, bf16[2,128,256]{2,1,0:T(8,128)(2,1)S(1)} %collective-permute-done.4.after_ref.refs_0_), custom_call_target="tpu_custom_call" | custom-call | flops 2000000000 | bytes 1048576 | tf_op jit(solution)/shard_map/split_weights/pallas_call | solution.py:318
  10.3 0.0 copy-start.1
  10.3 2.2 %collective-permute-start.5 = (bf16[4,128,256]{2,1,0:T(8,128)(2,1)S(1)}, bf16[4,128,256]{2,1,0:T(8,128)(2,1)S(1)}, u32[]{:S(2)}, u32[]{:S(2)}) collective-permute-start(bf16[4,128,256]{2,1,0:T(8,128)(2,1)S(1)} %pick.3), channel_id=1, source_target_pairs={{0,1},{1,0},{2,3},{3,2},{4,5},{5,4},{6,7},{7,6},{8,9},{9,8},{10,11... | collective-permute-start | bytes 786440 | tf_op jit(solution)/shard_map/ppermute | solution.py:358
  12.5 0.0 collective-permute-done.refs_1_.refs_6_
  12.5 0.7 %collective-permute-start.1 = (bf16[2,128,256]{2,1,0:T(8,128)(2,1)S(1)}, bf16[2,128,256]{2,1,0:T(8,128)(2,1)S(1)}, u32[]{:S(2)}, u32[]{:S(2)}) collective-permute-start(bf16[2,128,256]{2,1,0:T(8,128)(2,1)S(1)} %get-tuple-element.16), channel_id=1, source_target_pairs={{8,16},{16,8},{9,17},{17,9},{10,18},{18,10},{11,19},{19,11},{12,20... | collective-permute-start | bytes 393224 | tf_op jit(solution)/shard_map/ppermute | solution.py:362
  13.2 4.5 %collective-permute-start.2 = (bf16[2,128,256]{2,1,0:T(8,128)(2,1)S(1)}, bf16[2,128,256]{2,1,0:T(8,128)(2,1)S(1)}, u32[]{:S(2)}, u32[]{:S(2)}) collective-permute-start(bf16[2,128,256]{2,1,0:T(8,128)(2,1)S(1)} %get-tuple-element.17), channel_id=1, source_target_pairs={{0,8},{8,0},{16,24},{24,16},{1,9},{9,1},{17,25},{25,17},{2,10},{10... | collective-permute-start | bytes 393224 | tf_op jit(solution)/shard_map/ppermute | solution.py:362
  17.6 0.0 copy-done.1
  17.6 2.5 %accumulate.4.refs_2_ = f32[16,128,256]{2,1,0:T(8,128)S(1)} custom-call(bf16[2,128,256]{2,1,0:T(8,128)(2,1)S(1)} %bitcast.4, bf16[2,128,256]{2,1,0:T(8,128)(2,1)S(1)} %early.1.refs_1_, bf16[7,128,256]{2,1,0:T(8,128)(2,1)S(1)} %get-tuple-element.21.refs_2_, bf16[5,128,256]{2,1,0:T(8,128)(2,1)S(1)} %get-tuple-element.14.rows_ref.refs_3_, ...), custom_call_target="tpu_custom_call" | custom-call | flops 2415919104 | bytes 1048576 | tf_op jit(solution)/shard_map/accumulate/pallas_call | solution.py:141
  20.2 0.4 %accumulate.5.refs_3_ = f32[16,128,256]{2,1,0:T(8,128)S(1)} custom-call(bf16[2,128,256]{2,1,0:T(8,128)(2,1)S(1)} %bitcast.3, bf16[3,3,256,256]{3,2,1,0:T(8,128)(2,1)S(1)} %get-tuple-element.19.refs_1_.refs_3_.refs_2_.w_ref, f32[16,128,256]{2,1,0:T(8,128)S(1)} %accumulate.4.refs_2_), custom_call_target="tpu_custom_call", output_to_operand_aliasing={{}: (2, {})} | custom-call | flops 301989888 | bytes 1048576 | tf_op jit(solution)/shard_map/accumulate/pallas_call | solution.py:141
  20.6 0.0 collective-permute-done.1.refs_2_.refs_0_
  20.6 0.0 collective-permute-done.2.refs_3_.refs_1_
  20.6 0.7 %collective-permute-start.7 = (bf16[2,18,256]{2,1,0:T(8,128)(2,1)S(1)}, bf16[2,18,256]{2,1,0:T(8,128)(2,1)S(1)}, u32[]{:S(2)}, u32[]{:S(2)}) collective-permute-start(bf16[2,18,256]{2,1,0:T(8,128)(2,1)S(1)} %get-tuple-element.18.after_ref.refs_4_), channel_id=1, source_target_pairs={{2,4},{4,2},{3,5},{5,3},{10,12},{12,10},{11,13},{13,11},{18,20},{2... | collective-permute-start | bytes 55304 | tf_op jit(solution)/shard_map/ppermute | solution.py:371
  21.3 2.9 %collective-permute-start.8 = (bf16[2,18,256]{2,1,0:T(8,128)(2,1)S(1)}, bf16[2,18,256]{2,1,0:T(8,128)(2,1)S(1)}, u32[]{:S(2)}, u32[]{:S(2)}) collective-permute-start(bf16[2,18,256]{2,1,0:T(8,128)(2,1)S(1)} %get-tuple-element.22.refs_5_), channel_id=1, source_target_pairs={{0,2},{2,0},{4,6},{6,4},{1,3},{3,1},{5,7},{7,5},{8,10},{10,8},{12,... | collective-permute-start | bytes 55304 | tf_op jit(solution)/shard_map/ppermute | solution.py:371
  24.3 1.4 %collective-permute-start.3 = (bf16[1,128,256]{2,1,0:T(8,128)(2,1)S(1)}, bf16[1,128,256]{2,1,0:T(8,128)(2,1)S(1)}, u32[]{:S(2)}, u32[]{:S(2)}) collective-permute-start(bf16[1,128,256]{2,1,0:T(8,128)(2,1)S(1)} %pick.2), channel_id=1, source_target_pairs={{0,1},{1,0},{2,3},{3,2},{4,5},{5,4},{6,7},{7,6},{8,9},{9,8},{10,11... | collective-permute-start | bytes 196616 | tf_op jit(solution)/shard_map/ppermute | solution.py:370
  25.6 0.4 %outer_rows.1.refs_4_.rows_ref = f32[2,128,256]{2,1,0:T(8,128)S(1)} custom-call(bf16[2,128,256]{2,1,0:T(8,128)(2,1)S(1)} %collective-permute-done.1.refs_2_.refs_0_, bf16[2,128,256]{2,1,0:T(8,128)(2,1)S(1)} %collective-permute-done.2.refs_3_.refs_1_, bf16[3,3,256,256]{3,2,1,0:T(8,128)(2,1)S(1)} %get-tuple-element.20.after_ref.refs_4_.refs_2_, ...), custom_call_target="tpu_custom_call" | custom-call | flops 201326592 | bytes 1048576 | tf_op jit(solution)/shard_map/outer_rows/pallas_call | solution.py:275
  26.0 0.0 collective-permute-done.6.refs_1_
  26.0 1.6 %accumulate.6.refs_4_.total_ref.refs_2_ = f32[16,128,256]{2,1,0:T(8,128)S(1)} custom-call(bf16[2,128,256]{2,1,0:T(8,128)(2,1)S(1)} %collective-permute-done.4.after_ref.refs_0_, bf16[7,128,256]{2,1,0:T(8,128)(2,1)S(1)} %collective-permute-done.6.refs_1_, ...), custom_call_target="tpu_custom_call", output_to_operand_aliasing={{}: (3, {})} | custom-call | flops 1358954496 | bytes 1048576 | tf_op jit(solution)/shard_map/accumulate/pallas_call | solution.py:141
  27.6 0.0 collective-permute-done.8.refs_1_
  27.6 0.0 collective-permute-done.7.refs_0_
  27.6 0.4 %outer_cols.1.cols_ref = f32[2,16,256]{2,1,0:T(8,128)S(1)} custom-call(bf16[2,18,256]{2,1,0:T(8,128)(2,1)S(1)} %collective-permute-done.7.refs_0_, bf16[2,18,256]{2,1,0:T(8,128)(2,1)S(1)} %collective-permute-done.8.refs_1_, bf16[3,3,256,256]{3,2,1,0:T(8,128)(2,1)S(1)} %get-tuple-element.20.after_ref.refs_4_.refs_2_, ...), custom_call_target="tpu_custom_call" | custom-call | flops 402653184 | bytes 1048576 | tf_op jit(solution)/shard_map/outer_cols/pallas_call | solution.py:275
  28.0 0.2 upper.1.refs_3_.upper_ref
  28.2 0.0 collective-permute-done.5.refs_0_
  28.2 0.8 %accumulate.7.total_ref = f32[16,128,256]{2,1,0:T(8,128)S(1)} custom-call(bf16[4,128,256]{2,1,0:T(8,128)(2,1)S(1)} %collective-permute-done.5.refs_0_, bf16[3,3,256,256]{3,2,1,0:T(8,128)(2,1)S(1)} %get-tuple-element.19.refs_1_.refs_3_.refs_2_.w_ref, f32[16,128,256]{2,1,0:T(8,128)S(1)} %accumulate.6.refs_4_.total_ref.refs_2_, ...), custom_call_target="tpu_custom_call", output_to_operand_aliasing={{}: (2, {})} | custom-call | flops 603979776 | bytes 1048576 | tf_op jit(solution)/shard_map/accumulate/pallas_call | solution.py:141
  29.0 0.1 middle.1.middle_ref
  29.1 0.0 collective-permute-done.3.piece
  29.1 1.3 %last.1 = bf16[256,16,128]{2,1,0:T(8,128)(2,1)} custom-call(bf16[1,128,256]{2,1,0:T(8,128)(2,1)S(1)} %collective-permute-done.3.piece, bf16[3,3,256,256]{3,2,1,0:T(8,128)(2,1)S(1)} %get-tuple-element.19.refs_1_.refs_3_.refs_2_.w_ref, f32[16,128,256]{2,1,0:T(8,128)S(1)} %accumulate.7.total_ref, f32[2,128,256]{2,1,0:T(8,128)S(1)} %outer_rows.1.refs_4_.rows_ref, ...), custom_call_target="tpu_custom_call" | custom-call | flops 301989888 | bytes 1048576 | tf_op jit(solution)/shard_map/last/pallas_call | solution.py:275
  (6 shorter events, 0.1 us)
Async XLA Ops:
  0.0 4.3 %copy-start = (bf16[256,16,128]{2,1,0:T(8,128)(2,1)S(1)}, bf16[256,16,128]{2,1,0:T(8,128)(2,1)}, u32[]{:S(2)}) copy-start(bf16[256,16,128]{2,1,0:T(8,128)(2,1)} %x_hbm.1) | copy-start | bytes 3145732
  1.3 7.3 %collective-permute-start.4 = (bf16[2,128,256]{2,1,0:T(8,128)(2,1)S(1)}, bf16[2,128,256]{2,1,0:T(8,128)(2,1)S(1)}, u32[]{:S(2)}, u32[]{:S(2)}) collective-permute-start(bf16[2,128,256]{2,1,0:T(8,128)(2,1)S(1)} %early.1.refs_1_), channel_id=1, source_target_pairs={{0,1},{1,0},{2,3},{3,2},{4,5},{5,4},{6,7},{7,6},{8,9},{9,8},{10,11... | collective-permute-start | bytes 393224 | tf_op jit(solution)/shard_map/ppermute | solution.py:343
  4.8 7.7 %collective-permute-start = (bf16[288,256]{1,0:T(8,128)(2,1)S(1)}, bf16[288,256]{1,0:T(8,128)(2,1)S(1)}, u32[]{:S(2)}, u32[]{:S(2)}) collective-permute-start(bf16[288,256]{1,0:T(8,128)(2,1)S(1)} %get-tuple-element.15.refs_0_), channel_id=1, source_target_pairs={{0,1},{1,0},{2,3},{3,2},{4,5},{5,4},{6,7},{7,6},{8,9},{9,8},{10,11... | collective-permute-start | bytes 442376 | tf_op jit(solution)/shard_map/ppermute | solution.py:345
  4.9 21.1 %collective-permute-start.6 = (bf16[7,128,256]{2,1,0:T(8,128)(2,1)S(1)}, bf16[7,128,256]{2,1,0:T(8,128)(2,1)S(1)}, u32[]{:S(2)}, u32[]{:S(2)}) collective-permute-start(bf16[7,128,256]{2,1,0:T(8,128)(2,1)S(1)} %get-tuple-element.21.refs_2_), channel_id=1, source_target_pairs={{0,1},{1,0},{2,3},{3,2},{4,5},{5,4},{6,7},{7,6},{8,9},{9,8},{10,11... | collective-permute-start | bytes 1376264 | tf_op jit(solution)/shard_map/ppermute | solution.py:346
  10.3 7.4 %copy-start.1 = (f32[512]{0:T(512)S(1)}, f32[512]{0:T(512)}, u32[]{:S(2)}) copy-start(f32[512]{0:T(512)} %param.5) | copy-start | bytes 6148
  10.3 17.9 %collective-permute-start.5 = (bf16[4,128,256]{2,1,0:T(8,128)(2,1)S(1)}, bf16[4,128,256]{2,1,0:T(8,128)(2,1)S(1)}, u32[]{:S(2)}, u32[]{:S(2)}) collective-permute-start(bf16[4,128,256]{2,1,0:T(8,128)(2,1)S(1)} %pick.3), channel_id=1, source_target_pairs={{0,1},{1,0},{2,3},{3,2},{4,5},{5,4},{6,7},{7,6},{8,9},{9,8},{10,11... | collective-permute-start | bytes 786440 | tf_op jit(solution)/shard_map/ppermute | solution.py:358
  12.5 8.1 %collective-permute-start.1 = (bf16[2,128,256]{2,1,0:T(8,128)(2,1)S(1)}, bf16[2,128,256]{2,1,0:T(8,128)(2,1)S(1)}, u32[]{:S(2)}, u32[]{:S(2)}) collective-permute-start(bf16[2,128,256]{2,1,0:T(8,128)(2,1)S(1)} %get-tuple-element.16), channel_id=1, source_target_pairs={{8,16},{16,8},{9,17},{17,9},{10,18},{18,10},{11,19},{19,11},{12,20... | collective-permute-start | bytes 393224 | tf_op jit(solution)/shard_map/ppermute | solution.py:362
  13.2 7.4 %collective-permute-start.2 = (bf16[2,128,256]{2,1,0:T(8,128)(2,1)S(1)}, bf16[2,128,256]{2,1,0:T(8,128)(2,1)S(1)}, u32[]{:S(2)}, u32[]{:S(2)}) collective-permute-start(bf16[2,128,256]{2,1,0:T(8,128)(2,1)S(1)} %get-tuple-element.17), channel_id=1, source_target_pairs={{0,8},{8,0},{16,24},{24,16},{1,9},{9,1},{17,25},{25,17},{2,10},{10... | collective-permute-start | bytes 393224 | tf_op jit(solution)/shard_map/ppermute | solution.py:362
  20.6 6.9 %collective-permute-start.7 = (bf16[2,18,256]{2,1,0:T(8,128)(2,1)S(1)}, bf16[2,18,256]{2,1,0:T(8,128)(2,1)S(1)}, u32[]{:S(2)}, u32[]{:S(2)}) collective-permute-start(bf16[2,18,256]{2,1,0:T(8,128)(2,1)S(1)} %get-tuple-element.18.after_ref.refs_4_), channel_id=1, source_target_pairs={{2,4},{4,2},{3,5},{5,3},{10,12},{12,10},{11,13},{13,11},{18,20},{2... | collective-permute-start | bytes 55304 | tf_op jit(solution)/shard_map/ppermute | solution.py:371
  21.3 6.2 %collective-permute-start.8 = (bf16[2,18,256]{2,1,0:T(8,128)(2,1)S(1)}, bf16[2,18,256]{2,1,0:T(8,128)(2,1)S(1)}, u32[]{:S(2)}, u32[]{:S(2)}) collective-permute-start(bf16[2,18,256]{2,1,0:T(8,128)(2,1)S(1)} %get-tuple-element.22.refs_5_), channel_id=1, source_target_pairs={{0,2},{2,0},{4,6},{6,4},{1,3},{3,1},{5,7},{7,5},{8,10},{10,8},{12,... | collective-permute-start | bytes 55304 | tf_op jit(solution)/shard_map/ppermute | solution.py:371
  24.3 4.9 %collective-permute-start.3 = (bf16[1,128,256]{2,1,0:T(8,128)(2,1)S(1)}, bf16[1,128,256]{2,1,0:T(8,128)(2,1)S(1)}, u32[]{:S(2)}, u32[]{:S(2)}) collective-permute-start(bf16[1,128,256]{2,1,0:T(8,128)(2,1)S(1)} %pick.2), channel_id=1, source_target_pairs={{0,1},{1,0},{2,3},{3,2},{4,5},{5,4},{6,7},{7,6},{8,9},{9,8},{10,11... | collective-permute-start | bytes 196616 | tf_op jit(solution)/shard_map/ppermute | solution.py:370

commit v12 on v11

--- a/solution.py
+++ b/solution.py
@@ -67,7 +67,7 @@
 def relayout(features, chunks):
     slab, rows, width = features.shape
     shapes = [(2 * width + 2 * rows, slab)] + [(last - first, width, slab) for first, last in chunks]
-    return calls(functools.partial(relayout_kernel, chunks), "relayout", shapes, [features], [pltpu.VMEM((2 * rows, slab), F32)])
+    return calls(functools.partial(relayout_kernel, chunks), "relayout", shapes, [features], [pltpu.VMEM((2 * rows, slab), F32)], pl.CostEstimate(flops=0 * 10**9, bytes_accessed=1 << 20, transcendentals=0))
 
 
 def put_row(x_ref, at, value):
@@ -297,7 +297,7 @@
     )(*operands)
 
 
-def weights_kernel(groups, kernel_ref, after_ref, *refs):
+def weights_kernel(groups, kernel_ref, *refs):
     outs, sems = refs[:-1], refs[-1]
     slab, width = outs[0].shape[2:]
     owner = lax.axis_index("filt")
@@ -313,18 +313,18 @@
         copy.wait()
 
 
-def split_weights(kernel, groups, slab, outs, after):
+def split_weights(kernel, groups, slab, outs):
     if outs % 128 == 0 and slab % 128 == 0:
         return pl.pallas_call(
             functools.partial(weights_kernel, groups),
             out_shape=[jax.ShapeDtypeStruct((3, 3, slab, outs), BF16)] * groups,
-            in_specs=[HBM, VMEM],
+            in_specs=[HBM],
             out_specs=[VMEM] * groups,
             scratch_shapes=[pltpu.SemaphoreType.DMA((groups, 3))],
             compiler_params=pltpu.CompilerParams(vmem_limit_bytes=48 << 20),
-            cost_estimate=pl.CostEstimate(flops=2 * 10**9, bytes_accessed=1 << 20, transcendentals=0),
+            cost_estimate=pl.CostEstimate(flops=3 * 10**9, bytes_accessed=1 << 20, transcendentals=0),
             name="split_weights",
-        )(kernel, after)
+        )(kernel)
     owner = lax.axis_index("filt")
     own = lax.dynamic_slice_in_dim(kernel, owner * outs, outs, 3)
     order = [lax.rem(owner - shift + groups, groups) for shift in range(groups)]
@@ -348,7 +348,7 @@
     outer = [(0, 0, 0, 1), (0, 1, height - 1, 1)]
     shape = (height, width, outs)
 
-    weights = split_weights(kernel, groups, slab, outs, soons[0])
+    weights = split_weights(kernel, groups, slab, outs)
     bias = bias[None, :]
     if outs % 128 != 0:
         bias = lax.dynamic_slice_in_dim(bias, lax.axis_index("filt") * outs, outs, 1)
@@ -358,7 +358,7 @@
         received.append(lax.ppermute(second, "filt", ring))
 
     row_pairs, col_pairs = swap_pairs("row"), swap_pairs("col")
-    sent = calls(functools.partial(outermost_kernel, groups), "outermost", [(groups, width, slab)] * 2, rims, estimate=WAIT)
+    sent = calls(functools.partial(outermost_kernel, groups), "outermost", [(groups, width, slab)] * 2, [*rims, soons[0]], estimate=pl.CostEstimate(flops=4 * 10**9, bytes_accessed=1 << 20, transcendentals=0))
     outer_rows = [lax.ppermute(v, "row", p) for v, p in zip(sent, row_pairs)]
     total = accumulate(spans, [pairs[0], soon, upper_rows, lower_rows], weights[0], None, shape, rims[-1], bias)
     for g in range(1, groups):

time: 30.6 us -> 30.6 us (level)
  starting transfers between devices: 17.4 us -> 16.1 us
  waiting for transfers between devices: 1.7 us -> 2.98 us
    ppermute x1, waiting for transfers between devices: 0.01 us -> 2.96 us  [body(): rims = [rim] + [lax.ppermute(rim, 'filt', ring) for ring in rings]]
    ppermute x1, starting transfers between devices: 2.18 us -> 0.14 us  [body(): received.append(lax.ppermute(second, 'filt', ring))]
    ppermute x1, waiting for transfers between devices: 1.68 us -> 0.01 us  [body(): soons = [lax.ppermute(soon, 'filt', ring) for ring in rings]]
    ppermute x2, starting transfers between devices: 5.13 us -> 5.64 us  [body(): outer_rows = [lax.ppermute(v, 'row', p) for v, p in zip(sent, row_pairs)]]
where the time goes in v12:
time: 30.6 us; the launch traced here: 30.4 us
  starting transfers between devices  16.1 us (53%)
  Pallas kernels  11.2 us (37%)
  waiting for transfers between devices  2.98 us (10%)
    ppermute x2, starting transfers between devices, body(): outer_rows = [lax.ppermute(v, 'row', p) for v, p in zip(sent, row_pairs)]  5.64 us
    pallas_call x4, Pallas kernels, accumulate(): pl.pallas_call(functools.partial(accumulate_kernel, spans, len(pieces), t...  5.27 us
    ppermute x2, starting transfers between devices, body(): outer_cols = [lax.ppermute(v, 'col', p) for v, p in zip(sent, col_pairs)]  3.58 us
    ppermute x1, starting transfers between devices, body(): soons = [lax.ppermute(soon, 'filt', ring) for ring in rings]  3.03 us
    ppermute x1, waiting for transfers between devices, body(): rims = [rim] + [lax.ppermute(rim, 'filt', ring) for ring in rings]  2.96 us
    pallas_call x7, Pallas kernels, call(): pl.pallas_call(kernel, out_shape=jax.ShapeDtypeStruct(shape, dtype), in_s...  2.43 us
    ppermute x1, starting transfers between devices, body(): sets = [[lax.ppermute(upper_rows, 'filt', ring)] for ring in rings]  1.96 us
    pallas_call x1, Pallas kernels, split_weights(): pl.pallas_call(functools.partial(weights_kernel, groups), out_shape=[jax....  1.68 us
  transfers between devices with their start and end apart: 9, of which 1 were waited for; matrix products, arithmetic and copies ran while one was open for 0% of the time, Pallas kernels for 28%

profile of v12, /device:TPU:0, one launch (start us, length us, event | category | flops | bytes accessed | tf_op | source)
XLA Modules:
  0.0 30.4 jit_solution(10050364535661952651)
XLA Ops:
  0.0 0.0 copy-start
  0.0 1.2 %early.1.refs_1_ = bf16[2,128,256]{2,1,0:T(8,128)(2,1)S(1)} custom-call(bf16[256,16,128]{2,1,0:T(8,128)(2,1)} %x_hbm.1), custom_call_target="tpu_custom_call" | custom-call | flops 4000000000 | bytes 1048576 | tf_op jit(solution)/shard_map/early/pallas_call | solution.py:34
  1.3 3.0 %collective-permute-start.1 = (bf16[2,128,256]{2,1,0:T(8,128)(2,1)S(1)}, bf16[2,128,256]{2,1,0:T(8,128)(2,1)S(1)}, u32[]{:S(2)}, u32[]{:S(2)}) collective-permute-start(bf16[2,128,256]{2,1,0:T(8,128)(2,1)S(1)} %early.1.refs_1_), channel_id=1, source_target_pairs={{0,1},{1,0},{2,3},{3,2},{4,5},{5,4},{6,7},{7,6},{8,9},{9,8},{10,11... | collective-permute-start | bytes 393224 | tf_op jit(solution)/shard_map/ppermute | solution.py:343
  4.3 0.0 copy-done
  4.3 0.5 %relayout.1 = (bf16[288,256]{1,0:T(8,128)(2,1)S(1)}, bf16[7,128,256]{2,1,0:T(8,128)(2,1)S(1)}, bf16[5,128,256]{2,1,0:T(8,128)(2,1)S(1)}) custom-call(bf16[256,16,128]{2,1,0:T(8,128)(2,1)S(1)} %copy-done), custom_call_target="tpu_custom_call" | custom-call | bytes 1048576 | tf_op jit(solution)/shard_map/relayout/pallas_call | solution.py:288
  4.8 0.1 collective-permute-start
  4.9 2.0 %collective-permute-start.6 = (bf16[7,128,256]{2,1,0:T(8,128)(2,1)S(1)}, bf16[7,128,256]{2,1,0:T(8,128)(2,1)S(1)}, u32[]{:S(2)}, u32[]{:S(2)}) collective-permute-start(bf16[7,128,256]{2,1,0:T(8,128)(2,1)S(1)} %get-tuple-element.21.refs_2_), channel_id=1, source_target_pairs={{0,1},{1,0},{2,3},{3,2},{4,5},{5,4},{6,7},{7,6},{8,9},{9,8},{10,11... | collective-permute-start | bytes 1376264 | tf_op jit(solution)/shard_map/ppermute | solution.py:346
  6.9 1.7 %split_weights.1 = (bf16[3,3,256,256]{3,2,1,0:T(8,128)(2,1)S(1)}, bf16[3,3,256,256]{3,2,1,0:T(8,128)(2,1)S(1)}) custom-call(bf16[3,3,512,512]{3,2,1,0:T(8,128)(2,1)} %kernel_ref.1), custom_call_target="tpu_custom_call" | custom-call | flops 3000000000 | bytes 1048576 | tf_op jit(solution)/shard_map/split_weights/pallas_call | solution.py:318
  8.6 0.1 collective-permute-start.5
  8.7 0.0 copy-start.1
  8.7 0.0 collective-permute-done.1.refs_2_.refs_0_
  8.8 3.0 %collective-permute-done.refs_1_.refs_6_ = bf16[288,256]{1,0:T(8,128)(2,1)S(1)} collective-permute-done((bf16[288,256]{1,0:T(8,128)(2,1)S(1)}, bf16[288,256]{1,0:T(8,128)(2,1)S(1)}, u32[]{:S(2)}, u32[]{:S(2)}) %collective-permute-start) | collective-permute-done | bytes 147488 | tf_op jit(solution)/shard_map/ppermute | solution.py:345
  11.7 0.7 %collective-permute-start.2 = (bf16[2,128,256]{2,1,0:T(8,128)(2,1)S(1)}, bf16[2,128,256]{2,1,0:T(8,128)(2,1)S(1)}, u32[]{:S(2)}, u32[]{:S(2)}) collective-permute-start(bf16[2,128,256]{2,1,0:T(8,128)(2,1)S(1)} %get-tuple-element.16), channel_id=1, source_target_pairs={{8,16},{16,8},{9,17},{17,9},{10,18},{18,10},{11,19},{19,11},{12,20... | collective-permute-start | bytes 393224 | tf_op jit(solution)/shard_map/ppermute | solution.py:362
  12.4 5.0 %collective-permute-start.3 = (bf16[2,128,256]{2,1,0:T(8,128)(2,1)S(1)}, bf16[2,128,256]{2,1,0:T(8,128)(2,1)S(1)}, u32[]{:S(2)}, u32[]{:S(2)}) collective-permute-start(bf16[2,128,256]{2,1,0:T(8,128)(2,1)S(1)} %get-tuple-element.17), channel_id=1, source_target_pairs={{0,8},{8,0},{16,24},{24,16},{1,9},{9,1},{17,25},{25,17},{2,10},{10... | collective-permute-start | bytes 393224 | tf_op jit(solution)/shard_map/ppermute | solution.py:362
  17.4 0.0 copy-done.1
  17.4 2.5 %accumulate.4.refs_2_ = f32[16,128,256]{2,1,0:T(8,128)S(1)} custom-call(bf16[2,128,256]{2,1,0:T(8,128)(2,1)S(1)} %bitcast.4, bf16[2,128,256]{2,1,0:T(8,128)(2,1)S(1)} %early.1.refs_1_, bf16[7,128,256]{2,1,0:T(8,128)(2,1)S(1)} %get-tuple-element.21.refs_2_, bf16[5,128,256]{2,1,0:T(8,128)(2,1)S(1)} %get-tuple-element.14.rows_ref.refs_3_, ...), custom_call_target="tpu_custom_call" | custom-call | flops 2415919104 | bytes 1048576 | tf_op jit(solution)/shard_map/accumulate/pallas_call | solution.py:141
  20.0 0.4 %accumulate.5.refs_3_ = f32[16,128,256]{2,1,0:T(8,128)S(1)} custom-call(bf16[2,128,256]{2,1,0:T(8,128)(2,1)S(1)} %bitcast.3, bf16[3,3,256,256]{3,2,1,0:T(8,128)(2,1)S(1)} %get-tuple-element.19.refs_1_.refs_3_.refs_2_.w_ref, f32[16,128,256]{2,1,0:T(8,128)S(1)} %accumulate.4.refs_2_), custom_call_target="tpu_custom_call", output_to_operand_aliasing={{}: (2, {})} | custom-call | flops 301989888 | bytes 1048576 | tf_op jit(solution)/shard_map/accumulate/pallas_call | solution.py:141
  20.3 0.0 collective-permute-done.2.refs_2_.refs_0_
  20.4 0.0 collective-permute-done.3.refs_3_.refs_1_
  20.4 0.7 %collective-permute-start.7 = (bf16[2,18,256]{2,1,0:T(8,128)(2,1)S(1)}, bf16[2,18,256]{2,1,0:T(8,128)(2,1)S(1)}, u32[]{:S(2)}, u32[]{:S(2)}) collective-permute-start(bf16[2,18,256]{2,1,0:T(8,128)(2,1)S(1)} %get-tuple-element.18.after_ref.refs_4_), channel_id=1, source_target_pairs={{2,4},{4,2},{3,5},{5,3},{10,12},{12,10},{11,13},{13,11},{18,20},{2... | collective-permute-start | bytes 55304 | tf_op jit(solution)/shard_map/ppermute | solution.py:371
  21.1 2.9 %collective-permute-start.8 = (bf16[2,18,256]{2,1,0:T(8,128)(2,1)S(1)}, bf16[2,18,256]{2,1,0:T(8,128)(2,1)S(1)}, u32[]{:S(2)}, u32[]{:S(2)}) collective-permute-start(bf16[2,18,256]{2,1,0:T(8,128)(2,1)S(1)} %get-tuple-element.22.refs_5_), channel_id=1, source_target_pairs={{0,2},{2,0},{4,6},{6,4},{1,3},{3,1},{5,7},{7,5},{8,10},{10,8},{12,... | collective-permute-start | bytes 55304 | tf_op jit(solution)/shard_map/ppermute | solution.py:371
  24.0 1.6 %collective-permute-start.4 = (bf16[1,128,256]{2,1,0:T(8,128)(2,1)S(1)}, bf16[1,128,256]{2,1,0:T(8,128)(2,1)S(1)}, u32[]{:S(2)}, u32[]{:S(2)}) collective-permute-start(bf16[1,128,256]{2,1,0:T(8,128)(2,1)S(1)} %pick.2), channel_id=1, source_target_pairs={{0,1},{1,0},{2,3},{3,2},{4,5},{5,4},{6,7},{7,6},{8,9},{9,8},{10,11... | collective-permute-start | bytes 196616 | tf_op jit(solution)/shard_map/ppermute | solution.py:370
  25.6 0.4 %outer_rows.1.refs_4_.rows_ref = f32[2,128,256]{2,1,0:T(8,128)S(1)} custom-call(bf16[2,128,256]{2,1,0:T(8,128)(2,1)S(1)} %collective-permute-done.2.refs_2_.refs_0_, bf16[2,128,256]{2,1,0:T(8,128)(2,1)S(1)} %collective-permute-done.3.refs_3_.refs_1_, bf16[3,3,256,256]{3,2,1,0:T(8,128)(2,1)S(1)} %get-tuple-element.20.after_ref.refs_4_.refs_2_, ...), custom_call_target="tpu_custom_call" | custom-call | flops 201326592 | bytes 1048576 | tf_op jit(solution)/shard_map/outer_rows/pallas_call | solution.py:275
  26.0 0.0 collective-permute-done.6.refs_1_
  26.0 1.6 %accumulate.6.refs_4_.total_ref.refs_2_ = f32[16,128,256]{2,1,0:T(8,128)S(1)} custom-call(bf16[2,128,256]{2,1,0:T(8,128)(2,1)S(1)} %collective-permute-done.1.refs_2_.refs_0_, bf16[7,128,256]{2,1,0:T(8,128)(2,1)S(1)} %collective-permute-done.6.refs_1_, ...), custom_call_target="tpu_custom_call", output_to_operand_aliasing={{}: (3, {})} | custom-call | flops 1358954496 | bytes 1048576 | tf_op jit(solution)/shard_map/accumulate/pallas_call | solution.py:141
  27.6 0.0 collective-permute-done.8.refs_1_
  27.6 0.0 collective-permute-done.7.refs_0_
  27.6 0.4 %outer_cols.1.cols_ref = f32[2,16,256]{2,1,0:T(8,128)S(1)} custom-call(bf16[2,18,256]{2,1,0:T(8,128)(2,1)S(1)} %collective-permute-done.7.refs_0_, bf16[2,18,256]{2,1,0:T(8,128)(2,1)S(1)} %collective-permute-done.8.refs_1_, bf16[3,3,256,256]{3,2,1,0:T(8,128)(2,1)S(1)} %get-tuple-element.20.after_ref.refs_4_.refs_2_, ...), custom_call_target="tpu_custom_call" | custom-call | flops 402653184 | bytes 1048576 | tf_op jit(solution)/shard_map/outer_cols/pallas_call | solution.py:275
  28.0 0.2 upper.1.refs_3_.upper_ref
  28.2 0.0 collective-permute-done.5.refs_0_
  28.2 0.8 %accumulate.7.total_ref = f32[16,128,256]{2,1,0:T(8,128)S(1)} custom-call(bf16[4,128,256]{2,1,0:T(8,128)(2,1)S(1)} %collective-permute-done.5.refs_0_, bf16[3,3,256,256]{3,2,1,0:T(8,128)(2,1)S(1)} %get-tuple-element.19.refs_1_.refs_3_.refs_2_.w_ref, f32[16,128,256]{2,1,0:T(8,128)S(1)} %accumulate.6.refs_4_.total_ref.refs_2_, ...), custom_call_target="tpu_custom_call", output_to_operand_aliasing={{}: (2, {})} | custom-call | flops 603979776 | bytes 1048576 | tf_op jit(solution)/shard_map/accumulate/pallas_call | solution.py:141
  29.0 0.1 middle.1.middle_ref
  29.1 0.0 collective-permute-done.4.piece
  29.2 1.3 %last.1 = bf16[256,16,128]{2,1,0:T(8,128)(2,1)} custom-call(bf16[1,128,256]{2,1,0:T(8,128)(2,1)S(1)} %collective-permute-done.4.piece, bf16[3,3,256,256]{3,2,1,0:T(8,128)(2,1)S(1)} %get-tuple-element.19.refs_1_.refs_3_.refs_2_.w_ref, f32[16,128,256]{2,1,0:T(8,128)S(1)} %accumulate.7.total_ref, f32[2,128,256]{2,1,0:T(8,128)S(1)} %outer_rows.1.refs_4_.rows_ref, ...), custom_call_target="tpu_custom_call" | custom-call | flops 301989888 | bytes 1048576 | tf_op jit(solution)/shard_map/last/pallas_call | solution.py:275
  (6 shorter events, 0.1 us)
Async XLA Ops:
  0.0 4.3 %copy-start = (bf16[256,16,128]{2,1,0:T(8,128)(2,1)S(1)}, bf16[256,16,128]{2,1,0:T(8,128)(2,1)}, u32[]{:S(2)}) copy-start(bf16[256,16,128]{2,1,0:T(8,128)(2,1)} %x_hbm.1) | copy-start | bytes 3145732
  1.3 7.5 %collective-permute-start.1 = (bf16[2,128,256]{2,1,0:T(8,128)(2,1)S(1)}, bf16[2,128,256]{2,1,0:T(8,128)(2,1)S(1)}, u32[]{:S(2)}, u32[]{:S(2)}) collective-permute-start(bf16[2,128,256]{2,1,0:T(8,128)(2,1)S(1)} %early.1.refs_1_), channel_id=1, source_target_pairs={{0,1},{1,0},{2,3},{3,2},{4,5},{5,4},{6,7},{7,6},{8,9},{9,8},{10,11... | collective-permute-start | bytes 393224 | tf_op jit(solution)/shard_map/ppermute | solution.py:343
  4.8 6.9 %collective-permute-start = (bf16[288,256]{1,0:T(8,128)(2,1)S(1)}, bf16[288,256]{1,0:T(8,128)(2,1)S(1)}, u32[]{:S(2)}, u32[]{:S(2)}) collective-permute-start(bf16[288,256]{1,0:T(8,128)(2,1)S(1)} %get-tuple-element.15.refs_0_), channel_id=1, source_target_pairs={{0,1},{1,0},{2,3},{3,2},{4,5},{5,4},{6,7},{7,6},{8,9},{9,8},{10,11... | collective-permute-start | bytes 442376 | tf_op jit(solution)/shard_map/ppermute | solution.py:345
  4.9 21.1 %collective-permute-start.6 = (bf16[7,128,256]{2,1,0:T(8,128)(2,1)S(1)}, bf16[7,128,256]{2,1,0:T(8,128)(2,1)S(1)}, u32[]{:S(2)}, u32[]{:S(2)}) collective-permute-start(bf16[7,128,256]{2,1,0:T(8,128)(2,1)S(1)} %get-tuple-element.21.refs_2_), channel_id=1, source_target_pairs={{0,1},{1,0},{2,3},{3,2},{4,5},{5,4},{6,7},{7,6},{8,9},{9,8},{10,11... | collective-permute-start | bytes 1376264 | tf_op jit(solution)/shard_map/ppermute | solution.py:346
  8.6 19.6 %collective-permute-start.5 = (bf16[4,128,256]{2,1,0:T(8,128)(2,1)S(1)}, bf16[4,128,256]{2,1,0:T(8,128)(2,1)S(1)}, u32[]{:S(2)}, u32[]{:S(2)}) collective-permute-start(bf16[4,128,256]{2,1,0:T(8,128)(2,1)S(1)} %pick.3), channel_id=1, source_target_pairs={{0,1},{1,0},{2,3},{3,2},{4,5},{5,4},{6,7},{7,6},{8,9},{9,8},{10,11... | collective-permute-start | bytes 786440 | tf_op jit(solution)/shard_map/ppermute | solution.py:358
  8.7 8.7 %copy-start.1 = (f32[512]{0:T(512)S(1)}, f32[512]{0:T(512)}, u32[]{:S(2)}) copy-start(f32[512]{0:T(512)} %param.5) | copy-start | bytes 6148
  11.7 8.6 %collective-permute-start.2 = (bf16[2,128,256]{2,1,0:T(8,128)(2,1)S(1)}, bf16[2,128,256]{2,1,0:T(8,128)(2,1)S(1)}, u32[]{:S(2)}, u32[]{:S(2)}) collective-permute-start(bf16[2,128,256]{2,1,0:T(8,128)(2,1)S(1)} %get-tuple-element.16), channel_id=1, source_target_pairs={{8,16},{16,8},{9,17},{17,9},{10,18},{18,10},{11,19},{19,11},{12,20... | collective-permute-start | bytes 393224 | tf_op jit(solution)/shard_map/ppermute | solution.py:362
  12.4 7.9 %collective-permute-start.3 = (bf16[2,128,256]{2,1,0:T(8,128)(2,1)S(1)}, bf16[2,128,256]{2,1,0:T(8,128)(2,1)S(1)}, u32[]{:S(2)}, u32[]{:S(2)}) collective-permute-start(bf16[2,128,256]{2,1,0:T(8,128)(2,1)S(1)} %get-tuple-element.17), channel_id=1, source_target_pairs={{0,8},{8,0},{16,24},{24,16},{1,9},{9,1},{17,25},{25,17},{2,10},{10... | collective-permute-start | bytes 393224 | tf_op jit(solution)/shard_map/ppermute | solution.py:362
  20.4 7.2 %collective-permute-start.7 = (bf16[2,18,256]{2,1,0:T(8,128)(2,1)S(1)}, bf16[2,18,256]{2,1,0:T(8,128)(2,1)S(1)}, u32[]{:S(2)}, u32[]{:S(2)}) collective-permute-start(bf16[2,18,256]{2,1,0:T(8,128)(2,1)S(1)} %get-tuple-element.18.after_ref.refs_4_), channel_id=1, source_target_pairs={{2,4},{4,2},{3,5},{5,3},{10,12},{12,10},{11,13},{13,11},{18,20},{2... | collective-permute-start | bytes 55304 | tf_op jit(solution)/shard_map/ppermute | solution.py:371
  21.1 6.5 %collective-permute-start.8 = (bf16[2,18,256]{2,1,0:T(8,128)(2,1)S(1)}, bf16[2,18,256]{2,1,0:T(8,128)(2,1)S(1)}, u32[]{:S(2)}, u32[]{:S(2)}) collective-permute-start(bf16[2,18,256]{2,1,0:T(8,128)(2,1)S(1)} %get-tuple-element.22.refs_5_), channel_id=1, source_target_pairs={{0,2},{2,0},{4,6},{6,4},{1,3},{3,1},{5,7},{7,5},{8,10},{10,8},{12,... | collective-permute-start | bytes 55304 | tf_op jit(solution)/shard_map/ppermute | solution.py:371
  24.0 5.1 %collective-permute-start.4 = (bf16[1,128,256]{2,1,0:T(8,128)(2,1)S(1)}, bf16[1,128,256]{2,1,0:T(8,128)(2,1)S(1)}, u32[]{:S(2)}, u32[]{:S(2)}) collective-permute-start(bf16[1,128,256]{2,1,0:T(8,128)(2,1)S(1)} %pick.2), channel_id=1, source_target_pairs={{0,1},{1,0},{2,3},{3,2},{4,5},{5,4},{6,7},{7,6},{8,9},{9,8},{10,11... | collective-permute-start | bytes 196616 | tf_op jit(solution)/shard_map/ppermute | solution.py:370

commit v13 on v10

--- a/solution.py
+++ b/solution.py
@@ -321,7 +321,7 @@
     slab, height, width = features.shape
     outs = kernel.shape[3] // groups
     half = height // 2
-    chunks = ((1, half + 2), (half + 2, height - 2), (height - 2, height - 1))
+    chunks = ((1, half + 3), (half + 3, height - 2), (height - 2, height - 1))
 
     rim, upper_rows, lower_rows = relayout(features, (chunks[0], (chunks[0][1], height - 1)))
     rings = [[(i, (i + shift) % groups) for i in range(groups)] for shift in range(1, groups)]
@@ -335,7 +335,7 @@
     bias = bias[None, :]
     if outs % 128 != 0:
         bias = lax.dynamic_slice_in_dim(bias, lax.axis_index("filt") * outs, outs, 1)
-    spans = [*outer, (1, 0, 1, half + 1), (2, 0, half + 2, height - half - 3)]
+    spans = [*outer, (1, 0, 1, half + 2), (2, 0, half + 3, height - half - 4)]
     second = pick(lower_rows, 0, chunks[1][1] - chunks[1][0], weights[0])
     for received, ring in zip(sets, rings):
         received.append(lax.ppermute(second, "filt", ring))

time: 29.9 us -> 29.7 us (level)
  transfers between devices with their start and end apart: 8 -> 8, of which waited for: 2 -> 2; matrix products, arithmetic and copies ran while one was open for 0% -> 0% of each run, Pallas kernels for 27% -> 28%
where the time goes in v13:
time: 29.7 us; the launch traced here: 29.5 us
  starting transfers between devices  15.9 us (54%)
  Pallas kernels  11 us (37%)
  waiting for transfers between devices  2.4 us (8%)
    ppermute x2, starting transfers between devices, body(): outer_rows = [lax.ppermute(v, 'row', p) for v, p in zip(sent, row_pairs)]  5.67 us
    pallas_call x4, Pallas kernels, accumulate(): pl.pallas_call(functools.partial(accumulate_kernel, spans, len(pieces), t...  5.29 us
    ppermute x2, starting transfers between devices, body(): outer_cols = [lax.ppermute(v, 'col', p) for v, p in zip(sent, col_pairs)]  3.58 us
    ppermute x1, starting transfers between devices, body(): rims = [rim] + [lax.ppermute(rim, 'filt', ring) for ring in rings]  3.03 us
    pallas_call x7, Pallas kernels, call(): pl.pallas_call(kernel, out_shape=jax.ShapeDtypeStruct(shape, dtype), in_s...  2.42 us
    ppermute x1, starting transfers between devices, body(): received.append(lax.ppermute(second, 'filt', ring))  2.01 us
    pallas_call x1, Pallas kernels, split_weights(): pl.pallas_call(functools.partial(weights_kernel, groups), out_shape=[jax....  1.68 us
    pallas_call x1, Pallas kernels, relayout(): pl.pallas_call(functools.partial(relayout_kernel, chunks), out_shape=[jax...  1.59 us
  transfers between devices with their start and end apart: 8, of which 2 were waited for; matrix products, arithmetic and copies ran while one was open for 0% of the time, Pallas kernels for 28%

profile of v13, /device:TPU:0, one launch (start us, length us, event | category | flops | bytes accessed | tf_op | source)
XLA Modules:
  0.0 29.5 jit_solution(10846967505289101395)
XLA Ops:
  0.0 1.6 %relayout.1 = (bf16[288,256]{1,0:T(8,128)(2,1)S(1)}, bf16[10,128,256]{2,1,0:T(8,128)(2,1)S(1)}, bf16[4,128,256]{2,1,0:T(8,128)(2,1)S(1)}) custom-call(bf16[256,16,128]{2,1,0:T(8,128)(2,1)} %x_hbm.1), custom_call_target="tpu_custom_call" | custom-call | tf_op jit(solution)/shard_map/relayout/pallas_call | solution.py:48
  1.6 3.0 %collective-permute-start = (bf16[288,256]{1,0:T(8,128)(2,1)S(1)}, bf16[288,256]{1,0:T(8,128)(2,1)S(1)}, u32[]{:S(2)}, u32[]{:S(2)}) collective-permute-start(bf16[288,256]{1,0:T(8,128)(2,1)S(1)} %get-tuple-element.15.refs_0_), channel_id=1, source_target_pairs={{0,1},{1,0},{2,3},{3,2},{4,5},{5,4},{6,7},{7,6},{8,9},{9,8},{10,11... | collective-permute-start | bytes 442376 | tf_op jit(solution)/shard_map/ppermute | solution.py:328
  4.6 0.1 collective-permute-start.5
  4.7 1.7 %split_weights.1 = (bf16[3,3,256,256]{3,2,1,0:T(8,128)(2,1)S(1)}, bf16[3,3,256,256]{3,2,1,0:T(8,128)(2,1)S(1)}) custom-call(bf16[3,3,512,512]{3,2,1,0:T(8,128)(2,1)} %kernel_ref.1), custom_call_target="tpu_custom_call" | custom-call | tf_op jit(solution)/shard_map/split_weights/pallas_call | solution.py:304
  6.4 2.0 %collective-permute-start.4 = (bf16[3,128,256]{2,1,0:T(8,128)(2,1)S(1)}, bf16[3,128,256]{2,1,0:T(8,128)(2,1)S(1)}, u32[]{:S(2)}, u32[]{:S(2)}) collective-permute-start(bf16[3,128,256]{2,1,0:T(8,128)(2,1)S(1)} %pick.3), channel_id=1, source_target_pairs={{0,1},{1,0},{2,3},{3,2},{4,5},{5,4},{6,7},{7,6},{8,9},{9,8},{10,11... | collective-permute-start | bytes 589832 | tf_op jit(solution)/shard_map/ppermute | solution.py:341
  8.5 0.0 copy-start
  8.5 0.8 %collective-permute-done.refs_1_.refs_5_ = bf16[288,256]{1,0:T(8,128)(2,1)S(1)} collective-permute-done((bf16[288,256]{1,0:T(8,128)(2,1)S(1)}, bf16[288,256]{1,0:T(8,128)(2,1)S(1)}, u32[]{:S(2)}, u32[]{:S(2)}) %collective-permute-start) | collective-permute-done | bytes 147488 | tf_op jit(solution)/shard_map/ppermute | solution.py:328
  9.3 0.7 %collective-permute-start.1 = (bf16[2,128,256]{2,1,0:T(8,128)(2,1)S(1)}, bf16[2,128,256]{2,1,0:T(8,128)(2,1)S(1)}, u32[]{:S(2)}, u32[]{:S(2)}) collective-permute-start(bf16[2,128,256]{2,1,0:T(8,128)(2,1)S(1)} %get-tuple-element.16), channel_id=1, source_target_pairs={{8,16},{16,8},{9,17},{17,9},{10,18},{18,10},{11,19},{19,11},{12,20... | collective-permute-start | bytes 393224 | tf_op jit(solution)/shard_map/ppermute | solution.py:345
  10.0 5.0 %collective-permute-start.2 = (bf16[2,128,256]{2,1,0:T(8,128)(2,1)S(1)}, bf16[2,128,256]{2,1,0:T(8,128)(2,1)S(1)}, u32[]{:S(2)}, u32[]{:S(2)}) collective-permute-start(bf16[2,128,256]{2,1,0:T(8,128)(2,1)S(1)} %get-tuple-element.17), channel_id=1, source_target_pairs={{0,8},{8,0},{16,24},{24,16},{1,9},{9,1},{17,25},{25,17},{2,10},{10... | collective-permute-start | bytes 393224 | tf_op jit(solution)/shard_map/ppermute | solution.py:345
  15.0 0.0 copy-done
  15.0 2.6 %accumulate.4.refs_2_ = f32[16,128,256]{2,1,0:T(8,128)S(1)} custom-call(bf16[2,128,256]{2,1,0:T(8,128)(2,1)S(1)} %bitcast.4, bf16[10,128,256]{2,1,0:T(8,128)(2,1)S(1)} %get-tuple-element.21.refs_1_, bf16[4,128,256]{2,1,0:T(8,128)(2,1)S(1)} %get-tuple-element.14.rows_ref.refs_2_, bf16[3,3,256,256]{3,2,1,0:T(8,128)(2,1)S(1)} %get-tuple-element.20.after_ref.refs_3_.refs_2_, ...), custom_call_target="tpu_custom_call" | custom-call | flops 2415919104 | bytes 1048576 | tf_op jit(solution)/shard_map/accumulate/pallas_call | solution.py:127
  17.6 0.4 %accumulate.5.refs_2_ = f32[16,128,256]{2,1,0:T(8,128)S(1)} custom-call(bf16[2,128,256]{2,1,0:T(8,128)(2,1)S(1)} %bitcast.3, bf16[3,3,256,256]{3,2,1,0:T(8,128)(2,1)S(1)} %get-tuple-element.19.refs_1_.refs_3_.w_ref, f32[16,128,256]{2,1,0:T(8,128)S(1)} %accumulate.4.refs_2_), custom_call_target="tpu_custom_call", output_to_operand_aliasing={{}: (2, {})} | custom-call | flops 301989888 | bytes 1048576 | tf_op jit(solution)/shard_map/accumulate/pallas_call | solution.py:127
  18.0 0.0 collective-permute-done.1.refs_2_.refs_0_
  18.0 0.0 collective-permute-done.2.refs_3_.refs_1_
  18.0 0.7 %collective-permute-start.6 = (bf16[2,18,256]{2,1,0:T(8,128)(2,1)S(1)}, bf16[2,18,256]{2,1,0:T(8,128)(2,1)S(1)}, u32[]{:S(2)}, u32[]{:S(2)}) collective-permute-start(bf16[2,18,256]{2,1,0:T(8,128)(2,1)S(1)} %get-tuple-element.18.after_ref.refs_4_), channel_id=1, source_target_pairs={{2,4},{4,2},{3,5},{5,3},{10,12},{12,10},{11,13},{13,11},{18,20},{2... | collective-permute-start | bytes 55304 | tf_op jit(solution)/shard_map/ppermute | solution.py:354
  18.7 2.9 %collective-permute-start.7 = (bf16[2,18,256]{2,1,0:T(8,128)(2,1)S(1)}, bf16[2,18,256]{2,1,0:T(8,128)(2,1)S(1)}, u32[]{:S(2)}, u32[]{:S(2)}) collective-permute-start(bf16[2,18,256]{2,1,0:T(8,128)(2,1)S(1)} %get-tuple-element.22.refs_5_), channel_id=1, source_target_pairs={{0,2},{2,0},{4,6},{6,4},{1,3},{3,1},{5,7},{7,5},{8,10},{10,8},{12,... | collective-permute-start | bytes 55304 | tf_op jit(solution)/shard_map/ppermute | solution.py:354
  21.6 1.5 %collective-permute-start.3 = (bf16[1,128,256]{2,1,0:T(8,128)(2,1)S(1)}, bf16[1,128,256]{2,1,0:T(8,128)(2,1)S(1)}, u32[]{:S(2)}, u32[]{:S(2)}) collective-permute-start(bf16[1,128,256]{2,1,0:T(8,128)(2,1)S(1)} %pick.2), channel_id=1, source_target_pairs={{0,1},{1,0},{2,3},{3,2},{4,5},{5,4},{6,7},{7,6},{8,9},{9,8},{10,11... | collective-permute-start | bytes 196616 | tf_op jit(solution)/shard_map/ppermute | solution.py:353
  23.2 0.4 %outer_rows.1.refs_3_.rows_ref = f32[2,128,256]{2,1,0:T(8,128)S(1)} custom-call(bf16[2,128,256]{2,1,0:T(8,128)(2,1)S(1)} %collective-permute-done.1.refs_2_.refs_0_, bf16[2,128,256]{2,1,0:T(8,128)(2,1)S(1)} %collective-permute-done.2.refs_3_.refs_1_, bf16[3,3,256,256]{3,2,1,0:T(8,128)(2,1)S(1)} %get-tuple-element.20.after_ref.refs_3_.refs_2_, ...), custom_call_target="tpu_custom_call" | custom-call | flops 201326592 | bytes 1048576 | tf_op jit(solution)/shard_map/outer_rows/pallas_call | solution.py:261
  23.6 0.0 collective-permute-done.5.refs_0_
  23.6 1.7 %accumulate.6.refs_4_.total_ref.refs_2_ = f32[16,128,256]{2,1,0:T(8,128)S(1)} custom-call(bf16[10,128,256]{2,1,0:T(8,128)(2,1)S(1)} %collective-permute-done.5.refs_0_, bf16[3,3,256,256]{3,2,1,0:T(8,128)(2,1)S(1)} %get-tuple-element.19.refs_1_.refs_3_.w_ref, f32[16,128,256]{2,1,0:T(8,128)S(1)} %accumulate.5.refs_2_, ...), custom_call_target="tpu_custom_call", output_to_operand_aliasing={{}: (2, {})} | custom-call | flops 1509949440 | bytes 1048576 | tf_op jit(solution)/shard_map/accumulate/pallas_call | solution.py:127
  25.3 0.0 collective-permute-done.7.refs_1_
  25.3 0.0 collective-permute-done.6.refs_0_
  25.3 0.4 %outer_cols.1.cols_ref = f32[2,16,256]{2,1,0:T(8,128)S(1)} custom-call(bf16[2,18,256]{2,1,0:T(8,128)(2,1)S(1)} %collective-permute-done.6.refs_0_, bf16[2,18,256]{2,1,0:T(8,128)(2,1)S(1)} %collective-permute-done.7.refs_1_, bf16[3,3,256,256]{3,2,1,0:T(8,128)(2,1)S(1)} %get-tuple-element.20.after_ref.refs_3_.refs_2_, ...), custom_call_target="tpu_custom_call" | custom-call | flops 402653184 | bytes 1048576 | tf_op jit(solution)/shard_map/outer_cols/pallas_call | solution.py:261
  25.7 0.2 upper.1.refs_3_.upper_ref
  25.9 1.5 %collective-permute-done.4.refs_0_ = bf16[3,128,256]{2,1,0:T(8,128)(2,1)S(1)} collective-permute-done((bf16[3,128,256]{2,1,0:T(8,128)(2,1)S(1)}, bf16[3,128,256]{2,1,0:T(8,128)(2,1)S(1)}, u32[]{:S(2)}, u32[]{:S(2)}) %collective-permute-start.4) | collective-permute-done | bytes 196640 | tf_op jit(solution)/shard_map/ppermute | solution.py:341
  27.4 0.6 %accumulate.7.total_ref = f32[16,128,256]{2,1,0:T(8,128)S(1)} custom-call(bf16[3,128,256]{2,1,0:T(8,128)(2,1)S(1)} %collective-permute-done.4.refs_0_, bf16[3,3,256,256]{3,2,1,0:T(8,128)(2,1)S(1)} %get-tuple-element.19.refs_1_.refs_3_.w_ref, f32[16,128,256]{2,1,0:T(8,128)S(1)} %accumulate.6.refs_4_.total_ref.refs_2_, ...), custom_call_target="tpu_custom_call", output_to_operand_aliasing={{}: (2, {})} | custom-call | flops 452984832 | bytes 1048576 | tf_op jit(solution)/shard_map/accumulate/pallas_call | solution.py:127
  28.1 0.1 middle.1.middle_ref
  28.2 0.0 collective-permute-done.3.piece
  28.2 1.3 %last.1 = bf16[256,16,128]{2,1,0:T(8,128)(2,1)} custom-call(bf16[1,128,256]{2,1,0:T(8,128)(2,1)S(1)} %collective-permute-done.3.piece, bf16[3,3,256,256]{3,2,1,0:T(8,128)(2,1)S(1)} %get-tuple-element.19.refs_1_.refs_3_.w_ref, f32[16,128,256]{2,1,0:T(8,128)S(1)} %accumulate.7.total_ref, f32[2,128,256]{2,1,0:T(8,128)S(1)} %outer_rows.1.refs_3_.rows_ref, ...), custom_call_target="tpu_custom_call" | custom-call | flops 301989888 | bytes 1048576 | tf_op jit(solution)/shard_map/last/pallas_call | solution.py:261
  (6 shorter events, 0.1 us)
Async XLA Ops:
  1.6 7.7 %collective-permute-start = (bf16[288,256]{1,0:T(8,128)(2,1)S(1)}, bf16[288,256]{1,0:T(8,128)(2,1)S(1)}, u32[]{:S(2)}, u32[]{:S(2)}) collective-permute-start(bf16[288,256]{1,0:T(8,128)(2,1)S(1)} %get-tuple-element.15.refs_0_), channel_id=1, source_target_pairs={{0,1},{1,0},{2,3},{3,2},{4,5},{5,4},{6,7},{7,6},{8,9},{9,8},{10,11... | collective-permute-start | bytes 442376 | tf_op jit(solution)/shard_map/ppermute | solution.py:328
  4.6 18.9 %collective-permute-start.5 = (bf16[10,128,256]{2,1,0:T(8,128)(2,1)S(1)}, bf16[10,128,256]{2,1,0:T(8,128)(2,1)S(1)}, u32[]{:S(2)}, u32[]{:S(2)}) collective-permute-start(bf16[10,128,256]{2,1,0:T(8,128)(2,1)S(1)} %get-tuple-element.21.refs_1_), channel_id=1, source_target_pairs={{0,1},{1,0},{2,3},{3,2},{4,5},{5,4},{6,7},{7,6},{8,9},{9,8},{10,11... | collective-permute-start | bytes 1966088 | tf_op jit(solution)/shard_map/ppermute | solution.py:329
  6.4 21.0 %collective-permute-start.4 = (bf16[3,128,256]{2,1,0:T(8,128)(2,1)S(1)}, bf16[3,128,256]{2,1,0:T(8,128)(2,1)S(1)}, u32[]{:S(2)}, u32[]{:S(2)}) collective-permute-start(bf16[3,128,256]{2,1,0:T(8,128)(2,1)S(1)} %pick.3), channel_id=1, source_target_pairs={{0,1},{1,0},{2,3},{3,2},{4,5},{5,4},{6,7},{7,6},{8,9},{9,8},{10,11... | collective-permute-start | bytes 589832 | tf_op jit(solution)/shard_map/ppermute | solution.py:341
  8.5 6.6 %copy-start = (f32[512]{0:T(512)S(1)}, f32[512]{0:T(512)}, u32[]{:S(2)}) copy-start(f32[512]{0:T(512)} %param.5) | copy-start | bytes 6148
  9.3 8.6 %collective-permute-start.1 = (bf16[2,128,256]{2,1,0:T(8,128)(2,1)S(1)}, bf16[2,128,256]{2,1,0:T(8,128)(2,1)S(1)}, u32[]{:S(2)}, u32[]{:S(2)}) collective-permute-start(bf16[2,128,256]{2,1,0:T(8,128)(2,1)S(1)} %get-tuple-element.16), channel_id=1, source_target_pairs={{8,16},{16,8},{9,17},{17,9},{10,18},{18,10},{11,19},{19,11},{12,20... | collective-permute-start | bytes 393224 | tf_op jit(solution)/shard_map/ppermute | solution.py:345
  10.0 8.0 %collective-permute-start.2 = (bf16[2,128,256]{2,1,0:T(8,128)(2,1)S(1)}, bf16[2,128,256]{2,1,0:T(8,128)(2,1)S(1)}, u32[]{:S(2)}, u32[]{:S(2)}) collective-permute-start(bf16[2,128,256]{2,1,0:T(8,128)(2,1)S(1)} %get-tuple-element.17), channel_id=1, source_target_pairs={{0,8},{8,0},{16,24},{24,16},{1,9},{9,1},{17,25},{25,17},{2,10},{10... | collective-permute-start | bytes 393224 | tf_op jit(solution)/shard_map/ppermute | solution.py:345
  18.0 7.3 %collective-permute-start.6 = (bf16[2,18,256]{2,1,0:T(8,128)(2,1)S(1)}, bf16[2,18,256]{2,1,0:T(8,128)(2,1)S(1)}, u32[]{:S(2)}, u32[]{:S(2)}) collective-permute-start(bf16[2,18,256]{2,1,0:T(8,128)(2,1)S(1)} %get-tuple-element.18.after_ref.refs_4_), channel_id=1, source_target_pairs={{2,4},{4,2},{3,5},{5,3},{10,12},{12,10},{11,13},{13,11},{18,20},{2... | collective-permute-start | bytes 55304 | tf_op jit(solution)/shard_map/ppermute | solution.py:354
  18.7 6.6 %collective-permute-start.7 = (bf16[2,18,256]{2,1,0:T(8,128)(2,1)S(1)}, bf16[2,18,256]{2,1,0:T(8,128)(2,1)S(1)}, u32[]{:S(2)}, u32[]{:S(2)}) collective-permute-start(bf16[2,18,256]{2,1,0:T(8,128)(2,1)S(1)} %get-tuple-element.22.refs_5_), channel_id=1, source_target_pairs={{0,2},{2,0},{4,6},{6,4},{1,3},{3,1},{5,7},{7,5},{8,10},{10,8},{12,... | collective-permute-start | bytes 55304 | tf_op jit(solution)/shard_map/ppermute | solution.py:354
  21.6 6.6 %collective-permute-start.3 = (bf16[1,128,256]{2,1,0:T(8,128)(2,1)S(1)}, bf16[1,128,256]{2,1,0:T(8,128)(2,1)S(1)}, u32[]{:S(2)}, u32[]{:S(2)}) collective-permute-start(bf16[1,128,256]{2,1,0:T(8,128)(2,1)S(1)} %pick.2), channel_id=1, source_target_pairs={{0,1},{1,0},{2,3},{3,2},{4,5},{5,4},{6,7},{7,6},{8,9},{9,8},{10,11... | collective-permute-start | bytes 196616 | tf_op jit(solution)/shard_map/ppermute | solution.py:353

commit v14 on v13

--- a/solution.py
+++ b/solution.py
@@ -70,7 +70,8 @@
     return part if b == 1 else pltpu.roll(part, 1 if b == 0 else part.shape[0] - 1, 0)
 
 
-def add_rows(spans, w_ref, total_ref, x_ref, written, initial=None):
+def add_rows(spans, w_ref, total_ref, x_ref, base):
+    written = set()
     height, width, _ = total_ref.shape
     slab = w_ref.shape[2]
     at = 0
@@ -94,16 +95,23 @@
                         if low + i in written:
                             total_ref[low + i] += term
                         else:
-                            total_ref[low + i] = term + initial
+                            total_ref[low + i] = term + base(low + i)
                             written.add(low + i)
             at += size
+    return written
 
 
 def accumulate_kernel(spans, n, started, *refs):
-    pieces, w_ref, total_ref, x_ref = refs[:n], refs[n], refs[-2], refs[-1]
-    written = set(range(total_ref.shape[0])) if started else set()
+    pieces, w_ref, start_ref, total_ref, x_ref = refs[:n], refs[n], refs[n + 1], refs[-2], refs[-1]
     spans = [(pieces[p], local, row, count) for p, local, row, count in spans]
-    add_rows(spans, w_ref, total_ref, x_ref, written, None if started else own_bias(refs[n + 1], total_ref.shape[2]))
+    if started:
+        written = add_rows(spans, w_ref, total_ref, x_ref, lambda h: start_ref[h])
+    else:
+        bias = own_bias(start_ref, total_ref.shape[2])
+        written = add_rows(spans, w_ref, total_ref, x_ref, lambda h: bias)
+    for h in range(total_ref.shape[0]):
+        if h not in written:
+            total_ref[h] = start_ref[h]
 
 
 def own_bias(bias_ref, outs):
@@ -115,13 +123,7 @@
 def accumulate(spans, pieces, weights, total, shape, after=None, bias=None):
     count = sum(s[3] for s in spans)
     width, slab = shape[1], weights.shape[2]
-    operands = [*pieces, weights]
-    aliases = {}
-    if total is not None:
-        aliases = {len(operands): 0}
-        operands.append(total)
-    else:
-        operands.append(bias)
+    operands = [*pieces, weights, bias if total is None else total]
     if after is not None:
         operands.append(after)
     return pl.pallas_call(
@@ -130,7 +132,6 @@
         in_specs=[VMEM] * len(operands),
         out_specs=VMEM,
         scratch_shapes=[pltpu.VMEM((3, count, width, slab), BF16)],
-        input_output_aliases=aliases,
         compiler_params=PARAMS,
         cost_estimate=cost(count * width * 9, slab, shape[2]),
         name="accumulate",
@@ -229,12 +230,18 @@
     out_ref[...] = jnp.swapaxes(jnp.stack(turned, 0), 0, 1)
 
 
-def middle_kernel(start, total_ref, rows_ref, cols_ref, out_ref):
-    for i in range(out_ref.shape[0]):
-        out_ref[i] = finish_row(total_ref[start + i], start + i, rows_ref, cols_ref)
-
-
-def last_kernel(piece, w_ref, total_ref, rows_ref, cols_ref, upper_ref, middle_ref, out_ref, x_ref, lower_ref, sems):
+def second_kernel(row, start, piece, w_ref, total_ref, rows_ref, cols_ref, after_ref, done_ref, rest_ref, sum_ref, x_ref):
+    count, done = piece.shape[0], done_ref.shape[0]
+    written = add_rows([(piece, 0, row, count)], w_ref, sum_ref, x_ref, lambda h: total_ref[h])
+    for i in range(done + rest_ref.shape[0]):
+        value = (sum_ref if start + i in written else total_ref)[start + i]
+        if i < done:
+            done_ref[i] = finish_row(value, start + i, rows_ref, cols_ref)
+        else:
+            rest_ref[i - done] = value
+
+
+def last_kernel(piece, w_ref, rest_ref, rows_ref, cols_ref, upper_ref, middle_ref, out_ref, x_ref, lower_ref, sems):
     outs, height, width = out_ref.shape
     half, done = upper_ref.shape[1], middle_ref.shape[0]
     first = pltpu.make_async_copy(upper_ref, out_ref.at[:, 0:half, :], sems.at[0])
@@ -242,7 +249,7 @@
     count = piece.shape[0]
     for i in range(count):
         put_row(x_ref, i, piece[i])
-    values = [total_ref[h] for h in range(half + done, height)]
+    values = [rest_ref[i] for i in range(height - half - done)]
     for a in range(3):
         for b in range(3):
             part = jnp.dot(x_ref[b].reshape(count * width, -1), w_ref[a, b], preferred_element_type=F32).reshape(count, width, outs)
@@ -344,8 +351,6 @@
     sent = calls(functools.partial(outermost_kernel, groups), "outermost", [(groups, width, slab)] * 2, rims, estimate=WAIT)
     outer_rows = [lax.ppermute(v, "row", p) for v, p in zip(sent, row_pairs)]
     total = accumulate(spans, [pairs[0], upper_rows, lower_rows], weights[0], None, shape, rims[-1], bias)
-    for g in range(1, groups):
-        total = accumulate(outer, [pairs[g]], weights[g], total, shape)
     edge = pltpu.VMEM((2, height + 2, slab), F32)
     sent = calls(functools.partial(edges_kernel, groups), "edges", [(groups, height + 2, slab)] * 2, [*rims, *outer_rows], [edge])
     third = pick(lower_rows, chunks[2][0] - chunks[1][0], chunks[2][1] - chunks[1][0], sent[0])
@@ -358,18 +363,27 @@
     )
     for g in range(1, groups):
         a, b, c = sets[g - 1]
-        total = accumulate([(0, 0, chunks[0][0], a.shape[0])], [a], weights[g], total, shape, rows_fix)
+        spans, chosen = [*outer, (1, 0, chunks[0][0], a.shape[0])], [pairs[g], a]
         if g < groups - 1:
-            total = accumulate([(0, 0, chunks[1][0], b.shape[0])], [b], weights[g], total, shape)
-            total = accumulate([(0, 0, chunks[2][0], c.shape[0])], [c], weights[g], total, shape)
+            spans += [(2, 0, chunks[1][0], b.shape[0]), (3, 0, chunks[2][0], c.shape[0])]
+            chosen += [b, c]
+        total = accumulate(spans, chosen, weights[g], total, shape, rows_fix)
     cols_fix = call(
         functools.partial(outer_cols_kernel, groups), "outer_cols", (2, height, outs), F32,
         [*outer_cols, *weights, total], cost(6 * 256 * groups, slab, outs),
     )
     top = call(upper_kernel, "upper", (outs, half, width), BF16, [total, rows_fix, cols_fix], cost(256, slab, outs))
-    total = accumulate([(0, 0, chunks[1][0], b.shape[0])], [b], weights[-1], total, shape, top)
     done = chunks[2][0] - 1 - half
-    middle = call(functools.partial(middle_kernel, half), "middle", (done, outs, width), BF16, [total, rows_fix, cols_fix], cost(1, 1, 1))
+    middle, rest = pl.pallas_call(
+        functools.partial(second_kernel, chunks[1][0], half),
+        out_shape=[jax.ShapeDtypeStruct((done, outs, width), BF16), jax.ShapeDtypeStruct((half - done, width, outs), F32)],
+        in_specs=[VMEM] * 6,
+        out_specs=[VMEM] * 2,
+        scratch_shapes=[pltpu.VMEM(shape, F32), pltpu.VMEM((3, b.shape[0], width, slab), BF16)],
+        compiler_params=PARAMS,
+        cost_estimate=cost(b.shape[0] * width * 9, slab, outs),
+        name="second",
+    )(b, weights[-1], total, rows_fix, cols_fix, top)
     scratch = [
         pltpu.VMEM((3, c.shape[0], width, slab), BF16),
         pltpu.VMEM((outs, height - half, width), BF16),
@@ -377,7 +391,7 @@
     ]
     return call(
         last_kernel, "last", (outs, height, width), BF16,
-        [c, weights[-1], total, rows_fix, cols_fix, top, middle], cost(9 * 256, slab, outs), scratch, HBM,
+        [c, weights[-1], rest, rows_fix, cols_fix, top, middle], cost(9 * 256, slab, outs), scratch, HBM,
     )
 
 

time: 29.7 us -> 29.6 us (level)
    pallas_call x4 -> x2, Pallas kernels: 5.29 us -> 4.48 us  [accumulate(): pl.pallas_call(functools.partial(accumulate_kernel, spans, len(pieces), t...]
    pallas_call x0 -> x1, Pallas kernels: none -> 0.69 us  [body(): pl.pallas_call(functools.partial(second_kernel, chunks[1][0], half), out_...]
    ppermute x2, waiting for transfers between devices: 0.01 us -> 0.36 us  [body(): outer_rows = [lax.ppermute(v, 'row', p) for v, p in zip(sent, row_pairs)]]
    pallas_call x7 -> x6, Pallas kernels: 2.42 us -> 2.28 us  [call(): pl.pallas_call(kernel, out_shape=jax.ShapeDtypeStruct(shape, dtype), in_s...]
  transfers between devices with their start and end apart: 8 -> 8, of which waited for: 2 -> 3; matrix products, arithmetic and copies ran while one was open for 0% -> 0% of each run, Pallas kernels for 28% -> 27%
where the time goes in v14:
time: 29.6 us; the launch traced here: 29.4 us
  starting transfers between devices  15.9 us (54%)
  Pallas kernels  10.8 us (36%)
  waiting for transfers between devices  2.6 us (9%)
    ppermute x2, starting transfers between devices, body(): outer_rows = [lax.ppermute(v, 'row', p) for v, p in zip(sent, row_pairs)]  5.67 us
    pallas_call x2, Pallas kernels, accumulate(): pl.pallas_call(functools.partial(accumulate_kernel, spans, len(pieces), t...  4.48 us
    ppermute x2, starting transfers between devices, body(): outer_cols = [lax.ppermute(v, 'col', p) for v, p in zip(sent, col_pairs)]  3.58 us
    ppermute x1, starting transfers between devices, body(): rims = [rim] + [lax.ppermute(rim, 'filt', ring) for ring in rings]  3.03 us
    pallas_call x6, Pallas kernels, call(): pl.pallas_call(kernel, out_shape=jax.ShapeDtypeStruct(shape, dtype), in_s...  2.28 us
    ppermute x1, starting transfers between devices, body(): received.append(lax.ppermute(second, 'filt', ring))  2.01 us
    pallas_call x1, Pallas kernels, split_weights(): pl.pallas_call(functools.partial(weights_kernel, groups), out_shape=[jax....  1.68 us
    pallas_call x1, Pallas kernels, relayout(): pl.pallas_call(functools.partial(relayout_kernel, chunks), out_shape=[jax...  1.59 us
  transfers between devices with their start and end apart: 8, of which 3 were waited for; matrix products, arithmetic and copies ran while one was open for 0% of the time, Pallas kernels for 27%

profile of v14, /device:TPU:0, one launch (start us, length us, event | category | flops | bytes accessed | tf_op | source)
XLA Modules:
  0.0 29.4 jit_solution(3813718960959449165)
XLA Ops:
  0.0 1.6 %relayout.1 = (bf16[288,256]{1,0:T(8,128)(2,1)S(1)}, bf16[10,128,256]{2,1,0:T(8,128)(2,1)S(1)}, bf16[4,128,256]{2,1,0:T(8,128)(2,1)S(1)}) custom-call(bf16[256,16,128]{2,1,0:T(8,128)(2,1)} %x_hbm.1), custom_call_target="tpu_custom_call" | custom-call | tf_op jit(solution)/shard_map/relayout/pallas_call | solution.py:48
  1.6 3.0 %collective-permute-start = (bf16[288,256]{1,0:T(8,128)(2,1)S(1)}, bf16[288,256]{1,0:T(8,128)(2,1)S(1)}, u32[]{:S(2)}, u32[]{:S(2)}) collective-permute-start(bf16[288,256]{1,0:T(8,128)(2,1)S(1)} %get-tuple-element.17.refs_0_), channel_id=1, source_target_pairs={{0,1},{1,0},{2,3},{3,2},{4,5},{5,4},{6,7},{7,6},{8,9},{9,8},{10,11... | collective-permute-start | bytes 442376 | tf_op jit(solution)/shard_map/ppermute | solution.py:335
  4.6 0.1 collective-permute-start.5
  4.7 1.7 %split_weights.1 = (bf16[3,3,256,256]{3,2,1,0:T(8,128)(2,1)S(1)}, bf16[3,3,256,256]{3,2,1,0:T(8,128)(2,1)S(1)}) custom-call(bf16[3,3,512,512]{3,2,1,0:T(8,128)(2,1)} %kernel_ref.1), custom_call_target="tpu_custom_call" | custom-call | tf_op jit(solution)/shard_map/split_weights/pallas_call | solution.py:311
  6.4 2.0 %collective-permute-start.4 = (bf16[3,128,256]{2,1,0:T(8,128)(2,1)S(1)}, bf16[3,128,256]{2,1,0:T(8,128)(2,1)S(1)}, u32[]{:S(2)}, u32[]{:S(2)}) collective-permute-start(bf16[3,128,256]{2,1,0:T(8,128)(2,1)S(1)} %pick.3), channel_id=1, source_target_pairs={{0,1},{1,0},{2,3},{3,2},{4,5},{5,4},{6,7},{7,6},{8,9},{9,8},{10,11... | collective-permute-start | bytes 589832 | tf_op jit(solution)/shard_map/ppermute | solution.py:348
  8.5 0.0 copy-start
  8.5 0.8 %collective-permute-done.refs_1_.refs_5_ = bf16[288,256]{1,0:T(8,128)(2,1)S(1)} collective-permute-done((bf16[288,256]{1,0:T(8,128)(2,1)S(1)}, bf16[288,256]{1,0:T(8,128)(2,1)S(1)}, u32[]{:S(2)}, u32[]{:S(2)}) %collective-permute-start) | collective-permute-done | bytes 147488 | tf_op jit(solution)/shard_map/ppermute | solution.py:335
  9.3 0.7 %collective-permute-start.1 = (bf16[2,128,256]{2,1,0:T(8,128)(2,1)S(1)}, bf16[2,128,256]{2,1,0:T(8,128)(2,1)S(1)}, u32[]{:S(2)}, u32[]{:S(2)}) collective-permute-start(bf16[2,128,256]{2,1,0:T(8,128)(2,1)S(1)} %get-tuple-element.18), channel_id=1, source_target_pairs={{8,16},{16,8},{9,17},{17,9},{10,18},{18,10},{11,19},{19,11},{12,20... | collective-permute-start | bytes 393224 | tf_op jit(solution)/shard_map/ppermute | solution.py:352
  10.0 5.0 %collective-permute-start.2 = (bf16[2,128,256]{2,1,0:T(8,128)(2,1)S(1)}, bf16[2,128,256]{2,1,0:T(8,128)(2,1)S(1)}, u32[]{:S(2)}, u32[]{:S(2)}) collective-permute-start(bf16[2,128,256]{2,1,0:T(8,128)(2,1)S(1)} %get-tuple-element.19), channel_id=1, source_target_pairs={{0,8},{8,0},{16,24},{24,16},{1,9},{9,1},{17,25},{25,17},{2,10},{10... | collective-permute-start | bytes 393224 | tf_op jit(solution)/shard_map/ppermute | solution.py:352
  15.0 0.0 copy-done
  15.0 2.5 %accumulate.2.refs_3_ = f32[16,128,256]{2,1,0:T(8,128)S(1)} custom-call(bf16[2,128,256]{2,1,0:T(8,128)(2,1)S(1)} %bitcast.4, bf16[10,128,256]{2,1,0:T(8,128)(2,1)S(1)} %get-tuple-element.23.refs_1_, bf16[4,128,256]{2,1,0:T(8,128)(2,1)S(1)} %get-tuple-element.16.rows_ref.refs_2_, bf16[3,3,256,256]{3,2,1,0:T(8,128)(2,1)S(1)} %get-tuple-element.22.after_ref.refs_3_.refs_2_, ...), custom_call_target="tpu_custom_call" | custom-call | flops 2415919104 | bytes 1048576 | tf_op jit(solution)/shard_map/accumulate/pallas_call | solution.py:129
  17.6 0.0 collective-permute-done.1.refs_2_.refs_0_
  17.6 0.4 %collective-permute-done.2.refs_3_.refs_1_ = bf16[2,128,256]{2,1,0:T(8,128)(2,1)S(1)} collective-permute-done((bf16[2,128,256]{2,1,0:T(8,128)(2,1)S(1)}, bf16[2,128,256]{2,1,0:T(8,128)(2,1)S(1)}, u32[]{:S(2)}, u32[]{:S(2)}) %collective-permute-start.2) | collective-permute-done | bytes 131104 | tf_op jit(solution)/shard_map/ppermute | solution.py:352
  18.0 0.7 %collective-permute-start.6 = (bf16[2,18,256]{2,1,0:T(8,128)(2,1)S(1)}, bf16[2,18,256]{2,1,0:T(8,128)(2,1)S(1)}, u32[]{:S(2)}, u32[]{:S(2)}) collective-permute-start(bf16[2,18,256]{2,1,0:T(8,128)(2,1)S(1)} %get-tuple-element.20.after_ref.refs_4_), channel_id=1, source_target_pairs={{2,4},{4,2},{3,5},{5,3},{10,12},{12,10},{11,13},{13,11},{18,20},{2... | collective-permute-start | bytes 55304 | tf_op jit(solution)/shard_map/ppermute | solution.py:359
  18.7 2.9 %collective-permute-start.7 = (bf16[2,18,256]{2,1,0:T(8,128)(2,1)S(1)}, bf16[2,18,256]{2,1,0:T(8,128)(2,1)S(1)}, u32[]{:S(2)}, u32[]{:S(2)}) collective-permute-start(bf16[2,18,256]{2,1,0:T(8,128)(2,1)S(1)} %get-tuple-element.24.refs_5_), channel_id=1, source_target_pairs={{0,2},{2,0},{4,6},{6,4},{1,3},{3,1},{5,7},{7,5},{8,10},{10,8},{12,... | collective-permute-start | bytes 55304 | tf_op jit(solution)/shard_map/ppermute | solution.py:359
  21.6 1.5 %collective-permute-start.3 = (bf16[1,128,256]{2,1,0:T(8,128)(2,1)S(1)}, bf16[1,128,256]{2,1,0:T(8,128)(2,1)S(1)}, u32[]{:S(2)}, u32[]{:S(2)}) collective-permute-start(bf16[1,128,256]{2,1,0:T(8,128)(2,1)S(1)} %pick.2), channel_id=1, source_target_pairs={{0,1},{1,0},{2,3},{3,2},{4,5},{5,4},{6,7},{7,6},{8,9},{9,8},{10,11... | collective-permute-start | bytes 196616 | tf_op jit(solution)/shard_map/ppermute | solution.py:358
  23.1 0.4 %outer_rows.1.refs_4_.rows_ref = f32[2,128,256]{2,1,0:T(8,128)S(1)} custom-call(bf16[2,128,256]{2,1,0:T(8,128)(2,1)S(1)} %collective-permute-done.1.refs_2_.refs_0_, bf16[2,128,256]{2,1,0:T(8,128)(2,1)S(1)} %collective-permute-done.2.refs_3_.refs_1_, bf16[3,3,256,256]{3,2,1,0:T(8,128)(2,1)S(1)} %get-tuple-element.22.after_ref.refs_3_.refs_2_, ...), custom_call_target="tpu_custom_call" | custom-call | flops 201326592 | bytes 1048576 | tf_op jit(solution)/shard_map/outer_rows/pallas_call | solution.py:268
  23.5 0.0 collective-permute-done.5.refs_1_
  23.5 1.9 %accumulate.3.refs_4_.total_ref = f32[16,128,256]{2,1,0:T(8,128)S(1)} custom-call(bf16[2,128,256]{2,1,0:T(8,128)(2,1)S(1)} %bitcast.3, bf16[10,128,256]{2,1,0:T(8,128)(2,1)S(1)} %collective-permute-done.5.refs_1_, bf16[3,3,256,256]{3,2,1,0:T(8,128)(2,1)S(1)} %get-tuple-element.21.refs_3_.refs_2_.w_ref, f32[16,128,256]{2,1,0:T(8,128)S(1)} %accumulate.2.refs_3_, ...), custom_call_target="tpu_custom_call" | custom-call | flops 1811939328 | bytes 1048576 | tf_op jit(solution)/shard_map/accumulate/pallas_call | solution.py:129
  25.4 0.0 collective-permute-done.7.refs_1_
  25.5 0.0 collective-permute-done.6.refs_0_
  25.5 0.4 %outer_cols.1.cols_ref = f32[2,16,256]{2,1,0:T(8,128)S(1)} custom-call(bf16[2,18,256]{2,1,0:T(8,128)(2,1)S(1)} %collective-permute-done.6.refs_0_, bf16[2,18,256]{2,1,0:T(8,128)(2,1)S(1)} %collective-permute-done.7.refs_1_, bf16[3,3,256,256]{3,2,1,0:T(8,128)(2,1)S(1)} %get-tuple-element.22.after_ref.refs_3_.refs_2_, ...), custom_call_target="tpu_custom_call" | custom-call | flops 402653184 | bytes 1048576 | tf_op jit(solution)/shard_map/outer_cols/pallas_call | solution.py:268
  25.8 0.2 upper.1.after_ref.upper_ref
  26.1 1.4 %collective-permute-done.4.piece = bf16[3,128,256]{2,1,0:T(8,128)(2,1)S(1)} collective-permute-done((bf16[3,128,256]{2,1,0:T(8,128)(2,1)S(1)}, bf16[3,128,256]{2,1,0:T(8,128)(2,1)S(1)}, u32[]{:S(2)}, u32[]{:S(2)}) %collective-permute-start.4) | collective-permute-done | bytes 196640 | tf_op jit(solution)/shard_map/ppermute | solution.py:348
  27.4 0.7 %second.1 = (bf16[5,256,128]{2,1,0:T(8,128)(2,1)S(1)}, f32[3,128,256]{2,1,0:T(8,128)S(1)}) custom-call(bf16[3,128,256]{2,1,0:T(8,128)(2,1)S(1)} %collective-permute-done.4.piece, bf16[3,3,256,256]{3,2,1,0:T(8,128)(2,1)S(1)} %get-tuple-element.21.refs_3_.refs_2_.w_ref, f32[16,128,256]{2,1,0:T(8,128)S(1)} %accumulate.3.refs_4_.total_ref, ...), custom_call_target="tpu_custom_call" | custom-call | flops 452984832 | bytes 1048576 | tf_op jit(solution)/shard_map/second/pallas_call | solution.py:377
  28.1 0.0 collective-permute-done.3.piece
  28.2 1.3 %last.1 = bf16[256,16,128]{2,1,0:T(8,128)(2,1)} custom-call(bf16[1,128,256]{2,1,0:T(8,128)(2,1)S(1)} %collective-permute-done.3.piece, bf16[3,3,256,256]{3,2,1,0:T(8,128)(2,1)S(1)} %get-tuple-element.21.refs_3_.refs_2_.w_ref, f32[3,128,256]{2,1,0:T(8,128)S(1)} %get-tuple-element.25.rest_ref, f32[2,128,256]{2,1,0:T(8,128)S(1)} %outer_rows.1.refs_4_.rows_ref, ...), custom_call_target="tpu_custom_call" | custom-call | flops 301989888 | bytes 1048576 | tf_op jit(solution)/shard_map/last/pallas_call | solution.py:268
  (6 shorter events, 0.1 us)
Async XLA Ops:
  1.6 7.7 %collective-permute-start = (bf16[288,256]{1,0:T(8,128)(2,1)S(1)}, bf16[288,256]{1,0:T(8,128)(2,1)S(1)}, u32[]{:S(2)}, u32[]{:S(2)}) collective-permute-start(bf16[288,256]{1,0:T(8,128)(2,1)S(1)} %get-tuple-element.17.refs_0_), channel_id=1, source_target_pairs={{0,1},{1,0},{2,3},{3,2},{4,5},{5,4},{6,7},{7,6},{8,9},{9,8},{10,11... | collective-permute-start | bytes 442376 | tf_op jit(solution)/shard_map/ppermute | solution.py:335
  4.6 18.9 %collective-permute-start.5 = (bf16[10,128,256]{2,1,0:T(8,128)(2,1)S(1)}, bf16[10,128,256]{2,1,0:T(8,128)(2,1)S(1)}, u32[]{:S(2)}, u32[]{:S(2)}) collective-permute-start(bf16[10,128,256]{2,1,0:T(8,128)(2,1)S(1)} %get-tuple-element.23.refs_1_), channel_id=1, source_target_pairs={{0,1},{1,0},{2,3},{3,2},{4,5},{5,4},{6,7},{7,6},{8,9},{9,8},{10,11... | collective-permute-start | bytes 1966088 | tf_op jit(solution)/shard_map/ppermute | solution.py:336
  6.4 21.0 %collective-permute-start.4 = (bf16[3,128,256]{2,1,0:T(8,128)(2,1)S(1)}, bf16[3,128,256]{2,1,0:T(8,128)(2,1)S(1)}, u32[]{:S(2)}, u32[]{:S(2)}) collective-permute-start(bf16[3,128,256]{2,1,0:T(8,128)(2,1)S(1)} %pick.3), channel_id=1, source_target_pairs={{0,1},{1,0},{2,3},{3,2},{4,5},{5,4},{6,7},{7,6},{8,9},{9,8},{10,11... | collective-permute-start | bytes 589832 | tf_op jit(solution)/shard_map/ppermute | solution.py:348
  8.5 6.6 %copy-start = (f32[512]{0:T(512)S(1)}, f32[512]{0:T(512)}, u32[]{:S(2)}) copy-start(f32[512]{0:T(512)} %param.5) | copy-start | bytes 6148
  9.3 8.3 %collective-permute-start.1 = (bf16[2,128,256]{2,1,0:T(8,128)(2,1)S(1)}, bf16[2,128,256]{2,1,0:T(8,128)(2,1)S(1)}, u32[]{:S(2)}, u32[]{:S(2)}) collective-permute-start(bf16[2,128,256]{2,1,0:T(8,128)(2,1)S(1)} %get-tuple-element.18), channel_id=1, source_target_pairs={{8,16},{16,8},{9,17},{17,9},{10,18},{18,10},{11,19},{19,11},{12,20... | collective-permute-start | bytes 393224 | tf_op jit(solution)/shard_map/ppermute | solution.py:352
  10.0 7.9 %collective-permute-start.2 = (bf16[2,128,256]{2,1,0:T(8,128)(2,1)S(1)}, bf16[2,128,256]{2,1,0:T(8,128)(2,1)S(1)}, u32[]{:S(2)}, u32[]{:S(2)}) collective-permute-start(bf16[2,128,256]{2,1,0:T(8,128)(2,1)S(1)} %get-tuple-element.19), channel_id=1, source_target_pairs={{0,8},{8,0},{16,24},{24,16},{1,9},{9,1},{17,25},{25,17},{2,10},{10... | collective-permute-start | bytes 393224 | tf_op jit(solution)/shard_map/ppermute | solution.py:352
  18.0 7.5 %collective-permute-start.6 = (bf16[2,18,256]{2,1,0:T(8,128)(2,1)S(1)}, bf16[2,18,256]{2,1,0:T(8,128)(2,1)S(1)}, u32[]{:S(2)}, u32[]{:S(2)}) collective-permute-start(bf16[2,18,256]{2,1,0:T(8,128)(2,1)S(1)} %get-tuple-element.20.after_ref.refs_4_), channel_id=1, source_target_pairs={{2,4},{4,2},{3,5},{5,3},{10,12},{12,10},{11,13},{13,11},{18,20},{2... | collective-permute-start | bytes 55304 | tf_op jit(solution)/shard_map/ppermute | solution.py:359
  18.7 6.8 %collective-permute-start.7 = (bf16[2,18,256]{2,1,0:T(8,128)(2,1)S(1)}, bf16[2,18,256]{2,1,0:T(8,128)(2,1)S(1)}, u32[]{:S(2)}, u32[]{:S(2)}) collective-permute-start(bf16[2,18,256]{2,1,0:T(8,128)(2,1)S(1)} %get-tuple-element.24.refs_5_), channel_id=1, source_target_pairs={{0,2},{2,0},{4,6},{6,4},{1,3},{3,1},{5,7},{7,5},{8,10},{10,8},{12,... | collective-permute-start | bytes 55304 | tf_op jit(solution)/shard_map/ppermute | solution.py:359
  21.6 6.6 %collective-permute-start.3 = (bf16[1,128,256]{2,1,0:T(8,128)(2,1)S(1)}, bf16[1,128,256]{2,1,0:T(8,128)(2,1)S(1)}, u32[]{:S(2)}, u32[]{:S(2)}) collective-permute-start(bf16[1,128,256]{2,1,0:T(8,128)(2,1)S(1)} %pick.2), channel_id=1, source_target_pairs={{0,1},{1,0},{2,3},{3,2},{4,5},{5,4},{6,7},{7,6},{8,9},{9,8},{10,11... | collective-permute-start | bytes 196616 | tf_op jit(solution)/shard_map/ppermute | solution.py:358
